TPU v7x, 32 devices: a whole 2x2x4 slice. The times are simulated.
32 devices in a mesh: grp: 2 (over y), pix: 4 (over z), ori: 2 (over x), pat: 2 (over core).
Axes of the slice: x: 2, y: 2, z: 4, core: 2. Of those that a mesh axis runs over, the one named last changes fastest.
Arguments:
- patterns: bfloat16 [2048, 65536], P(('grp', 'pat'), 'pix'), parts along dimension 0, may hold values from -40 to 40
- model: bfloat16 [131072, 2048], P(('grp', 'pix'), 'ori'), parts along dimension 0, may hold values from -6 to 6
- scale_table: float32 [32], P('grp'), parts along dimension 0, may hold values from 0.5 to 2
- scale_index: int32 [2048], P(('grp', 'pat')), parts along dimension 0, may hold values from 0 to 15
- weight_table: float32 [16], P('grp'), parts along dimension 0, may hold values from -1 to 1
- weight_class: int32 [4096], P(('grp', 'ori')), parts along dimension 0, may hold values from 0 to 7
Outputs:
- new_model: bfloat16 [131072, 2048], P(('grp', 'pix', 'pat'), 'ori'), parts along dimension 0
There are 2 independent parts, one for each index of `grp`. A program takes and returns all parts, laid end to end along the dimension named above; each array names one. Nothing has to cross between parts.
All inputs are finite; a program needn't handle non-finite values.
Results may differ from a plain program's by a relative error of at most 0.0034.
Values may be sent and summed in bfloat16 or wider, within the bound.
No kernel may reach another device: no remote copies, remote signals or barrier semaphores. Data moves between devices by JAX's collectives and lax.ppermute only.
A program may use at most 256 MiB of HBM per device.

v0:
```python
import jax
import jax.numpy as jnp
from jax import lax
from jax.sharding import PartitionSpec as P

P_SIZE = 65536


prior_weight = 0.5


def table_lookup(table, index):
    levels = jnp.arange(table.shape[0], dtype=jnp.int32)
    return jnp.sum(jnp.where(index[:, None] == levels[None, :], table[None, :], 0.0), axis=1)


def normalize(scores, phi):
    top = jnp.max(scores, axis=1)
    top = lax.pmax(top, "ori")
    total = lax.psum(jnp.sum(jnp.exp(scores - top[:, None]), axis=1), "ori")
    lse = top + jnp.log(total)
    prob = jnp.exp(scores - lse[:, None])
    weights = (prob * phi[:, None]).astype(jnp.bfloat16)
    den_part = jnp.sum(prob * (phi * phi)[:, None], axis=0)
    return (weights, den_part)


def local(patterns, model, scale_table, scale_index, weight_table, weight_class):
    phi = table_lookup(scale_table, scale_index)
    logw = table_lookup(weight_table, weight_class)
    cross = jnp.dot(patterns, model, preferred_element_type=jnp.float32)
    squares = jnp.sum(jnp.square(model.astype(jnp.float32)), axis=0)
    beta = P_SIZE ** (-0.5)
    partial_term = beta * (phi[:, None] * cross - 0.5 * (phi * phi)[:, None] * squares[None, :])
    share = lax.psum_scatter(partial_term, "pix", scatter_dimension=0, tiled=True)
    count = share.shape[0]
    phi_share = lax.dynamic_slice_in_dim(phi, lax.axis_index("pix") * count, count)
    weights, den_part = normalize(share + logw[None, :], phi_share)
    den = prior_weight + lax.psum(den_part, ("pix", "pat"))
    weights = lax.all_gather(weights, "pix", axis=0, tiled=True)
    half = model.shape[0] // lax.axis_size("pat")
    numer = lax.psum_scatter(
        lax.dot_general(
            patterns, weights, (((0,), (0,)), ((), ())), preferred_element_type=jnp.float32
        ),
        "pat",
        scatter_dimension=0,
        tiled=True,
    )
    own_rows = lax.dynamic_slice_in_dim(model, lax.axis_index("pat") * half, half, 0)
    numer = numer + prior_weight * own_rows.astype(jnp.float32)
    return (numer / den[None, :]).astype(jnp.bfloat16)


def solution(mesh):
    placed = (
        P(("grp", "pat"), "pix"),
        P(("grp", "pix"), "ori"),
        P("grp"),
        P(("grp", "pat")),
        P("grp"),
        P(("grp", "ori")),
    )
    return jax.shard_map(
        local,
        mesh=mesh,
        in_specs=placed,
        out_specs=P(("grp", "pix", "pat"), "ori"),
        check_vma=False,
    )
```

profile of v0, /device:TPU:0, one launch (start us, length us, event | category | flops | bytes accessed | tf_op | source)
XLA Modules:
  0.0 301.9 jit_solution(14089476186193129577)
XLA Ops:
  6.5 0.0 reduce-scatter.3.cloned.1.call-start
  6.5 0.8 select_reduce_fusion.1
  7.3 19.1 %multiply_reduce_fusion = f32[1024]{0:T(1024)S(1)} fusion(bf16[16384,1024]{1,0:T(8,128)(2,1)} %param.7), kind=kLoop, calls=%fused_computation | loop fusion | flops 50330624 | bytes 33558528 | tf_op jit(solution)/shard_map/reduce_sum | solution.py:32
  26.4 0.0 copy-start
  26.4 0.0 copy-start.1
  26.4 27.0 %subtract_multiply_fusion = f32[512,1024]{1,0:T(8,128)} fusion(bf16[512,16384]{1,0:T(8,128)(2,1)} %param.6, bf16[16384,1024]{1,0:T(8,128)(2,1)} %param.7, f32[1024]{0:T(1024)S(1)} %multiply_reduce_fusion, f32[512]{0:T(512)S(1)} %multiply_multiply_fusion, f32[512]{0:T(512)S(1)} %select_reduce_fusion.1), kind=kOutput, calls=%fused_computation.3 | convolution fusion | flops 17181966336 | bytes 52436992 | tf_op jit(solution)/shard_map/dot_general | solution.py:31
  53.4 0.0 reduce-scatter.3.cloned.1.call-update
  53.5 0.0 all-gather.2.cloned.1.call-start
  53.5 0.1 fusion
  53.6 0.0 copy-done
  53.6 0.0 copy-done.1
  53.6 0.1 select_reduce_fusion
  53.7 46.3 %reduce-scatter.3.cloned.1.call-done = f32[128,1024]{1,0:T(8,128)} async-done(((f32[512,1024]{1,0:T(8,128)}), f32[128,1024]{1,0:T(8,128)}) %reduce-scatter.3.cloned.1.call-update) | async-done | bytes 524304 | tf_op jit(solution)/shard_map/reduce_scatter | solution.py:35
  100.0 1.2 add_reduce_fusion
  101.1 4.9 %pmax.7 = f32[128]{0:T(128)S(1)} all-reduce(f32[128]{0:T(128)S(1)} %add_reduce_fusion), channel_id=1, replica_groups=mesh['grp'=2,'pix'=4,'ori'=2,'pat'=2] {'ori'}, use_global_device_ids=true, to_apply=%region_5.6 | all-reduce | flops 128 | bytes 1024 | tf_op jit(solution)/shard_map/pmax | solution.py:19
  106.0 1.3 exponential_reduce_fusion
  107.3 4.9 %psum.14 = f32[128]{0:T(128)S(1)} all-reduce(f32[128]{0:T(128)S(1)} %exponential_reduce_fusion), channel_id=1, replica_groups=mesh['grp'=2,'pix'=4,'ori'=2,'pat'=2] {'ori'}, use_global_device_ids=true, to_apply=%region_7.8 | all-reduce | flops 128 | bytes 1024 | tf_op jit(solution)/shard_map/psum | solution.py:20
  112.3 1.9 multiply_reduce_fusion.1
  114.2 0.0 all-gather.2.cloned.1.call-update
  114.2 0.0 reduce-scatter.5.cloned.1.call-start
  114.3 27.3 %all-gather.2.cloned.1.call-done = bf16[512,1024]{1,0:T(8,128)(2,1)} async-done(((bf16[128,1024]{1,0:T(8,128)(2,1)}), bf16[512,1024]{1,0:T(8,128)(2,1)}) %all-gather.2.cloned.1.call-update) | async-done | bytes 1048592 | tf_op jit(solution)/shard_map/all_gather | solution.py:40
  141.6 32.5 %convolution_bitcast_fusion = f32[16384,1024]{0,1:T(8,128)} fusion(bf16[512,1024]{1,0:T(8,128)(2,1)} %all-gather.2.cloned.1.call-done, bf16[512,16384]{1,0:T(8,128)(2,1)} %param.6), kind=kOutput, calls=%fused_computation.1 | convolution fusion | flops 17179869184 | bytes 84934656 | tf_op jit(solution)/shard_map/dot_general | solution.py:43
  174.1 0.0 reduce-scatter.5.cloned.1.call-update
  174.2 15.2 %constant_dynamic-slice_fusion = bf16[8192,1024]{1,0:T(8,128)(2,1)} fusion(bf16[16384,1024]{1,0:T(8,128)(2,1)} %param.7, s32[]{:T(128)S(6)} %select_n.17), kind=kLoop, calls=%fused_computation.16 | loop fusion | bytes 33554436 | tf_op jit(solution)/shard_map/dynamic_slice | solution.py:50
  189.3 23.4 %copy.11 = bf16[8192,1024]{0,1:T(8,128)(2,1)} copy(bf16[8192,1024]{1,0:T(8,128)(2,1)} %constant_dynamic-slice_fusion) | data formatting | bytes 33554432
  212.8 14.5 %psum.15 = f32[1024]{0:T(1024)S(1)} all-reduce(f32[1024]{0:T(1024)S(1)} %get-tuple-element.7), channel_id=1, replica_groups=mesh['grp'=2,'pix'=4,'ori'=2,'pat'=2] {'pix','pat'}, use_global_device_ids=true, to_apply=%region_10.11 | all-reduce | flops 1024 | bytes 8192 | tf_op jit(solution)/shard_map/psum | solution.py:39
  227.2 23.6 %reduce-scatter.5.cloned.1.call-done = f32[8192,1024]{0,1:T(8,128)} async-done(((f32[16384,1024]{0,1:T(8,128)}), f32[8192,1024]{0,1:T(8,128)}) %reduce-scatter.5.cloned.1.call-update) | async-done | bytes 33554448 | tf_op jit(solution)/shard_map/reduce_scatter | solution.py:42
  250.8 22.1 %divide_convert_fusion = bf16[8192,1024]{0,1:T(8,128)(2,1)} fusion(f32[8192,1024]{0,1:T(8,128)} %reduce-scatter.5.cloned.1.call-done, bf16[8192,1024]{0,1:T(8,128)(2,1)} %copy.11, f32[1024]{0:T(1024)S(1)} %broadcast_add_fusion), kind=kLoop, calls=%fused_computation.2 | loop fusion | flops 41943040 | bytes 67112960 | tf_op jit(solution)/shard_map/convert_element_type | solution.py:52
  273.0 22.4 %copy.10 = bf16[8192,1024]{1,0:T(8,128)(2,1)} copy(bf16[8192,1024]{0,1:T(8,128)(2,1)} %divide_convert_fusion) | data formatting | bytes 33554432 | tf_op jit(solution)/shard_map/convert_element_type | solution.py:52
  (3 shorter events, 0.0 us)
Async XLA Ops:
  6.5 93.4 %reduce-scatter.3.cloned.1.call-start = ((), (), s32[]{:S(2)}) async-start(), calls=%async_computation.2 | async-start | bytes 2621440 | tf_op jit(solution)/shard_map/reduce_scatter | solution.py:35
  26.4 27.2 %copy-start = (s32[1024]{0:T(1024)S(1)}, s32[1024]{0:T(1024)}, u32[]{:S(2)}) copy-start(s32[1024]{0:T(1024)} %param.11) | copy-start | bytes 12292
  26.4 27.2 %copy-start.1 = (f32[8]{0:T(128)S(1)}, f32[8]{0:T(128)}, u32[]{:S(2)}) copy-start(f32[8]{0:T(128)} %param.10) | copy-start | bytes 100
  53.5 88.1 %all-gather.2.cloned.1.call-start = ((), (), s32[]{:S(2)}) async-start(), calls=%async_computation.3 | async-start | bytes 1310720 | tf_op jit(solution)/shard_map/all_gather | solution.py:40
  114.2 136.6 %reduce-scatter.5.cloned.1.call-start = ((), (), s32[]{:S(2)}) async-start(), calls=%async_computation.4 | async-start | bytes 100663296 | tf_op jit(solution)/shard_map/reduce_scatter | solution.py:42
Sparse Core Ops, SparseCore 0:
  53.6 46.3 reduce-scatter.2
  114.3 27.2 all-gather.1
  174.3 76.5 reduce-scatter.4
where the time goes:
time: 303 us; the launch traced here: 302 us
  waiting for transfers between devices  97.3 us (32%)
  local copies, waits for them, and re-layouts  61 us (20%)
  matrix products  59.5 us (20%)
  other arithmetic  46.5 us (15%)
  blocking collectives  24.3 us (8%)
  between operations  13.1 us (4%)
    reduce_scatter x1, waiting for transfers between devices, local(): lax.psum_scatter(partial_term, 'pix', scatter_dimension=0, tiled=True)  46.3 us
    dot_general x1, matrix products, local(): lax.dot_general(patterns, weights, (((0,), (0,)), ((), ())), preferred_el...  32.5 us
    all_gather x1, waiting for transfers between devices, local(): weights = lax.all_gather(weights, 'pix', axis=0, tiled=True)  27.3 us
    dot_general x1, matrix products, local(): cross = jnp.dot(patterns, model, preferred_element_type=jnp.float32)  27 us
    reduce_scatter x1, waiting for transfers between devices, local(): lax.psum_scatter(lax.dot_general(patterns, weights, (((0,), (0,)), ((), (...  23.6 us
    unnamed x5, local copies, waits for them, and re-layouts  23.4 us
    convert_element_type x1, local copies, waits for them, and re-layouts, local(): return (numer / den[None, :]).astype(jnp.bfloat16)  22.4 us
    convert_element_type x1, other arithmetic, local(): return (numer / den[None, :]).astype(jnp.bfloat16)  22.1 us
  transfers between devices with their start and end apart: 3, of which 3 were waited for; matrix products, arithmetic and copies ran while one was open for 13% of the time, Pallas kernels for 0%

commit v1 on v0

v1 whole, which is shorter than its diff:
```python
import functools

import jax
import jax.numpy as jnp
from jax import lax
from jax.experimental import pallas as pl
from jax.experimental.pallas import tpu as pltpu
from jax.sharding import PartitionSpec as P

prior_weight = 0.5
MIB = 1 << 20
SLOTS = 6


def table_lookup(table, index):
    levels = jnp.arange(table.shape[0], dtype=jnp.int32)
    return jnp.sum(jnp.where(index[:, None] == levels[None, :], table[None, :], 0.0), axis=1)


def params(limit):
    return pltpu.CompilerParams(vmem_limit_bytes=limit)


def cost(flops, moved):
    return pl.CostEstimate(flops=flops, bytes_accessed=moved, transcendentals=0)


def bit_reverse(value, bits):
    return sum(((value >> i) & 1) << (bits - 1 - i) for i in range(bits))


def cross_kernel(where, phi, patterns, model, send, keep, pbuf, mbuf, acc, squares, psem, msem, *, column, tk, steps, beta):
    tn = acc.shape[1]

    def copies(i):
        slot = lax.rem(i, SLOTS)
        at = pl.multiple_of(i * tk, tk)
        return (
            pltpu.make_async_copy(patterns.at[:, pl.ds(at, tk)], pbuf.at[slot], psem.at[slot]),
            pltpu.make_async_copy(model.at[pl.ds(at, tk), pl.ds(column, tn)], mbuf.at[slot], msem.at[slot]),
        )

    for i in range(min(SLOTS - 1, steps)):
        for copy in copies(i):
            copy.start()
    acc[...] = jnp.zeros_like(acc)
    squares[...] = jnp.zeros_like(squares)

    def body(i, carry):
        for copy in copies(i):
            copy.wait()

        @pl.when(i + SLOTS - 1 < steps)
        def _():
            for copy in copies(i + SLOTS - 1):
                copy.start()

        slot = lax.rem(i, SLOTS)
        tile = mbuf[slot]
        acc[...] += jnp.dot(pbuf[slot], tile, preferred_element_type=jnp.float32)
        wide = tile.astype(jnp.float32)
        squares[...] += jnp.sum((wide * wide).reshape(tk // 8, 8, tn), axis=0)
        return carry

    lax.fori_loop(0, steps, body, 0)
    sq = jnp.sum(squares[...], axis=0, keepdims=True)
    scale = phi[...]
    acc[...] = beta * (scale * acc[...] - 0.5 * (scale * scale) * sq)
    half = send.shape[0]
    send[...] = acc[pl.ds(pl.multiple_of((1 - where[0]) * half, half), half), :]
    keep[...] = acc[pl.ds(pl.multiple_of(where[0] * half, half), half), :]


def cross_chunk(where, phi, patterns, model, column, tn, beta):
    rows, depth = patterns.shape
    tk = min(1024, depth)
    half = rows // 2
    out = jax.ShapeDtypeStruct((half, tn), jnp.float32)
    anywhere = pl.BlockSpec(memory_space=pl.ANY)
    return pl.pallas_call(
        functools.partial(cross_kernel, column=column, tk=tk, steps=depth // tk, beta=beta),
        out_shape=(out, out),
        grid_spec=pltpu.PrefetchScalarGridSpec(
            num_scalar_prefetch=1,
            grid=(1,),
            in_specs=[pl.BlockSpec((rows, 1), lambda i, s: (0, 0)), anywhere, anywhere],
            out_specs=(pl.BlockSpec((half, tn), lambda i, s: (0, 0)),) * 2,
            scratch_shapes=[
                pltpu.VMEM((SLOTS, rows, tk), jnp.bfloat16),
                pltpu.VMEM((SLOTS, tk, tn), jnp.bfloat16),
                pltpu.VMEM((rows, tn), jnp.float32),
                pltpu.VMEM((8, tn), jnp.float32),
                pltpu.SemaphoreType.DMA((SLOTS,)),
                pltpu.SemaphoreType.DMA((SLOTS,)),
            ],
        ),
        compiler_params=params(24 * MIB),
        cost_estimate=cost(2 * rows * depth * tn, 2 * depth * (rows + tn)),
        name="cross",
    )(where, phi, patterns, model)


def softmax_kernel(where, table, classes, *refs, chunks, terms):
    parts, (exps, stats) = refs[:-2], refs[-2:]
    count = exps.shape[0]
    tn = exps.shape[1] // chunks
    logw = jnp.zeros(classes.shape, jnp.float32)
    for q in range(table.shape[0]):
        logw = logw + jnp.where(classes[...] == q, table[q], 0.0)
    for c in range(chunks):
        total = None
        for t in range(terms):
            rows = pl.ds(pl.multiple_of(where[t], count), count)
            part = parts[c * terms + t][rows, :]
            total = part if total is None else total + part
        exps[:, c * tn : (c + 1) * tn] = total + logw[:, c * tn : (c + 1) * tn]
    top = jnp.max(exps[...], axis=1, keepdims=True)
    exps[...] = jnp.exp(exps[...] - top)
    total = jnp.sum(exps[...], axis=1, keepdims=True)
    lanes = (count, 128)
    stats[:8, :] = jnp.transpose(jnp.broadcast_to(top, lanes))[:8, :]
    stats[8:, :] = jnp.transpose(jnp.broadcast_to(total, lanes))[:8, :]


def softmax_stage(where, table, classes, parts, count, chunks):
    terms = len(parts) // chunks
    columns = classes.shape[1]
    full = pl.BlockSpec(memory_space=pltpu.VMEM)
    scalar = pl.BlockSpec(memory_space=pltpu.SMEM)
    return pl.pallas_call(
        functools.partial(softmax_kernel, chunks=chunks, terms=terms),
        out_shape=(
            jax.ShapeDtypeStruct((count, columns), jnp.float32),
            jax.ShapeDtypeStruct((16, count), jnp.float32),
        ),
        in_specs=[scalar, scalar, full] + [full] * len(parts),
        out_specs=(full, full),
        compiler_params=params(16 * MIB),
        name="softmax",
    )(where, table, classes, *parts)


def combine(mine, other):
    top = jnp.maximum(mine[:8], other[:8])
    total = mine[8:] * jnp.exp(mine[:8] - top) + other[8:] * jnp.exp(other[:8] - top)
    return jnp.concatenate([top, total], axis=0)


def weight_kernel(where, phi, exps, own, mine, other, *outs):
    count = exps.shape[0]

    def column(row):
        return jnp.transpose(jnp.broadcast_to(row[:1, :], (128, count)))[:, :1]

    top = jnp.maximum(mine[:8, :], other[:8, :])
    total = mine[8:, :] * jnp.exp(mine[:8, :] - top) + other[8:, :] * jnp.exp(other[:8, :] - top)
    factor = column(jnp.exp(own[:8, :] - top) / total)
    factor = factor * phi[pl.ds(pl.multiple_of(where[0], count), count), :]
    tn = outs[0].shape[1]
    for c, out in enumerate(outs):
        out[...] = (exps[:, c * tn : (c + 1) * tn] * factor).astype(jnp.bfloat16)


def weight_stage(where, phi, exps, own, mine, other, chunks):
    count, columns = exps.shape
    full = pl.BlockSpec(memory_space=pltpu.VMEM)
    return pl.pallas_call(
        weight_kernel,
        out_shape=(jax.ShapeDtypeStruct((count, columns // chunks), jnp.bfloat16),) * chunks,
        in_specs=[pl.BlockSpec(memory_space=pltpu.SMEM)] + [full] * 5,
        out_specs=(full,) * chunks,
        compiler_params=params(8 * MIB),
        name="weights",
    )(where, phi, exps, own, mine, other)


def pack_kernel(where, *refs):
    parts, out = refs[:-1], refs[-1]
    count = parts[0].shape[0]
    for d, part in enumerate(parts):
        out[pl.ds(pl.multiple_of(where[d], count), count), :] = part[...]


def pack(where, parts):
    count, tn = parts[0].shape
    full = pl.BlockSpec(memory_space=pltpu.VMEM)
    return pl.pallas_call(
        pack_kernel,
        out_shape=jax.ShapeDtypeStruct((count * len(parts), tn), jnp.bfloat16),
        in_specs=[pl.BlockSpec(memory_space=pltpu.SMEM)] + [full] * len(parts),
        out_specs=full,
        compiler_params=params(8 * MIB),
        name="pack",
    )(where, *parts)


def numer_kernel(where, pown, psib, wown, wsib, fown, fsib, model, *refs, sub):
    out, scale = refs[-2:]

    @pl.when(pl.program_id(0) == 0)
    def _():
        den = jnp.sum(wown[...].astype(jnp.float32) * fown[...], axis=0, keepdims=True)
        den = den + jnp.sum(wsib[...].astype(jnp.float32) * fsib[...], axis=0, keepdims=True)
        scale[...] = 1.0 / (prior_weight + den)

    dims = (((0,), (0,)), ((), ()))
    for r in range(0, out.shape[0], sub):
        rows = slice(r, r + sub)
        acc = lax.dot_general(pown[:, rows], wown[...], dims, preferred_element_type=jnp.float32)
        acc = acc + lax.dot_general(psib[:, rows], wsib[...], dims, preferred_element_type=jnp.float32)
        acc = acc + prior_weight * model[rows, :].astype(jnp.float32)
        out[rows, :] = (acc * scale[...]).astype(jnp.bfloat16)


def numer_chunk(where, pown, psib, wown, wsib, fown, fsib, model, chunk, previous):
    depth, tn = wown.shape
    pixels, columns = model.shape[0] // 2, model.shape[1]
    tm = min(1024, pixels)
    blocks = pixels // tm
    in_specs = [
        pl.BlockSpec((depth, tm), lambda i, s: (0, s[0] * blocks + i)),
        pl.BlockSpec((depth, tm), lambda i, s: (0, s[0] * blocks + i)),
        pl.BlockSpec((depth, tn), lambda i, s: (0, 0)),
        pl.BlockSpec((depth, tn), lambda i, s: (0, 0)),
        pl.BlockSpec((depth, 1), lambda i, s: (0, 0)),
        pl.BlockSpec((depth, 1), lambda i, s: (0, 0)),
        pl.BlockSpec((tm, tn), lambda i, s: (s[0] * blocks + i, chunk)),
    ]
    args = [where, pown, psib, wown, wsib, fown, fsib, model]
    aliases = {}
    if previous is not None:
        in_specs.append(pl.BlockSpec(memory_space=pl.ANY))
        args.append(previous)
        aliases = {len(args) - 1: 0}
    return pl.pallas_call(
        functools.partial(numer_kernel, sub=min(256, tm)),
        out_shape=jax.ShapeDtypeStruct((pixels, columns), jnp.bfloat16),
        grid_spec=pltpu.PrefetchScalarGridSpec(
            num_scalar_prefetch=1,
            grid=(blocks,),
            in_specs=in_specs,
            out_specs=pl.BlockSpec((tm, tn), lambda i, s: (i, chunk)),
            scratch_shapes=[pltpu.VMEM((1, tn), jnp.float32)],
        ),
        input_output_aliases=aliases,
        compiler_params=params(24 * MIB),
        cost_estimate=cost(4 * depth * pixels * tn, 4 * pixels * (depth + tn)),
        name="numer",
    )(*args)


def exchange(value, axis, size, distance):
    return lax.ppermute(value, axis, [(i, i ^ distance) for i in range(size)])


def local(patterns, model, scale_table, scale_index, weight_table, weight_class, *, sizes):
    pix, ori = sizes["pix"], sizes["ori"]
    hops = pix.bit_length() - 1
    rows, columns = patterns.shape[0], model.shape[1]
    count = rows // pix
    tn = min(256, columns)
    chunks = columns // tn
    beta = (patterns.shape[1] * pix) ** -0.5
    place = lax.axis_index("pix")
    bits = [(place >> i) & 1 for i in range(hops)]

    phi = table_lookup(scale_table, scale_index)[:, None]
    phi_sib = exchange(phi, "pat", 2, 1)
    classes = weight_class[None, :]

    first = jnp.stack([bits[0]])
    held = []
    for c in range(chunks):
        send, keep = cross_chunk(first, phi, patterns, model, c * tn, tn, beta)
        terms = [keep, exchange(send, "pix", pix, 1)]
        offsets = [0, 0]
        size = rows // 2
        for hop in range(1, hops):
            size //= 2
            away = None
            for k, term in enumerate(terms):
                part = lax.dynamic_slice_in_dim(term, offsets[k] + (1 - bits[hop]) * size, size, 0)
                away = part if away is None else away + part
            offsets = [o + bits[hop] * size for o in offsets] + [0]
            terms.append(exchange(away, "pix", pix, 1 << hop))
        held.extend(terms)
    behind, _ = lax.optimization_barrier((patterns, held[-len(terms)]))
    psib = exchange(behind, "pat", 2, 1)

    where = jnp.stack([jnp.asarray(o, jnp.int32) for o in offsets])
    exps, own = softmax_stage(where, weight_table, classes, held, count, chunks)
    mine = own
    other = None
    for hop in range(ori.bit_length() - 1):
        if other is not None:
            mine = combine(mine, other)
        other = exchange(mine, "ori", ori, 1 << hop)
    share = bit_reverse(place, hops)
    weights = weight_stage(jnp.stack([share * count]), phi, exps, own, mine, other, chunks)

    order = jnp.stack([(share ^ bit_reverse(d, hops)) * count for d in range(pix)])
    side = jnp.stack([lax.axis_index("pat")])
    result = None
    for c in range(chunks):
        parts = [weights[c]] + [exchange(weights[c], "pix", pix, d) for d in range(1, pix)]
        wown = pack(order, parts)
        wsib = exchange(wown, "pat", 2, 1)
        result = numer_chunk(side, patterns, psib, wown, wsib, phi, phi_sib, model, c, result)
    return result


def solution(mesh):
    placed = (
        P(("grp", "pat"), "pix"),
        P(("grp", "pix"), "ori"),
        P("grp"),
        P(("grp", "pat")),
        P("grp"),
        P(("grp", "ori")),
    )
    return jax.shard_map(
        functools.partial(local, sizes=dict(mesh.shape)),
        mesh=mesh,
        in_specs=placed,
        out_specs=P(("grp", "pix", "pat"), "ori"),
        check_vma=False,
    )
```

time: 303 us -> 162 us (0.53)
  Pallas kernels: 0 us -> 93.5 us
  local copies, waits for them, and re-layouts: 61 us -> 0.16 us
  matrix products: 59.5 us -> 0 us
  waiting for transfers between devices: 97.3 us -> 38.6 us
  other arithmetic: 46.5 us -> 1.66 us
  starting transfers between devices: 0.09 us -> 27.5 us
  blocking collectives: 24.3 us -> 0 us
  between operations: 13.1 us -> 0.18 us
    pallas_call x0 -> x14, Pallas kernels: none -> 93.5 us  [the longest x4 52.7 us: numer_chunk(): pl.pallas_call(functools.partial(numer_kernel, sub=min(256, tm)), out_sha...]
    reduce_scatter x2 -> x0, waiting for transfers between devices: 69.9 us -> none  [the longest x1 46.3 us: local(): lax.psum_scatter(partial_term, 'pix', scatter_dimension=0, tiled=True)]
    dot_general x2 -> x0, matrix products: 59.5 us -> none  [the longest x1 32.5 us: local(): lax.dot_general(patterns, weights, (((0,), (0,)), ((), ())), preferred_el...]
    ppermute x0 -> x27, waiting for transfers between devices: none -> 38.6 us  [exchange(): return lax.ppermute(value, axis, [(i, i ^ distance) for i in range(size)])]
    ppermute x0 -> x27, starting transfers between devices: none -> 27.5 us  [exchange(): return lax.ppermute(value, axis, [(i, i ^ distance) for i in range(size)])]
    all_gather x1 -> x0, waiting for transfers between devices: 27.3 us -> none  [local(): weights = lax.all_gather(weights, 'pix', axis=0, tiled=True)]
    unnamed x5 -> x4, local copies, waits for them, and re-layouts: 23.4 us -> 0.01 us
    convert_element_type x1 -> x0, local copies, waits for them, and re-layouts: 22.4 us -> none  [local(): return (numer / den[None, :]).astype(jnp.bfloat16)]
  transfers between devices with their start and end apart: 3 -> 27, of which waited for: 3 -> 12; matrix products, arithmetic and copies ran while one was open for 13% -> 1% of each run, Pallas kernels for 0% -> 44%
where the time goes in v1:
time: 162 us
  Pallas kernels  93.5 us (58%)
  waiting for transfers between devices  38.6 us (24%)
  starting transfers between devices  27.5 us (17%)
  other arithmetic  1.66 us (1%)
    pallas_call x4, Pallas kernels, numer_chunk(): pl.pallas_call(functools.partial(numer_kernel, sub=min(256, tm)), out_sha...  52.7 us
    ppermute x27, waiting for transfers between devices, exchange(): return lax.ppermute(value, axis, [(i, i ^ distance) for i in range(size)])  38.6 us
    pallas_call x4, Pallas kernels, cross_chunk(): pl.pallas_call(functools.partial(cross_kernel, column=column, tk=tk, step...  37.6 us
    ppermute x27, starting transfers between devices, exchange(): return lax.ppermute(value, axis, [(i, i ^ distance) for i in range(size)])  27.5 us
  transfers between devices with their start and end apart: 27, of which 12 were waited for; matrix products, arithmetic and copies ran while one was open for 1% of the time, Pallas kernels for 44%

profile of v1, /device:TPU:0, one launch (start us, length us, event | category | flops | bytes accessed | tf_op | source)
XLA Modules:
  0.0 161.6 jit_solution(12077584973015720639)
XLA Ops:
  0.0 0.8 select_reduce_fusion
  0.8 0.1 copy.20.phi.fown
  0.9 9.4 %cross.4 = (f32[256,256]{1,0:T(8,128)S(1)}, f32[256,256]{1,0:T(8,128)S(1)}) custom-call(s32[1]{0:T(128)} %bitcast.1.where, f32[512,1]{1,0:T(8,128)S(1)} %copy.20.phi.fown, bf16[512,16384]{1,0:T(8,128)(2,1)} %pown.7, bf16[16384,1024]{1,0:T(8,128)(2,1)} %model.15), custom_call_target="tpu_custom_call" | custom-call | flops 4294967296 | bytes 25165824 | tf_op jit(solution)/shard_map/cross/pallas_call | solution.py:80
  10.4 0.6 collective-permute-start
  10.9 2.6 %collective-permute-start.7 = (f32[256,256]{1,0:T(8,128)S(1)}, f32[256,256]{1,0:T(8,128)S(1)}, u32[]{:S(2)}, u32[]{:S(2)}) collective-permute-start(f32[256,256]{1,0:T(8,128)S(1)} %get-tuple-element.28), channel_id=1, source_target_pairs={{0,4},{4,0},{8,12},{12,8},{1,5},{5,1},{9,13},{13,9},{2,6},{6,2},{1... | collective-permute-start | bytes 786440 | tf_op jit(solution)/shard_map/ppermute | solution.py:253
  13.6 9.4 %cross.5 = (f32[256,256]{1,0:T(8,128)S(1)}, f32[256,256]{1,0:T(8,128)S(1)}) custom-call(s32[1]{0:T(128)} %bitcast.1.where, f32[512,1]{1,0:T(8,128)S(1)} %copy.20.phi.fown, bf16[512,16384]{1,0:T(8,128)(2,1)} %pown.7, bf16[16384,1024]{1,0:T(8,128)(2,1)} %model.15), custom_call_target="tpu_custom_call" | custom-call | flops 4294967296 | bytes 25165824 | tf_op jit(solution)/shard_map/cross/pallas_call | solution.py:80
  23.0 0.1 collective-permute-start.1
  23.1 9.4 %cross.6 = (f32[256,256]{1,0:T(8,128)S(1)}, f32[256,256]{1,0:T(8,128)S(1)}) custom-call(s32[1]{0:T(128)} %bitcast.1.where, f32[512,1]{1,0:T(8,128)S(1)} %copy.20.phi.fown, bf16[512,16384]{1,0:T(8,128)(2,1)} %pown.7, bf16[16384,1024]{1,0:T(8,128)(2,1)} %model.15), custom_call_target="tpu_custom_call" | custom-call | flops 4294967296 | bytes 25165824 | tf_op jit(solution)/shard_map/cross/pallas_call | solution.py:80
  32.5 0.0 copy-start
  32.5 0.0 copy-start.1
  32.5 2.1 %collective-permute-start.3 = (f32[256,256]{1,0:T(8,128)S(1)}, f32[256,256]{1,0:T(8,128)S(1)}, u32[]{:S(2)}, u32[]{:S(2)}) collective-permute-start(f32[256,256]{1,0:T(8,128)S(1)} %get-tuple-element.25), channel_id=1, source_target_pairs={{0,4},{4,0},{8,12},{12,8},{1,5},{5,1},{9,13},{13,9},{2,6},{6,2},{1... | collective-permute-start | bytes 786440 | tf_op jit(solution)/shard_map/ppermute | solution.py:253
  34.6 9.4 %cross.7 = (f32[256,256]{1,0:T(8,128)S(1)}, f32[256,256]{1,0:T(8,128)S(1)}) custom-call(s32[1]{0:T(128)} %bitcast.1.where, f32[512,1]{1,0:T(8,128)S(1)} %copy.20.phi.fown, bf16[512,16384]{1,0:T(8,128)(2,1)} %pown.7, bf16[16384,1024]{1,0:T(8,128)(2,1)} %model.15), custom_call_target="tpu_custom_call" | custom-call | flops 4294967296 | bytes 25165824 | tf_op jit(solution)/shard_map/cross/pallas_call | solution.py:80
  44.0 0.1 collective-permute-start.5
  44.1 0.0 collective-permute-done.7.refs_10_
  44.1 3.1 %collective-permute-start.8 = (f32[128,256]{1,0:T(8,128)S(1)}, f32[128,256]{1,0:T(8,128)S(1)}, u32[]{:S(2)}, u32[]{:S(2)}) collective-permute-start(f32[128,256]{1,0:T(8,128)S(1)} %dynamic-slice_add_fusion), channel_id=1, source_target_pairs={{0,8},{4,12},{8,0},{12,4},{1,9},{5,13},{9,1},{13,5},{2,10},{6,14},... | collective-permute-start | bytes 393224 | tf_op jit(solution)/shard_map/ppermute | solution.py:253
  47.2 0.0 collective-permute-done.1.refs_1_
  47.2 0.7 dynamic-slice_add_fusion.3
  47.9 0.0 collective-permute-start.2
  47.9 0.0 collective-permute-done.3.refs_4_
  47.9 3.0 %collective-permute-start.4 = (f32[128,256]{1,0:T(8,128)S(1)}, f32[128,256]{1,0:T(8,128)S(1)}, u32[]{:S(2)}, u32[]{:S(2)}) collective-permute-start(f32[128,256]{1,0:T(8,128)S(1)} %dynamic-slice_add_fusion.2), channel_id=1, source_target_pairs={{0,8},{4,12},{8,0},{12,4},{1,9},{5,13},{9,1},{13,5},{2,10},{6,14},... | collective-permute-start | bytes 393224 | tf_op jit(solution)/shard_map/ppermute | solution.py:253
  50.9 7.2 %collective-permute-done.5.refs_7_ = f32[256,256]{1,0:T(8,128)S(1)} collective-permute-done((f32[256,256]{1,0:T(8,128)S(1)}, f32[256,256]{1,0:T(8,128)S(1)}, u32[]{:S(2)}, u32[]{:S(2)}) %collective-permute-start.5) | collective-permute-done | bytes 262176 | tf_op jit(solution)/shard_map/ppermute | solution.py:253
  58.1 0.1 collective-permute-start.6
  58.2 0.1 pad_add_fusion.1.where
  58.2 8.3 %collective-permute-done.2.refs_2_ = f32[128,256]{1,0:T(8,128)S(1)} collective-permute-done((f32[128,256]{1,0:T(8,128)}, f32[128,256]{1,0:T(8,128)S(1)}, u32[]{:S(2)}, u32[]{:S(2)}) %collective-permute-start.2) | collective-permute-done | bytes 131104 | tf_op jit(solution)/shard_map/ppermute | solution.py:253
  66.5 2.3 %collective-permute-done.4.refs_5_ = f32[128,256]{1,0:T(8,128)S(1)} collective-permute-done((f32[128,256]{1,0:T(8,128)S(1)}, f32[128,256]{1,0:T(8,128)S(1)}, u32[]{:S(2)}, u32[]{:S(2)}) %collective-permute-start.4) | collective-permute-done | bytes 131104 | tf_op jit(solution)/shard_map/ppermute | solution.py:253
  68.8 1.4 collective-permute-done.6.refs_8_
  70.2 0.8 softmax.1
  71.0 1.5 collective-permute-start.9
  72.6 2.2 %collective-permute-done.9.other = f32[16,128]{1,0:T(8,128)S(1)} collective-permute-done((f32[16,128]{1,0:T(8,128)S(1)}, f32[16,128]{1,0:T(8,128)S(1)}, u32[]{:S(2)}, u32[]{:S(2)}) %collective-permute-start.9) | collective-permute-done | bytes 8224 | tf_op jit(solution)/shard_map/ppermute | solution.py:253
  74.7 0.2 weights.1
  74.9 0.5 collective-permute-start.23
  75.5 3.4 %collective-permute-start.24 = (bf16[128,256]{1,0:T(8,128)(2,1)S(1)}, bf16[128,256]{1,0:T(8,128)(2,1)S(1)}, u32[]{:S(2)}, u32[]{:S(2)}) collective-permute-start(bf16[128,256]{1,0:T(8,128)(2,1)S(1)} %get-tuple-element.34.refs_0_), channel_id=1, source_target_pairs={{0,8},{4,12},{8,0},{12,4},{1,9},{5,13},{9,1},{13,5},{2,10},{6,14},... | collective-permute-start | bytes 196616 | tf_op jit(solution)/shard_map/ppermute | solution.py:253
  78.8 0.6 collective-permute-start.25
  79.4 0.1 pad_add_fusion.where
  79.5 0.0 collective-permute-done.23.refs_1_
  79.5 2.8 %collective-permute-done.24.refs_2_ = bf16[128,256]{1,0:T(8,128)(2,1)S(1)} collective-permute-done((bf16[128,256]{1,0:T(8,128)(2,1)S(1)}, bf16[128,256]{1,0:T(8,128)(2,1)S(1)}, u32[]{:S(2)}, u32[]{:S(2)}) %collective-permute-start.24) | collective-permute-done | bytes 65568 | tf_op jit(solution)/shard_map/ppermute | solution.py:253
  82.3 2.6 %collective-permute-done.25.refs_3_ = bf16[128,256]{1,0:T(8,128)(2,1)S(1)} collective-permute-done((bf16[128,256]{1,0:T(8,128)(2,1)S(1)}, bf16[128,256]{1,0:T(8,128)(2,1)S(1)}, u32[]{:S(2)}, u32[]{:S(2)}) %collective-permute-start.25) | collective-permute-done | bytes 65568 | tf_op jit(solution)/shard_map/ppermute | solution.py:253
  84.9 0.6 pack.7.wown
  85.5 0.1 collective-permute-start.26
  85.6 0.1 collective-permute-start.19
  85.6 1.3 collective-permute-start.20
  86.9 3.1 %collective-permute-start.21 = (bf16[128,256]{1,0:T(8,128)(2,1)S(1)}, bf16[128,256]{1,0:T(8,128)(2,1)S(1)}, u32[]{:S(2)}, u32[]{:S(2)}) collective-permute-start(bf16[128,256]{1,0:T(8,128)(2,1)S(1)} %get-tuple-element.33.refs_0_), channel_id=1, source_target_pairs={{0,12},{4,8},{8,4},{12,0},{1,13},{5,9},{9,5},{13,1},{2,14},{6,10},... | collective-permute-start | bytes 196616 | tf_op jit(solution)/shard_map/ppermute | solution.py:253
  90.0 1.1 collective-permute-done.19.refs_1_
  91.1 3.3 %collective-permute-done.20.refs_2_ = bf16[128,256]{1,0:T(8,128)(2,1)S(1)} collective-permute-done((bf16[128,256]{1,0:T(8,128)(2,1)S(1)}, bf16[128,256]{1,0:T(8,128)(2,1)S(1)}, u32[]{:S(2)}, u32[]{:S(2)}) %collective-permute-start.20) | collective-permute-done | bytes 65568 | tf_op jit(solution)/shard_map/ppermute | solution.py:253
  94.4 2.0 %collective-permute-start.17 = (bf16[128,256]{1,0:T(8,128)(2,1)S(1)}, bf16[128,256]{1,0:T(8,128)(2,1)S(1)}, u32[]{:S(2)}, u32[]{:S(2)}) collective-permute-start(bf16[128,256]{1,0:T(8,128)(2,1)S(1)} %get-tuple-element.32.refs_0_), channel_id=1, source_target_pairs={{0,12},{4,8},{8,4},{12,0},{1,13},{5,9},{9,5},{13,1},{2,14},{6,10},... | collective-permute-start | bytes 196616 | tf_op jit(solution)/shard_map/ppermute | solution.py:253
  96.4 0.0 collective-permute-done.15.refs_1_
  96.4 1.5 collective-permute-start.10
  97.9 3.8 %collective-permute-done.16.refs_2_ = bf16[128,256]{1,0:T(8,128)(2,1)S(1)} collective-permute-done((bf16[128,256]{1,0:T(8,128)(2,1)S(1)}, bf16[128,256]{1,0:T(8,128)(2,1)S(1)}, u32[]{:S(2)}, u32[]{:S(2)}) %collective-permute-start.16) | collective-permute-done | bytes 65568 | tf_op jit(solution)/shard_map/ppermute | solution.py:253
  101.7 0.0 collective-permute-start.11
  101.7 1.3 collective-permute-start.12
  102.9 0.0 collective-permute-done.10.refs_1_
  103.0 0.0 collective-permute-start.14
  103.0 0.6 pack.6.wown
  103.5 0.6 pack.5.wown
  104.1 2.7 %collective-permute-done.11.refs_2_ = bf16[128,256]{1,0:T(8,128)(2,1)S(1)} collective-permute-done((bf16[128,256]{1,0:T(8,128)(2,1)S(1)}, bf16[128,256]{1,0:T(8,128)(2,1)S(1)}, u32[]{:S(2)}, u32[]{:S(2)}) %collective-permute-start.11) | collective-permute-done | bytes 65568 | tf_op jit(solution)/shard_map/ppermute | solution.py:253
  106.8 0.0 collective-permute-start.22
  106.8 0.9 collective-permute-done.12.refs_3_
  107.7 0.0 collective-permute-start.18
  107.7 0.6 pack.4.wown
  108.3 0.6 collective-permute-start.13
  108.9 13.1 %numer.4.refs_0_ = bf16[8192,1024]{1,0:T(8,128)(2,1)} custom-call(s32[1]{0:T(128)} %bitcast.where, bf16[512,16384]{1,0:T(8,128)(2,1)} %pown.7, bf16[512,16384]{1,0:T(8,128)(2,1)} %collective-permute-done.psib, bf16[512,256]{1,0:T(8,128)(2,1)S(1)} %pack.7.wown, bf16[512,256]{1,0:T(8,128)(2,1)S(1)} %collective-permute-done.26.wsib, ...), custom_call_target="tpu_custom_call" | custom-call | flops 4294967296 | bytes 25165824 | tf_op jit(solution)/shard_map/numer/pallas_call | solution.py:235
  122.0 13.2 %numer.5.refs_0_ = bf16[8192,1024]{1,0:T(8,128)(2,1)} custom-call(s32[1]{0:T(128)} %bitcast.where, bf16[512,16384]{1,0:T(8,128)(2,1)} %pown.7, bf16[512,16384]{1,0:T(8,128)(2,1)} %collective-permute-done.psib, bf16[512,256]{1,0:T(8,128)(2,1)S(1)} %pack.6.wown, bf16[512,256]{1,0:T(8,128)(2,1)S(1)} %collective-permute-done.22.wsib, ...), custom_call_target="tpu_custom_call", output_to_operand_aliasing={{}: (8, {})} | custom-call | flops 4294967296 | bytes 25165824 | tf_op jit(solution)/shard_map/numer/pallas_call | solution.py:235
  135.3 13.2 %numer.6.refs_0_ = bf16[8192,1024]{1,0:T(8,128)(2,1)} custom-call(s32[1]{0:T(128)} %bitcast.where, bf16[512,16384]{1,0:T(8,128)(2,1)} %pown.7, bf16[512,16384]{1,0:T(8,128)(2,1)} %collective-permute-done.psib, bf16[512,256]{1,0:T(8,128)(2,1)S(1)} %pack.5.wown, bf16[512,256]{1,0:T(8,128)(2,1)S(1)} %collective-permute-done.18.wsib, ...), custom_call_target="tpu_custom_call", output_to_operand_aliasing={{}: (8, {})} | custom-call | flops 4294967296 | bytes 25165824 | tf_op jit(solution)/shard_map/numer/pallas_call | solution.py:235
  148.4 13.2 %numer.7 = bf16[8192,1024]{1,0:T(8,128)(2,1)} custom-call(s32[1]{0:T(128)} %bitcast.where, bf16[512,16384]{1,0:T(8,128)(2,1)} %pown.7, bf16[512,16384]{1,0:T(8,128)(2,1)} %collective-permute-done.psib, bf16[512,256]{1,0:T(8,128)(2,1)S(1)} %pack.4.wown, bf16[512,256]{1,0:T(8,128)(2,1)S(1)} %collective-permute-done.13.wsib, ...), custom_call_target="tpu_custom_call", output_to_operand_aliasing={{}: (8, {})} | custom-call | flops 4294967296 | bytes 25165824 | tf_op jit(solution)/shard_map/numer/pallas_call | solution.py:235
  (16 shorter events, 0.1 us)
Async XLA Ops:
  10.4 98.6 %collective-permute-start = (bf16[512,16384]{1,0:T(8,128)(2,1)}, bf16[512,16384]{1,0:T(8,128)(2,1)}, u32[]{:S(2)}, u32[]{:S(2)}) collective-permute-start(bf16[512,16384]{1,0:T(8,128)(2,1)} %pown.7), channel_id=1, source_target_pairs={{0,1},{1,0},{2,3},{3,2},{4,5},{5,4},{6,7},{7,6},{8,9},{9,8},{10,11... | collective-permute-start | bytes 50331656 | tf_op jit(solution)/shard_map/ppermute | solution.py:253
  10.9 33.1 %collective-permute-start.7 = (f32[256,256]{1,0:T(8,128)S(1)}, f32[256,256]{1,0:T(8,128)S(1)}, u32[]{:S(2)}, u32[]{:S(2)}) collective-permute-start(f32[256,256]{1,0:T(8,128)S(1)} %get-tuple-element.28), channel_id=1, source_target_pairs={{0,4},{4,0},{8,12},{12,8},{1,5},{5,1},{9,13},{13,9},{2,6},{6,2},{1... | collective-permute-start | bytes 786440 | tf_op jit(solution)/shard_map/ppermute | solution.py:253
  23.0 24.2 %collective-permute-start.1 = (f32[256,256]{1,0:T(8,128)S(1)}, f32[256,256]{1,0:T(8,128)S(1)}, u32[]{:S(2)}, u32[]{:S(2)}) collective-permute-start(f32[256,256]{1,0:T(8,128)S(1)} %get-tuple-element.23), channel_id=1, source_target_pairs={{0,4},{4,0},{8,12},{12,8},{1,5},{5,1},{9,13},{13,9},{2,6},{6,2},{1... | collective-permute-start | bytes 786440 | tf_op jit(solution)/shard_map/ppermute | solution.py:253
  32.5 37.7 %copy-start = (s32[1024]{0:T(1024)S(1)}, s32[1024]{0:T(1024)}, u32[]{:S(2)}) copy-start(s32[1024]{0:T(1024)} %param.11) | copy-start | bytes 12292
  32.5 37.7 %copy-start.1 = (f32[8]{0:T(128)S(1)}, f32[8]{0:T(128)}, u32[]{:S(2)}) copy-start(f32[8]{0:T(128)} %table.1) | copy-start | bytes 100
  32.5 15.4 %collective-permute-start.3 = (f32[256,256]{1,0:T(8,128)S(1)}, f32[256,256]{1,0:T(8,128)S(1)}, u32[]{:S(2)}, u32[]{:S(2)}) collective-permute-start(f32[256,256]{1,0:T(8,128)S(1)} %get-tuple-element.25), channel_id=1, source_target_pairs={{0,4},{4,0},{8,12},{12,8},{1,5},{5,1},{9,13},{13,9},{2,6},{6,2},{1... | collective-permute-start | bytes 786440 | tf_op jit(solution)/shard_map/ppermute | solution.py:253
  44.0 14.1 %collective-permute-start.5 = (f32[256,256]{1,0:T(8,128)S(1)}, f32[256,256]{1,0:T(8,128)S(1)}, u32[]{:S(2)}, u32[]{:S(2)}) collective-permute-start(f32[256,256]{1,0:T(8,128)S(1)} %get-tuple-element.27), channel_id=1, source_target_pairs={{0,4},{4,0},{8,12},{12,8},{1,5},{5,1},{9,13},{13,9},{2,6},{6,2},{1... | collective-permute-start | bytes 786440 | tf_op jit(solution)/shard_map/ppermute | solution.py:253
  44.1 14.1 %collective-permute-start.8 = (f32[128,256]{1,0:T(8,128)S(1)}, f32[128,256]{1,0:T(8,128)S(1)}, u32[]{:S(2)}, u32[]{:S(2)}) collective-permute-start(f32[128,256]{1,0:T(8,128)S(1)} %dynamic-slice_add_fusion), channel_id=1, source_target_pairs={{0,8},{4,12},{8,0},{12,4},{1,9},{5,13},{9,1},{13,5},{2,10},{6,14},... | collective-permute-start | bytes 393224 | tf_op jit(solution)/shard_map/ppermute | solution.py:253
  47.9 18.7 %collective-permute-start.2 = (f32[128,256]{1,0:T(8,128)}, f32[128,256]{1,0:T(8,128)S(1)}, u32[]{:S(2)}, u32[]{:S(2)}) collective-permute-start(f32[128,256]{1,0:T(8,128)} %dynamic-slice_add_fusion.3), channel_id=1, source_target_pairs={{0,8},{4,12},{8,0},{12,4},{1,9},{5,13},{9,1},{13,5},{2,10},{6,14},... | collective-permute-start | bytes 393224 | tf_op jit(solution)/shard_map/ppermute | solution.py:253
  47.9 20.9 %collective-permute-start.4 = (f32[128,256]{1,0:T(8,128)S(1)}, f32[128,256]{1,0:T(8,128)S(1)}, u32[]{:S(2)}, u32[]{:S(2)}) collective-permute-start(f32[128,256]{1,0:T(8,128)S(1)} %dynamic-slice_add_fusion.2), channel_id=1, source_target_pairs={{0,8},{4,12},{8,0},{12,4},{1,9},{5,13},{9,1},{13,5},{2,10},{6,14},... | collective-permute-start | bytes 393224 | tf_op jit(solution)/shard_map/ppermute | solution.py:253
  58.1 12.1 %collective-permute-start.6 = (f32[128,256]{1,0:T(8,128)S(1)}, f32[128,256]{1,0:T(8,128)S(1)}, u32[]{:S(2)}, u32[]{:S(2)}) collective-permute-start(f32[128,256]{1,0:T(8,128)S(1)} %dynamic-slice_add_fusion.1), channel_id=1, source_target_pairs={{0,8},{4,12},{8,0},{12,4},{1,9},{5,13},{9,1},{13,5},{2,10},{6,14},... | collective-permute-start | bytes 393224 | tf_op jit(solution)/shard_map/ppermute | solution.py:253
  71.0 3.7 %collective-permute-start.9 = (f32[16,128]{1,0:T(8,128)S(1)}, f32[16,128]{1,0:T(8,128)S(1)}, u32[]{:S(2)}, u32[]{:S(2)}) collective-permute-start(f32[16,128]{1,0:T(8,128)S(1)} %get-tuple-element.30.own.mine), channel_id=1, source_target_pairs={{0,2},{2,0},{1,3},{3,1},{4,6},{6,4},{5,7},{7,5},{8,10},{10,8},{9,1... | collective-permute-start | bytes 24584 | tf_op jit(solution)/shard_map/ppermute | solution.py:253
  74.9 4.5 %collective-permute-start.23 = (bf16[128,256]{1,0:T(8,128)(2,1)S(1)}, bf16[128,256]{1,0:T(8,128)(2,1)S(1)}, u32[]{:S(2)}, u32[]{:S(2)}) collective-permute-start(bf16[128,256]{1,0:T(8,128)(2,1)S(1)} %get-tuple-element.34.refs_0_), channel_id=1, source_target_pairs={{0,4},{4,0},{8,12},{12,8},{1,5},{5,1},{9,13},{13,9},{2,6},{6,2},{1... | collective-permute-start | bytes 196616 | tf_op jit(solution)/shard_map/ppermute | solution.py:253
  75.5 6.9 %collective-permute-start.24 = (bf16[128,256]{1,0:T(8,128)(2,1)S(1)}, bf16[128,256]{1,0:T(8,128)(2,1)S(1)}, u32[]{:S(2)}, u32[]{:S(2)}) collective-permute-start(bf16[128,256]{1,0:T(8,128)(2,1)S(1)} %get-tuple-element.34.refs_0_), channel_id=1, source_target_pairs={{0,8},{4,12},{8,0},{12,4},{1,9},{5,13},{9,1},{13,5},{2,10},{6,14},... | collective-permute-start | bytes 196616 | tf_op jit(solution)/shard_map/ppermute | solution.py:253
  78.8 6.1 %collective-permute-start.25 = (bf16[128,256]{1,0:T(8,128)(2,1)S(1)}, bf16[128,256]{1,0:T(8,128)(2,1)S(1)}, u32[]{:S(2)}, u32[]{:S(2)}) collective-permute-start(bf16[128,256]{1,0:T(8,128)(2,1)S(1)} %get-tuple-element.34.refs_0_), channel_id=1, source_target_pairs={{0,12},{4,8},{8,4},{12,0},{1,13},{5,9},{9,5},{13,1},{2,14},{6,10},... | collective-permute-start | bytes 196616 | tf_op jit(solution)/shard_map/ppermute | solution.py:253
  85.5 23.4 %collective-permute-start.26 = (bf16[512,256]{1,0:T(8,128)(2,1)S(1)}, bf16[512,256]{1,0:T(8,128)(2,1)S(1)}, u32[]{:S(2)}, u32[]{:S(2)}) collective-permute-start(bf16[512,256]{1,0:T(8,128)(2,1)S(1)} %pack.7.wown), channel_id=1, source_target_pairs={{0,1},{1,0},{2,3},{3,2},{4,5},{5,4},{6,7},{7,6},{8,9},{9,8},{10,11... | collective-permute-start | bytes 786440 | tf_op jit(solution)/shard_map/ppermute | solution.py:253
  85.6 5.5 %collective-permute-start.19 = (bf16[128,256]{1,0:T(8,128)(2,1)S(1)}, bf16[128,256]{1,0:T(8,128)(2,1)S(1)}, u32[]{:S(2)}, u32[]{:S(2)}) collective-permute-start(bf16[128,256]{1,0:T(8,128)(2,1)S(1)} %get-tuple-element.33.refs_0_), channel_id=1, source_target_pairs={{0,4},{4,0},{8,12},{12,8},{1,5},{5,1},{9,13},{13,9},{2,6},{6,2},{1... | collective-permute-start | bytes 196616 | tf_op jit(solution)/shard_map/ppermute | solution.py:253
  85.6 8.7 %collective-permute-start.20 = (bf16[128,256]{1,0:T(8,128)(2,1)S(1)}, bf16[128,256]{1,0:T(8,128)(2,1)S(1)}, u32[]{:S(2)}, u32[]{:S(2)}) collective-permute-start(bf16[128,256]{1,0:T(8,128)(2,1)S(1)} %get-tuple-element.33.refs_0_), channel_id=1, source_target_pairs={{0,8},{4,12},{8,0},{12,4},{1,9},{5,13},{9,1},{13,5},{2,10},{6,14},... | collective-permute-start | bytes 196616 | tf_op jit(solution)/shard_map/ppermute | solution.py:253
  86.9 7.5 %collective-permute-start.21 = (bf16[128,256]{1,0:T(8,128)(2,1)S(1)}, bf16[128,256]{1,0:T(8,128)(2,1)S(1)}, u32[]{:S(2)}, u32[]{:S(2)}) collective-permute-start(bf16[128,256]{1,0:T(8,128)(2,1)S(1)} %get-tuple-element.33.refs_0_), channel_id=1, source_target_pairs={{0,12},{4,8},{8,4},{12,0},{1,13},{5,9},{9,5},{13,1},{2,14},{6,10},... | collective-permute-start | bytes 196616 | tf_op jit(solution)/shard_map/ppermute | solution.py:253
  91.1 5.3 %collective-permute-start.15 = (bf16[128,256]{1,0:T(8,128)(2,1)S(1)}, bf16[128,256]{1,0:T(8,128)(2,1)S(1)}, u32[]{:S(2)}, u32[]{:S(2)}) collective-permute-start(bf16[128,256]{1,0:T(8,128)(2,1)S(1)} %get-tuple-element.32.refs_0_), channel_id=1, source_target_pairs={{0,4},{4,0},{8,12},{12,8},{1,5},{5,1},{9,13},{13,9},{2,6},{6,2},{1... | collective-permute-start | bytes 196616 | tf_op jit(solution)/shard_map/ppermute | solution.py:253
  94.4 7.3 %collective-permute-start.16 = (bf16[128,256]{1,0:T(8,128)(2,1)S(1)}, bf16[128,256]{1,0:T(8,128)(2,1)S(1)}, u32[]{:S(2)}, u32[]{:S(2)}) collective-permute-start(bf16[128,256]{1,0:T(8,128)(2,1)S(1)} %get-tuple-element.32.refs_0_), channel_id=1, source_target_pairs={{0,8},{4,12},{8,0},{12,4},{1,9},{5,13},{9,1},{13,5},{2,10},{6,14},... | collective-permute-start | bytes 196616 | tf_op jit(solution)/shard_map/ppermute | solution.py:253
  94.4 7.3 %collective-permute-start.17 = (bf16[128,256]{1,0:T(8,128)(2,1)S(1)}, bf16[128,256]{1,0:T(8,128)(2,1)S(1)}, u32[]{:S(2)}, u32[]{:S(2)}) collective-permute-start(bf16[128,256]{1,0:T(8,128)(2,1)S(1)} %get-tuple-element.32.refs_0_), channel_id=1, source_target_pairs={{0,12},{4,8},{8,4},{12,0},{1,13},{5,9},{9,5},{13,1},{2,14},{6,10},... | collective-permute-start | bytes 196616 | tf_op jit(solution)/shard_map/ppermute | solution.py:253
  96.4 6.6 %collective-permute-start.10 = (bf16[128,256]{1,0:T(8,128)(2,1)S(1)}, bf16[128,256]{1,0:T(8,128)(2,1)S(1)}, u32[]{:S(2)}, u32[]{:S(2)}) collective-permute-start(bf16[128,256]{1,0:T(8,128)(2,1)S(1)} %get-tuple-element.31.refs_0_), channel_id=1, source_target_pairs={{0,4},{4,0},{8,12},{12,8},{1,5},{5,1},{9,13},{13,9},{2,6},{6,2},{1... | collective-permute-start | bytes 196616 | tf_op jit(solution)/shard_map/ppermute | solution.py:253
  101.7 5.2 %collective-permute-start.11 = (bf16[128,256]{1,0:T(8,128)(2,1)S(1)}, bf16[128,256]{1,0:T(8,128)(2,1)S(1)}, u32[]{:S(2)}, u32[]{:S(2)}) collective-permute-start(bf16[128,256]{1,0:T(8,128)(2,1)S(1)} %get-tuple-element.31.refs_0_), channel_id=1, source_target_pairs={{0,8},{4,12},{8,0},{12,4},{1,9},{5,13},{9,1},{13,5},{2,10},{6,14},... | collective-permute-start | bytes 196616 | tf_op jit(solution)/shard_map/ppermute | solution.py:253
  101.7 6.1 %collective-permute-start.12 = (bf16[128,256]{1,0:T(8,128)(2,1)S(1)}, bf16[128,256]{1,0:T(8,128)(2,1)S(1)}, u32[]{:S(2)}, u32[]{:S(2)}) collective-permute-start(bf16[128,256]{1,0:T(8,128)(2,1)S(1)} %get-tuple-element.31.refs_0_), channel_id=1, source_target_pairs={{0,12},{4,8},{8,4},{12,0},{1,13},{5,9},{9,5},{13,1},{2,14},{6,10},... | collective-permute-start | bytes 196616 | tf_op jit(solution)/shard_map/ppermute | solution.py:253
  103.0 5.4 %collective-permute-start.14 = (f32[512,1]{1,0:T(8,128)S(1)}, f32[512,1]{1,0:T(8,128)S(1)}, u32[]{:S(2)}, u32[]{:S(2)}) collective-permute-start(f32[512,1]{1,0:T(8,128)S(1)} %copy.20.phi.fown), channel_id=1, source_target_pairs={{0,1},{1,0},{2,3},{3,2},{4,5},{5,4},{6,7},{7,6},{8,9},{9,8},{10,11... | collective-permute-start | bytes 6152 | tf_op jit(solution)/shard_map/ppermute | solution.py:253
  106.8 15.2 %collective-permute-start.22 = (bf16[512,256]{1,0:T(8,128)(2,1)S(1)}, bf16[512,256]{1,0:T(8,128)(2,1)S(1)}, u32[]{:S(2)}, u32[]{:S(2)}) collective-permute-start(bf16[512,256]{1,0:T(8,128)(2,1)S(1)} %pack.6.wown), channel_id=1, source_target_pairs={{0,1},{1,0},{2,3},{3,2},{4,5},{5,4},{6,7},{7,6},{8,9},{9,8},{10,11... | collective-permute-start | bytes 786440 | tf_op jit(solution)/shard_map/ppermute | solution.py:253
  107.7 27.5 %collective-permute-start.18 = (bf16[512,256]{1,0:T(8,128)(2,1)S(1)}, bf16[512,256]{1,0:T(8,128)(2,1)S(1)}, u32[]{:S(2)}, u32[]{:S(2)}) collective-permute-start(bf16[512,256]{1,0:T(8,128)(2,1)S(1)} %pack.5.wown), channel_id=1, source_target_pairs={{0,1},{1,0},{2,3},{3,2},{4,5},{5,4},{6,7},{7,6},{8,9},{9,8},{10,11... | collective-permute-start | bytes 786440 | tf_op jit(solution)/shard_map/ppermute | solution.py:253
  108.3 40.1 %collective-permute-start.13 = (bf16[512,256]{1,0:T(8,128)(2,1)S(1)}, bf16[512,256]{1,0:T(8,128)(2,1)S(1)}, u32[]{:S(2)}, u32[]{:S(2)}) collective-permute-start(bf16[512,256]{1,0:T(8,128)(2,1)S(1)} %pack.4.wown), channel_id=1, source_target_pairs={{0,1},{1,0},{2,3},{3,2},{4,5},{5,4},{6,7},{7,6},{8,9},{9,8},{10,11... | collective-permute-start | bytes 786440 | tf_op jit(solution)/shard_map/ppermute | solution.py:253

commit v2 on v1

v2 whole, which is shorter than its diff:
```python
import functools

import jax
import jax.numpy as jnp
from jax import lax
from jax.experimental import pallas as pl
from jax.experimental.pallas import tpu as pltpu
from jax.sharding import PartitionSpec as P

prior_weight = 0.5
MIB = 1 << 20
SLOTS = 6
VMEM = pl.BlockSpec(memory_space=pltpu.VMEM)
SMEM = pl.BlockSpec(memory_space=pltpu.SMEM)
HBM = pl.BlockSpec(memory_space=pltpu.HBM)
ANY = pl.BlockSpec(memory_space=pl.ANY)


def table_lookup(table, index):
    levels = jnp.arange(table.shape[0], dtype=jnp.int32)
    return jnp.sum(jnp.where(index[:, None] == levels[None, :], table[None, :], 0.0), axis=1)


def params(limit):
    return pltpu.CompilerParams(vmem_limit_bytes=limit)


def cost(flops, moved):
    return pl.CostEstimate(flops=flops, bytes_accessed=moved, transcendentals=0)


def bit_reverse(value, bits):
    return sum(((value >> i) & 1) << (bits - 1 - i) for i in range(bits))


def cross_kernel(where, phi, patterns, model, after, send, keep, *refs, column, tk, steps, beta, first, turns):
    turned, refs = refs[: len(turns)], refs[len(turns) :]
    if first:
        held, mbuf, acc, squares, msem, psem = refs
    else:
        held, (mbuf, acc, squares, msem) = patterns, refs
    tn = acc.shape[1]

    def copies(i):
        slot = lax.rem(i, SLOTS)
        at = pl.multiple_of(i * tk, tk)
        both = [pltpu.make_async_copy(model.at[pl.ds(at, tk), pl.ds(column, tn)], mbuf.at[slot], msem.at[slot])]
        if first:
            both.append(pltpu.make_async_copy(patterns.at[:, pl.ds(at, tk)], held.at[:, pl.ds(at, tk)], psem.at[slot]))
        return both

    for i in range(min(SLOTS - 1, steps)):
        for copy in copies(i):
            copy.start()
    acc[...] = jnp.zeros_like(acc)
    squares[...] = jnp.zeros_like(squares)

    def body(i, carry):
        for copy in copies(i):
            copy.wait()

        @pl.when(i + SLOTS - 1 < steps)
        def _():
            for copy in copies(i + SLOTS - 1):
                copy.start()

        tile = mbuf[lax.rem(i, SLOTS)]
        part = held[:, pl.ds(pl.multiple_of(i * tk, tk), tk)]
        acc[...] += jnp.dot(part, tile, preferred_element_type=jnp.float32)
        wide = tile.astype(jnp.float32)
        squares[...] += jnp.sum((wide * wide).reshape(tk // 8, 8, tn), axis=0)
        for own, out in zip(turns, turned):
            pixels = out.shape[0]
            width = pixels // steps
            side = where[1] if own else 1 - where[1]
            piece = held[:, pl.ds(pl.multiple_of(side * pixels + i * width, width), width)]
            out[pl.ds(pl.multiple_of(i * width, width), width), :] = piece.T
        return carry

    lax.fori_loop(0, steps, body, 0)
    sq = jnp.sum(squares[...], axis=0, keepdims=True)
    scale = phi[...]
    acc[...] = beta * (scale * acc[...] - 0.5 * (scale * scale) * sq)
    half = send.shape[0]
    send[...] = acc[pl.ds(pl.multiple_of((1 - where[0]) * half, half), half), :]
    keep[...] = acc[pl.ds(pl.multiple_of(where[0] * half, half), half), :]


def cross_chunk(where, phi, patterns, model, after, column, tn, beta, first, turns):
    rows, depth = patterns.shape
    tk = min(1024, depth)
    half = rows // 2
    shapes = [jax.ShapeDtypeStruct((half, tn), jnp.float32)] * 2
    shapes += [(pltpu.VMEM if own else pltpu.HBM)((depth // 2, rows), patterns.dtype) for own in turns]
    scratch = [
        pltpu.VMEM((SLOTS, tk, tn), jnp.bfloat16),
        pltpu.VMEM((rows, tn), jnp.float32),
        pltpu.VMEM((8, tn), jnp.float32),
        pltpu.SemaphoreType.DMA((SLOTS,)),
    ]
    if first:
        shapes.append(pltpu.VMEM(patterns.shape, patterns.dtype))
        scratch.append(pltpu.SemaphoreType.DMA((SLOTS,)))
    patterns = pltpu.with_memory_space_constraint(patterns, pltpu.HBM if first else pltpu.VMEM)
    model = pltpu.with_memory_space_constraint(model, pltpu.HBM)
    return pl.pallas_call(
        functools.partial(
            cross_kernel, column=column, tk=tk, steps=depth // tk, beta=beta, first=first, turns=turns
        ),
        out_shape=shapes,
        in_specs=[SMEM, VMEM, HBM if first else VMEM, HBM, ANY],
        out_specs=[VMEM] * len(shapes),
        scratch_shapes=scratch,
        compiler_params=params(20 * MIB),
        cost_estimate=cost(2 * rows * depth * tn, 2 * depth * (rows + tn)),
        name="cross",
    )(where, phi, patterns, model, after)


def forward_kernel(where, *refs, base):
    parts, out = refs[:-1], refs[-1]
    size = out.shape[0]
    total = None
    for t, part in enumerate(parts):
        piece = part[pl.ds(pl.multiple_of(where[base + t], size), size), :]
        total = piece if total is None else total + piece
    out[...] = total


def forward(where, base, parts, size):
    return pl.pallas_call(
        functools.partial(forward_kernel, base=base),
        out_shape=jax.ShapeDtypeStruct((size, parts[0].shape[1]), jnp.float32),
        in_specs=[SMEM] + [VMEM] * len(parts),
        out_specs=VMEM,
        compiler_params=params(8 * MIB),
        name="forward",
    )(where, *parts)


def softmax_kernel(where, table, classes, after, *refs, chunks, terms, base):
    parts, (exps, stats) = refs[:-2], refs[-2:]
    count = exps.shape[0]
    tn = exps.shape[1] // chunks
    logw = jnp.zeros(classes.shape, jnp.float32)
    for q in range(table.shape[0]):
        logw = logw + jnp.where(classes[...] == q, table[q], 0.0)
    for c in range(chunks):
        total = None
        for t in range(terms):
            rows = pl.ds(pl.multiple_of(where[base + t], count), count)
            part = parts[c * terms + t][rows, :]
            total = part if total is None else total + part
        exps[:, c * tn : (c + 1) * tn] = total + logw[:, c * tn : (c + 1) * tn]
    top = jnp.max(exps[...], axis=1, keepdims=True)
    exps[...] = jnp.exp(exps[...] - top)
    total = jnp.sum(exps[...], axis=1, keepdims=True)
    lanes = (count, 128)
    stats[:8, :] = jnp.transpose(jnp.broadcast_to(top, lanes))[:8, :]
    stats[8:, :] = jnp.transpose(jnp.broadcast_to(total, lanes))[:8, :]


def softmax_stage(where, base, table, classes, after, parts, count, chunks):
    terms = len(parts) // chunks
    columns = classes.shape[1]
    return pl.pallas_call(
        functools.partial(softmax_kernel, chunks=chunks, terms=terms, base=base),
        out_shape=(
            jax.ShapeDtypeStruct((count, columns), jnp.float32),
            jax.ShapeDtypeStruct((16, count), jnp.float32),
        ),
        in_specs=[SMEM, SMEM, VMEM, ANY] + [VMEM] * len(parts),
        out_specs=(VMEM, VMEM),
        compiler_params=params(16 * MIB),
        name="softmax",
    )(where, table, classes, after, *parts)


def combine(mine, other):
    top = jnp.maximum(mine[:8], other[:8])
    total = mine[8:] * jnp.exp(mine[:8] - top) + other[8:] * jnp.exp(other[:8] - top)
    return jnp.concatenate([top, total], axis=0)


def weight_kernel(where, phi, exps, own, mine, other, *outs, base):
    count = exps.shape[0]

    def column(row):
        return jnp.transpose(jnp.broadcast_to(row[:1, :], (128, count)))[:, :1]

    top = jnp.maximum(mine[:8, :], other[:8, :])
    total = mine[8:, :] * jnp.exp(mine[:8, :] - top) + other[8:, :] * jnp.exp(other[:8, :] - top)
    factor = column(jnp.exp(own[:8, :] - top) / total)
    factor = factor * phi[pl.ds(pl.multiple_of(where[base], count), count), :]
    at = 0
    for out in outs:
        tn = out.shape[1]
        out[...] = (exps[:, at : at + tn] * factor).astype(jnp.bfloat16)
        at += tn


def weight_stage(where, base, phi, exps, own, mine, other, widths):
    count = exps.shape[0]
    return pl.pallas_call(
        functools.partial(weight_kernel, base=base),
        out_shape=[jax.ShapeDtypeStruct((count, tn), jnp.bfloat16) for tn in widths],
        in_specs=[SMEM] + [VMEM] * 5,
        out_specs=[VMEM] * len(widths),
        compiler_params=params(8 * MIB),
        name="weights",
    )(where, phi, exps, own, mine, other)


def pack_kernel(where, *refs, base):
    parts, out = refs[:-2], refs[-1]
    count = parts[0].shape[0]
    for d, part in enumerate(parts):
        out[pl.ds(pl.multiple_of(where[base + d], count), count), :] = part[...]


def pack(where, base, parts, after):
    count, tn = parts[0].shape
    after = pltpu.with_memory_space_constraint(after, pltpu.HBM)
    return pl.pallas_call(
        functools.partial(pack_kernel, base=base),
        out_shape=jax.ShapeDtypeStruct((count * len(parts), tn), jnp.bfloat16),
        in_specs=[SMEM] + [VMEM] * len(parts) + [HBM],
        out_specs=VMEM,
        compiler_params=params(8 * MIB),
        name="pack",
    )(where, *parts, after)


def numer_kernel(where, pown, psib, wown, wsib, fown, fsib, model, *refs, column, tm, sub):
    out, mbuf, obuf, msem, osem = refs[-5:]
    pixels, tn = pown.shape[0], wown.shape[1]
    steps = pixels // tm

    def fetch(i):
        slot = lax.rem(i, 3)
        at = pl.multiple_of(where[1] * pixels + i * tm, tm)
        return pltpu.make_async_copy(model.at[pl.ds(at, tm), pl.ds(column, tn)], mbuf.at[slot], msem.at[slot])

    def store(i):
        slot = lax.rem(i, 2)
        at = pl.multiple_of(i * tm, tm)
        return pltpu.make_async_copy(obuf.at[slot], out.at[pl.ds(at, tm), pl.ds(column, tn)], osem.at[slot])

    for i in range(min(2, steps)):
        fetch(i).start()
    den = jnp.sum(wown[...].astype(jnp.float32) * fown[...], axis=0, keepdims=True)
    den = den + jnp.sum(wsib[...].astype(jnp.float32) * fsib[...], axis=0, keepdims=True)
    scale = 1.0 / (prior_weight + den)

    def body(i, carry):
        fetch(i).wait()

        @pl.when(i + 2 < steps)
        def _():
            fetch(i + 2).start()

        @pl.when(i >= 2)
        def _():
            store(i - 2).wait()

        for r in range(0, tm, sub):
            rows = pl.ds(pl.multiple_of(i * tm + r, sub), sub)
            acc = jnp.dot(pown[rows, :], wown[...], preferred_element_type=jnp.float32)
            acc = acc + jnp.dot(psib[rows, :], wsib[...], preferred_element_type=jnp.float32)
            acc = acc + prior_weight * mbuf[lax.rem(i, 3), r : r + sub, :].astype(jnp.float32)
            obuf[lax.rem(i, 2), r : r + sub, :] = (acc * scale).astype(jnp.bfloat16)
        store(i).start()
        return carry

    lax.fori_loop(0, steps, body, 0)
    for i in range(max(0, steps - 2), steps):
        store(i).wait()


def numer_chunk(where, pown, psib, wown, wsib, fown, fsib, model, column, previous):
    depth, tn = wown.shape
    pixels, columns = pown.shape[0], model.shape[1]
    tm = min(1024, pixels)
    pown = pltpu.with_memory_space_constraint(pown, pltpu.VMEM)
    psib = pltpu.with_memory_space_constraint(psib, pltpu.VMEM)
    model = pltpu.with_memory_space_constraint(model, pltpu.HBM)
    args = [where, pown, psib, wown, wsib, fown, fsib, model]
    in_specs = [SMEM] + [VMEM] * 6 + [HBM]
    aliases = {}
    if previous is not None:
        in_specs.append(HBM)
        args.append(pltpu.with_memory_space_constraint(previous, pltpu.HBM))
        aliases = {len(args) - 1: 0}
    return pl.pallas_call(
        functools.partial(numer_kernel, column=column, tm=tm, sub=min(512, tm)),
        out_shape=jax.ShapeDtypeStruct((pixels, columns), jnp.bfloat16),
        in_specs=in_specs,
        out_specs=HBM,
        scratch_shapes=[
            pltpu.VMEM((3, tm, tn), jnp.bfloat16),
            pltpu.VMEM((2, tm, tn), jnp.bfloat16),
            pltpu.SemaphoreType.DMA((3,)),
            pltpu.SemaphoreType.DMA((2,)),
        ],
        input_output_aliases=aliases,
        compiler_params=params(24 * MIB),
        cost_estimate=cost(4 * depth * pixels * tn, 4 * pixels * (depth + tn)),
        name="numer",
    )(*args)


def exchange(value, axis, size, distance):
    return lax.ppermute(value, axis, [(i, i ^ distance) for i in range(size)])


def local(patterns, model, scale_table, scale_index, weight_table, weight_class, *, sizes):
    pix, ori = sizes["pix"], sizes["ori"]
    hops = pix.bit_length() - 1
    rows, columns = patterns.shape[0], model.shape[1]
    count = rows // pix
    tn = min(256, columns)
    chunks = columns // tn
    beta = (patterns.shape[1] * pix) ** -0.5
    place = lax.axis_index("pix")
    bits = [(place >> i) & 1 for i in range(hops)]

    phi = table_lookup(scale_table, scale_index)[:, None]
    classes = weight_class[None, :]
    side = lax.axis_index("pat")

    share = bit_reverse(place, hops) * count
    entries = [bits[0], side]
    starts, offsets, size = {}, [0, 0], rows // 2
    for hop in range(1, hops):
        size //= 2
        starts[hop] = len(entries)
        entries += [o + (1 - bits[hop]) * size for o in offsets]
        offsets = [o + bits[hop] * size for o in offsets] + [0]
    starts["terms"] = len(entries)
    entries += offsets
    starts["share"] = len(entries)
    entries.append(share)
    starts["order"] = len(entries)
    entries += [share ^ (bit_reverse(d, hops) * count) for d in range(pix)]
    where = jnp.stack([jnp.asarray(e, jnp.int32) for e in entries])

    later = min(2, chunks - 1)
    turned, terms = {}, {}
    source, after = patterns, phi

    def reduce_further(c):
        size = rows // 2
        for hop in range(1, hops):
            size //= 2
            away = forward(where, starts[hop], terms[c], size)
            terms[c].append(exchange(away, "pix", pix, 1 << hop))
        return away

    for c in range(chunks):
        turns = ((False,) if c == 1 else ()) + ((True,) if c == later else ())
        send, keep, *rest = cross_chunk(where, phi, source, model, after, c * tn, tn, beta, c == 0, turns)
        if c == 0:
            source = rest[-1]
        for own, value in zip(turns, rest):
            turned[own] = value
        terms[c] = [keep, exchange(send, "pix", pix, 1)]
        if c >= 1:
            after = reduce_further(c - 1)
        if c == 1:
            psib = exchange(turned[False], "pat", 2, 1)
    reduce_further(chunks - 1)
    held = [term for c in range(chunks) for term in terms[c]]
    phi_sib = exchange(phi, "pat", 2, 1)

    exps, own = softmax_stage(where, starts["terms"], weight_table, classes, psib, held, count, chunks)
    mine = own
    other = None
    for hop in range(ori.bit_length() - 1):
        if other is not None:
            mine = combine(mine, other)
        other = exchange(mine, "ori", ori, 1 << hop)
    widths = [tn] * min(2, chunks)
    if chunks > 2:
        widths.append(tn * (chunks - 2))
    weights = weight_stage(where, starts["share"], phi, exps, own, mine, other, widths)

    gathered = [[w] + [exchange(w, "pix", pix, d) for d in range(1, pix)] for w in weights]
    at, result, after = 0, None, model
    for width, parts in zip(widths, gathered):
        wown = pack(where, starts["order"], parts, after)
        wsib = exchange(wown, "pat", 2, 1)
        result = numer_chunk(where, turned[True], psib, wown, wsib, phi, phi_sib, model, at, result)
        after = result
        at += width
    return result


def solution(mesh):
    placed = (
        P(("grp", "pat"), "pix"),
        P(("grp", "pix"), "ori"),
        P("grp"),
        P(("grp", "pat")),
        P("grp"),
        P(("grp", "ori")),
    )
    return jax.shard_map(
        functools.partial(local, sizes=dict(mesh.shape)),
        mesh=mesh,
        in_specs=placed,
        out_specs=P(("grp", "pix", "pat"), "ori"),
        check_vma=False,
    )
```

time: 162 us -> 143 us (0.88)
  Pallas kernels: 93.5 us -> 76.5 us
  waiting for transfers between devices: 38.6 us -> 33.7 us
  local copies, waits for them, and re-layouts: 0.16 us -> 3.65 us
    pallas_call x9 -> x11, Pallas kernels: 55.1 us -> 35.1 us  [the longest x3 30.4 us: numer_chunk(): pl.pallas_call(functools.partial(numer_kernel, column=column, tm=tm, sub=...]
    ppermute x27 -> x23, waiting for transfers between devices: 38.6 us -> 33.7 us  [exchange(): return lax.ppermute(value, axis, [(i, i ^ distance) for i in range(size)])]
    unnamed x4 -> x14, local copies, waits for them, and re-layouts: 0.01 us -> 3.41 us
    pallas_call x4, Pallas kernels: 37.6 us -> 40.6 us  [cross_chunk(): pl.pallas_call(functools.partial(cross_kernel, column=column, tk=tk, step...]
    ppermute x27 -> x23, starting transfers between devices: 27.5 us -> 27.9 us  [exchange(): return lax.ppermute(value, axis, [(i, i ^ distance) for i in range(size)])]
  transfers between devices with their start and end apart: 27 -> 23, of which waited for: 12 -> 10; matrix products, arithmetic and copies ran while one was open for 1% -> 0% of each run, Pallas kernels for 44% -> 26%
where the time goes in v2:
time: 143 us
  Pallas kernels  76.5 us (53%)
  waiting for transfers between devices  33.7 us (24%)
  starting transfers between devices  27.9 us (20%)
  local copies, waits for them, and re-layouts  3.65 us (3%)
    pallas_call x4, Pallas kernels, cross_chunk(): pl.pallas_call(functools.partial(cross_kernel, column=column, tk=tk, step...  40.6 us
    ppermute x23, waiting for transfers between devices, exchange(): return lax.ppermute(value, axis, [(i, i ^ distance) for i in range(size)])  33.7 us
    pallas_call x3, Pallas kernels, numer_chunk(): pl.pallas_call(functools.partial(numer_kernel, column=column, tm=tm, sub=...  30.4 us
    ppermute x23, starting transfers between devices, exchange(): return lax.ppermute(value, axis, [(i, i ^ distance) for i in range(size)])  27.9 us
    unnamed x14, local copies, waits for them, and re-layouts  3.41 us
  transfers between devices with their start and end apart: 23, of which 10 were waited for; matrix products, arithmetic and copies ran while one was open for 0% of the time, Pallas kernels for 26%

profile of v2, /device:TPU:0, one launch (start us, length us, event | category | flops | bytes accessed | tf_op | source)
XLA Modules:
  0.0 142.9 jit_solution(2644904898854650560)
XLA Ops:
  0.0 0.8 select_reduce_fusion
  0.8 0.1 copy.22.phi.after.fown
  0.9 0.1 stack.38.where
  1.0 10.0 %cross.4 = (f32[256,256]{1,0:T(8,128)S(1)}, f32[256,256]{1,0:T(8,128)S(1)}, bf16[512,16384]{1,0:T(8,128)(2,1)S(1)}) custom-call(s32[12]{0:T(128)S(1)} %stack.38.where, f32[512,1]{1,0:T(8,128)S(1)} %copy.22.phi.after.fown, bf16[512,16384]{1,0:T(8,128)(2,1)} %patterns.1, bf16[16384,1024]{1,0:T(8,128)(2,1)} %model.13, f32[512,1]{1,0:T(8,128)S(1)} %copy.22.phi.after.fown), custom_call_target="tpu_custom_call" | custom-call | flops 4294967296 | bytes 25165824 | tf_op jit(solution)/shard_map/cross/pallas_call | solution.py:106
  11.0 12.3 %cross.6 = (f32[256,256]{1,0:T(8,128)S(1)}, f32[256,256]{1,0:T(8,128)S(1)}, bf16[8192,512]{1,0:T(8,128)(2,1)}) custom-call(s32[12]{0:T(128)S(1)} %stack.38.where, f32[512,1]{1,0:T(8,128)S(1)} %copy.22.phi.after.fown, bf16[512,16384]{1,0:T(8,128)(2,1)S(1)} %get-tuple-element.21.patterns, bf16[16384,1024]{1,0:T(8,128)(2,1)} %model.13, ...), custom_call_target="tpu_custom_call" | custom-call | flops 4294967296 | bytes 25165824 | tf_op jit(solution)/shard_map/cross/pallas_call | solution.py:106
  23.3 0.6 collective-permute-start.1
  23.9 2.6 %collective-permute-start = (f32[256,256]{1,0:T(8,128)S(1)}, f32[256,256]{1,0:T(8,128)S(1)}, u32[]{:S(2)}, u32[]{:S(2)}) collective-permute-start(f32[256,256]{1,0:T(8,128)S(1)} %get-tuple-element.23), channel_id=1, source_target_pairs={{0,4},{4,0},{8,12},{12,8},{1,5},{5,1},{9,13},{13,9},{2,6},{6,2},{1... | collective-permute-start | bytes 786440 | tf_op jit(solution)/shard_map/ppermute | solution.py:313
  26.5 0.1 collective-permute-start.3
  26.6 7.1 %collective-permute-done.refs_1_ = f32[256,256]{1,0:T(8,128)S(1)} collective-permute-done((f32[256,256]{1,0:T(8,128)S(1)}, f32[256,256]{1,0:T(8,128)S(1)}, u32[]{:S(2)}, u32[]{:S(2)}) %collective-permute-start) | collective-permute-done | bytes 262176 | tf_op jit(solution)/shard_map/ppermute | solution.py:313
  33.7 0.6 forward.4.after
  34.2 9.2 %cross.5 = (f32[256,256]{1,0:T(8,128)S(1)}, f32[256,256]{1,0:T(8,128)S(1)}, bf16[8192,512]{1,0:T(8,128)(2,1)S(1)}) custom-call(s32[12]{0:T(128)S(1)} %stack.38.where, f32[512,1]{1,0:T(8,128)S(1)} %copy.22.phi.after.fown, bf16[512,16384]{1,0:T(8,128)(2,1)S(1)} %get-tuple-element.21.patterns, bf16[16384,1024]{1,0:T(8,128)(2,1)} %model.13, ...), custom_call_target="tpu_custom_call" | custom-call | flops 4294967296 | bytes 25165824 | tf_op jit(solution)/shard_map/cross/pallas_call | solution.py:106
  43.5 0.0 copy-start.2
  43.5 2.1 %collective-permute-start.5 = (f32[256,256]{1,0:T(8,128)S(1)}, f32[256,256]{1,0:T(8,128)S(1)}, u32[]{:S(2)}, u32[]{:S(2)}) collective-permute-start(f32[256,256]{1,0:T(8,128)S(1)} %get-tuple-element.29), channel_id=1, source_target_pairs={{0,4},{4,0},{8,12},{12,8},{1,5},{5,1},{9,13},{13,9},{2,6},{6,2},{1... | collective-permute-start | bytes 786440 | tf_op jit(solution)/shard_map/ppermute | solution.py:313
  45.6 0.0 collective-permute-done.3.refs_1_.refs_4_
  45.6 0.6 forward.5.after
  46.1 0.0 copy-start.3
  46.1 0.0 copy-start.4
  46.2 9.1 %cross.7 = (f32[256,256]{1,0:T(8,128)S(1)}, f32[256,256]{1,0:T(8,128)S(1)}) custom-call(s32[12]{0:T(128)S(1)} %stack.38.where, f32[512,1]{1,0:T(8,128)S(1)} %copy.22.phi.after.fown, bf16[512,16384]{1,0:T(8,128)(2,1)S(1)} %get-tuple-element.21.patterns, bf16[16384,1024]{1,0:T(8,128)(2,1)} %model.13, f32[128,256]{1,0:T(8,128)S(1)} %forward.5.after), custom_call_target="tpu_custom_call" | custom-call | flops 4294967296 | bytes 25165824 | tf_op jit(solution)/shard_map/cross/pallas_call | solution.py:106
  55.3 0.9 collective-permute-start.7
  56.2 2.9 %collective-permute-start.2 = (f32[128,256]{1,0:T(8,128)S(1)}, f32[128,256]{1,0:T(8,128)S(1)}, u32[]{:S(2)}, u32[]{:S(2)}) collective-permute-start(f32[128,256]{1,0:T(8,128)S(1)} %forward.4.after), channel_id=1, source_target_pairs={{0,8},{4,12},{8,0},{12,4},{1,9},{5,13},{9,1},{13,5},{2,10},{6,14},... | collective-permute-start | bytes 393224 | tf_op jit(solution)/shard_map/ppermute | solution.py:313
  59.1 0.0 collective-permute-start.4
  59.1 0.0 collective-permute-done.5.refs_1_.refs_7_
  59.1 0.6 forward.6
  59.7 3.0 %collective-permute-start.6 = (f32[128,256]{1,0:T(8,128)S(1)}, f32[128,256]{1,0:T(8,128)S(1)}, u32[]{:S(2)}, u32[]{:S(2)}) collective-permute-start(f32[128,256]{1,0:T(8,128)S(1)} %forward.6), channel_id=1, source_target_pairs={{0,8},{4,12},{8,0},{12,4},{1,9},{5,13},{9,1},{13,5},{2,10},{6,14},... | collective-permute-start | bytes 393224 | tf_op jit(solution)/shard_map/ppermute | solution.py:313
  62.6 5.6 %collective-permute-done.7.refs_1_.refs_10_ = f32[256,256]{1,0:T(8,128)S(1)} collective-permute-done((f32[256,256]{1,0:T(8,128)S(1)}, f32[256,256]{1,0:T(8,128)S(1)}, u32[]{:S(2)}, u32[]{:S(2)}) %collective-permute-start.7) | collective-permute-done | bytes 262176 | tf_op jit(solution)/shard_map/ppermute | solution.py:313
  68.3 0.6 forward.7
  68.8 0.1 collective-permute-start.8
  68.9 8.5 %collective-permute-done.4.refs_5_ = f32[128,256]{1,0:T(8,128)S(1)} collective-permute-done((f32[128,256]{1,0:T(8,128)S(1)}, f32[128,256]{1,0:T(8,128)S(1)}, u32[]{:S(2)}, u32[]{:S(2)}) %collective-permute-start.4) | collective-permute-done | bytes 131104 | tf_op jit(solution)/shard_map/ppermute | solution.py:313
  77.4 2.8 %collective-permute-done.6.refs_8_ = f32[128,256]{1,0:T(8,128)S(1)} collective-permute-done((f32[128,256]{1,0:T(8,128)S(1)}, f32[128,256]{1,0:T(8,128)S(1)}, u32[]{:S(2)}, u32[]{:S(2)}) %collective-permute-start.6) | collective-permute-done | bytes 131104 | tf_op jit(solution)/shard_map/ppermute | solution.py:313
  80.2 1.6 %collective-permute-done.8.refs_11_ = f32[128,256]{1,0:T(8,128)S(1)} collective-permute-done((f32[128,256]{1,0:T(8,128)S(1)}, f32[128,256]{1,0:T(8,128)S(1)}, u32[]{:S(2)}, u32[]{:S(2)}) %collective-permute-start.8) | collective-permute-done | bytes 131104 | tf_op jit(solution)/shard_map/ppermute | solution.py:313
  81.8 0.8 softmax.1
  82.6 1.7 %collective-permute-start.9 = (f32[16,128]{1,0:T(8,128)S(1)}, f32[16,128]{1,0:T(8,128)S(1)}, u32[]{:S(2)}, u32[]{:S(2)}) collective-permute-start(f32[16,128]{1,0:T(8,128)S(1)} %get-tuple-element.33.own.mine), channel_id=1, source_target_pairs={{0,2},{2,0},{1,3},{3,1},{4,6},{6,4},{5,7},{7,5},{8,10},{10,8},{9,1... | collective-permute-start | bytes 24584 | tf_op jit(solution)/shard_map/ppermute | solution.py:313
  84.3 2.0 %collective-permute-done.9.other = f32[16,128]{1,0:T(8,128)S(1)} collective-permute-done((f32[16,128]{1,0:T(8,128)S(1)}, f32[16,128]{1,0:T(8,128)S(1)}, u32[]{:S(2)}, u32[]{:S(2)}) %collective-permute-start.9) | collective-permute-done | bytes 8224 | tf_op jit(solution)/shard_map/ppermute | solution.py:313
  86.3 0.7 weights.1
  87.1 0.0 slice-start
  87.1 0.0 slice-start.1
  87.1 2.6 %collective-permute-start.18 = (bf16[128,256]{1,0:T(8,128)(2,1)S(1)}, bf16[128,256]{1,0:T(8,128)(2,1)S(1)}, u32[]{:S(2)}, u32[]{:S(2)}) collective-permute-start(bf16[128,256]{1,0:T(8,128)(2,1)S(1)} %get-tuple-element.36.refs_0_), channel_id=1, source_target_pairs={{0,12},{4,8},{8,4},{12,0},{1,13},{5,9},{9,5},{13,1},{2,14},{6,10},... | collective-permute-start | bytes 196616 | tf_op jit(solution)/shard_map/ppermute | solution.py:313
  89.6 0.0 collective-permute-start.17
  89.6 1.9 %collective-permute-start.16 = (bf16[128,256]{1,0:T(8,128)(2,1)S(1)}, bf16[128,256]{1,0:T(8,128)(2,1)S(1)}, u32[]{:S(2)}, u32[]{:S(2)}) collective-permute-start(bf16[128,256]{1,0:T(8,128)(2,1)S(1)} %get-tuple-element.36.refs_0_), channel_id=1, source_target_pairs={{0,4},{4,0},{8,12},{12,8},{1,5},{5,1},{9,13},{13,9},{2,6},{6,2},{1... | collective-permute-start | bytes 196616 | tf_op jit(solution)/shard_map/ppermute | solution.py:313
  91.5 1.7 %collective-permute-done.18.refs_3_ = bf16[128,256]{1,0:T(8,128)(2,1)S(1)} collective-permute-done((bf16[128,256]{1,0:T(8,128)(2,1)S(1)}, bf16[128,256]{1,0:T(8,128)(2,1)S(1)}, u32[]{:S(2)}, u32[]{:S(2)}) %collective-permute-start.18) | collective-permute-done | bytes 65568 | tf_op jit(solution)/shard_map/ppermute | solution.py:313
  93.2 1.6 %collective-permute-done.17.refs_2_ = bf16[128,256]{1,0:T(8,128)(2,1)S(1)} collective-permute-done((bf16[128,256]{1,0:T(8,128)(2,1)S(1)}, bf16[128,256]{1,0:T(8,128)(2,1)S(1)}, u32[]{:S(2)}, u32[]{:S(2)}) %collective-permute-start.17) | collective-permute-done | bytes 65568 | tf_op jit(solution)/shard_map/ppermute | solution.py:313
  94.8 0.6 pack.3.wown
  95.4 0.1 collective-permute-start.19
  95.5 0.5 collective-permute-start.20
  96.0 2.3 %collective-permute-start.15 = (bf16[128,256]{1,0:T(8,128)(2,1)S(1)}, bf16[128,256]{1,0:T(8,128)(2,1)S(1)}, u32[]{:S(2)}, u32[]{:S(2)}) collective-permute-start(bf16[128,256]{1,0:T(8,128)(2,1)S(1)} %get-tuple-element.35.refs_0_), channel_id=1, source_target_pairs={{0,12},{4,8},{8,4},{12,0},{1,13},{5,9},{9,5},{13,1},{2,14},{6,10},... | collective-permute-start | bytes 196616 | tf_op jit(solution)/shard_map/ppermute | solution.py:313
  98.3 0.2 collective-permute-start.14
  98.4 1.9 %collective-permute-start.13 = (bf16[128,256]{1,0:T(8,128)(2,1)S(1)}, bf16[128,256]{1,0:T(8,128)(2,1)S(1)}, u32[]{:S(2)}, u32[]{:S(2)}) collective-permute-start(bf16[128,256]{1,0:T(8,128)(2,1)S(1)} %get-tuple-element.35.refs_0_), channel_id=1, source_target_pairs={{0,4},{4,0},{8,12},{12,8},{1,5},{5,1},{9,13},{13,9},{2,6},{6,2},{1... | collective-permute-start | bytes 196616 | tf_op jit(solution)/shard_map/ppermute | solution.py:313
  100.4 3.4 %copy-done.1 = bf16[8192,512]{1,0:T(8,128)(2,1)S(1)} copy-done((bf16[8192,512]{1,0:T(8,128)(2,1)S(1)}, bf16[8192,512]{1,0:T(8,128)(2,1)}, u32[]{:S(2)}) %copy-start.1) | copy-done | bytes 8388632
  103.8 8.5 %numer.3.refs_4_.refs_0_ = bf16[8192,1024]{1,0:T(8,128)(2,1)} custom-call(s32[12]{0:T(128)S(1)} %stack.38.where, bf16[8192,512]{1,0:T(8,128)(2,1)S(1)} %bitcast.11, bf16[8192,512]{1,0:T(8,128)(2,1)S(1)} %copy-done.1, bf16[512,256]{1,0:T(8,128)(2,1)S(1)} %pack.3.wown, bf16[512,256]{1,0:T(8,128)(2,1)S(1)} %collective-permute-done.19.wsib, ...), custom_call_target="tpu_custom_call" | custom-call | flops 4294967296 | bytes 25165824 | tf_op jit(solution)/shard_map/numer/pallas_call | solution.py:294
  112.3 0.0 collective-permute-done.14.refs_2_
  112.3 0.0 collective-permute-done.13.refs_1_
  112.3 0.6 pack.4.wown
  112.9 0.1 collective-permute-start.21
  113.0 2.4 %collective-permute-start.12 = (bf16[128,512]{1,0:T(8,128)(2,1)S(1)}, bf16[128,512]{1,0:T(8,128)(2,1)S(1)}, u32[]{:S(2)}, u32[]{:S(2)}) collective-permute-start(bf16[128,512]{1,0:T(8,128)(2,1)S(1)} %get-tuple-element.34.refs_0_), channel_id=1, source_target_pairs={{0,12},{4,8},{8,4},{12,0},{1,13},{5,9},{9,5},{13,1},{2,14},{6,10},... | collective-permute-start | bytes 393224 | tf_op jit(solution)/shard_map/ppermute | solution.py:313
  115.4 0.0 collective-permute-start.11
  115.4 2.1 %collective-permute-start.10 = (bf16[128,512]{1,0:T(8,128)(2,1)S(1)}, bf16[128,512]{1,0:T(8,128)(2,1)S(1)}, u32[]{:S(2)}, u32[]{:S(2)}) collective-permute-start(bf16[128,512]{1,0:T(8,128)(2,1)S(1)} %get-tuple-element.34.refs_0_), channel_id=1, source_target_pairs={{0,4},{4,0},{8,12},{12,8},{1,5},{5,1},{9,13},{13,9},{2,6},{6,2},{1... | collective-permute-start | bytes 393224 | tf_op jit(solution)/shard_map/ppermute | solution.py:313
  117.4 0.0 collective-permute-done.21.wsib
  117.5 8.4 %numer.4.refs_4_.refs_0_ = bf16[8192,1024]{1,0:T(8,128)(2,1)} custom-call(s32[12]{0:T(128)S(1)} %stack.38.where, bf16[8192,512]{1,0:T(8,128)(2,1)S(1)} %bitcast.11, bf16[8192,512]{1,0:T(8,128)(2,1)S(1)} %copy-done.1, bf16[512,256]{1,0:T(8,128)(2,1)S(1)} %pack.4.wown, ...), custom_call_target="tpu_custom_call", output_to_operand_aliasing={{}: (8, {})} | custom-call | flops 4294967296 | bytes 25165824 | tf_op jit(solution)/shard_map/numer/pallas_call | solution.py:294
  125.9 0.0 collective-permute-done.12.refs_3_
  125.9 1.0 collective-permute-done.11.refs_2_
  126.9 0.6 pack.5.wown
  127.5 0.1 collective-permute-start.22
  127.6 1.9 %collective-permute-done.22.wsib = bf16[512,512]{1,0:T(8,128)(2,1)S(1)} collective-permute-done((bf16[512,512]{1,0:T(8,128)(2,1)S(1)}, bf16[512,512]{1,0:T(8,128)(2,1)S(1)}, u32[]{:S(2)}, u32[]{:S(2)}) %collective-permute-start.22) | collective-permute-done | bytes 524320 | tf_op jit(solution)/shard_map/ppermute | solution.py:313
  129.5 13.4 %numer.5 = bf16[8192,1024]{1,0:T(8,128)(2,1)} custom-call(s32[12]{0:T(128)S(1)} %stack.38.where, bf16[8192,512]{1,0:T(8,128)(2,1)S(1)} %bitcast.11, bf16[8192,512]{1,0:T(8,128)(2,1)S(1)} %copy-done.1, bf16[512,512]{1,0:T(8,128)(2,1)S(1)} %pack.5.wown, bf16[512,512]{1,0:T(8,128)(2,1)S(1)} %collective-permute-done.22.wsib, ...), custom_call_target="tpu_custom_call", output_to_operand_aliasing={{}: (8, {})} | custom-call | flops 8589934592 | bytes 33554432 | tf_op jit(solution)/shard_map/numer/pallas_call | solution.py:294
  (16 shorter events, 0.0 us)
Async XLA Ops:
  23.3 58.4 %collective-permute-start.1 = (bf16[8192,512]{1,0:T(8,128)(2,1)}, bf16[8192,512]{1,0:T(8,128)(2,1)S(1)}, u32[]{:S(2)}, u32[]{:S(2)}) collective-permute-start(bf16[8192,512]{1,0:T(8,128)(2,1)} %get-tuple-element.25), channel_id=1, source_target_pairs={{0,1},{1,0},{2,3},{3,2},{4,5},{5,4},{6,7},{7,6},{8,9},{9,8},{10,11... | collective-permute-start | bytes 25165832 | tf_op jit(solution)/shard_map/ppermute | solution.py:313
  23.9 9.8 %collective-permute-start = (f32[256,256]{1,0:T(8,128)S(1)}, f32[256,256]{1,0:T(8,128)S(1)}, u32[]{:S(2)}, u32[]{:S(2)}) collective-permute-start(f32[256,256]{1,0:T(8,128)S(1)} %get-tuple-element.23), channel_id=1, source_target_pairs={{0,4},{4,0},{8,12},{12,8},{1,5},{5,1},{9,13},{13,9},{2,6},{6,2},{1... | collective-permute-start | bytes 786440 | tf_op jit(solution)/shard_map/ppermute | solution.py:313
  26.5 19.0 %collective-permute-start.3 = (f32[256,256]{1,0:T(8,128)S(1)}, f32[256,256]{1,0:T(8,128)S(1)}, u32[]{:S(2)}, u32[]{:S(2)}) collective-permute-start(f32[256,256]{1,0:T(8,128)S(1)} %get-tuple-element.27), channel_id=1, source_target_pairs={{0,4},{4,0},{8,12},{12,8},{1,5},{5,1},{9,13},{13,9},{2,6},{6,2},{1... | collective-permute-start | bytes 786440 | tf_op jit(solution)/shard_map/ppermute | solution.py:313
  43.5 11.8 %copy-start.2 = (bf16[8192,512]{1,0:T(8,128)(2,1)}, bf16[8192,512]{1,0:T(8,128)(2,1)S(1)}, u32[]{:S(2)}) copy-start(bf16[8192,512]{1,0:T(8,128)(2,1)S(1)} %get-tuple-element.24.pown) | copy-start | bytes 25165828
  43.5 15.6 %collective-permute-start.5 = (f32[256,256]{1,0:T(8,128)S(1)}, f32[256,256]{1,0:T(8,128)S(1)}, u32[]{:S(2)}, u32[]{:S(2)}) collective-permute-start(f32[256,256]{1,0:T(8,128)S(1)} %get-tuple-element.29), channel_id=1, source_target_pairs={{0,4},{4,0},{8,12},{12,8},{1,5},{5,1},{9,13},{13,9},{2,6},{6,2},{1... | collective-permute-start | bytes 786440 | tf_op jit(solution)/shard_map/ppermute | solution.py:313
  46.1 35.6 %copy-start.3 = (s32[1024]{0:T(1024)S(1)}, s32[1024]{0:T(1024)}, u32[]{:S(2)}) copy-start(s32[1024]{0:T(1024)} %param.11) | copy-start | bytes 12292
  46.1 35.6 %copy-start.4 = (f32[8]{0:T(128)S(1)}, f32[8]{0:T(128)}, u32[]{:S(2)}) copy-start(f32[8]{0:T(128)} %table.1) | copy-start | bytes 100
  55.3 13.0 %collective-permute-start.7 = (f32[256,256]{1,0:T(8,128)S(1)}, f32[256,256]{1,0:T(8,128)S(1)}, u32[]{:S(2)}, u32[]{:S(2)}) collective-permute-start(f32[256,256]{1,0:T(8,128)S(1)} %get-tuple-element.31), channel_id=1, source_target_pairs={{0,4},{4,0},{8,12},{12,8},{1,5},{5,1},{9,13},{13,9},{2,6},{6,2},{1... | collective-permute-start | bytes 786440 | tf_op jit(solution)/shard_map/ppermute | solution.py:313
  56.2 12.7 %collective-permute-start.2 = (f32[128,256]{1,0:T(8,128)S(1)}, f32[128,256]{1,0:T(8,128)S(1)}, u32[]{:S(2)}, u32[]{:S(2)}) collective-permute-start(f32[128,256]{1,0:T(8,128)S(1)} %forward.4.after), channel_id=1, source_target_pairs={{0,8},{4,12},{8,0},{12,4},{1,9},{5,13},{9,1},{13,5},{2,10},{6,14},... | collective-permute-start | bytes 393224 | tf_op jit(solution)/shard_map/ppermute | solution.py:313
  59.1 18.3 %collective-permute-start.4 = (f32[128,256]{1,0:T(8,128)S(1)}, f32[128,256]{1,0:T(8,128)S(1)}, u32[]{:S(2)}, u32[]{:S(2)}) collective-permute-start(f32[128,256]{1,0:T(8,128)S(1)} %forward.5.after), channel_id=1, source_target_pairs={{0,8},{4,12},{8,0},{12,4},{1,9},{5,13},{9,1},{13,5},{2,10},{6,14},... | collective-permute-start | bytes 393224 | tf_op jit(solution)/shard_map/ppermute | solution.py:313
  59.7 20.5 %collective-permute-start.6 = (f32[128,256]{1,0:T(8,128)S(1)}, f32[128,256]{1,0:T(8,128)S(1)}, u32[]{:S(2)}, u32[]{:S(2)}) collective-permute-start(f32[128,256]{1,0:T(8,128)S(1)} %forward.6), channel_id=1, source_target_pairs={{0,8},{4,12},{8,0},{12,4},{1,9},{5,13},{9,1},{13,5},{2,10},{6,14},... | collective-permute-start | bytes 393224 | tf_op jit(solution)/shard_map/ppermute | solution.py:313
  68.8 12.9 %collective-permute-start.8 = (f32[128,256]{1,0:T(8,128)S(1)}, f32[128,256]{1,0:T(8,128)S(1)}, u32[]{:S(2)}, u32[]{:S(2)}) collective-permute-start(f32[128,256]{1,0:T(8,128)S(1)} %forward.7), channel_id=1, source_target_pairs={{0,8},{4,12},{8,0},{12,4},{1,9},{5,13},{9,1},{13,5},{2,10},{6,14},... | collective-permute-start | bytes 393224 | tf_op jit(solution)/shard_map/ppermute | solution.py:313
  81.8 13.6 %copy-start = (bf16[8192,512]{1,0:T(8,128)(2,1)}, bf16[8192,512]{1,0:T(8,128)(2,1)S(1)}, u32[]{:S(2)}) copy-start(bf16[8192,512]{1,0:T(8,128)(2,1)S(1)} %collective-permute-done.1.after.psib) | copy-start | bytes 25165828
  82.6 3.7 %collective-permute-start.9 = (f32[16,128]{1,0:T(8,128)S(1)}, f32[16,128]{1,0:T(8,128)S(1)}, u32[]{:S(2)}, u32[]{:S(2)}) collective-permute-start(f32[16,128]{1,0:T(8,128)S(1)} %get-tuple-element.33.own.mine), channel_id=1, source_target_pairs={{0,2},{2,0},{1,3},{3,1},{4,6},{6,4},{5,7},{7,5},{8,10},{10,8},{9,1... | collective-permute-start | bytes 24584 | tf_op jit(solution)/shard_map/ppermute | solution.py:313
  87.1 13.3 %slice-start = ((s8[8388608]{0:T(1024)(128)(4,1)}), s8[4194304]{0:T(1024)(128)(4,1)S(1)}, s32[]{:S(2)}) async-start(s8[8388608]{0:T(1024)(128)(4,1)} %bitcast.10), calls=%async_computation | async-start | bytes 8388608
  87.1 13.3 %slice-start.1 = ((s8[8388608]{0:T(1024)(128)(4,1)}), s8[4194304]{0:T(1024)(128)(4,1)S(1)}, s32[]{:S(2)}) async-start(s8[8388608]{0:T(1024)(128)(4,1)} %bitcast.10), calls=%async_computation.1 | async-start | bytes 8388608
  87.1 6.1 %collective-permute-start.18 = (bf16[128,256]{1,0:T(8,128)(2,1)S(1)}, bf16[128,256]{1,0:T(8,128)(2,1)S(1)}, u32[]{:S(2)}, u32[]{:S(2)}) collective-permute-start(bf16[128,256]{1,0:T(8,128)(2,1)S(1)} %get-tuple-element.36.refs_0_), channel_id=1, source_target_pairs={{0,12},{4,8},{8,4},{12,0},{1,13},{5,9},{9,5},{13,1},{2,14},{6,10},... | collective-permute-start | bytes 196616 | tf_op jit(solution)/shard_map/ppermute | solution.py:313
  89.6 5.2 %collective-permute-start.17 = (bf16[128,256]{1,0:T(8,128)(2,1)S(1)}, bf16[128,256]{1,0:T(8,128)(2,1)S(1)}, u32[]{:S(2)}, u32[]{:S(2)}) collective-permute-start(bf16[128,256]{1,0:T(8,128)(2,1)S(1)} %get-tuple-element.36.refs_0_), channel_id=1, source_target_pairs={{0,8},{4,12},{8,0},{12,4},{1,9},{5,13},{9,1},{13,5},{2,10},{6,14},... | collective-permute-start | bytes 196616 | tf_op jit(solution)/shard_map/ppermute | solution.py:313
  89.6 5.2 %collective-permute-start.16 = (bf16[128,256]{1,0:T(8,128)(2,1)S(1)}, bf16[128,256]{1,0:T(8,128)(2,1)S(1)}, u32[]{:S(2)}, u32[]{:S(2)}) collective-permute-start(bf16[128,256]{1,0:T(8,128)(2,1)S(1)} %get-tuple-element.36.refs_0_), channel_id=1, source_target_pairs={{0,4},{4,0},{8,12},{12,8},{1,5},{5,1},{9,13},{13,9},{2,6},{6,2},{1... | collective-permute-start | bytes 196616 | tf_op jit(solution)/shard_map/ppermute | solution.py:313
  95.4 5.0 %collective-permute-start.19 = (bf16[512,256]{1,0:T(8,128)(2,1)S(1)}, bf16[512,256]{1,0:T(8,128)(2,1)S(1)}, u32[]{:S(2)}, u32[]{:S(2)}) collective-permute-start(bf16[512,256]{1,0:T(8,128)(2,1)S(1)} %pack.3.wown), channel_id=1, source_target_pairs={{0,1},{1,0},{2,3},{3,2},{4,5},{5,4},{6,7},{7,6},{8,9},{9,8},{10,11... | collective-permute-start | bytes 786440 | tf_op jit(solution)/shard_map/ppermute | solution.py:313
  95.5 4.9 %collective-permute-start.20 = (f32[512,1]{1,0:T(8,128)S(1)}, f32[512,1]{1,0:T(8,128)S(1)}, u32[]{:S(2)}, u32[]{:S(2)}) collective-permute-start(f32[512,1]{1,0:T(8,128)S(1)} %copy.22.phi.after.fown), channel_id=1, source_target_pairs={{0,1},{1,0},{2,3},{3,2},{4,5},{5,4},{6,7},{7,6},{8,9},{9,8},{10,11... | collective-permute-start | bytes 6152 | tf_op jit(solution)/shard_map/ppermute | solution.py:313
  96.0 16.3 %collective-permute-start.15 = (bf16[128,256]{1,0:T(8,128)(2,1)S(1)}, bf16[128,256]{1,0:T(8,128)(2,1)S(1)}, u32[]{:S(2)}, u32[]{:S(2)}) collective-permute-start(bf16[128,256]{1,0:T(8,128)(2,1)S(1)} %get-tuple-element.35.refs_0_), channel_id=1, source_target_pairs={{0,12},{4,8},{8,4},{12,0},{1,13},{5,9},{9,5},{13,1},{2,14},{6,10},... | collective-permute-start | bytes 196616 | tf_op jit(solution)/shard_map/ppermute | solution.py:313
  98.3 14.1 %collective-permute-start.14 = (bf16[128,256]{1,0:T(8,128)(2,1)S(1)}, bf16[128,256]{1,0:T(8,128)(2,1)S(1)}, u32[]{:S(2)}, u32[]{:S(2)}) collective-permute-start(bf16[128,256]{1,0:T(8,128)(2,1)S(1)} %get-tuple-element.35.refs_0_), channel_id=1, source_target_pairs={{0,8},{4,12},{8,0},{12,4},{1,9},{5,13},{9,1},{13,5},{2,10},{6,14},... | collective-permute-start | bytes 196616 | tf_op jit(solution)/shard_map/ppermute | solution.py:313
  98.4 13.9 %collective-permute-start.13 = (bf16[128,256]{1,0:T(8,128)(2,1)S(1)}, bf16[128,256]{1,0:T(8,128)(2,1)S(1)}, u32[]{:S(2)}, u32[]{:S(2)}) collective-permute-start(bf16[128,256]{1,0:T(8,128)(2,1)S(1)} %get-tuple-element.35.refs_0_), channel_id=1, source_target_pairs={{0,4},{4,0},{8,12},{12,8},{1,5},{5,1},{9,13},{13,9},{2,6},{6,2},{1... | collective-permute-start | bytes 196616 | tf_op jit(solution)/shard_map/ppermute | solution.py:313
  100.4 3.4 %copy-start.1 = (bf16[8192,512]{1,0:T(8,128)(2,1)S(1)}, bf16[8192,512]{1,0:T(8,128)(2,1)}, u32[]{:S(2)}) copy-start(bf16[8192,512]{1,0:T(8,128)(2,1)} %copy-done) | copy-start | bytes 25165828
  112.9 4.5 %collective-permute-start.21 = (bf16[512,256]{1,0:T(8,128)(2,1)S(1)}, bf16[512,256]{1,0:T(8,128)(2,1)S(1)}, u32[]{:S(2)}, u32[]{:S(2)}) collective-permute-start(bf16[512,256]{1,0:T(8,128)(2,1)S(1)} %pack.4.wown), channel_id=1, source_target_pairs={{0,1},{1,0},{2,3},{3,2},{4,5},{5,4},{6,7},{7,6},{8,9},{9,8},{10,11... | collective-permute-start | bytes 786440 | tf_op jit(solution)/shard_map/ppermute | solution.py:313
  113.0 12.9 %collective-permute-start.12 = (bf16[128,512]{1,0:T(8,128)(2,1)S(1)}, bf16[128,512]{1,0:T(8,128)(2,1)S(1)}, u32[]{:S(2)}, u32[]{:S(2)}) collective-permute-start(bf16[128,512]{1,0:T(8,128)(2,1)S(1)} %get-tuple-element.34.refs_0_), channel_id=1, source_target_pairs={{0,12},{4,8},{8,4},{12,0},{1,13},{5,9},{9,5},{13,1},{2,14},{6,10},... | collective-permute-start | bytes 393224 | tf_op jit(solution)/shard_map/ppermute | solution.py:313
  115.4 11.5 %collective-permute-start.11 = (bf16[128,512]{1,0:T(8,128)(2,1)S(1)}, bf16[128,512]{1,0:T(8,128)(2,1)S(1)}, u32[]{:S(2)}, u32[]{:S(2)}) collective-permute-start(bf16[128,512]{1,0:T(8,128)(2,1)S(1)} %get-tuple-element.34.refs_0_), channel_id=1, source_target_pairs={{0,8},{4,12},{8,0},{12,4},{1,9},{5,13},{9,1},{13,5},{2,10},{6,14},... | collective-permute-start | bytes 393224 | tf_op jit(solution)/shard_map/ppermute | solution.py:313
  115.4 11.5 %collective-permute-start.10 = (bf16[128,512]{1,0:T(8,128)(2,1)S(1)}, bf16[128,512]{1,0:T(8,128)(2,1)S(1)}, u32[]{:S(2)}, u32[]{:S(2)}) collective-permute-start(bf16[128,512]{1,0:T(8,128)(2,1)S(1)} %get-tuple-element.34.refs_0_), channel_id=1, source_target_pairs={{0,4},{4,0},{8,12},{12,8},{1,5},{5,1},{9,13},{13,9},{2,6},{6,2},{1... | collective-permute-start | bytes 393224 | tf_op jit(solution)/shard_map/ppermute | solution.py:313
  127.5 2.0 %collective-permute-start.22 = (bf16[512,512]{1,0:T(8,128)(2,1)S(1)}, bf16[512,512]{1,0:T(8,128)(2,1)S(1)}, u32[]{:S(2)}, u32[]{:S(2)}) collective-permute-start(bf16[512,512]{1,0:T(8,128)(2,1)S(1)} %pack.5.wown), channel_id=1, source_target_pairs={{0,1},{1,0},{2,3},{3,2},{4,5},{5,4},{6,7},{7,6},{8,9},{9,8},{10,11... | collective-permute-start | bytes 1572872 | tf_op jit(solution)/shard_map/ppermute | solution.py:313

commit v3 on v2

--- a/solution.py
+++ b/solution.py
@@ -231,6 +231,29 @@
     )(where, *parts, after)
 
 
+def load_kernel(source, after, out, sems):
+    n = sems.shape[0]
+    rows = out.shape[0] // n
+    pieces = [pl.ds(i * rows, rows) for i in range(n)]
+    copies = [pltpu.make_async_copy(source.at[p], out.at[p], sems.at[i]) for i, p in enumerate(pieces)]
+    for copy in copies:
+        copy.start()
+    for copy in copies:
+        copy.wait()
+
+
+def load(source, after):
+    return pl.pallas_call(
+        load_kernel,
+        out_shape=pltpu.VMEM(source.shape, source.dtype),
+        in_specs=[HBM, ANY],
+        out_specs=VMEM,
+        scratch_shapes=[pltpu.SemaphoreType.DMA((4,))],
+        compiler_params=params(8 * MIB),
+        name="load",
+    )(pltpu.with_memory_space_constraint(source, pltpu.HBM), after)
+
+
 def numer_kernel(where, pown, psib, wown, wsib, fown, fsib, model, *refs, column, tm, sub):
     out, mbuf, obuf, msem, osem = refs[-5:]
     pixels, tn = pown.shape[0], wown.shape[1]
@@ -292,7 +315,7 @@
         args.append(pltpu.with_memory_space_constraint(previous, pltpu.HBM))
         aliases = {len(args) - 1: 0}
     return pl.pallas_call(
-        functools.partial(numer_kernel, column=column, tm=tm, sub=min(512, tm)),
+        functools.partial(numer_kernel, column=column, tm=tm, sub=min(256, tm)),
         out_shape=jax.ShapeDtypeStruct((pixels, columns), jnp.bfloat16),
         in_specs=in_specs,
         out_specs=HBM,
@@ -313,7 +336,7 @@
     return lax.ppermute(value, axis, [(i, i ^ distance) for i in range(size)])
 
 
-def local(patterns, model, scale_table, scale_index, weight_table, weight_class, *, sizes):
+def iteration(patterns, model, scale_table, scale_index, weight_table, weight_class, *, sizes):
     pix, ori = sizes["pix"], sizes["ori"]
     hops = pix.bit_length() - 1
     rows, columns = patterns.shape[0], model.shape[1]
@@ -368,7 +391,8 @@
             after = reduce_further(c - 1)
         if c == 1:
             psib = exchange(turned[False], "pat", 2, 1)
-    reduce_further(chunks - 1)
+    last = reduce_further(chunks - 1)
+    psib = load(psib, last)
     held = [term for c in range(chunks) for term in terms[c]]
     phi_sib = exchange(phi, "pat", 2, 1)
 
@@ -405,7 +429,7 @@
         P(("grp", "ori")),
     )
     return jax.shard_map(
-        functools.partial(local, sizes=dict(mesh.shape)),
+        functools.partial(iteration, sizes=dict(mesh.shape)),
         mesh=mesh,
         in_specs=placed,
         out_specs=P(("grp", "pix", "pat"), "ori"),

time: 143 us -> 139 us (0.972)
  Pallas kernels: 76.5 us -> 80.1 us
  local copies, waits for them, and re-layouts: 3.65 us -> 0.25 us
  waiting for transfers between devices: 33.7 us -> 30.4 us
    pallas_call x0 -> x1, Pallas kernels: none -> 3.5 us  [load(): pl.pallas_call(load_kernel, out_shape=pltpu.VMEM(source.shape, source.dty...]
    unnamed x14 -> x4, local copies, waits for them, and re-layouts: 3.41 us -> 0.01 us
    ppermute x23, waiting for transfers between devices: 33.7 us -> 30.4 us  [exchange(): return lax.ppermute(value, axis, [(i, i ^ distance) for i in range(size)])]
  transfers between devices with their start and end apart: 23 -> 23, of which waited for: 10 -> 10; matrix products, arithmetic and copies ran while one was open for 0% -> 0% of each run, Pallas kernels for 26% -> 30%
where the time goes in v3:
time: 139 us
  Pallas kernels  80.1 us (58%)
  waiting for transfers between devices  30.4 us (22%)
  starting transfers between devices  27.2 us (20%)
    pallas_call x4, Pallas kernels, cross_chunk(): pl.pallas_call(functools.partial(cross_kernel, column=column, tk=tk, step...  40.7 us
    ppermute x23, waiting for transfers between devices, exchange(): return lax.ppermute(value, axis, [(i, i ^ distance) for i in range(size)])  30.4 us
    pallas_call x3, Pallas kernels, numer_chunk(): pl.pallas_call(functools.partial(numer_kernel, column=column, tm=tm, sub=...  30.4 us
    ppermute x23, starting transfers between devices, exchange(): return lax.ppermute(value, axis, [(i, i ^ distance) for i in range(size)])  27.2 us
    pallas_call x1, Pallas kernels, load(): pl.pallas_call(load_kernel, out_shape=pltpu.VMEM(source.shape, source.dty...  3.5 us
  transfers between devices with their start and end apart: 23, of which 10 were waited for; matrix products, arithmetic and copies ran while one was open for 0% of the time, Pallas kernels for 30%

profile of v3, /device:TPU:0, one launch (start us, length us, event | category | flops | bytes accessed | tf_op | source)
XLA Modules:
  0.0 139.1 jit_solution(3929412714359927380)
XLA Ops:
  0.0 0.8 select_reduce_fusion
  0.8 0.1 copy.22.phi.after.fown
  0.9 0.1 stack.38.where
  1.0 10.0 %cross.4 = (f32[256,256]{1,0:T(8,128)S(1)}, f32[256,256]{1,0:T(8,128)S(1)}, bf16[512,16384]{1,0:T(8,128)(2,1)S(1)}) custom-call(s32[12]{0:T(128)S(1)} %stack.38.where, f32[512,1]{1,0:T(8,128)S(1)} %copy.22.phi.after.fown, bf16[512,16384]{1,0:T(8,128)(2,1)} %patterns.1, bf16[16384,1024]{1,0:T(8,128)(2,1)} %model.13, f32[512,1]{1,0:T(8,128)S(1)} %copy.22.phi.after.fown), custom_call_target="tpu_custom_call" | custom-call | flops 4294967296 | bytes 25165824 | tf_op jit(solution)/shard_map/cross/pallas_call | solution.py:106
  11.0 12.4 %cross.6 = (f32[256,256]{1,0:T(8,128)S(1)}, f32[256,256]{1,0:T(8,128)S(1)}, bf16[8192,512]{1,0:T(8,128)(2,1)}) custom-call(s32[12]{0:T(128)S(1)} %stack.38.where, f32[512,1]{1,0:T(8,128)S(1)} %copy.22.phi.after.fown, bf16[512,16384]{1,0:T(8,128)(2,1)S(1)} %get-tuple-element.21.patterns, bf16[16384,1024]{1,0:T(8,128)(2,1)} %model.13, ...), custom_call_target="tpu_custom_call" | custom-call | flops 4294967296 | bytes 25165824 | tf_op jit(solution)/shard_map/cross/pallas_call | solution.py:106
  23.5 0.6 collective-permute-start.1
  24.0 2.6 %collective-permute-start = (f32[256,256]{1,0:T(8,128)S(1)}, f32[256,256]{1,0:T(8,128)S(1)}, u32[]{:S(2)}, u32[]{:S(2)}) collective-permute-start(f32[256,256]{1,0:T(8,128)S(1)} %get-tuple-element.23), channel_id=1, source_target_pairs={{0,4},{4,0},{8,12},{12,8},{1,5},{5,1},{9,13},{13,9},{2,6},{6,2},{1... | collective-permute-start | bytes 786440 | tf_op jit(solution)/shard_map/ppermute | solution.py:336
  26.7 0.1 collective-permute-start.2
  26.7 7.1 %collective-permute-done.refs_1_ = f32[256,256]{1,0:T(8,128)S(1)} collective-permute-done((f32[256,256]{1,0:T(8,128)S(1)}, f32[256,256]{1,0:T(8,128)S(1)}, u32[]{:S(2)}, u32[]{:S(2)}) %collective-permute-start) | collective-permute-done | bytes 262176 | tf_op jit(solution)/shard_map/ppermute | solution.py:336
  33.8 0.6 forward.4.after
  34.4 9.2 %cross.5 = (f32[256,256]{1,0:T(8,128)S(1)}, f32[256,256]{1,0:T(8,128)S(1)}, bf16[8192,512]{1,0:T(8,128)(2,1)S(1)}) custom-call(s32[12]{0:T(128)S(1)} %stack.38.where, f32[512,1]{1,0:T(8,128)S(1)} %copy.22.phi.after.fown, bf16[512,16384]{1,0:T(8,128)(2,1)S(1)} %get-tuple-element.21.patterns, bf16[16384,1024]{1,0:T(8,128)(2,1)} %model.13, ...), custom_call_target="tpu_custom_call" | custom-call | flops 4294967296 | bytes 25165824 | tf_op jit(solution)/shard_map/cross/pallas_call | solution.py:106
  43.6 2.1 %collective-permute-start.6 = (f32[256,256]{1,0:T(8,128)S(1)}, f32[256,256]{1,0:T(8,128)S(1)}, u32[]{:S(2)}, u32[]{:S(2)}) collective-permute-start(f32[256,256]{1,0:T(8,128)S(1)} %get-tuple-element.31), channel_id=1, source_target_pairs={{0,4},{4,0},{8,12},{12,8},{1,5},{5,1},{9,13},{13,9},{2,6},{6,2},{1... | collective-permute-start | bytes 786440 | tf_op jit(solution)/shard_map/ppermute | solution.py:336
  45.7 0.0 collective-permute-done.2.refs_1_.refs_4_
  45.7 0.6 forward.5.after
  46.2 9.1 %cross.7 = (f32[256,256]{1,0:T(8,128)S(1)}, f32[256,256]{1,0:T(8,128)S(1)}) custom-call(s32[12]{0:T(128)S(1)} %stack.38.where, f32[512,1]{1,0:T(8,128)S(1)} %copy.22.phi.after.fown, bf16[512,16384]{1,0:T(8,128)(2,1)S(1)} %get-tuple-element.21.patterns, bf16[16384,1024]{1,0:T(8,128)(2,1)} %model.13, f32[128,256]{1,0:T(8,128)S(1)} %forward.5.after), custom_call_target="tpu_custom_call" | custom-call | flops 4294967296 | bytes 25165824 | tf_op jit(solution)/shard_map/cross/pallas_call | solution.py:106
  55.4 0.0 copy-start
  55.4 0.0 copy-start.1
  55.4 0.1 collective-permute-start.3
  55.5 3.0 %collective-permute-start.4 = (f32[128,256]{1,0:T(8,128)S(1)}, f32[128,256]{1,0:T(8,128)S(1)}, u32[]{:S(2)}, u32[]{:S(2)}) collective-permute-start(f32[128,256]{1,0:T(8,128)S(1)} %forward.4.after), channel_id=1, source_target_pairs={{0,8},{4,12},{8,0},{12,4},{1,9},{5,13},{9,1},{13,5},{2,10},{6,14},... | collective-permute-start | bytes 393224 | tf_op jit(solution)/shard_map/ppermute | solution.py:336
  58.5 0.0 collective-permute-start.5
  58.5 0.0 collective-permute-done.6.refs_1_.refs_7_
  58.5 0.6 forward.7
  59.1 3.0 %collective-permute-start.7 = (f32[128,256]{1,0:T(8,128)S(1)}, f32[128,256]{1,0:T(8,128)S(1)}, u32[]{:S(2)}, u32[]{:S(2)}) collective-permute-start(f32[128,256]{1,0:T(8,128)S(1)} %forward.7), channel_id=1, source_target_pairs={{0,8},{4,12},{8,0},{12,4},{1,9},{5,13},{9,1},{13,5},{2,10},{6,14},... | collective-permute-start | bytes 393224 | tf_op jit(solution)/shard_map/ppermute | solution.py:336
  62.1 6.3 %collective-permute-done.3.refs_1_.refs_10_ = f32[256,256]{1,0:T(8,128)S(1)} collective-permute-done((f32[256,256]{1,0:T(8,128)S(1)}, f32[256,256]{1,0:T(8,128)S(1)}, u32[]{:S(2)}, u32[]{:S(2)}) %collective-permute-start.3) | collective-permute-done | bytes 262176 | tf_op jit(solution)/shard_map/ppermute | solution.py:336
  68.3 0.6 forward.6.after
  68.9 0.1 collective-permute-start.8
  69.0 0.0 collective-permute-done.1.source
  69.0 3.5 %load.1.after.psib = bf16[8192,512]{1,0:T(8,128)(2,1)S(1)} custom-call(bf16[8192,512]{1,0:T(8,128)(2,1)} %collective-permute-done.1.source, f32[128,256]{1,0:T(8,128)S(1)} %forward.6.after), custom_call_target="tpu_custom_call" | custom-call | tf_op jit(solution)/shard_map/load/pallas_call | solution.py:246
  72.5 0.0 collective-permute-done.4.refs_2_
  72.5 4.3 %collective-permute-done.5.refs_5_ = f32[128,256]{1,0:T(8,128)S(1)} collective-permute-done((f32[128,256]{1,0:T(8,128)S(1)}, f32[128,256]{1,0:T(8,128)S(1)}, u32[]{:S(2)}, u32[]{:S(2)}) %collective-permute-start.5) | collective-permute-done | bytes 131104 | tf_op jit(solution)/shard_map/ppermute | solution.py:336
  76.8 2.8 %collective-permute-done.7.refs_8_ = f32[128,256]{1,0:T(8,128)S(1)} collective-permute-done((f32[128,256]{1,0:T(8,128)S(1)}, f32[128,256]{1,0:T(8,128)S(1)}, u32[]{:S(2)}, u32[]{:S(2)}) %collective-permute-start.7) | collective-permute-done | bytes 131104 | tf_op jit(solution)/shard_map/ppermute | solution.py:336
  79.6 1.6 %collective-permute-done.8.refs_11_ = f32[128,256]{1,0:T(8,128)S(1)} collective-permute-done((f32[128,256]{1,0:T(8,128)S(1)}, f32[128,256]{1,0:T(8,128)S(1)}, u32[]{:S(2)}, u32[]{:S(2)}) %collective-permute-start.8) | collective-permute-done | bytes 131104 | tf_op jit(solution)/shard_map/ppermute | solution.py:336
  81.2 0.8 softmax.1
  82.0 1.7 %collective-permute-start.9 = (f32[16,128]{1,0:T(8,128)S(1)}, f32[16,128]{1,0:T(8,128)S(1)}, u32[]{:S(2)}, u32[]{:S(2)}) collective-permute-start(f32[16,128]{1,0:T(8,128)S(1)} %get-tuple-element.33.own.mine), channel_id=1, source_target_pairs={{0,2},{2,0},{1,3},{3,1},{4,6},{6,4},{5,7},{7,5},{8,10},{10,8},{9,1... | collective-permute-start | bytes 24584 | tf_op jit(solution)/shard_map/ppermute | solution.py:336
  83.7 2.0 %collective-permute-done.9.other = f32[16,128]{1,0:T(8,128)S(1)} collective-permute-done((f32[16,128]{1,0:T(8,128)S(1)}, f32[16,128]{1,0:T(8,128)S(1)}, u32[]{:S(2)}, u32[]{:S(2)}) %collective-permute-start.9) | collective-permute-done | bytes 8224 | tf_op jit(solution)/shard_map/ppermute | solution.py:336
  85.7 0.7 weights.1
  86.4 2.9 %collective-permute-start.18 = (bf16[128,256]{1,0:T(8,128)(2,1)S(1)}, bf16[128,256]{1,0:T(8,128)(2,1)S(1)}, u32[]{:S(2)}, u32[]{:S(2)}) collective-permute-start(bf16[128,256]{1,0:T(8,128)(2,1)S(1)} %get-tuple-element.36.refs_0_), channel_id=1, source_target_pairs={{0,12},{4,8},{8,4},{12,0},{1,13},{5,9},{9,5},{13,1},{2,14},{6,10},... | collective-permute-start | bytes 196616 | tf_op jit(solution)/shard_map/ppermute | solution.py:336
  89.4 1.5 %collective-permute-start.16 = (bf16[128,256]{1,0:T(8,128)(2,1)S(1)}, bf16[128,256]{1,0:T(8,128)(2,1)S(1)}, u32[]{:S(2)}, u32[]{:S(2)}) collective-permute-start(bf16[128,256]{1,0:T(8,128)(2,1)S(1)} %get-tuple-element.36.refs_0_), channel_id=1, source_target_pairs={{0,4},{4,0},{8,12},{12,8},{1,5},{5,1},{9,13},{13,9},{2,6},{6,2},{1... | collective-permute-start | bytes 196616 | tf_op jit(solution)/shard_map/ppermute | solution.py:336
  90.9 1.7 %collective-permute-done.18.refs_3_ = bf16[128,256]{1,0:T(8,128)(2,1)S(1)} collective-permute-done((bf16[128,256]{1,0:T(8,128)(2,1)S(1)}, bf16[128,256]{1,0:T(8,128)(2,1)S(1)}, u32[]{:S(2)}, u32[]{:S(2)}) %collective-permute-start.18) | collective-permute-done | bytes 65568 | tf_op jit(solution)/shard_map/ppermute | solution.py:336
  92.6 1.9 %collective-permute-done.17.refs_2_ = bf16[128,256]{1,0:T(8,128)(2,1)S(1)} collective-permute-done((bf16[128,256]{1,0:T(8,128)(2,1)S(1)}, bf16[128,256]{1,0:T(8,128)(2,1)S(1)}, u32[]{:S(2)}, u32[]{:S(2)}) %collective-permute-start.17) | collective-permute-done | bytes 65568 | tf_op jit(solution)/shard_map/ppermute | solution.py:336
  94.5 0.0 collective-permute-done.16.refs_1_
  94.5 0.6 pack.3.wown
  95.1 0.1 collective-permute-start.19
  95.2 0.5 collective-permute-start.20
  95.7 2.3 %collective-permute-start.15 = (bf16[128,256]{1,0:T(8,128)(2,1)S(1)}, bf16[128,256]{1,0:T(8,128)(2,1)S(1)}, u32[]{:S(2)}, u32[]{:S(2)}) collective-permute-start(bf16[128,256]{1,0:T(8,128)(2,1)S(1)} %get-tuple-element.35.refs_0_), channel_id=1, source_target_pairs={{0,12},{4,8},{8,4},{12,0},{1,13},{5,9},{9,5},{13,1},{2,14},{6,10},... | collective-permute-start | bytes 196616 | tf_op jit(solution)/shard_map/ppermute | solution.py:336
  98.0 0.0 collective-permute-start.14
  98.0 2.1 %collective-permute-start.13 = (bf16[128,256]{1,0:T(8,128)(2,1)S(1)}, bf16[128,256]{1,0:T(8,128)(2,1)S(1)}, u32[]{:S(2)}, u32[]{:S(2)}) collective-permute-start(bf16[128,256]{1,0:T(8,128)(2,1)S(1)} %get-tuple-element.35.refs_0_), channel_id=1, source_target_pairs={{0,4},{4,0},{8,12},{12,8},{1,5},{5,1},{9,13},{13,9},{2,6},{6,2},{1... | collective-permute-start | bytes 196616 | tf_op jit(solution)/shard_map/ppermute | solution.py:336
  100.1 0.0 collective-permute-done.20.fsib
  100.1 0.0 collective-permute-done.19.wsib
  100.1 8.6 %numer.3.refs_4_.refs_0_ = bf16[8192,1024]{1,0:T(8,128)(2,1)} custom-call(s32[12]{0:T(128)S(1)} %stack.38.where, bf16[8192,512]{1,0:T(8,128)(2,1)S(1)} %get-tuple-element.24.pown, bf16[8192,512]{1,0:T(8,128)(2,1)S(1)} %load.1.after.psib, bf16[512,256]{1,0:T(8,128)(2,1)S(1)} %pack.3.wown, bf16[512,256]{1,0:T(8,128)(2,1)S(1)} %collective-permute-done.19.wsib, ...), custom_call_target="tpu_custom_call" | custom-call | flops 4294967296 | bytes 25165824 | tf_op jit(solution)/shard_map/numer/pallas_call | solution.py:317
  108.6 0.0 collective-permute-done.15.refs_3_
  108.6 0.0 collective-permute-done.14.refs_2_
  108.7 0.6 pack.4.wown
  109.2 0.1 collective-permute-start.21
  109.3 2.4 %collective-permute-start.12 = (bf16[128,512]{1,0:T(8,128)(2,1)S(1)}, bf16[128,512]{1,0:T(8,128)(2,1)S(1)}, u32[]{:S(2)}, u32[]{:S(2)}) collective-permute-start(bf16[128,512]{1,0:T(8,128)(2,1)S(1)} %get-tuple-element.34.refs_0_), channel_id=1, source_target_pairs={{0,12},{4,8},{8,4},{12,0},{1,13},{5,9},{9,5},{13,1},{2,14},{6,10},... | collective-permute-start | bytes 393224 | tf_op jit(solution)/shard_map/ppermute | solution.py:336
  111.7 0.0 collective-permute-start.11
  111.7 2.1 %collective-permute-start.10 = (bf16[128,512]{1,0:T(8,128)(2,1)S(1)}, bf16[128,512]{1,0:T(8,128)(2,1)S(1)}, u32[]{:S(2)}, u32[]{:S(2)}) collective-permute-start(bf16[128,512]{1,0:T(8,128)(2,1)S(1)} %get-tuple-element.34.refs_0_), channel_id=1, source_target_pairs={{0,4},{4,0},{8,12},{12,8},{1,5},{5,1},{9,13},{13,9},{2,6},{6,2},{1... | collective-permute-start | bytes 393224 | tf_op jit(solution)/shard_map/ppermute | solution.py:336
  113.8 0.0 collective-permute-done.21.wsib
  113.8 8.4 %numer.4.refs_4_.refs_0_ = bf16[8192,1024]{1,0:T(8,128)(2,1)} custom-call(s32[12]{0:T(128)S(1)} %stack.38.where, bf16[8192,512]{1,0:T(8,128)(2,1)S(1)} %get-tuple-element.24.pown, bf16[8192,512]{1,0:T(8,128)(2,1)S(1)} %load.1.after.psib, bf16[512,256]{1,0:T(8,128)(2,1)S(1)} %pack.4.wown, ...), custom_call_target="tpu_custom_call", output_to_operand_aliasing={{}: (8, {})} | custom-call | flops 4294967296 | bytes 25165824 | tf_op jit(solution)/shard_map/numer/pallas_call | solution.py:317
  122.2 0.9 collective-permute-done.11.refs_2_
  123.1 0.6 pack.5.wown
  123.7 0.1 collective-permute-start.22
  123.8 1.9 %collective-permute-done.22.wsib = bf16[512,512]{1,0:T(8,128)(2,1)S(1)} collective-permute-done((bf16[512,512]{1,0:T(8,128)(2,1)S(1)}, bf16[512,512]{1,0:T(8,128)(2,1)S(1)}, u32[]{:S(2)}, u32[]{:S(2)}) %collective-permute-start.22) | collective-permute-done | bytes 524320 | tf_op jit(solution)/shard_map/ppermute | solution.py:336
  125.7 13.4 %numer.5 = bf16[8192,1024]{1,0:T(8,128)(2,1)} custom-call(s32[12]{0:T(128)S(1)} %stack.38.where, bf16[8192,512]{1,0:T(8,128)(2,1)S(1)} %get-tuple-element.24.pown, bf16[8192,512]{1,0:T(8,128)(2,1)S(1)} %load.1.after.psib, bf16[512,512]{1,0:T(8,128)(2,1)S(1)} %pack.5.wown, ...), custom_call_target="tpu_custom_call", output_to_operand_aliasing={{}: (8, {})} | custom-call | flops 8589934592 | bytes 33554432 | tf_op jit(solution)/shard_map/numer/pallas_call | solution.py:317
  (6 shorter events, 0.0 us)
Async XLA Ops:
  23.5 45.5 %collective-permute-start.1 = (bf16[8192,512]{1,0:T(8,128)(2,1)}, bf16[8192,512]{1,0:T(8,128)(2,1)}, u32[]{:S(2)}, u32[]{:S(2)}) collective-permute-start(bf16[8192,512]{1,0:T(8,128)(2,1)} %get-tuple-element.25), channel_id=1, source_target_pairs={{0,1},{1,0},{2,3},{3,2},{4,5},{5,4},{6,7},{7,6},{8,9},{9,8},{10,11... | collective-permute-start | bytes 25165832 | tf_op jit(solution)/shard_map/ppermute | solution.py:336
  24.0 9.8 %collective-permute-start = (f32[256,256]{1,0:T(8,128)S(1)}, f32[256,256]{1,0:T(8,128)S(1)}, u32[]{:S(2)}, u32[]{:S(2)}) collective-permute-start(f32[256,256]{1,0:T(8,128)S(1)} %get-tuple-element.23), channel_id=1, source_target_pairs={{0,4},{4,0},{8,12},{12,8},{1,5},{5,1},{9,13},{13,9},{2,6},{6,2},{1... | collective-permute-start | bytes 786440 | tf_op jit(solution)/shard_map/ppermute | solution.py:336
  26.7 19.0 %collective-permute-start.2 = (f32[256,256]{1,0:T(8,128)S(1)}, f32[256,256]{1,0:T(8,128)S(1)}, u32[]{:S(2)}, u32[]{:S(2)}) collective-permute-start(f32[256,256]{1,0:T(8,128)S(1)} %get-tuple-element.27), channel_id=1, source_target_pairs={{0,4},{4,0},{8,12},{12,8},{1,5},{5,1},{9,13},{13,9},{2,6},{6,2},{1... | collective-permute-start | bytes 786440 | tf_op jit(solution)/shard_map/ppermute | solution.py:336
  43.6 15.0 %collective-permute-start.6 = (f32[256,256]{1,0:T(8,128)S(1)}, f32[256,256]{1,0:T(8,128)S(1)}, u32[]{:S(2)}, u32[]{:S(2)}) collective-permute-start(f32[256,256]{1,0:T(8,128)S(1)} %get-tuple-element.31), channel_id=1, source_target_pairs={{0,4},{4,0},{8,12},{12,8},{1,5},{5,1},{9,13},{13,9},{2,6},{6,2},{1... | collective-permute-start | bytes 786440 | tf_op jit(solution)/shard_map/ppermute | solution.py:336
  55.4 25.8 %copy-start = (s32[1024]{0:T(1024)S(1)}, s32[1024]{0:T(1024)}, u32[]{:S(2)}) copy-start(s32[1024]{0:T(1024)} %param.11) | copy-start | bytes 12292
  55.4 25.8 %copy-start.1 = (f32[8]{0:T(128)S(1)}, f32[8]{0:T(128)}, u32[]{:S(2)}) copy-start(f32[8]{0:T(128)} %table.1) | copy-start | bytes 100
  55.4 12.9 %collective-permute-start.3 = (f32[256,256]{1,0:T(8,128)S(1)}, f32[256,256]{1,0:T(8,128)S(1)}, u32[]{:S(2)}, u32[]{:S(2)}) collective-permute-start(f32[256,256]{1,0:T(8,128)S(1)} %get-tuple-element.29), channel_id=1, source_target_pairs={{0,4},{4,0},{8,12},{12,8},{1,5},{5,1},{9,13},{13,9},{2,6},{6,2},{1... | collective-permute-start | bytes 786440 | tf_op jit(solution)/shard_map/ppermute | solution.py:336
  55.5 17.0 %collective-permute-start.4 = (f32[128,256]{1,0:T(8,128)S(1)}, f32[128,256]{1,0:T(8,128)S(1)}, u32[]{:S(2)}, u32[]{:S(2)}) collective-permute-start(f32[128,256]{1,0:T(8,128)S(1)} %forward.4.after), channel_id=1, source_target_pairs={{0,8},{4,12},{8,0},{12,4},{1,9},{5,13},{9,1},{13,5},{2,10},{6,14},... | collective-permute-start | bytes 393224 | tf_op jit(solution)/shard_map/ppermute | solution.py:336
  58.5 18.3 %collective-permute-start.5 = (f32[128,256]{1,0:T(8,128)S(1)}, f32[128,256]{1,0:T(8,128)S(1)}, u32[]{:S(2)}, u32[]{:S(2)}) collective-permute-start(f32[128,256]{1,0:T(8,128)S(1)} %forward.5.after), channel_id=1, source_target_pairs={{0,8},{4,12},{8,0},{12,4},{1,9},{5,13},{9,1},{13,5},{2,10},{6,14},... | collective-permute-start | bytes 393224 | tf_op jit(solution)/shard_map/ppermute | solution.py:336
  59.1 20.5 %collective-permute-start.7 = (f32[128,256]{1,0:T(8,128)S(1)}, f32[128,256]{1,0:T(8,128)S(1)}, u32[]{:S(2)}, u32[]{:S(2)}) collective-permute-start(f32[128,256]{1,0:T(8,128)S(1)} %forward.7), channel_id=1, source_target_pairs={{0,8},{4,12},{8,0},{12,4},{1,9},{5,13},{9,1},{13,5},{2,10},{6,14},... | collective-permute-start | bytes 393224 | tf_op jit(solution)/shard_map/ppermute | solution.py:336
  68.9 12.3 %collective-permute-start.8 = (f32[128,256]{1,0:T(8,128)S(1)}, f32[128,256]{1,0:T(8,128)S(1)}, u32[]{:S(2)}, u32[]{:S(2)}) collective-permute-start(f32[128,256]{1,0:T(8,128)S(1)} %forward.6.after), channel_id=1, source_target_pairs={{0,8},{4,12},{8,0},{12,4},{1,9},{5,13},{9,1},{13,5},{2,10},{6,14},... | collective-permute-start | bytes 393224 | tf_op jit(solution)/shard_map/ppermute | solution.py:336
  82.0 3.7 %collective-permute-start.9 = (f32[16,128]{1,0:T(8,128)S(1)}, f32[16,128]{1,0:T(8,128)S(1)}, u32[]{:S(2)}, u32[]{:S(2)}) collective-permute-start(f32[16,128]{1,0:T(8,128)S(1)} %get-tuple-element.33.own.mine), channel_id=1, source_target_pairs={{0,2},{2,0},{1,3},{3,1},{4,6},{6,4},{5,7},{7,5},{8,10},{10,8},{9,1... | collective-permute-start | bytes 24584 | tf_op jit(solution)/shard_map/ppermute | solution.py:336
  86.4 6.1 %collective-permute-start.18 = (bf16[128,256]{1,0:T(8,128)(2,1)S(1)}, bf16[128,256]{1,0:T(8,128)(2,1)S(1)}, u32[]{:S(2)}, u32[]{:S(2)}) collective-permute-start(bf16[128,256]{1,0:T(8,128)(2,1)S(1)} %get-tuple-element.36.refs_0_), channel_id=1, source_target_pairs={{0,12},{4,8},{8,4},{12,0},{1,13},{5,9},{9,5},{13,1},{2,14},{6,10},... | collective-permute-start | bytes 196616 | tf_op jit(solution)/shard_map/ppermute | solution.py:336
  89.3 5.2 %collective-permute-start.17 = (bf16[128,256]{1,0:T(8,128)(2,1)S(1)}, bf16[128,256]{1,0:T(8,128)(2,1)S(1)}, u32[]{:S(2)}, u32[]{:S(2)}) collective-permute-start(bf16[128,256]{1,0:T(8,128)(2,1)S(1)} %get-tuple-element.36.refs_0_), channel_id=1, source_target_pairs={{0,8},{4,12},{8,0},{12,4},{1,9},{5,13},{9,1},{13,5},{2,10},{6,14},... | collective-permute-start | bytes 196616 | tf_op jit(solution)/shard_map/ppermute | solution.py:336
  89.4 5.2 %collective-permute-start.16 = (bf16[128,256]{1,0:T(8,128)(2,1)S(1)}, bf16[128,256]{1,0:T(8,128)(2,1)S(1)}, u32[]{:S(2)}, u32[]{:S(2)}) collective-permute-start(bf16[128,256]{1,0:T(8,128)(2,1)S(1)} %get-tuple-element.36.refs_0_), channel_id=1, source_target_pairs={{0,4},{4,0},{8,12},{12,8},{1,5},{5,1},{9,13},{13,9},{2,6},{6,2},{1... | collective-permute-start | bytes 196616 | tf_op jit(solution)/shard_map/ppermute | solution.py:336
  95.1 5.0 %collective-permute-start.19 = (bf16[512,256]{1,0:T(8,128)(2,1)S(1)}, bf16[512,256]{1,0:T(8,128)(2,1)S(1)}, u32[]{:S(2)}, u32[]{:S(2)}) collective-permute-start(bf16[512,256]{1,0:T(8,128)(2,1)S(1)} %pack.3.wown), channel_id=1, source_target_pairs={{0,1},{1,0},{2,3},{3,2},{4,5},{5,4},{6,7},{7,6},{8,9},{9,8},{10,11... | collective-permute-start | bytes 786440 | tf_op jit(solution)/shard_map/ppermute | solution.py:336
  95.2 4.9 %collective-permute-start.20 = (f32[512,1]{1,0:T(8,128)S(1)}, f32[512,1]{1,0:T(8,128)S(1)}, u32[]{:S(2)}, u32[]{:S(2)}) collective-permute-start(f32[512,1]{1,0:T(8,128)S(1)} %copy.22.phi.after.fown), channel_id=1, source_target_pairs={{0,1},{1,0},{2,3},{3,2},{4,5},{5,4},{6,7},{7,6},{8,9},{9,8},{10,11... | collective-permute-start | bytes 6152 | tf_op jit(solution)/shard_map/ppermute | solution.py:336
  95.7 13.0 %collective-permute-start.15 = (bf16[128,256]{1,0:T(8,128)(2,1)S(1)}, bf16[128,256]{1,0:T(8,128)(2,1)S(1)}, u32[]{:S(2)}, u32[]{:S(2)}) collective-permute-start(bf16[128,256]{1,0:T(8,128)(2,1)S(1)} %get-tuple-element.35.refs_0_), channel_id=1, source_target_pairs={{0,12},{4,8},{8,4},{12,0},{1,13},{5,9},{9,5},{13,1},{2,14},{6,10},... | collective-permute-start | bytes 196616 | tf_op jit(solution)/shard_map/ppermute | solution.py:336
  98.0 10.7 %collective-permute-start.14 = (bf16[128,256]{1,0:T(8,128)(2,1)S(1)}, bf16[128,256]{1,0:T(8,128)(2,1)S(1)}, u32[]{:S(2)}, u32[]{:S(2)}) collective-permute-start(bf16[128,256]{1,0:T(8,128)(2,1)S(1)} %get-tuple-element.35.refs_0_), channel_id=1, source_target_pairs={{0,8},{4,12},{8,0},{12,4},{1,9},{5,13},{9,1},{13,5},{2,10},{6,14},... | collective-permute-start | bytes 196616 | tf_op jit(solution)/shard_map/ppermute | solution.py:336
  98.0 10.7 %collective-permute-start.13 = (bf16[128,256]{1,0:T(8,128)(2,1)S(1)}, bf16[128,256]{1,0:T(8,128)(2,1)S(1)}, u32[]{:S(2)}, u32[]{:S(2)}) collective-permute-start(bf16[128,256]{1,0:T(8,128)(2,1)S(1)} %get-tuple-element.35.refs_0_), channel_id=1, source_target_pairs={{0,4},{4,0},{8,12},{12,8},{1,5},{5,1},{9,13},{13,9},{2,6},{6,2},{1... | collective-permute-start | bytes 196616 | tf_op jit(solution)/shard_map/ppermute | solution.py:336
  109.2 4.5 %collective-permute-start.21 = (bf16[512,256]{1,0:T(8,128)(2,1)S(1)}, bf16[512,256]{1,0:T(8,128)(2,1)S(1)}, u32[]{:S(2)}, u32[]{:S(2)}) collective-permute-start(bf16[512,256]{1,0:T(8,128)(2,1)S(1)} %pack.4.wown), channel_id=1, source_target_pairs={{0,1},{1,0},{2,3},{3,2},{4,5},{5,4},{6,7},{7,6},{8,9},{9,8},{10,11... | collective-permute-start | bytes 786440 | tf_op jit(solution)/shard_map/ppermute | solution.py:336
  109.3 12.9 %collective-permute-start.12 = (bf16[128,512]{1,0:T(8,128)(2,1)S(1)}, bf16[128,512]{1,0:T(8,128)(2,1)S(1)}, u32[]{:S(2)}, u32[]{:S(2)}) collective-permute-start(bf16[128,512]{1,0:T(8,128)(2,1)S(1)} %get-tuple-element.34.refs_0_), channel_id=1, source_target_pairs={{0,12},{4,8},{8,4},{12,0},{1,13},{5,9},{9,5},{13,1},{2,14},{6,10},... | collective-permute-start | bytes 393224 | tf_op jit(solution)/shard_map/ppermute | solution.py:336
  111.7 11.4 %collective-permute-start.11 = (bf16[128,512]{1,0:T(8,128)(2,1)S(1)}, bf16[128,512]{1,0:T(8,128)(2,1)S(1)}, u32[]{:S(2)}, u32[]{:S(2)}) collective-permute-start(bf16[128,512]{1,0:T(8,128)(2,1)S(1)} %get-tuple-element.34.refs_0_), channel_id=1, source_target_pairs={{0,8},{4,12},{8,0},{12,4},{1,9},{5,13},{9,1},{13,5},{2,10},{6,14},... | collective-permute-start | bytes 393224 | tf_op jit(solution)/shard_map/ppermute | solution.py:336
  111.7 11.4 %collective-permute-start.10 = (bf16[128,512]{1,0:T(8,128)(2,1)S(1)}, bf16[128,512]{1,0:T(8,128)(2,1)S(1)}, u32[]{:S(2)}, u32[]{:S(2)}) collective-permute-start(bf16[128,512]{1,0:T(8,128)(2,1)S(1)} %get-tuple-element.34.refs_0_), channel_id=1, source_target_pairs={{0,4},{4,0},{8,12},{12,8},{1,5},{5,1},{9,13},{13,9},{2,6},{6,2},{1... | collective-permute-start | bytes 393224 | tf_op jit(solution)/shard_map/ppermute | solution.py:336
  123.7 2.0 %collective-permute-start.22 = (bf16[512,512]{1,0:T(8,128)(2,1)S(1)}, bf16[512,512]{1,0:T(8,128)(2,1)S(1)}, u32[]{:S(2)}, u32[]{:S(2)}) collective-permute-start(bf16[512,512]{1,0:T(8,128)(2,1)S(1)} %pack.5.wown), channel_id=1, source_target_pairs={{0,1},{1,0},{2,3},{3,2},{4,5},{5,4},{6,7},{7,6},{8,9},{9,8},{10,11... | collective-permute-start | bytes 1572872 | tf_op jit(solution)/shard_map/ppermute | solution.py:336

commit v4 on v3

--- a/solution.py
+++ b/solution.py
@@ -9,7 +9,7 @@
 
 prior_weight = 0.5
 MIB = 1 << 20
-SLOTS = 6
+SLOTS = 4
 VMEM = pl.BlockSpec(memory_space=pltpu.VMEM)
 SMEM = pl.BlockSpec(memory_space=pltpu.SMEM)
 HBM = pl.BlockSpec(memory_space=pltpu.HBM)
@@ -88,7 +88,7 @@
 
 def cross_chunk(where, phi, patterns, model, after, column, tn, beta, first, turns):
     rows, depth = patterns.shape
-    tk = min(1024, depth)
+    tk = min(2048, depth)
     half = rows // 2
     shapes = [jax.ShapeDtypeStruct((half, tn), jnp.float32)] * 2
     shapes += [(pltpu.VMEM if own else pltpu.HBM)((depth // 2, rows), patterns.dtype) for own in turns]
@@ -117,7 +117,7 @@
     )(where, phi, patterns, model, after)
 
 
-def forward_kernel(where, *refs, base):
+def forward_kernel(where, after, *refs, base):
     parts, out = refs[:-1], refs[-1]
     size = out.shape[0]
     total = None
@@ -127,31 +127,33 @@
     out[...] = total
 
 
-def forward(where, base, parts, size):
+def forward(where, base, parts, size, after):
     return pl.pallas_call(
         functools.partial(forward_kernel, base=base),
         out_shape=jax.ShapeDtypeStruct((size, parts[0].shape[1]), jnp.float32),
-        in_specs=[SMEM] + [VMEM] * len(parts),
+        in_specs=[SMEM, ANY] + [VMEM] * len(parts),
         out_specs=VMEM,
         compiler_params=params(8 * MIB),
         name="forward",
-    )(where, *parts)
+    )(where, after, *parts)
 
 
 def softmax_kernel(where, table, classes, after, *refs, chunks, terms, base):
     parts, (exps, stats) = refs[:-2], refs[-2:]
     count = exps.shape[0]
-    tn = exps.shape[1] // chunks
     logw = jnp.zeros(classes.shape, jnp.float32)
     for q in range(table.shape[0]):
         logw = logw + jnp.where(classes[...] == q, table[q], 0.0)
+    at = 0
     for c in range(chunks):
+        tn = parts[c * terms].shape[1]
         total = None
         for t in range(terms):
             rows = pl.ds(pl.multiple_of(where[base + t], count), count)
             part = parts[c * terms + t][rows, :]
             total = part if total is None else total + part
-        exps[:, c * tn : (c + 1) * tn] = total + logw[:, c * tn : (c + 1) * tn]
+        exps[:, at : at + tn] = total + logw[:, at : at + tn]
+        at += tn
     top = jnp.max(exps[...], axis=1, keepdims=True)
     exps[...] = jnp.exp(exps[...] - top)
     total = jnp.sum(exps[...], axis=1, keepdims=True)
@@ -276,20 +278,21 @@
     scale = 1.0 / (prior_weight + den)
 
     def body(i, carry):
-        fetch(i).wait()
-
         @pl.when(i + 2 < steps)
         def _():
             fetch(i + 2).start()
-
-        @pl.when(i >= 2)
-        def _():
-            store(i - 2).wait()
 
         for r in range(0, tm, sub):
             rows = pl.ds(pl.multiple_of(i * tm + r, sub), sub)
             acc = jnp.dot(pown[rows, :], wown[...], preferred_element_type=jnp.float32)
             acc = acc + jnp.dot(psib[rows, :], wsib[...], preferred_element_type=jnp.float32)
+            if r == 0:
+                fetch(i).wait()
+
+                @pl.when(i >= 2)
+                def _():
+                    store(i - 2).wait()
+
             acc = acc + prior_weight * mbuf[lax.rem(i, 3), r : r + sub, :].astype(jnp.float32)
             obuf[lax.rem(i, 2), r : r + sub, :] = (acc * scale).astype(jnp.bfloat16)
         store(i).start()
@@ -343,6 +346,9 @@
     count = rows // pix
     tn = min(256, columns)
     chunks = columns // tn
+    widths = [2 * tn] + [tn] * (chunks - 2) if chunks >= 4 else [tn] * chunks
+    starts = [sum(widths[:c]) for c in range(len(widths))]
+    chunks = len(widths)
     beta = (patterns.shape[1] * pix) ** -0.5
     place = lax.axis_index("pix")
     bits = [(place >> i) & 1 for i in range(hops)]
@@ -353,65 +359,60 @@
 
     share = bit_reverse(place, hops) * count
     entries = [bits[0], side]
-    starts, offsets, size = {}, [0, 0], rows // 2
+    places, offsets, size = {}, [0, 0], rows // 2
     for hop in range(1, hops):
         size //= 2
-        starts[hop] = len(entries)
+        places[hop] = len(entries)
         entries += [o + (1 - bits[hop]) * size for o in offsets]
         offsets = [o + bits[hop] * size for o in offsets] + [0]
-    starts["terms"] = len(entries)
+    places["terms"] = len(entries)
     entries += offsets
-    starts["share"] = len(entries)
+    places["share"] = len(entries)
     entries.append(share)
-    starts["order"] = len(entries)
+    places["order"] = len(entries)
     entries += [share ^ (bit_reverse(d, hops) * count) for d in range(pix)]
     where = jnp.stack([jnp.asarray(e, jnp.int32) for e in entries])
 
     later = min(2, chunks - 1)
     turned, terms = {}, {}
-    source, after = patterns, phi
-
-    def reduce_further(c):
-        size = rows // 2
-        for hop in range(1, hops):
-            size //= 2
-            away = forward(where, starts[hop], terms[c], size)
-            terms[c].append(exchange(away, "pix", pix, 1 << hop))
-        return away
-
+    source = patterns
     for c in range(chunks):
         turns = ((False,) if c == 1 else ()) + ((True,) if c == later else ())
-        send, keep, *rest = cross_chunk(where, phi, source, model, after, c * tn, tn, beta, c == 0, turns)
+        send, keep, *rest = cross_chunk(
+            where, phi, source, model, phi if c == 0 else terms[c - 1][0], starts[c], widths[c], beta, c == 0, turns
+        )
         if c == 0:
             source = rest[-1]
         for own, value in zip(turns, rest):
             turned[own] = value
         terms[c] = [keep, exchange(send, "pix", pix, 1)]
-        if c >= 1:
-            after = reduce_further(c - 1)
         if c == 1:
             psib = exchange(turned[False], "pat", 2, 1)
-    last = reduce_further(chunks - 1)
-    psib = load(psib, last)
+    after = keep
+    for c in range(chunks):
+        size = rows // 2
+        for hop in range(1, hops):
+            size //= 2
+            after = forward(where, places[hop], terms[c], size, after)
+            terms[c].append(exchange(after, "pix", pix, 1 << hop))
+    psib = load(psib, after)
     held = [term for c in range(chunks) for term in terms[c]]
     phi_sib = exchange(phi, "pat", 2, 1)
 
-    exps, own = softmax_stage(where, starts["terms"], weight_table, classes, psib, held, count, chunks)
+    exps, own = softmax_stage(where, places["terms"], weight_table, classes, psib, held, count, chunks)
     mine = own
     other = None
     for hop in range(ori.bit_length() - 1):
         if other is not None:
             mine = combine(mine, other)
         other = exchange(mine, "ori", ori, 1 << hop)
-    widths = [tn] * min(2, chunks)
-    if chunks > 2:
-        widths.append(tn * (chunks - 2))
-    weights = weight_stage(where, starts["share"], phi, exps, own, mine, other, widths)
+    shares = [columns // 2] * 2 if columns >= 512 else [columns]
+    weights = weight_stage(where, places["share"], phi, exps, own, mine, other, shares)
 
     gathered = [[w] + [exchange(w, "pix", pix, d) for d in range(1, pix)] for w in weights]
     at, result, after = 0, None, model
-    for width, parts in zip(widths, gathered):
-        wown = pack(where, starts["order"], parts, after)
+    for width, parts in zip(shares, gathered):
+        wown = pack(where, places["order"], parts, after)
         wsib = exchange(wown, "pat", 2, 1)
         result = numer_chunk(where, turned[True], psib, wown, wsib, phi, phi_sib, model, at, result)
         after = result

time: 139 us -> 127 us (0.914)
  Pallas kernels: 80.1 us -> 70.7 us
  starting transfers between devices: 27.2 us -> 23.5 us
    pallas_call x4 -> x3, Pallas kernels: 40.7 us -> 32.8 us  [cross_chunk(): pl.pallas_call(functools.partial(cross_kernel, column=column, tk=tk, step...]
    ppermute x23 -> x17, starting transfers between devices: 27.2 us -> 23.5 us  [exchange(): return lax.ppermute(value, axis, [(i, i ^ distance) for i in range(size)])]
    ppermute x23 -> x17, waiting for transfers between devices: 30.4 us -> 31.6 us  [exchange(): return lax.ppermute(value, axis, [(i, i ^ distance) for i in range(size)])]
    pallas_call x3 -> x2, Pallas kernels: 30.4 us -> 29.9 us  [numer_chunk(): pl.pallas_call(functools.partial(numer_kernel, column=column, tm=tm, sub=...]
  transfers between devices with their start and end apart: 23 -> 17, of which waited for: 10 -> 9; matrix products, arithmetic and copies ran while one was open for 0% -> 0% of each run, Pallas kernels for 30% -> 22%
where the time goes in v4:
time: 127 us
  Pallas kernels  70.7 us (56%)
  waiting for transfers between devices  31.6 us (25%)
  starting transfers between devices  23.5 us (19%)
    pallas_call x3, Pallas kernels, cross_chunk(): pl.pallas_call(functools.partial(cross_kernel, column=column, tk=tk, step...  32.8 us
    ppermute x17, waiting for transfers between devices, exchange(): return lax.ppermute(value, axis, [(i, i ^ distance) for i in range(size)])  31.6 us
    pallas_call x2, Pallas kernels, numer_chunk(): pl.pallas_call(functools.partial(numer_kernel, column=column, tm=tm, sub=...  29.9 us
    ppermute x17, starting transfers between devices, exchange(): return lax.ppermute(value, axis, [(i, i ^ distance) for i in range(size)])  23.5 us
    pallas_call x1, Pallas kernels, load(): pl.pallas_call(load_kernel, out_shape=pltpu.VMEM(source.shape, source.dty...  3.5 us
  transfers between devices with their start and end apart: 17, of which 9 were waited for; matrix products, arithmetic and copies ran while one was open for 0% of the time, Pallas kernels for 22%

profile of v4, /device:TPU:0, one launch (start us, length us, event | category | flops | bytes accessed | tf_op | source)
XLA Modules:
  0.0 127.0 jit_solution(17824654927832385963)
XLA Ops:
  0.0 0.8 select_reduce_fusion
  0.8 0.1 copy.19.phi.after.fown
  0.9 0.1 stack.38.where
  1.0 13.4 %cross.3 = (f32[256,512]{1,0:T(8,128)S(1)}, f32[256,512]{1,0:T(8,128)S(1)}, bf16[512,16384]{1,0:T(8,128)(2,1)S(1)}) custom-call(s32[12]{0:T(128)S(1)} %stack.38.where, f32[512,1]{1,0:T(8,128)S(1)} %copy.19.phi.after.fown, bf16[512,16384]{1,0:T(8,128)(2,1)} %patterns.1, bf16[16384,1024]{1,0:T(8,128)(2,1)} %model.9, f32[512,1]{1,0:T(8,128)S(1)} %copy.19.phi.after.fown), custom_call_target="tpu_custom_call" | custom-call | flops 8589934592 | bytes 33554432 | tf_op jit(solution)/shard_map/cross/pallas_call | solution.py:106
  14.5 11.3 %cross.4 = (f32[256,256]{1,0:T(8,128)S(1)}, f32[256,256]{1,0:T(8,128)S(1)}, bf16[8192,512]{1,0:T(8,128)(2,1)}) custom-call(s32[12]{0:T(128)S(1)} %stack.38.where, f32[512,1]{1,0:T(8,128)S(1)} %copy.19.phi.after.fown, bf16[512,16384]{1,0:T(8,128)(2,1)S(1)} %get-tuple-element.18.patterns, bf16[16384,1024]{1,0:T(8,128)(2,1)} %model.9, ...), custom_call_target="tpu_custom_call" | custom-call | flops 4294967296 | bytes 25165824 | tf_op jit(solution)/shard_map/cross/pallas_call | solution.py:106
  25.8 0.6 collective-permute-start
  26.4 2.6 %collective-permute-start.1 = (f32[256,512]{1,0:T(8,128)S(1)}, f32[256,512]{1,0:T(8,128)S(1)}, u32[]{:S(2)}, u32[]{:S(2)}) collective-permute-start(f32[256,512]{1,0:T(8,128)S(1)} %get-tuple-element.24), channel_id=1, source_target_pairs={{0,4},{4,0},{8,12},{12,8},{1,5},{5,1},{9,13},{13,9},{2,6},{6,2},{1... | collective-permute-start | bytes 1572872 | tf_op jit(solution)/shard_map/ppermute | solution.py:339
  29.0 0.1 collective-permute-start.2
  29.1 8.1 %cross.5 = (f32[256,256]{1,0:T(8,128)S(1)}, f32[256,256]{1,0:T(8,128)S(1)}, bf16[8192,512]{1,0:T(8,128)(2,1)S(1)}) custom-call(s32[12]{0:T(128)S(1)} %stack.38.where, f32[512,1]{1,0:T(8,128)S(1)} %copy.19.phi.after.fown, bf16[512,16384]{1,0:T(8,128)(2,1)S(1)} %get-tuple-element.18.patterns, bf16[16384,1024]{1,0:T(8,128)(2,1)} %model.9, ...), custom_call_target="tpu_custom_call" | custom-call | flops 4294967296 | bytes 25165824 | tf_op jit(solution)/shard_map/cross/pallas_call | solution.py:106
  37.2 0.0 copy-start
  37.2 0.0 copy-start.1
  37.2 2.0 %collective-permute-start.3 = (f32[256,256]{1,0:T(8,128)S(1)}, f32[256,256]{1,0:T(8,128)S(1)}, u32[]{:S(2)}, u32[]{:S(2)}) collective-permute-start(f32[256,256]{1,0:T(8,128)S(1)} %get-tuple-element.26), channel_id=1, source_target_pairs={{0,4},{4,0},{8,12},{12,8},{1,5},{5,1},{9,13},{13,9},{2,6},{6,2},{1... | collective-permute-start | bytes 786440 | tf_op jit(solution)/shard_map/ppermute | solution.py:339
  39.2 2.6 %collective-permute-done.1.refs_1_ = f32[256,512]{1,0:T(8,128)S(1)} collective-permute-done((f32[256,512]{1,0:T(8,128)S(1)}, f32[256,512]{1,0:T(8,128)S(1)}, u32[]{:S(2)}, u32[]{:S(2)}) %collective-permute-start.1) | collective-permute-done | bytes 524320 | tf_op jit(solution)/shard_map/ppermute | solution.py:339
  41.8 0.6 forward.3.after
  42.4 3.1 %collective-permute-start.4 = (f32[128,512]{1,0:T(8,128)S(1)}, f32[128,512]{1,0:T(8,128)S(1)}, u32[]{:S(2)}, u32[]{:S(2)}) collective-permute-start(f32[128,512]{1,0:T(8,128)S(1)} %forward.3.after), channel_id=1, source_target_pairs={{0,8},{4,12},{8,0},{12,4},{1,9},{5,13},{9,1},{13,5},{2,10},{6,14},... | collective-permute-start | bytes 786440 | tf_op jit(solution)/shard_map/ppermute | solution.py:339
  45.4 7.6 %collective-permute-done.2.refs_1_.refs_4_ = f32[256,256]{1,0:T(8,128)S(1)} collective-permute-done((f32[256,256]{1,0:T(8,128)S(1)}, f32[256,256]{1,0:T(8,128)S(1)}, u32[]{:S(2)}, u32[]{:S(2)}) %collective-permute-start.2) | collective-permute-done | bytes 262176 | tf_op jit(solution)/shard_map/ppermute | solution.py:339
  53.0 0.6 forward.4.after
  53.6 2.2 %collective-permute-start.5 = (f32[128,256]{1,0:T(8,128)S(1)}, f32[128,256]{1,0:T(8,128)S(1)}, u32[]{:S(2)}, u32[]{:S(2)}) collective-permute-start(f32[128,256]{1,0:T(8,128)S(1)} %forward.4.after), channel_id=1, source_target_pairs={{0,8},{4,12},{8,0},{12,4},{1,9},{5,13},{9,1},{13,5},{2,10},{6,14},... | collective-permute-start | bytes 393224 | tf_op jit(solution)/shard_map/ppermute | solution.py:339
  55.8 2.7 %collective-permute-done.3.refs_1_.refs_7_ = f32[256,256]{1,0:T(8,128)S(1)} collective-permute-done((f32[256,256]{1,0:T(8,128)S(1)}, f32[256,256]{1,0:T(8,128)S(1)}, u32[]{:S(2)}, u32[]{:S(2)}) %collective-permute-start.3) | collective-permute-done | bytes 262176 | tf_op jit(solution)/shard_map/ppermute | solution.py:339
  58.5 0.6 forward.5.after
  59.0 1.9 %collective-permute-start.6 = (f32[128,256]{1,0:T(8,128)S(1)}, f32[128,256]{1,0:T(8,128)S(1)}, u32[]{:S(2)}, u32[]{:S(2)}) collective-permute-start(f32[128,256]{1,0:T(8,128)S(1)} %forward.5.after), channel_id=1, source_target_pairs={{0,8},{4,12},{8,0},{12,4},{1,9},{5,13},{9,1},{13,5},{2,10},{6,14},... | collective-permute-start | bytes 393224 | tf_op jit(solution)/shard_map/ppermute | solution.py:339
  60.9 0.0 collective-permute-done.source
  61.0 3.5 %load.1.after.psib = bf16[8192,512]{1,0:T(8,128)(2,1)S(1)} custom-call(bf16[8192,512]{1,0:T(8,128)(2,1)} %collective-permute-done.source, f32[128,256]{1,0:T(8,128)S(1)} %forward.5.after), custom_call_target="tpu_custom_call" | custom-call | tf_op jit(solution)/shard_map/load/pallas_call | solution.py:248
  64.5 4.6 %collective-permute-done.5.refs_5_ = f32[128,256]{1,0:T(8,128)S(1)} collective-permute-done((f32[128,256]{1,0:T(8,128)S(1)}, f32[128,256]{1,0:T(8,128)S(1)}, u32[]{:S(2)}, u32[]{:S(2)}) %collective-permute-start.5) | collective-permute-done | bytes 131104 | tf_op jit(solution)/shard_map/ppermute | solution.py:339
  69.1 2.7 %collective-permute-done.6.refs_8_ = f32[128,256]{1,0:T(8,128)S(1)} collective-permute-done((f32[128,256]{1,0:T(8,128)S(1)}, f32[128,256]{1,0:T(8,128)S(1)}, u32[]{:S(2)}, u32[]{:S(2)}) %collective-permute-start.6) | collective-permute-done | bytes 131104 | tf_op jit(solution)/shard_map/ppermute | solution.py:339
  71.8 0.0 collective-permute-done.4.refs_2_
  71.8 0.0 copy-done
  71.8 0.0 copy-done.1
  71.8 0.8 softmax.1
  72.6 1.5 %collective-permute-start.7 = (f32[16,128]{1,0:T(8,128)S(1)}, f32[16,128]{1,0:T(8,128)S(1)}, u32[]{:S(2)}, u32[]{:S(2)}) collective-permute-start(f32[16,128]{1,0:T(8,128)S(1)} %get-tuple-element.28.own.mine), channel_id=1, source_target_pairs={{0,2},{2,0},{1,3},{3,1},{4,6},{6,4},{5,7},{7,5},{8,10},{10,8},{9,1... | collective-permute-start | bytes 24584 | tf_op jit(solution)/shard_map/ppermute | solution.py:339
  74.2 2.2 %collective-permute-done.7.other = f32[16,128]{1,0:T(8,128)S(1)} collective-permute-done((f32[16,128]{1,0:T(8,128)S(1)}, f32[16,128]{1,0:T(8,128)S(1)}, u32[]{:S(2)}, u32[]{:S(2)}) %collective-permute-start.7) | collective-permute-done | bytes 8224 | tf_op jit(solution)/shard_map/ppermute | solution.py:339
  76.3 0.7 weights.1
  77.1 1.4 %collective-permute-start.13 = (bf16[128,512]{1,0:T(8,128)(2,1)S(1)}, bf16[128,512]{1,0:T(8,128)(2,1)S(1)}, u32[]{:S(2)}, u32[]{:S(2)}) collective-permute-start(bf16[128,512]{1,0:T(8,128)(2,1)S(1)} %get-tuple-element.30.refs_0_), channel_id=1, source_target_pairs={{0,12},{4,8},{8,4},{12,0},{1,13},{5,9},{9,5},{13,1},{2,14},{6,10},... | collective-permute-start | bytes 393224 | tf_op jit(solution)/shard_map/ppermute | solution.py:339
  78.5 0.0 collective-permute-start.12
  78.5 3.0 %collective-permute-start.11 = (bf16[128,512]{1,0:T(8,128)(2,1)S(1)}, bf16[128,512]{1,0:T(8,128)(2,1)S(1)}, u32[]{:S(2)}, u32[]{:S(2)}) collective-permute-start(bf16[128,512]{1,0:T(8,128)(2,1)S(1)} %get-tuple-element.30.refs_0_), channel_id=1, source_target_pairs={{0,4},{4,0},{8,12},{12,8},{1,5},{5,1},{9,13},{13,9},{2,6},{6,2},{1... | collective-permute-start | bytes 393224 | tf_op jit(solution)/shard_map/ppermute | solution.py:339
  81.5 3.8 %collective-permute-done.13.refs_3_ = bf16[128,512]{1,0:T(8,128)(2,1)S(1)} collective-permute-done((bf16[128,512]{1,0:T(8,128)(2,1)S(1)}, bf16[128,512]{1,0:T(8,128)(2,1)S(1)}, u32[]{:S(2)}, u32[]{:S(2)}) %collective-permute-start.13) | collective-permute-done | bytes 131104 | tf_op jit(solution)/shard_map/ppermute | solution.py:339
  85.4 3.5 %collective-permute-done.12.refs_2_ = bf16[128,512]{1,0:T(8,128)(2,1)S(1)} collective-permute-done((bf16[128,512]{1,0:T(8,128)(2,1)S(1)}, bf16[128,512]{1,0:T(8,128)(2,1)S(1)}, u32[]{:S(2)}, u32[]{:S(2)}) %collective-permute-start.12) | collective-permute-done | bytes 131104 | tf_op jit(solution)/shard_map/ppermute | solution.py:339
  88.9 0.0 collective-permute-done.11.refs_1_
  88.9 0.6 pack.2.wown
  89.4 0.1 collective-permute-start.14
  89.5 0.5 collective-permute-start.15
  90.0 2.1 %collective-permute-start.10 = (bf16[128,512]{1,0:T(8,128)(2,1)S(1)}, bf16[128,512]{1,0:T(8,128)(2,1)S(1)}, u32[]{:S(2)}, u32[]{:S(2)}) collective-permute-start(bf16[128,512]{1,0:T(8,128)(2,1)S(1)} %get-tuple-element.29.refs_0_), channel_id=1, source_target_pairs={{0,12},{4,8},{8,4},{12,0},{1,13},{5,9},{9,5},{13,1},{2,14},{6,10},... | collective-permute-start | bytes 393224 | tf_op jit(solution)/shard_map/ppermute | solution.py:339
  92.1 0.0 collective-permute-start.9
  92.1 2.3 %collective-permute-start.8 = (bf16[128,512]{1,0:T(8,128)(2,1)S(1)}, bf16[128,512]{1,0:T(8,128)(2,1)S(1)}, u32[]{:S(2)}, u32[]{:S(2)}) collective-permute-start(bf16[128,512]{1,0:T(8,128)(2,1)S(1)} %get-tuple-element.29.refs_0_), channel_id=1, source_target_pairs={{0,4},{4,0},{8,12},{12,8},{1,5},{5,1},{9,13},{13,9},{2,6},{6,2},{1... | collective-permute-start | bytes 393224 | tf_op jit(solution)/shard_map/ppermute | solution.py:339
  94.4 0.0 collective-permute-done.15.fsib
  94.4 0.0 collective-permute-done.14.wsib
  94.4 14.9 %numer.2.refs_4_.refs_0_ = bf16[8192,1024]{1,0:T(8,128)(2,1)} custom-call(s32[12]{0:T(128)S(1)} %stack.38.where, bf16[8192,512]{1,0:T(8,128)(2,1)S(1)} %get-tuple-element.21.pown, bf16[8192,512]{1,0:T(8,128)(2,1)S(1)} %load.1.after.psib, bf16[512,512]{1,0:T(8,128)(2,1)S(1)} %pack.2.wown, bf16[512,512]{1,0:T(8,128)(2,1)S(1)} %collective-permute-done.14.wsib, ...), custom_call_target="tpu_custom_call" | custom-call | flops 8589934592 | bytes 33554432 | tf_op jit(solution)/shard_map/numer/pallas_call | solution.py:320
  109.3 0.0 collective-permute-done.10.refs_3_
  109.4 0.0 collective-permute-done.9.refs_2_
  109.4 0.0 collective-permute-done.8.refs_1_
  109.4 0.6 pack.3.wown
  110.0 0.1 collective-permute-start.16
  110.0 1.9 %collective-permute-done.16.wsib = bf16[512,512]{1,0:T(8,128)(2,1)S(1)} collective-permute-done((bf16[512,512]{1,0:T(8,128)(2,1)S(1)}, bf16[512,512]{1,0:T(8,128)(2,1)S(1)}, u32[]{:S(2)}, u32[]{:S(2)}) %collective-permute-start.16) | collective-permute-done | bytes 524320 | tf_op jit(solution)/shard_map/ppermute | solution.py:339
  111.9 15.0 %numer.3 = bf16[8192,1024]{1,0:T(8,128)(2,1)} custom-call(s32[12]{0:T(128)S(1)} %stack.38.where, bf16[8192,512]{1,0:T(8,128)(2,1)S(1)} %get-tuple-element.21.pown, bf16[8192,512]{1,0:T(8,128)(2,1)S(1)} %load.1.after.psib, bf16[512,512]{1,0:T(8,128)(2,1)S(1)} %pack.3.wown, ...), custom_call_target="tpu_custom_call", output_to_operand_aliasing={{}: (8, {})} | custom-call | flops 8589934592 | bytes 33554432 | tf_op jit(solution)/shard_map/numer/pallas_call | solution.py:320
Async XLA Ops:
  25.8 35.2 %collective-permute-start = (bf16[8192,512]{1,0:T(8,128)(2,1)}, bf16[8192,512]{1,0:T(8,128)(2,1)}, u32[]{:S(2)}, u32[]{:S(2)}) collective-permute-start(bf16[8192,512]{1,0:T(8,128)(2,1)} %get-tuple-element.22), channel_id=1, source_target_pairs={{0,1},{1,0},{2,3},{3,2},{4,5},{5,4},{6,7},{7,6},{8,9},{9,8},{10,11... | collective-permute-start | bytes 25165832 | tf_op jit(solution)/shard_map/ppermute | solution.py:339
  26.4 15.4 %collective-permute-start.1 = (f32[256,512]{1,0:T(8,128)S(1)}, f32[256,512]{1,0:T(8,128)S(1)}, u32[]{:S(2)}, u32[]{:S(2)}) collective-permute-start(f32[256,512]{1,0:T(8,128)S(1)} %get-tuple-element.24), channel_id=1, source_target_pairs={{0,4},{4,0},{8,12},{12,8},{1,5},{5,1},{9,13},{13,9},{2,6},{6,2},{1... | collective-permute-start | bytes 1572872 | tf_op jit(solution)/shard_map/ppermute | solution.py:339
  29.0 24.0 %collective-permute-start.2 = (f32[256,256]{1,0:T(8,128)S(1)}, f32[256,256]{1,0:T(8,128)S(1)}, u32[]{:S(2)}, u32[]{:S(2)}) collective-permute-start(f32[256,256]{1,0:T(8,128)S(1)} %get-tuple-element.25), channel_id=1, source_target_pairs={{0,4},{4,0},{8,12},{12,8},{1,5},{5,1},{9,13},{13,9},{2,6},{6,2},{1... | collective-permute-start | bytes 786440 | tf_op jit(solution)/shard_map/ppermute | solution.py:339
  37.2 34.6 %copy-start = (s32[1024]{0:T(1024)S(1)}, s32[1024]{0:T(1024)}, u32[]{:S(2)}) copy-start(s32[1024]{0:T(1024)} %param.11) | copy-start | bytes 12292
  37.2 34.6 %copy-start.1 = (f32[8]{0:T(128)S(1)}, f32[8]{0:T(128)}, u32[]{:S(2)}) copy-start(f32[8]{0:T(128)} %table.1) | copy-start | bytes 100
  37.2 21.3 %collective-permute-start.3 = (f32[256,256]{1,0:T(8,128)S(1)}, f32[256,256]{1,0:T(8,128)S(1)}, u32[]{:S(2)}, u32[]{:S(2)}) collective-permute-start(f32[256,256]{1,0:T(8,128)S(1)} %get-tuple-element.26), channel_id=1, source_target_pairs={{0,4},{4,0},{8,12},{12,8},{1,5},{5,1},{9,13},{13,9},{2,6},{6,2},{1... | collective-permute-start | bytes 786440 | tf_op jit(solution)/shard_map/ppermute | solution.py:339
  42.4 29.4 %collective-permute-start.4 = (f32[128,512]{1,0:T(8,128)S(1)}, f32[128,512]{1,0:T(8,128)S(1)}, u32[]{:S(2)}, u32[]{:S(2)}) collective-permute-start(f32[128,512]{1,0:T(8,128)S(1)} %forward.3.after), channel_id=1, source_target_pairs={{0,8},{4,12},{8,0},{12,4},{1,9},{5,13},{9,1},{13,5},{2,10},{6,14},... | collective-permute-start | bytes 786440 | tf_op jit(solution)/shard_map/ppermute | solution.py:339
  53.6 15.5 %collective-permute-start.5 = (f32[128,256]{1,0:T(8,128)S(1)}, f32[128,256]{1,0:T(8,128)S(1)}, u32[]{:S(2)}, u32[]{:S(2)}) collective-permute-start(f32[128,256]{1,0:T(8,128)S(1)} %forward.4.after), channel_id=1, source_target_pairs={{0,8},{4,12},{8,0},{12,4},{1,9},{5,13},{9,1},{13,5},{2,10},{6,14},... | collective-permute-start | bytes 393224 | tf_op jit(solution)/shard_map/ppermute | solution.py:339
  59.0 12.8 %collective-permute-start.6 = (f32[128,256]{1,0:T(8,128)S(1)}, f32[128,256]{1,0:T(8,128)S(1)}, u32[]{:S(2)}, u32[]{:S(2)}) collective-permute-start(f32[128,256]{1,0:T(8,128)S(1)} %forward.5.after), channel_id=1, source_target_pairs={{0,8},{4,12},{8,0},{12,4},{1,9},{5,13},{9,1},{13,5},{2,10},{6,14},... | collective-permute-start | bytes 393224 | tf_op jit(solution)/shard_map/ppermute | solution.py:339
  72.6 3.7 %collective-permute-start.7 = (f32[16,128]{1,0:T(8,128)S(1)}, f32[16,128]{1,0:T(8,128)S(1)}, u32[]{:S(2)}, u32[]{:S(2)}) collective-permute-start(f32[16,128]{1,0:T(8,128)S(1)} %get-tuple-element.28.own.mine), channel_id=1, source_target_pairs={{0,2},{2,0},{1,3},{3,1},{4,6},{6,4},{5,7},{7,5},{8,10},{10,8},{9,1... | collective-permute-start | bytes 24584 | tf_op jit(solution)/shard_map/ppermute | solution.py:339
  77.1 8.3 %collective-permute-start.13 = (bf16[128,512]{1,0:T(8,128)(2,1)S(1)}, bf16[128,512]{1,0:T(8,128)(2,1)S(1)}, u32[]{:S(2)}, u32[]{:S(2)}) collective-permute-start(bf16[128,512]{1,0:T(8,128)(2,1)S(1)} %get-tuple-element.30.refs_0_), channel_id=1, source_target_pairs={{0,12},{4,8},{8,4},{12,0},{1,13},{5,9},{9,5},{13,1},{2,14},{6,10},... | collective-permute-start | bytes 393224 | tf_op jit(solution)/shard_map/ppermute | solution.py:339
  78.5 10.4 %collective-permute-start.12 = (bf16[128,512]{1,0:T(8,128)(2,1)S(1)}, bf16[128,512]{1,0:T(8,128)(2,1)S(1)}, u32[]{:S(2)}, u32[]{:S(2)}) collective-permute-start(bf16[128,512]{1,0:T(8,128)(2,1)S(1)} %get-tuple-element.30.refs_0_), channel_id=1, source_target_pairs={{0,8},{4,12},{8,0},{12,4},{1,9},{5,13},{9,1},{13,5},{2,10},{6,14},... | collective-permute-start | bytes 393224 | tf_op jit(solution)/shard_map/ppermute | solution.py:339
  78.5 10.4 %collective-permute-start.11 = (bf16[128,512]{1,0:T(8,128)(2,1)S(1)}, bf16[128,512]{1,0:T(8,128)(2,1)S(1)}, u32[]{:S(2)}, u32[]{:S(2)}) collective-permute-start(bf16[128,512]{1,0:T(8,128)(2,1)S(1)} %get-tuple-element.30.refs_0_), channel_id=1, source_target_pairs={{0,4},{4,0},{8,12},{12,8},{1,5},{5,1},{9,13},{13,9},{2,6},{6,2},{1... | collective-permute-start | bytes 393224 | tf_op jit(solution)/shard_map/ppermute | solution.py:339
  89.4 5.0 %collective-permute-start.14 = (bf16[512,512]{1,0:T(8,128)(2,1)S(1)}, bf16[512,512]{1,0:T(8,128)(2,1)S(1)}, u32[]{:S(2)}, u32[]{:S(2)}) collective-permute-start(bf16[512,512]{1,0:T(8,128)(2,1)S(1)} %pack.2.wown), channel_id=1, source_target_pairs={{0,1},{1,0},{2,3},{3,2},{4,5},{5,4},{6,7},{7,6},{8,9},{9,8},{10,11... | collective-permute-start | bytes 1572872 | tf_op jit(solution)/shard_map/ppermute | solution.py:339
  89.5 4.9 %collective-permute-start.15 = (f32[512,1]{1,0:T(8,128)S(1)}, f32[512,1]{1,0:T(8,128)S(1)}, u32[]{:S(2)}, u32[]{:S(2)}) collective-permute-start(f32[512,1]{1,0:T(8,128)S(1)} %copy.19.phi.after.fown), channel_id=1, source_target_pairs={{0,1},{1,0},{2,3},{3,2},{4,5},{5,4},{6,7},{7,6},{8,9},{9,8},{10,11... | collective-permute-start | bytes 6152 | tf_op jit(solution)/shard_map/ppermute | solution.py:339
  90.0 19.3 %collective-permute-start.10 = (bf16[128,512]{1,0:T(8,128)(2,1)S(1)}, bf16[128,512]{1,0:T(8,128)(2,1)S(1)}, u32[]{:S(2)}, u32[]{:S(2)}) collective-permute-start(bf16[128,512]{1,0:T(8,128)(2,1)S(1)} %get-tuple-element.29.refs_0_), channel_id=1, source_target_pairs={{0,12},{4,8},{8,4},{12,0},{1,13},{5,9},{9,5},{13,1},{2,14},{6,10},... | collective-permute-start | bytes 393224 | tf_op jit(solution)/shard_map/ppermute | solution.py:339
  92.1 17.2 %collective-permute-start.9 = (bf16[128,512]{1,0:T(8,128)(2,1)S(1)}, bf16[128,512]{1,0:T(8,128)(2,1)S(1)}, u32[]{:S(2)}, u32[]{:S(2)}) collective-permute-start(bf16[128,512]{1,0:T(8,128)(2,1)S(1)} %get-tuple-element.29.refs_0_), channel_id=1, source_target_pairs={{0,8},{4,12},{8,0},{12,4},{1,9},{5,13},{9,1},{13,5},{2,10},{6,14},... | collective-permute-start | bytes 393224 | tf_op jit(solution)/shard_map/ppermute | solution.py:339
  92.1 17.2 %collective-permute-start.8 = (bf16[128,512]{1,0:T(8,128)(2,1)S(1)}, bf16[128,512]{1,0:T(8,128)(2,1)S(1)}, u32[]{:S(2)}, u32[]{:S(2)}) collective-permute-start(bf16[128,512]{1,0:T(8,128)(2,1)S(1)} %get-tuple-element.29.refs_0_), channel_id=1, source_target_pairs={{0,4},{4,0},{8,12},{12,8},{1,5},{5,1},{9,13},{13,9},{2,6},{6,2},{1... | collective-permute-start | bytes 393224 | tf_op jit(solution)/shard_map/ppermute | solution.py:339
  110.0 2.0 %collective-permute-start.16 = (bf16[512,512]{1,0:T(8,128)(2,1)S(1)}, bf16[512,512]{1,0:T(8,128)(2,1)S(1)}, u32[]{:S(2)}, u32[]{:S(2)}) collective-permute-start(bf16[512,512]{1,0:T(8,128)(2,1)S(1)} %pack.3.wown), channel_id=1, source_target_pairs={{0,1},{1,0},{2,3},{3,2},{4,5},{5,4},{6,7},{7,6},{8,9},{9,8},{10,11... | collective-permute-start | bytes 1572872 | tf_op jit(solution)/shard_map/ppermute | solution.py:339

commit v5 on v4

--- a/solution.py
+++ b/solution.py
@@ -10,6 +10,7 @@
 prior_weight = 0.5
 MIB = 1 << 20
 SLOTS = 4
+PARTS = 4
 VMEM = pl.BlockSpec(memory_space=pltpu.VMEM)
 SMEM = pl.BlockSpec(memory_space=pltpu.SMEM)
 HBM = pl.BlockSpec(memory_space=pltpu.HBM)
@@ -91,7 +92,7 @@
     tk = min(2048, depth)
     half = rows // 2
     shapes = [jax.ShapeDtypeStruct((half, tn), jnp.float32)] * 2
-    shapes += [(pltpu.VMEM if own else pltpu.HBM)((depth // 2, rows), patterns.dtype) for own in turns]
+    shapes += [pltpu.VMEM((depth // 2, rows), patterns.dtype)] * len(turns)
     scratch = [
         pltpu.VMEM((SLOTS, tk, tn), jnp.bfloat16),
         pltpu.VMEM((rows, tn), jnp.float32),
@@ -133,7 +134,7 @@
         out_shape=jax.ShapeDtypeStruct((size, parts[0].shape[1]), jnp.float32),
         in_specs=[SMEM, ANY] + [VMEM] * len(parts),
         out_specs=VMEM,
-        compiler_params=params(8 * MIB),
+        compiler_params=params(4 * MIB),
         name="forward",
     )(where, after, *parts)
 
@@ -173,7 +174,7 @@
         ),
         in_specs=[SMEM, SMEM, VMEM, ANY] + [VMEM] * len(parts),
         out_specs=(VMEM, VMEM),
-        compiler_params=params(16 * MIB),
+        compiler_params=params(6 * MIB),
         name="softmax",
     )(where, table, classes, after, *parts)
 
@@ -208,7 +209,7 @@
         out_shape=[jax.ShapeDtypeStruct((count, tn), jnp.bfloat16) for tn in widths],
         in_specs=[SMEM] + [VMEM] * 5,
         out_specs=[VMEM] * len(widths),
-        compiler_params=params(8 * MIB),
+        compiler_params=params(4 * MIB),
         name="weights",
     )(where, phi, exps, own, mine, other)
 
@@ -256,6 +257,135 @@
     )(pltpu.with_memory_space_constraint(source, pltpu.HBM), after)
 
 
+def pass_kernel(where, pown, psib, *refs, blocks, first, last, base, side, tm):
+    count = pown.shape[1] // blocks[1]
+    mine = 2 * len(blocks[0])
+    pairs, refs = refs[:mine], refs[mine:]
+    pixels = pown.shape[0]
+    steps = pixels // tm
+    *refs, tiles, tsem = refs
+    factors, refs = refs[:2], refs[2:]
+    if first:
+        model, *sums, den, wide, buf, sem = refs
+        seen = prior_weight
+    elif last:
+        seen, *totals, out, wide, buf, sem = refs
+        seen = seen[...]
+    else:
+        seen, *totals = refs[: PARTS + 1]
+        *sums, den, wide = refs[PARTS + 1 :]
+        seen = seen[...]
+    for k in range(mine):
+        wide[k * count : (k + 1) * count, :] = pairs[k][...]
+
+    def pieces(i):
+        slot = lax.rem(i, 3)
+        rows = pl.ds(pl.multiple_of(i * tm, tm), tm)
+        for k in range(mine):
+            columns = pl.ds(pl.multiple_of(where[base + blocks[0][k // 2]], count), count)
+            part = (pown, psib)[k % 2].at[rows, columns]
+            yield pltpu.make_async_copy(part, tiles.at[slot, :, pl.ds(k * count, count)], tsem.at[slot, k])
+
+    def fetch(i):
+        slot = lax.rem(i, 3)
+        at = pl.multiple_of(where[side] * pixels + i * tm, tm)
+        return pltpu.make_async_copy(model.at[pl.ds(at, tm)], buf.at[slot], sem.at[slot])
+
+    def store(i):
+        slot = lax.rem(i, 2)
+        return pltpu.make_async_copy(buf.at[slot], out.at[pl.ds(pl.multiple_of(i * tm, tm), tm)], sem.at[slot])
+
+    for i in range(min(2, steps)):
+        for copy in pieces(i):
+            copy.start()
+        if first:
+            fetch(i).start()
+    for k, part in enumerate(pairs):
+        rows = pl.ds(pl.multiple_of(where[base + blocks[0][k // 2]], count), count)
+        seen = seen + jnp.sum(part[...].astype(jnp.float32) * factors[k % 2][rows, :], axis=0, keepdims=True)
+    if last:
+        scale = 1.0 / seen
+    else:
+        den[...] = seen
+
+    def body(part, i, carry):
+        local = pl.ds(pl.multiple_of(i * tm - part * (pixels // PARTS), tm), tm)
+        for copy in pieces(i):
+            copy.wait()
+        if first:
+            fetch(i).wait()
+
+        @pl.when(i + 2 < steps)
+        def _():
+            for copy in pieces(i + 2):
+                copy.start()
+            if first:
+                fetch(i + 2).start()
+
+        if last:
+
+            @pl.when(i >= 2)
+            def _():
+                store(i - 2).wait()
+
+        acc = jnp.dot(tiles[lax.rem(i, 3)], wide[...], preferred_element_type=jnp.float32)
+        if first:
+            sums[part][local, :] = acc + prior_weight * buf[lax.rem(i, 3)].astype(jnp.float32)
+        elif last:
+            buf[lax.rem(i, 2)] = ((acc + totals[part][local, :]) * scale).astype(jnp.bfloat16)
+            store(i).start()
+        else:
+            sums[part][local, :] = acc + totals[part][local, :]
+        return carry
+
+    for part in range(PARTS):
+        lax.fori_loop(part * steps // PARTS, (part + 1) * steps // PARTS, functools.partial(body, part), 0)
+    if last:
+        for i in range(max(0, steps - 2), steps):
+            store(i).wait()
+
+
+def numer_pass(where, base, pown, psib, blocks, pairs, phis, pix, model=None, total=None, last=False):
+    first = model is not None
+    pixels, count, columns = pown.shape[0], pairs[0].shape[0], pairs[0].shape[1]
+    tm = min(512, pixels // PARTS)
+    constrain = pltpu.with_memory_space_constraint
+    args = [where, constrain(pown, pltpu.HBM), constrain(psib, pltpu.HBM), *pairs, *phis]
+    in_specs = [SMEM, HBM, HBM] + [VMEM] * (len(pairs) + 2)
+    scratch = [pltpu.VMEM((len(pairs) * count, columns), jnp.bfloat16)]
+    shape, aliases = [pltpu.VMEM((pixels // PARTS, columns), jnp.float32)] * PARTS, {}
+    shape.append(jax.ShapeDtypeStruct((1, columns), jnp.float32))
+    if first:
+        args.append(constrain(model, pltpu.HBM))
+        in_specs.append(HBM)
+        scratch += [pltpu.VMEM((3, tm, columns), jnp.bfloat16), pltpu.SemaphoreType.DMA((3,))]
+    else:
+        args += [total[-1], *(constrain(part, pltpu.VMEM) for part in total[:-1])]
+        in_specs += [VMEM] * (PARTS + 1)
+    if last:
+        shape = jax.ShapeDtypeStruct((pixels, columns), jnp.bfloat16)
+        scratch += [pltpu.VMEM((2, tm, columns), jnp.bfloat16), pltpu.SemaphoreType.DMA((2,))]
+    elif not first:
+        aliases = {len(args) - PARTS + part: part for part in range(PARTS)}
+    scratch += [
+        pltpu.VMEM((3, tm, len(pairs) * count), jnp.bfloat16),
+        pltpu.SemaphoreType.DMA((3, len(pairs))),
+    ]
+    return pl.pallas_call(
+        functools.partial(
+            pass_kernel, blocks=(blocks, pix), first=first, last=last, base=base, side=1, tm=tm
+        ),
+        out_shape=shape,
+        in_specs=in_specs,
+        out_specs=HBM if last else [VMEM] * (PARTS + 1),
+        scratch_shapes=scratch,
+        input_output_aliases=aliases,
+        compiler_params=params(14 * MIB),
+        cost_estimate=cost(2 * pixels * columns * count * len(pairs), 4 * pixels * columns),
+        name="numer",
+    )(*args)
+
+
 def numer_kernel(where, pown, psib, wown, wsib, fown, fsib, model, *refs, column, tm, sub):
     out, mbuf, obuf, msem, osem = refs[-5:]
     pixels, tn = pown.shape[0], wown.shape[1]
@@ -278,21 +408,20 @@
     scale = 1.0 / (prior_weight + den)
 
     def body(i, carry):
+        fetch(i).wait()
+
         @pl.when(i + 2 < steps)
         def _():
             fetch(i + 2).start()
+
+        @pl.when(i >= 2)
+        def _():
+            store(i - 2).wait()
 
         for r in range(0, tm, sub):
             rows = pl.ds(pl.multiple_of(i * tm + r, sub), sub)
             acc = jnp.dot(pown[rows, :], wown[...], preferred_element_type=jnp.float32)
             acc = acc + jnp.dot(psib[rows, :], wsib[...], preferred_element_type=jnp.float32)
-            if r == 0:
-                fetch(i).wait()
-
-                @pl.when(i >= 2)
-                def _():
-                    store(i - 2).wait()
-
             acc = acc + prior_weight * mbuf[lax.rem(i, 3), r : r + sub, :].astype(jnp.float32)
             obuf[lax.rem(i, 2), r : r + sub, :] = (acc * scale).astype(jnp.bfloat16)
         store(i).start()
@@ -375,11 +504,20 @@
 
     later = min(2, chunks - 1)
     turned, terms = {}, {}
-    source = patterns
+    source, after = patterns, phi
+
+    def relay(c, after):
+        size = rows // 2
+        for hop in range(1, hops):
+            size //= 2
+            after = forward(where, places[hop], terms[c], size, after)
+            terms[c].append(exchange(after, "pix", pix, 1 << hop))
+        return after
+
     for c in range(chunks):
         turns = ((False,) if c == 1 else ()) + ((True,) if c == later else ())
         send, keep, *rest = cross_chunk(
-            where, phi, source, model, phi if c == 0 else terms[c - 1][0], starts[c], widths[c], beta, c == 0, turns
+            where, phi, source, model, after, starts[c], widths[c], beta, c == 0, turns
         )
         if c == 0:
             source = rest[-1]
@@ -388,26 +526,36 @@
         terms[c] = [keep, exchange(send, "pix", pix, 1)]
         if c == 1:
             psib = exchange(turned[False], "pat", 2, 1)
-    after = keep
-    for c in range(chunks):
-        size = rows // 2
-        for hop in range(1, hops):
-            size //= 2
-            after = forward(where, places[hop], terms[c], size, after)
-            terms[c].append(exchange(after, "pix", pix, 1 << hop))
-    psib = load(psib, after)
+        if c >= 1 and c < chunks:
+            after = relay(c - 1, keep)
+    after = relay(chunks - 1, keep)
+    split = pix == 4 and count % 128 == 0
+    if split:
+        token = phi
+    else:
+        token = psib = load(psib, after)
     held = [term for c in range(chunks) for term in terms[c]]
     phi_sib = exchange(phi, "pat", 2, 1)
 
-    exps, own = softmax_stage(where, places["terms"], weight_table, classes, psib, held, count, chunks)
+    exps, own = softmax_stage(where, places["terms"], weight_table, classes, token, held, count, chunks)
     mine = own
     other = None
     for hop in range(ori.bit_length() - 1):
         if other is not None:
             mine = combine(mine, other)
         other = exchange(mine, "ori", ori, 1 << hop)
-    shares = [columns // 2] * 2 if columns >= 512 else [columns]
+    shares = [columns] if split or columns < 512 else [columns // 2] * 2
     weights = weight_stage(where, places["share"], phi, exps, own, mine, other, shares)
+
+    if split:
+        base = places["order"]
+        own = [weights[0], exchange(weights[0], "pix", pix, 1), exchange(weights[0], "pix", pix, 2)]
+        own.append(exchange(own[2], "pix", pix, 1))
+        pairs = [(w, exchange(w, "pat", 2, 1)) for w in own]
+        phis = (phi, phi_sib)
+        total = numer_pass(where, base, turned[True], psib, (0,), pairs[0], phis, pix, model=model)
+        total = numer_pass(where, base, turned[True], psib, (1,), pairs[1], phis, pix, total=total)
+        return numer_pass(where, base, turned[True], psib, (2, 3), pairs[2] + pairs[3], phis, pix, total=total, last=True)
 
     gathered = [[w] + [exchange(w, "pix", pix, d) for d in range(1, pix)] for w in weights]
     at, result, after = 0, None, model

time: 127 us -> 142 us (1.12)
  waiting for transfers between devices: 31.6 us -> 49.4 us
  starting transfers between devices: 23.5 us -> 14.5 us
  local copies, waits for them, and re-layouts: 0.25 us -> 3.5 us
  Pallas kernels: 70.7 us -> 73.5 us
    ppermute x17 -> x16, waiting for transfers between devices: 31.6 us -> 49.4 us  [exchange(): return lax.ppermute(value, axis, [(i, i ^ distance) for i in range(size)])]
    ppermute x17 -> x16, starting transfers between devices: 23.5 us -> 14.5 us  [exchange(): return lax.ppermute(value, axis, [(i, i ^ distance) for i in range(size)])]
    pallas_call x5 -> x3, Pallas kernels: 34.6 us -> 40.6 us  [numer_pass(): pl.pallas_call(functools.partial(pass_kernel, blocks=(blocks, pix), first...]
    unnamed x4 -> x6, local copies, waits for them, and re-layouts: 0.01 us -> 3.26 us
    pallas_call x3, Pallas kernels: 32.8 us -> 29.6 us  [cross_chunk(): pl.pallas_call(functools.partial(cross_kernel, column=column, tk=tk, step...]
  transfers between devices with their start and end apart: 17 -> 16, of which waited for: 9 -> 8; matrix products, arithmetic and copies ran while one was open for 0% -> 0% of each run, Pallas kernels for 22% -> 25%
where the time goes in v5:
time: 142 us
  Pallas kernels  73.5 us (52%)
  waiting for transfers between devices  49.4 us (35%)
  starting transfers between devices  14.5 us (10%)
  local copies, waits for them, and re-layouts  3.5 us (2%)
    ppermute x16, waiting for transfers between devices, exchange(): return lax.ppermute(value, axis, [(i, i ^ distance) for i in range(size)])  49.4 us
    pallas_call x3, Pallas kernels, numer_pass(): pl.pallas_call(functools.partial(pass_kernel, blocks=(blocks, pix), first...  40.6 us
    pallas_call x3, Pallas kernels, cross_chunk(): pl.pallas_call(functools.partial(cross_kernel, column=column, tk=tk, step...  29.6 us
    ppermute x16, starting transfers between devices, exchange(): return lax.ppermute(value, axis, [(i, i ^ distance) for i in range(size)])  14.5 us
    unnamed x6, local copies, waits for them, and re-layouts  3.26 us
  transfers between devices with their start and end apart: 16, of which 8 were waited for; matrix products, arithmetic and copies ran while one was open for 0% of the time, Pallas kernels for 25%

profile of v5, /device:TPU:0, one launch (start us, length us, event | category | flops | bytes accessed | tf_op | source)
XLA Modules:
  0.0 141.8 jit_solution(8108404449885128289)
XLA Ops:
  0.0 0.8 select_reduce_fusion
  0.8 0.1 copy.26.phi.after.refs_2_.refs_4_
  0.9 0.1 stack.38.where
  1.0 13.4 %cross.3 = (f32[256,512]{1,0:T(8,128)S(1)}, f32[256,512]{1,0:T(8,128)S(1)}, bf16[512,16384]{1,0:T(8,128)(2,1)S(1)}) custom-call(s32[12]{0:T(128)S(1)} %stack.38.where, f32[512,1]{1,0:T(8,128)S(1)} %copy.26.phi.after.refs_2_.refs_4_, bf16[512,16384]{1,0:T(8,128)(2,1)} %patterns.1, bf16[16384,1024]{1,0:T(8,128)(2,1)} %refs_4_.1, ...), custom_call_target="tpu_custom_call" | custom-call | flops 8589934592 | bytes 33554432 | tf_op jit(solution)/shard_map/cross/pallas_call | solution.py:107
  14.5 8.1 %cross.4 = (f32[256,256]{1,0:T(8,128)S(1)}, f32[256,256]{1,0:T(8,128)S(1)}, bf16[8192,512]{1,0:T(8,128)(2,1)S(1)}) custom-call(s32[12]{0:T(128)S(1)} %stack.38.where, f32[512,1]{1,0:T(8,128)S(1)} %copy.26.phi.after.refs_2_.refs_4_, bf16[512,16384]{1,0:T(8,128)(2,1)S(1)} %get-tuple-element.26.patterns, bf16[16384,1024]{1,0:T(8,128)(2,1)} %refs_4_.1, ...), custom_call_target="tpu_custom_call" | custom-call | flops 4294967296 | bytes 25165824 | tf_op jit(solution)/shard_map/cross/pallas_call | solution.py:107
  22.6 0.6 collective-permute-start.1
  23.1 2.6 %collective-permute-start = (f32[256,512]{1,0:T(8,128)S(1)}, f32[256,512]{1,0:T(8,128)S(1)}, u32[]{:S(2)}, u32[]{:S(2)}) collective-permute-start(f32[256,512]{1,0:T(8,128)S(1)} %get-tuple-element.29), channel_id=1, source_target_pairs={{0,4},{4,0},{8,12},{12,8},{1,5},{5,1},{9,13},{13,9},{2,6},{6,2},{1... | collective-permute-start | bytes 1572872 | tf_op jit(solution)/shard_map/ppermute | solution.py:468
  25.8 0.1 collective-permute-start.3
  25.8 12.7 %collective-permute-done.refs_1_ = f32[256,512]{1,0:T(8,128)S(1)} collective-permute-done((f32[256,512]{1,0:T(8,128)S(1)}, f32[256,512]{1,0:T(8,128)S(1)}, u32[]{:S(2)}, u32[]{:S(2)}) %collective-permute-start) | collective-permute-done | bytes 524320 | tf_op jit(solution)/shard_map/ppermute | solution.py:468
  38.5 0.6 forward.3.after
  39.1 0.0 copy-start.1
  39.1 0.0 copy-start.2
  39.1 8.1 %cross.5 = (f32[256,256]{1,0:T(8,128)S(1)}, f32[256,256]{1,0:T(8,128)S(1)}, bf16[8192,512]{1,0:T(8,128)(2,1)S(1)}) custom-call(s32[12]{0:T(128)S(1)} %stack.38.where, f32[512,1]{1,0:T(8,128)S(1)} %copy.26.phi.after.refs_2_.refs_4_, bf16[512,16384]{1,0:T(8,128)(2,1)S(1)} %get-tuple-element.26.patterns, bf16[16384,1024]{1,0:T(8,128)(2,1)} %refs_4_.1, ...), custom_call_target="tpu_custom_call" | custom-call | flops 4294967296 | bytes 25165824 | tf_op jit(solution)/shard_map/cross/pallas_call | solution.py:107
  47.2 0.0 copy-start
  47.2 3.2 %copy-done = bf16[8192,512]{1,0:T(8,128)(2,1)} copy-done((bf16[8192,512]{1,0:T(8,128)(2,1)}, bf16[8192,512]{1,0:T(8,128)(2,1)S(1)}, u32[]{:S(2)}) %copy-start) | copy-done | bytes 8388632
  50.5 2.0 %collective-permute-start.5 = (f32[256,256]{1,0:T(8,128)S(1)}, f32[256,256]{1,0:T(8,128)S(1)}, u32[]{:S(2)}, u32[]{:S(2)}) collective-permute-start(f32[256,256]{1,0:T(8,128)S(1)} %get-tuple-element.34), channel_id=1, source_target_pairs={{0,4},{4,0},{8,12},{12,8},{1,5},{5,1},{9,13},{13,9},{2,6},{6,2},{1... | collective-permute-start | bytes 786440 | tf_op jit(solution)/shard_map/ppermute | solution.py:468
  52.5 2.6 %collective-permute-start.2 = (f32[128,512]{1,0:T(8,128)S(1)}, f32[128,512]{1,0:T(8,128)S(1)}, u32[]{:S(2)}, u32[]{:S(2)}) collective-permute-start(f32[128,512]{1,0:T(8,128)S(1)} %forward.3.after), channel_id=1, source_target_pairs={{0,8},{4,12},{8,0},{12,4},{1,9},{5,13},{9,1},{13,5},{2,10},{6,14},... | collective-permute-start | bytes 786440 | tf_op jit(solution)/shard_map/ppermute | solution.py:468
  55.1 0.0 collective-permute-done.3.refs_1_.refs_4_
  55.1 0.6 forward.4
  55.7 0.4 collective-permute-start.4
  56.1 7.7 %collective-permute-done.5.refs_1_.refs_7_ = f32[256,256]{1,0:T(8,128)S(1)} collective-permute-done((f32[256,256]{1,0:T(8,128)S(1)}, f32[256,256]{1,0:T(8,128)S(1)}, u32[]{:S(2)}, u32[]{:S(2)}) %collective-permute-start.5) | collective-permute-done | bytes 262176 | tf_op jit(solution)/shard_map/ppermute | solution.py:468
  63.8 0.6 forward.5
  64.4 0.5 collective-permute-start.6
  64.9 11.0 %collective-permute-done.4.refs_5_ = f32[128,256]{1,0:T(8,128)S(1)} collective-permute-done((f32[128,256]{1,0:T(8,128)S(1)}, f32[128,256]{1,0:T(8,128)S(1)}, u32[]{:S(2)}, u32[]{:S(2)}) %collective-permute-start.4) | collective-permute-done | bytes 131104 | tf_op jit(solution)/shard_map/ppermute | solution.py:468
  75.9 0.0 collective-permute-done.2.refs_2_
  75.9 1.4 collective-permute-done.6.refs_8_
  77.3 0.0 copy-done.1
  77.3 0.0 copy-done.2
  77.3 0.8 softmax.1
  78.1 1.5 %collective-permute-start.7 = (f32[16,128]{1,0:T(8,128)S(1)}, f32[16,128]{1,0:T(8,128)S(1)}, u32[]{:S(2)}, u32[]{:S(2)}) collective-permute-start(f32[16,128]{1,0:T(8,128)S(1)} %get-tuple-element.36.own.mine), channel_id=1, source_target_pairs={{0,2},{2,0},{1,3},{3,1},{4,6},{6,4},{5,7},{7,5},{8,10},{10,8},{9,1... | collective-permute-start | bytes 24584 | tf_op jit(solution)/shard_map/ppermute | solution.py:468
  79.6 2.2 %collective-permute-done.7.other = f32[16,128]{1,0:T(8,128)S(1)} collective-permute-done((f32[16,128]{1,0:T(8,128)S(1)}, f32[16,128]{1,0:T(8,128)S(1)}, u32[]{:S(2)}, u32[]{:S(2)}) %collective-permute-start.7) | collective-permute-done | bytes 8224 | tf_op jit(solution)/shard_map/ppermute | solution.py:468
  81.8 0.7 weights.1.refs_0_
  82.5 0.1 collective-permute-start.8
  82.6 3.0 %collective-permute-start.13 = (bf16[128,1024]{1,0:T(8,128)(2,1)S(1)}, bf16[128,1024]{1,0:T(8,128)(2,1)S(1)}, u32[]{:S(2)}, u32[]{:S(2)}) collective-permute-start(bf16[128,1024]{1,0:T(8,128)(2,1)S(1)} %weights.1.refs_0_), channel_id=1, source_target_pairs={{0,4},{4,0},{8,12},{12,8},{1,5},{5,1},{9,13},{13,9},{2,6},{6,2},{1... | collective-permute-start | bytes 786440 | tf_op jit(solution)/shard_map/ppermute | solution.py:468
  85.6 8.4 %collective-permute-done.8.refs_0_ = bf16[128,1024]{1,0:T(8,128)(2,1)S(1)} collective-permute-done((bf16[128,1024]{1,0:T(8,128)(2,1)S(1)}, bf16[128,1024]{1,0:T(8,128)(2,1)S(1)}, u32[]{:S(2)}, u32[]{:S(2)}) %collective-permute-start.8) | collective-permute-done | bytes 262176 | tf_op jit(solution)/shard_map/ppermute | solution.py:468
  94.1 0.0 collective-permute-start.10
  94.1 0.0 collective-permute-start.15
  94.1 0.5 collective-permute-start.12
  94.6 1.4 collective-permute-done.12.refs_3_.refs_5_
  96.0 0.1 collective-permute-start.9
  96.1 0.0 collective-permute-done.13.refs_0_
  96.1 0.4 collective-permute-start.14
  96.5 4.6 %collective-permute-done.10.refs_2_ = bf16[128,1024]{1,0:T(8,128)(2,1)S(1)} collective-permute-done((bf16[128,1024]{1,0:T(8,128)(2,1)S(1)}, bf16[128,1024]{1,0:T(8,128)(2,1)S(1)}, u32[]{:S(2)}, u32[]{:S(2)}) %collective-permute-start.10) | collective-permute-done | bytes 262176 | tf_op jit(solution)/shard_map/ppermute | solution.py:468
  101.1 0.0 collective-permute-start.11
  101.1 0.0 collective-permute-done.15.refs_1_
  101.1 0.0 collective-permute-done.1.psib
  101.1 13.0 %numer.3 = (f32[2048,1024]{1,0:T(8,128)S(1)}, f32[2048,1024]{1,0:T(8,128)S(1)}, f32[2048,1024]{1,0:T(8,128)S(1)}, f32[2048,1024]{1,0:T(8,128)S(1)}, f32[1,1024]{1,0:T(1,128)S(1)}) custom-call(s32[12]{0:T(128)S(1)} %stack.38.where, bf16[8192,512]{1,0:T(8,128)(2,1)} %copy-done, bf16[8192,512]{1,0:T(8,128)(2,1)} %collective-permute-done.1.psib, ...), custom_call_target="tpu_custom_call" | custom-call | flops 4294967296 | bytes 33554432 | tf_op jit(solution)/shard_map/numer/pallas_call | solution.py:374
  114.1 0.0 collective-permute-done.14.refs_1_
  114.1 11.3 %numer.4 = (f32[2048,1024]{1,0:T(8,128)S(1)}, f32[2048,1024]{1,0:T(8,128)S(1)}, f32[2048,1024]{1,0:T(8,128)S(1)}, f32[2048,1024]{1,0:T(8,128)S(1)}, f32[1,1024]{1,0:T(1,128)S(1)}) custom-call(s32[12]{0:T(128)S(1)} %stack.38.where, bf16[8192,512]{1,0:T(8,128)(2,1)} %copy-done, ...), custom_call_target="tpu_custom_call", output_to_operand_aliasing={{0}: (8, {}), {1}: (9, {}), {2}: (10, {}), {3}: (11, {})} | custom-call | flops 4294967296 | bytes 33554432 | tf_op jit(solution)/shard_map/numer/pallas_call | solution.py:374
  125.4 0.0 collective-permute-done.9.refs_1_
  125.4 0.0 collective-permute-done.11.refs_3_
  125.4 16.4 %numer.5 = bf16[8192,1024]{1,0:T(8,128)(2,1)} custom-call(s32[12]{0:T(128)S(1)} %stack.38.where, bf16[8192,512]{1,0:T(8,128)(2,1)} %copy-done, bf16[8192,512]{1,0:T(8,128)(2,1)} %collective-permute-done.1.psib, bf16[128,1024]{1,0:T(8,128)(2,1)S(1)} %collective-permute-done.8.refs_0_, bf16[128,1024]{1,0:T(8,128)(2,1)S(1)} %collective-permute-done.9.refs_1_, ...), custom_call_target="tpu_custom_call" | custom-call | flops 8589934592 | bytes 33554432 | tf_op jit(solution)/shard_map/numer/pallas_call | solution.py:374
Async XLA Ops:
  22.6 78.5 %collective-permute-start.1 = (bf16[8192,512]{1,0:T(8,128)(2,1)S(1)}, bf16[8192,512]{1,0:T(8,128)(2,1)}, u32[]{:S(2)}, u32[]{:S(2)}) collective-permute-start(bf16[8192,512]{1,0:T(8,128)(2,1)S(1)} %get-tuple-element.31), channel_id=1, source_target_pairs={{0,1},{1,0},{2,3},{3,2},{4,5},{5,4},{6,7},{7,6},{8,9},{9,8},{10,11... | collective-permute-start | bytes 25165832 | tf_op jit(solution)/shard_map/ppermute | solution.py:468
  23.1 15.4 %collective-permute-start = (f32[256,512]{1,0:T(8,128)S(1)}, f32[256,512]{1,0:T(8,128)S(1)}, u32[]{:S(2)}, u32[]{:S(2)}) collective-permute-start(f32[256,512]{1,0:T(8,128)S(1)} %get-tuple-element.29), channel_id=1, source_target_pairs={{0,4},{4,0},{8,12},{12,8},{1,5},{5,1},{9,13},{13,9},{2,6},{6,2},{1... | collective-permute-start | bytes 1572872 | tf_op jit(solution)/shard_map/ppermute | solution.py:468
  25.8 29.3 %collective-permute-start.3 = (f32[256,256]{1,0:T(8,128)S(1)}, f32[256,256]{1,0:T(8,128)S(1)}, u32[]{:S(2)}, u32[]{:S(2)}) collective-permute-start(f32[256,256]{1,0:T(8,128)S(1)} %get-tuple-element.32), channel_id=1, source_target_pairs={{0,4},{4,0},{8,12},{12,8},{1,5},{5,1},{9,13},{13,9},{2,6},{6,2},{1... | collective-permute-start | bytes 786440 | tf_op jit(solution)/shard_map/ppermute | solution.py:468
  39.1 38.2 %copy-start.1 = (s32[1024]{0:T(1024)S(1)}, s32[1024]{0:T(1024)}, u32[]{:S(2)}) copy-start(s32[1024]{0:T(1024)} %param.11) | copy-start | bytes 12292
  39.1 38.1 %copy-start.2 = (f32[8]{0:T(128)S(1)}, f32[8]{0:T(128)}, u32[]{:S(2)}) copy-start(f32[8]{0:T(128)} %table.1) | copy-start | bytes 100
  47.2 3.3 %copy-start = (bf16[8192,512]{1,0:T(8,128)(2,1)}, bf16[8192,512]{1,0:T(8,128)(2,1)S(1)}, u32[]{:S(2)}) copy-start(bf16[8192,512]{1,0:T(8,128)(2,1)S(1)} %get-tuple-element.30.pown) | copy-start | bytes 25165828
  50.5 13.3 %collective-permute-start.5 = (f32[256,256]{1,0:T(8,128)S(1)}, f32[256,256]{1,0:T(8,128)S(1)}, u32[]{:S(2)}, u32[]{:S(2)}) collective-permute-start(f32[256,256]{1,0:T(8,128)S(1)} %get-tuple-element.34), channel_id=1, source_target_pairs={{0,4},{4,0},{8,12},{12,8},{1,5},{5,1},{9,13},{13,9},{2,6},{6,2},{1... | collective-permute-start | bytes 786440 | tf_op jit(solution)/shard_map/ppermute | solution.py:468
  52.5 23.4 %collective-permute-start.2 = (f32[128,512]{1,0:T(8,128)S(1)}, f32[128,512]{1,0:T(8,128)S(1)}, u32[]{:S(2)}, u32[]{:S(2)}) collective-permute-start(f32[128,512]{1,0:T(8,128)S(1)} %forward.3.after), channel_id=1, source_target_pairs={{0,8},{4,12},{8,0},{12,4},{1,9},{5,13},{9,1},{13,5},{2,10},{6,14},... | collective-permute-start | bytes 786440 | tf_op jit(solution)/shard_map/ppermute | solution.py:468
  55.7 20.2 %collective-permute-start.4 = (f32[128,256]{1,0:T(8,128)S(1)}, f32[128,256]{1,0:T(8,128)S(1)}, u32[]{:S(2)}, u32[]{:S(2)}) collective-permute-start(f32[128,256]{1,0:T(8,128)S(1)} %forward.4), channel_id=1, source_target_pairs={{0,8},{4,12},{8,0},{12,4},{1,9},{5,13},{9,1},{13,5},{2,10},{6,14},... | collective-permute-start | bytes 393224 | tf_op jit(solution)/shard_map/ppermute | solution.py:468
  64.4 12.9 %collective-permute-start.6 = (f32[128,256]{1,0:T(8,128)S(1)}, f32[128,256]{1,0:T(8,128)S(1)}, u32[]{:S(2)}, u32[]{:S(2)}) collective-permute-start(f32[128,256]{1,0:T(8,128)S(1)} %forward.5), channel_id=1, source_target_pairs={{0,8},{4,12},{8,0},{12,4},{1,9},{5,13},{9,1},{13,5},{2,10},{6,14},... | collective-permute-start | bytes 393224 | tf_op jit(solution)/shard_map/ppermute | solution.py:468
  78.1 3.7 %collective-permute-start.7 = (f32[16,128]{1,0:T(8,128)S(1)}, f32[16,128]{1,0:T(8,128)S(1)}, u32[]{:S(2)}, u32[]{:S(2)}) collective-permute-start(f32[16,128]{1,0:T(8,128)S(1)} %get-tuple-element.36.own.mine), channel_id=1, source_target_pairs={{0,2},{2,0},{1,3},{3,1},{4,6},{6,4},{5,7},{7,5},{8,10},{10,8},{9,1... | collective-permute-start | bytes 24584 | tf_op jit(solution)/shard_map/ppermute | solution.py:468
  82.5 11.6 %collective-permute-start.8 = (bf16[128,1024]{1,0:T(8,128)(2,1)S(1)}, bf16[128,1024]{1,0:T(8,128)(2,1)S(1)}, u32[]{:S(2)}, u32[]{:S(2)}) collective-permute-start(bf16[128,1024]{1,0:T(8,128)(2,1)S(1)} %weights.1.refs_0_), channel_id=1, source_target_pairs={{0,8},{4,12},{8,0},{12,4},{1,9},{5,13},{9,1},{13,5},{2,10},{6,14},... | collective-permute-start | bytes 786440 | tf_op jit(solution)/shard_map/ppermute | solution.py:468
  82.6 13.5 %collective-permute-start.13 = (bf16[128,1024]{1,0:T(8,128)(2,1)S(1)}, bf16[128,1024]{1,0:T(8,128)(2,1)S(1)}, u32[]{:S(2)}, u32[]{:S(2)}) collective-permute-start(bf16[128,1024]{1,0:T(8,128)(2,1)S(1)} %weights.1.refs_0_), channel_id=1, source_target_pairs={{0,4},{4,0},{8,12},{12,8},{1,5},{5,1},{9,13},{13,9},{2,6},{6,2},{1... | collective-permute-start | bytes 786440 | tf_op jit(solution)/shard_map/ppermute | solution.py:468
  94.1 7.0 %collective-permute-start.10 = (bf16[128,1024]{1,0:T(8,128)(2,1)S(1)}, bf16[128,1024]{1,0:T(8,128)(2,1)S(1)}, u32[]{:S(2)}, u32[]{:S(2)}) collective-permute-start(bf16[128,1024]{1,0:T(8,128)(2,1)S(1)} %collective-permute-done.8.refs_0_), channel_id=1, source_target_pairs={{0,4},{4,0},{8,12},{12,8},{1,5},{5,1},{9,13},{13,9},{2,6},{6,2},{1... | collective-permute-start | bytes 786440 | tf_op jit(solution)/shard_map/ppermute | solution.py:468
  94.1 7.0 %collective-permute-start.15 = (bf16[128,1024]{1,0:T(8,128)(2,1)S(1)}, bf16[128,1024]{1,0:T(8,128)(2,1)S(1)}, u32[]{:S(2)}, u32[]{:S(2)}) collective-permute-start(bf16[128,1024]{1,0:T(8,128)(2,1)S(1)} %weights.1.refs_0_), channel_id=1, source_target_pairs={{0,1},{1,0},{2,3},{3,2},{4,5},{5,4},{6,7},{7,6},{8,9},{9,8},{10,11... | collective-permute-start | bytes 786440 | tf_op jit(solution)/shard_map/ppermute | solution.py:468
  94.1 1.9 %collective-permute-start.12 = (f32[512,1]{1,0:T(8,128)S(1)}, f32[512,1]{1,0:T(8,128)S(1)}, u32[]{:S(2)}, u32[]{:S(2)}) collective-permute-start(f32[512,1]{1,0:T(8,128)S(1)} %copy.26.phi.after.refs_2_.refs_4_), channel_id=1, source_target_pairs={{0,1},{1,0},{2,3},{3,2},{4,5},{5,4},{6,7},{7,6},{8,9},{9,8},{10,11... | collective-permute-start | bytes 6152 | tf_op jit(solution)/shard_map/ppermute | solution.py:468
  96.0 29.4 %collective-permute-start.9 = (bf16[128,1024]{1,0:T(8,128)(2,1)S(1)}, bf16[128,1024]{1,0:T(8,128)(2,1)S(1)}, u32[]{:S(2)}, u32[]{:S(2)}) collective-permute-start(bf16[128,1024]{1,0:T(8,128)(2,1)S(1)} %collective-permute-done.8.refs_0_), channel_id=1, source_target_pairs={{0,1},{1,0},{2,3},{3,2},{4,5},{5,4},{6,7},{7,6},{8,9},{9,8},{10,11... | collective-permute-start | bytes 786440 | tf_op jit(solution)/shard_map/ppermute | solution.py:468
  96.1 18.0 %collective-permute-start.14 = (bf16[128,1024]{1,0:T(8,128)(2,1)S(1)}, bf16[128,1024]{1,0:T(8,128)(2,1)S(1)}, u32[]{:S(2)}, u32[]{:S(2)}) collective-permute-start(bf16[128,1024]{1,0:T(8,128)(2,1)S(1)} %collective-permute-done.13.refs_0_), channel_id=1, source_target_pairs={{0,1},{1,0},{2,3},{3,2},{4,5},{5,4},{6,7},{7,6},{8,9},{9,8},{10,11... | collective-permute-start | bytes 786440 | tf_op jit(solution)/shard_map/ppermute | solution.py:468
  101.1 24.3 %collective-permute-start.11 = (bf16[128,1024]{1,0:T(8,128)(2,1)S(1)}, bf16[128,1024]{1,0:T(8,128)(2,1)S(1)}, u32[]{:S(2)}, u32[]{:S(2)}) collective-permute-start(bf16[128,1024]{1,0:T(8,128)(2,1)S(1)} %collective-permute-done.10.refs_2_), channel_id=1, source_target_pairs={{0,1},{1,0},{2,3},{3,2},{4,5},{5,4},{6,7},{7,6},{8,9},{9,8},{10,11... | collective-permute-start | bytes 786440 | tf_op jit(solution)/shard_map/ppermute | solution.py:468

commit v6 on v5

--- a/solution.py
+++ b/solution.py
@@ -11,6 +11,7 @@
 MIB = 1 << 20
 SLOTS = 4
 PARTS = 4
+SUB = 256
 VMEM = pl.BlockSpec(memory_space=pltpu.VMEM)
 SMEM = pl.BlockSpec(memory_space=pltpu.SMEM)
 HBM = pl.BlockSpec(memory_space=pltpu.HBM)
@@ -257,24 +258,60 @@
     )(pltpu.with_memory_space_constraint(source, pltpu.HBM), after)
 
 
-def pass_kernel(where, pown, psib, *refs, blocks, first, last, base, side, tm):
-    count = pown.shape[1] // blocks[1]
-    mine = 2 * len(blocks[0])
-    pairs, refs = refs[:mine], refs[mine:]
+def begin_kernel(where, model, after, *refs, side, tm):
+    *sums, token, buf, sem = refs
+    token[...] = jnp.zeros_like(token)
+    size = sums[0].shape[0]
+    steps = size * PARTS // tm
+
+    def fetch(i):
+        slot = lax.rem(i, 4)
+        at = pl.multiple_of(where[side] * size * PARTS + i * tm, tm)
+        return pltpu.make_async_copy(model.at[pl.ds(at, tm)], buf.at[slot], sem.at[slot])
+
+    for i in range(min(3, steps)):
+        fetch(i).start()
+
+    def body(part, i, carry):
+        fetch(i).wait()
+
+        @pl.when(i + 3 < steps)
+        def _():
+            fetch(i + 3).start()
+
+        rows = pl.ds(pl.multiple_of(i * tm - part * size, tm), tm)
+        sums[part][rows, :] = prior_weight * buf[lax.rem(i, 4)].astype(jnp.float32)
+        return carry
+
+    for part in range(PARTS):
+        lax.fori_loop(part * steps // PARTS, (part + 1) * steps // PARTS, functools.partial(body, part), 0)
+
+
+def begin(where, model, after):
+    pixels, columns = model.shape[0] // 2, model.shape[1]
+    tm = min(512, pixels // PARTS)
+    *total, token = pl.pallas_call(
+        functools.partial(begin_kernel, side=1, tm=tm),
+        out_shape=[pltpu.VMEM((pixels // PARTS, columns), jnp.float32)] * PARTS
+        + [jax.ShapeDtypeStruct((8, 128), jnp.float32)],
+        in_specs=[SMEM, HBM, ANY],
+        out_specs=[VMEM] * (PARTS + 1),
+        scratch_shapes=[pltpu.VMEM((4, tm, columns), jnp.bfloat16), pltpu.SemaphoreType.DMA((4,))],
+        compiler_params=params(10 * MIB),
+        name="begin",
+    )(where, pltpu.with_memory_space_constraint(model, pltpu.HBM), after)
+    return total, token
+
+
+def pass_kernel(where, pown, psib, *refs, blocks, pix, first, last, base, tm, sub):
+    mine = 2 * len(blocks)
+    count = pown.shape[1] // pix
     pixels = pown.shape[0]
     steps = pixels // tm
-    *refs, tiles, tsem = refs
-    factors, refs = refs[:2], refs[2:]
-    if first:
-        model, *sums, den, wide, buf, sem = refs
-        seen = prior_weight
-    elif last:
-        seen, *totals, out, wide, buf, sem = refs
-        seen = seen[...]
-    else:
-        seen, *totals = refs[: PARTS + 1]
-        *sums, den, wide = refs[PARTS + 1 :]
-        seen = seen[...]
+    pairs, factors, refs = refs[:mine], refs[mine : mine + 2], refs[mine + 2 :]
+    seen, refs = (prior_weight, refs) if first else (refs[0][...], refs[1:])
+    totals, refs = refs[:PARTS], refs[PARTS:]
+    *refs, wide, tiles, tsem = refs
     for k in range(mine):
         wide[k * count : (k + 1) * count, :] = pairs[k][...]
 
@@ -282,45 +319,35 @@
         slot = lax.rem(i, 3)
         rows = pl.ds(pl.multiple_of(i * tm, tm), tm)
         for k in range(mine):
-            columns = pl.ds(pl.multiple_of(where[base + blocks[0][k // 2]], count), count)
+            columns = pl.ds(pl.multiple_of(where[base + blocks[k // 2]], count), count)
             part = (pown, psib)[k % 2].at[rows, columns]
             yield pltpu.make_async_copy(part, tiles.at[slot, :, pl.ds(k * count, count)], tsem.at[slot, k])
 
-    def fetch(i):
-        slot = lax.rem(i, 3)
-        at = pl.multiple_of(where[side] * pixels + i * tm, tm)
-        return pltpu.make_async_copy(model.at[pl.ds(at, tm)], buf.at[slot], sem.at[slot])
+    for i in range(min(2, steps)):
+        for copy in pieces(i):
+            copy.start()
+    for k, part in enumerate(pairs):
+        rows = pl.ds(pl.multiple_of(where[base + blocks[k // 2]], count), count)
+        seen = seen + jnp.sum(part[...].astype(jnp.float32) * factors[k % 2][rows, :], axis=0, keepdims=True)
+    if last:
+        out, buf, sem = refs
+        scale = 1.0 / seen
+    else:
+        *sums, den = refs
+        den[...] = seen
 
     def store(i):
         slot = lax.rem(i, 2)
         return pltpu.make_async_copy(buf.at[slot], out.at[pl.ds(pl.multiple_of(i * tm, tm), tm)], sem.at[slot])
 
-    for i in range(min(2, steps)):
-        for copy in pieces(i):
-            copy.start()
-        if first:
-            fetch(i).start()
-    for k, part in enumerate(pairs):
-        rows = pl.ds(pl.multiple_of(where[base + blocks[0][k // 2]], count), count)
-        seen = seen + jnp.sum(part[...].astype(jnp.float32) * factors[k % 2][rows, :], axis=0, keepdims=True)
-    if last:
-        scale = 1.0 / seen
-    else:
-        den[...] = seen
-
     def body(part, i, carry):
-        local = pl.ds(pl.multiple_of(i * tm - part * (pixels // PARTS), tm), tm)
         for copy in pieces(i):
             copy.wait()
-        if first:
-            fetch(i).wait()
 
         @pl.when(i + 2 < steps)
         def _():
             for copy in pieces(i + 2):
                 copy.start()
-            if first:
-                fetch(i + 2).start()
 
         if last:
 
@@ -328,14 +355,15 @@
             def _():
                 store(i - 2).wait()
 
-        acc = jnp.dot(tiles[lax.rem(i, 3)], wide[...], preferred_element_type=jnp.float32)
-        if first:
-            sums[part][local, :] = acc + prior_weight * buf[lax.rem(i, 3)].astype(jnp.float32)
-        elif last:
-            buf[lax.rem(i, 2)] = ((acc + totals[part][local, :]) * scale).astype(jnp.bfloat16)
+        for r in range(0, tm, sub):
+            rows = pl.ds(pl.multiple_of(i * tm + r - part * (pixels // PARTS), sub), sub)
+            dot = jnp.dot(tiles[lax.rem(i, 3), r : r + sub, :], wide[...], preferred_element_type=jnp.float32)
+            if last:
+                buf[lax.rem(i, 2), r : r + sub, :] = ((dot + totals[part][rows, :]) * scale).astype(jnp.bfloat16)
+            else:
+                sums[part][rows, :] += dot
+        if last:
             store(i).start()
-        else:
-            sums[part][local, :] = acc + totals[part][local, :]
         return carry
 
     for part in range(PARTS):
@@ -345,45 +373,41 @@
             store(i).wait()
 
 
-def numer_pass(where, base, pown, psib, blocks, pairs, phis, pix, model=None, total=None, last=False):
-    first = model is not None
+def numer_pass(where, base, pown, psib, blocks, pairs, phis, pix, total, den=None, last=False):
+    first = den is None
     pixels, count, columns = pown.shape[0], pairs[0].shape[0], pairs[0].shape[1]
     tm = min(512, pixels // PARTS)
     constrain = pltpu.with_memory_space_constraint
     args = [where, constrain(pown, pltpu.HBM), constrain(psib, pltpu.HBM), *pairs, *phis]
-    in_specs = [SMEM, HBM, HBM] + [VMEM] * (len(pairs) + 2)
-    scratch = [pltpu.VMEM((len(pairs) * count, columns), jnp.bfloat16)]
-    shape, aliases = [pltpu.VMEM((pixels // PARTS, columns), jnp.float32)] * PARTS, {}
-    shape.append(jax.ShapeDtypeStruct((1, columns), jnp.float32))
-    if first:
-        args.append(constrain(model, pltpu.HBM))
-        in_specs.append(HBM)
-        scratch += [pltpu.VMEM((3, tm, columns), jnp.bfloat16), pltpu.SemaphoreType.DMA((3,))]
-    else:
-        args += [total[-1], *(constrain(part, pltpu.VMEM) for part in total[:-1])]
-        in_specs += [VMEM] * (PARTS + 1)
-    if last:
-        shape = jax.ShapeDtypeStruct((pixels, columns), jnp.bfloat16)
-        scratch += [pltpu.VMEM((2, tm, columns), jnp.bfloat16), pltpu.SemaphoreType.DMA((2,))]
-    elif not first:
-        aliases = {len(args) - PARTS + part: part for part in range(PARTS)}
-    scratch += [
+    args += [] if first else [den]
+    args += [constrain(part, pltpu.VMEM) for part in total]
+    in_specs = [SMEM, HBM, HBM] + [VMEM] * (len(args) - 3)
+    scratch = [
+        pltpu.VMEM((len(pairs) * count, columns), jnp.bfloat16),
         pltpu.VMEM((3, tm, len(pairs) * count), jnp.bfloat16),
         pltpu.SemaphoreType.DMA((3, len(pairs))),
     ]
-    return pl.pallas_call(
+    if last:
+        shape, out_specs, aliases = jax.ShapeDtypeStruct((pixels, columns), jnp.bfloat16), HBM, {}
+        scratch = [pltpu.VMEM((2, tm, columns), jnp.bfloat16), pltpu.SemaphoreType.DMA((2,))] + scratch
+    else:
+        shape = [pltpu.VMEM(total[0].shape, jnp.float32)] * PARTS + [jax.ShapeDtypeStruct((1, columns), jnp.float32)]
+        out_specs = [VMEM] * (PARTS + 1)
+        aliases = {len(args) - PARTS + part: part for part in range(PARTS)}
+    result = pl.pallas_call(
         functools.partial(
-            pass_kernel, blocks=(blocks, pix), first=first, last=last, base=base, side=1, tm=tm
+            pass_kernel, blocks=blocks, pix=pix, first=first, last=last, base=base, tm=tm, sub=min(SUB if last else 512, tm)
         ),
         out_shape=shape,
         in_specs=in_specs,
-        out_specs=HBM if last else [VMEM] * (PARTS + 1),
+        out_specs=out_specs,
         scratch_shapes=scratch,
         input_output_aliases=aliases,
-        compiler_params=params(14 * MIB),
+        compiler_params=params(12 * MIB),
         cost_estimate=cost(2 * pixels * columns * count * len(pairs), 4 * pixels * columns),
         name="numer",
     )(*args)
+    return result if last else (result[:-1], result[-1])
 
 
 def numer_kernel(where, pown, psib, wown, wsib, fown, fsib, model, *refs, column, tm, sub):
@@ -515,7 +539,7 @@
         return after
 
     for c in range(chunks):
-        turns = ((False,) if c == 1 else ()) + ((True,) if c == later else ())
+        turns = ((True,) if c == 1 else ()) + ((False,) if c == later else ())
         send, keep, *rest = cross_chunk(
             where, phi, source, model, after, starts[c], widths[c], beta, c == 0, turns
         )
@@ -524,14 +548,14 @@
         for own, value in zip(turns, rest):
             turned[own] = value
         terms[c] = [keep, exchange(send, "pix", pix, 1)]
-        if c == 1:
+        if c == later:
             psib = exchange(turned[False], "pat", 2, 1)
         if c >= 1 and c < chunks:
             after = relay(c - 1, keep)
     after = relay(chunks - 1, keep)
     split = pix == 4 and count % 128 == 0
     if split:
-        token = phi
+        total, token = begin(where, model, after)
     else:
         token = psib = load(psib, after)
     held = [term for c in range(chunks) for term in terms[c]]
@@ -552,10 +576,11 @@
         own = [weights[0], exchange(weights[0], "pix", pix, 1), exchange(weights[0], "pix", pix, 2)]
         own.append(exchange(own[2], "pix", pix, 1))
         pairs = [(w, exchange(w, "pat", 2, 1)) for w in own]
+        fixed = (where, base, turned[True], psib)
         phis = (phi, phi_sib)
-        total = numer_pass(where, base, turned[True], psib, (0,), pairs[0], phis, pix, model=model)
-        total = numer_pass(where, base, turned[True], psib, (1,), pairs[1], phis, pix, total=total)
-        return numer_pass(where, base, turned[True], psib, (2, 3), pairs[2] + pairs[3], phis, pix, total=total, last=True)
+        total, den = numer_pass(*fixed, (0,), pairs[0], phis, pix, total)
+        total, den = numer_pass(*fixed, (1,), pairs[1], phis, pix, total, den)
+        return numer_pass(*fixed, (2, 3), pairs[2] + pairs[3], phis, pix, total, den, last=True)
 
     gathered = [[w] + [exchange(w, "pix", pix, d) for d in range(1, pix)] for w in weights]
     at, result, after = 0, None, model

time: 142 us -> 138 us (0.972)
  waiting for transfers between devices: 49.4 us -> 35.6 us
  Pallas kernels: 73.5 us -> 80.8 us
  starting transfers between devices: 14.5 us -> 16.4 us
    ppermute x16, waiting for transfers between devices: 49.4 us -> 35.6 us  [exchange(): return lax.ppermute(value, axis, [(i, i ^ distance) for i in range(size)])]
    pallas_call x3 -> x4, Pallas kernels: 40.6 us -> 44.7 us  [the longest x3 35.9 us: numer_pass(): pl.pallas_call(functools.partial(pass_kernel, blocks=blocks, pix=pix, fir...]
    pallas_call x3, Pallas kernels: 29.6 us -> 32.8 us  [cross_chunk(): pl.pallas_call(functools.partial(cross_kernel, column=column, tk=tk, step...]
    ppermute x16, starting transfers between devices: 14.5 us -> 16.4 us  [exchange(): return lax.ppermute(value, axis, [(i, i ^ distance) for i in range(size)])]
  transfers between devices with their start and end apart: 16 -> 16, of which waited for: 8 -> 8; matrix products, arithmetic and copies ran while one was open for 0% -> 0% of each run, Pallas kernels for 25% -> 28%
where the time goes in v6:
time: 138 us; the launch traced here: 137 us
  Pallas kernels  80.8 us (59%)
  waiting for transfers between devices  35.6 us (26%)
  starting transfers between devices  16.4 us (12%)
  local copies, waits for them, and re-layouts  3.5 us (3%)
    pallas_call x3, Pallas kernels, numer_pass(): pl.pallas_call(functools.partial(pass_kernel, blocks=blocks, pix=pix, fir...  35.9 us
    ppermute x16, waiting for transfers between devices, exchange(): return lax.ppermute(value, axis, [(i, i ^ distance) for i in range(size)])  35.6 us
    pallas_call x3, Pallas kernels, cross_chunk(): pl.pallas_call(functools.partial(cross_kernel, column=column, tk=tk, step...  32.8 us
    ppermute x16, starting transfers between devices, exchange(): return lax.ppermute(value, axis, [(i, i ^ distance) for i in range(size)])  16.4 us
    pallas_call x1, Pallas kernels, begin(): pl.pallas_call(functools.partial(begin_kernel, side=1, tm=tm), out_shape=...  8.81 us
    unnamed x6, local copies, waits for them, and re-layouts  3.26 us
  transfers between devices with their start and end apart: 16, of which 8 were waited for; matrix products, arithmetic and copies ran while one was open for 0% of the time, Pallas kernels for 28%

profile of v6, /device:TPU:0, one launch (start us, length us, event | category | flops | bytes accessed | tf_op | source)
XLA Modules:
  0.0 137.2 jit_solution(15015845857305255357)
XLA Ops:
  0.0 0.8 select_reduce_fusion
  0.8 0.1 copy.27.phi.after.refs_2_.refs_4_
  0.9 0.1 stack.38.where
  1.0 13.4 %cross.3 = (f32[256,512]{1,0:T(8,128)S(1)}, f32[256,512]{1,0:T(8,128)S(1)}, bf16[512,16384]{1,0:T(8,128)(2,1)S(1)}) custom-call(s32[12]{0:T(128)S(1)} %stack.38.where, f32[512,1]{1,0:T(8,128)S(1)} %copy.27.phi.after.refs_2_.refs_4_, bf16[512,16384]{1,0:T(8,128)(2,1)} %patterns.1, bf16[16384,1024]{1,0:T(8,128)(2,1)} %model.7, ...), custom_call_target="tpu_custom_call" | custom-call | flops 8589934592 | bytes 33554432 | tf_op jit(solution)/shard_map/cross/pallas_call | solution.py:108
  14.5 3.1 %collective-permute-start = (f32[256,512]{1,0:T(8,128)S(1)}, f32[256,512]{1,0:T(8,128)S(1)}, u32[]{:S(2)}, u32[]{:S(2)}) collective-permute-start(f32[256,512]{1,0:T(8,128)S(1)} %get-tuple-element.35), channel_id=1, source_target_pairs={{0,4},{4,0},{8,12},{12,8},{1,5},{5,1},{9,13},{13,9},{2,6},{6,2},{1... | collective-permute-start | bytes 1572872 | tf_op jit(solution)/shard_map/ppermute | solution.py:492
  17.6 8.1 %cross.4 = (f32[256,256]{1,0:T(8,128)S(1)}, f32[256,256]{1,0:T(8,128)S(1)}, bf16[8192,512]{1,0:T(8,128)(2,1)S(1)}) custom-call(s32[12]{0:T(128)S(1)} %stack.38.where, f32[512,1]{1,0:T(8,128)S(1)} %copy.27.phi.after.refs_2_.refs_4_, bf16[512,16384]{1,0:T(8,128)(2,1)S(1)} %get-tuple-element.31.patterns, bf16[16384,1024]{1,0:T(8,128)(2,1)} %model.7, ...), custom_call_target="tpu_custom_call" | custom-call | flops 4294967296 | bytes 25165824 | tf_op jit(solution)/shard_map/cross/pallas_call | solution.py:108
  25.7 0.0 copy-start
  25.7 3.2 %copy-done = bf16[8192,512]{1,0:T(8,128)(2,1)} copy-done((bf16[8192,512]{1,0:T(8,128)(2,1)}, bf16[8192,512]{1,0:T(8,128)(2,1)S(1)}, u32[]{:S(2)}) %copy-start) | copy-done | bytes 8388632
  28.9 0.6 collective-permute-done.refs_1_
  29.5 0.6 forward.3.after
  30.1 11.3 %cross.5 = (f32[256,256]{1,0:T(8,128)S(1)}, f32[256,256]{1,0:T(8,128)S(1)}, bf16[8192,512]{1,0:T(8,128)(2,1)}) custom-call(s32[12]{0:T(128)S(1)} %stack.38.where, f32[512,1]{1,0:T(8,128)S(1)} %copy.27.phi.after.refs_2_.refs_4_, bf16[512,16384]{1,0:T(8,128)(2,1)S(1)} %get-tuple-element.31.patterns, bf16[16384,1024]{1,0:T(8,128)(2,1)} %model.7, ...), custom_call_target="tpu_custom_call" | custom-call | flops 4294967296 | bytes 25165824 | tf_op jit(solution)/shard_map/cross/pallas_call | solution.py:108
  41.4 0.1 collective-permute-start.1
  41.5 1.8 %collective-permute-start.4 = (f32[256,256]{1,0:T(8,128)S(1)}, f32[256,256]{1,0:T(8,128)S(1)}, u32[]{:S(2)}, u32[]{:S(2)}) collective-permute-start(f32[256,256]{1,0:T(8,128)S(1)} %get-tuple-element.40), channel_id=1, source_target_pairs={{0,4},{4,0},{8,12},{12,8},{1,5},{5,1},{9,13},{13,9},{2,6},{6,2},{1... | collective-permute-start | bytes 786440 | tf_op jit(solution)/shard_map/ppermute | solution.py:492
  43.3 0.3 collective-permute-start.2
  43.6 2.8 %collective-permute-start.3 = (f32[128,512]{1,0:T(8,128)S(1)}, f32[128,512]{1,0:T(8,128)S(1)}, u32[]{:S(2)}, u32[]{:S(2)}) collective-permute-start(f32[128,512]{1,0:T(8,128)S(1)} %forward.3.after), channel_id=1, source_target_pairs={{0,8},{4,12},{8,0},{12,4},{1,9},{5,13},{9,1},{13,5},{2,10},{6,14},... | collective-permute-start | bytes 786440 | tf_op jit(solution)/shard_map/ppermute | solution.py:492
  46.3 10.0 %collective-permute-done.4.refs_1_.refs_4_ = f32[256,256]{1,0:T(8,128)S(1)} collective-permute-done((f32[256,256]{1,0:T(8,128)S(1)}, f32[256,256]{1,0:T(8,128)S(1)}, u32[]{:S(2)}, u32[]{:S(2)}) %collective-permute-start.4) | collective-permute-done | bytes 262176 | tf_op jit(solution)/shard_map/ppermute | solution.py:492
  56.4 0.6 forward.5
  56.9 1.9 %collective-permute-start.5 = (f32[128,256]{1,0:T(8,128)S(1)}, f32[128,256]{1,0:T(8,128)S(1)}, u32[]{:S(2)}, u32[]{:S(2)}) collective-permute-start(f32[128,256]{1,0:T(8,128)S(1)} %forward.5), channel_id=1, source_target_pairs={{0,8},{4,12},{8,0},{12,4},{1,9},{5,13},{9,1},{13,5},{2,10},{6,14},... | collective-permute-start | bytes 393224 | tf_op jit(solution)/shard_map/ppermute | solution.py:492
  58.8 2.7 %collective-permute-done.2.refs_1_.refs_7_ = f32[256,256]{1,0:T(8,128)S(1)} collective-permute-done((f32[256,256]{1,0:T(8,128)S(1)}, f32[256,256]{1,0:T(8,128)S(1)}, u32[]{:S(2)}, u32[]{:S(2)}) %collective-permute-start.2) | collective-permute-done | bytes 262176 | tf_op jit(solution)/shard_map/ppermute | solution.py:492
  61.5 0.6 forward.4.after
  62.1 0.0 copy-start.1
  62.1 0.0 copy-start.2
  62.1 1.9 %collective-permute-start.6 = (f32[128,256]{1,0:T(8,128)S(1)}, f32[128,256]{1,0:T(8,128)S(1)}, u32[]{:S(2)}, u32[]{:S(2)}) collective-permute-start(f32[128,256]{1,0:T(8,128)S(1)} %forward.4.after), channel_id=1, source_target_pairs={{0,8},{4,12},{8,0},{12,4},{1,9},{5,13},{9,1},{13,5},{2,10},{6,14},... | collective-permute-start | bytes 393224 | tf_op jit(solution)/shard_map/ppermute | solution.py:492
  64.0 8.8 %begin.1 = (f32[2048,1024]{1,0:T(8,128)S(1)}, f32[2048,1024]{1,0:T(8,128)S(1)}, f32[2048,1024]{1,0:T(8,128)S(1)}, f32[2048,1024]{1,0:T(8,128)S(1)}, f32[8,128]{1,0:T(8,128)S(1)}) custom-call(s32[12]{0:T(128)S(1)} %stack.38.where, bf16[16384,1024]{1,0:T(8,128)(2,1)} %model.7, f32[128,256]{1,0:T(8,128)S(1)} %forward.4.after), custom_call_target="tpu_custom_call" | custom-call | tf_op jit(solution)/shard_map/begin/pallas_call | solution.py:293
  72.9 0.0 collective-permute-done.5.refs_5_
  72.9 0.0 collective-permute-done.3.refs_2_
  72.9 2.0 %collective-permute-done.6.refs_8_ = f32[128,256]{1,0:T(8,128)S(1)} collective-permute-done((f32[128,256]{1,0:T(8,128)S(1)}, f32[128,256]{1,0:T(8,128)S(1)}, u32[]{:S(2)}, u32[]{:S(2)}) %collective-permute-start.6) | collective-permute-done | bytes 131104 | tf_op jit(solution)/shard_map/ppermute | solution.py:492
  74.9 0.0 copy-done.1
  74.9 0.0 copy-done.2
  74.9 0.8 softmax.1
  75.7 1.5 %collective-permute-start.7 = (f32[16,128]{1,0:T(8,128)S(1)}, f32[16,128]{1,0:T(8,128)S(1)}, u32[]{:S(2)}, u32[]{:S(2)}) collective-permute-start(f32[16,128]{1,0:T(8,128)S(1)} %get-tuple-element.42.own.mine), channel_id=1, source_target_pairs={{0,2},{2,0},{1,3},{3,1},{4,6},{6,4},{5,7},{7,5},{8,10},{10,8},{9,1... | collective-permute-start | bytes 24584 | tf_op jit(solution)/shard_map/ppermute | solution.py:492
  77.2 2.2 %collective-permute-done.7.other = f32[16,128]{1,0:T(8,128)S(1)} collective-permute-done((f32[16,128]{1,0:T(8,128)S(1)}, f32[16,128]{1,0:T(8,128)S(1)}, u32[]{:S(2)}, u32[]{:S(2)}) %collective-permute-start.7) | collective-permute-done | bytes 8224 | tf_op jit(solution)/shard_map/ppermute | solution.py:492
  79.4 0.7 weights.1.refs_0_
  80.1 0.1 collective-permute-start.8
  80.2 1.9 %collective-permute-start.13 = (bf16[128,1024]{1,0:T(8,128)(2,1)S(1)}, bf16[128,1024]{1,0:T(8,128)(2,1)S(1)}, u32[]{:S(2)}, u32[]{:S(2)}) collective-permute-start(bf16[128,1024]{1,0:T(8,128)(2,1)S(1)} %weights.1.refs_0_), channel_id=1, source_target_pairs={{0,4},{4,0},{8,12},{12,8},{1,5},{5,1},{9,13},{13,9},{2,6},{6,2},{1... | collective-permute-start | bytes 786440 | tf_op jit(solution)/shard_map/ppermute | solution.py:492
  82.1 10.9 %collective-permute-done.8.refs_0_ = bf16[128,1024]{1,0:T(8,128)(2,1)S(1)} collective-permute-done((bf16[128,1024]{1,0:T(8,128)(2,1)S(1)}, bf16[128,1024]{1,0:T(8,128)(2,1)S(1)}, u32[]{:S(2)}, u32[]{:S(2)}) %collective-permute-start.8) | collective-permute-done | bytes 262176 | tf_op jit(solution)/shard_map/ppermute | solution.py:492
  93.0 0.0 collective-permute-start.10
  93.0 0.0 collective-permute-start.15
  93.0 0.5 collective-permute-start.12
  93.5 1.4 %collective-permute-done.12.refs_3_.refs_5_ = f32[512,1]{1,0:T(8,128)S(1)} collective-permute-done((f32[512,1]{1,0:T(8,128)S(1)}, f32[512,1]{1,0:T(8,128)S(1)}, u32[]{:S(2)}, u32[]{:S(2)}) %collective-permute-start.12) | collective-permute-done | bytes 2080 | tf_op jit(solution)/shard_map/ppermute | solution.py:492
  94.9 0.1 collective-permute-start.9
  95.1 0.0 collective-permute-done.13.refs_0_
  95.1 0.4 collective-permute-start.14
  95.4 5.8 %collective-permute-done.10.refs_2_ = bf16[128,1024]{1,0:T(8,128)(2,1)S(1)} collective-permute-done((bf16[128,1024]{1,0:T(8,128)(2,1)S(1)}, bf16[128,1024]{1,0:T(8,128)(2,1)S(1)}, u32[]{:S(2)}, u32[]{:S(2)}) %collective-permute-start.10) | collective-permute-done | bytes 262176 | tf_op jit(solution)/shard_map/ppermute | solution.py:492
  101.2 0.0 collective-permute-start.11
  101.3 0.0 collective-permute-done.15.refs_1_
  101.3 0.0 collective-permute-done.1.psib
  101.3 9.7 %numer.3 = (f32[2048,1024]{1,0:T(8,128)S(1)}, f32[2048,1024]{1,0:T(8,128)S(1)}, f32[2048,1024]{1,0:T(8,128)S(1)}, f32[2048,1024]{1,0:T(8,128)S(1)}, f32[1,1024]{1,0:T(1,128)S(1)}) custom-call(s32[12]{0:T(128)S(1)} %stack.38.where, bf16[8192,512]{1,0:T(8,128)(2,1)} %copy-done, ...), custom_call_target="tpu_custom_call", output_to_operand_aliasing={{0}: (7, {}), {1}: (8, {}), {2}: (9, {}), {3}: (10, {})} | custom-call | flops 4294967296 | bytes 33554432 | tf_op jit(solution)/shard_map/numer/pallas_call | solution.py:397
  111.0 0.0 collective-permute-done.14.refs_1_
  111.0 9.7 %numer.4 = (f32[2048,1024]{1,0:T(8,128)S(1)}, f32[2048,1024]{1,0:T(8,128)S(1)}, f32[2048,1024]{1,0:T(8,128)S(1)}, f32[2048,1024]{1,0:T(8,128)S(1)}, f32[1,1024]{1,0:T(1,128)S(1)}) custom-call(s32[12]{0:T(128)S(1)} %stack.38.where, bf16[8192,512]{1,0:T(8,128)(2,1)} %copy-done, ...), custom_call_target="tpu_custom_call", output_to_operand_aliasing={{0}: (8, {}), {1}: (9, {}), {2}: (10, {}), {3}: (11, {})} | custom-call | flops 4294967296 | bytes 33554432 | tf_op jit(solution)/shard_map/numer/pallas_call | solution.py:397
  120.7 0.0 collective-permute-done.9.refs_1_
  120.7 0.0 collective-permute-done.11.refs_3_
  120.7 16.5 %numer.5 = bf16[8192,1024]{1,0:T(8,128)(2,1)} custom-call(s32[12]{0:T(128)S(1)} %stack.38.where, bf16[8192,512]{1,0:T(8,128)(2,1)} %copy-done, bf16[8192,512]{1,0:T(8,128)(2,1)} %collective-permute-done.1.psib, bf16[128,1024]{1,0:T(8,128)(2,1)S(1)} %collective-permute-done.8.refs_0_, bf16[128,1024]{1,0:T(8,128)(2,1)S(1)} %collective-permute-done.9.refs_1_, ...), custom_call_target="tpu_custom_call" | custom-call | flops 8589934592 | bytes 33554432 | tf_op jit(solution)/shard_map/numer/pallas_call | solution.py:397
Async XLA Ops:
  14.5 15.0 %collective-permute-start = (f32[256,512]{1,0:T(8,128)S(1)}, f32[256,512]{1,0:T(8,128)S(1)}, u32[]{:S(2)}, u32[]{:S(2)}) collective-permute-start(f32[256,512]{1,0:T(8,128)S(1)} %get-tuple-element.35), channel_id=1, source_target_pairs={{0,4},{4,0},{8,12},{12,8},{1,5},{5,1},{9,13},{13,9},{2,6},{6,2},{1... | collective-permute-start | bytes 1572872 | tf_op jit(solution)/shard_map/ppermute | solution.py:492
  25.7 3.3 %copy-start = (bf16[8192,512]{1,0:T(8,128)(2,1)}, bf16[8192,512]{1,0:T(8,128)(2,1)S(1)}, u32[]{:S(2)}) copy-start(bf16[8192,512]{1,0:T(8,128)(2,1)S(1)} %get-tuple-element.32.pown) | copy-start | bytes 25165828
  41.4 59.8 %collective-permute-start.1 = (bf16[8192,512]{1,0:T(8,128)(2,1)}, bf16[8192,512]{1,0:T(8,128)(2,1)}, u32[]{:S(2)}, u32[]{:S(2)}) collective-permute-start(bf16[8192,512]{1,0:T(8,128)(2,1)} %get-tuple-element.36), channel_id=1, source_target_pairs={{0,1},{1,0},{2,3},{3,2},{4,5},{5,4},{6,7},{7,6},{8,9},{9,8},{10,11... | collective-permute-start | bytes 25165832 | tf_op jit(solution)/shard_map/ppermute | solution.py:492
  41.5 14.9 %collective-permute-start.4 = (f32[256,256]{1,0:T(8,128)S(1)}, f32[256,256]{1,0:T(8,128)S(1)}, u32[]{:S(2)}, u32[]{:S(2)}) collective-permute-start(f32[256,256]{1,0:T(8,128)S(1)} %get-tuple-element.40), channel_id=1, source_target_pairs={{0,4},{4,0},{8,12},{12,8},{1,5},{5,1},{9,13},{13,9},{2,6},{6,2},{1... | collective-permute-start | bytes 786440 | tf_op jit(solution)/shard_map/ppermute | solution.py:492
  43.3 18.2 %collective-permute-start.2 = (f32[256,256]{1,0:T(8,128)S(1)}, f32[256,256]{1,0:T(8,128)S(1)}, u32[]{:S(2)}, u32[]{:S(2)}) collective-permute-start(f32[256,256]{1,0:T(8,128)S(1)} %get-tuple-element.38), channel_id=1, source_target_pairs={{0,4},{4,0},{8,12},{12,8},{1,5},{5,1},{9,13},{13,9},{2,6},{6,2},{1... | collective-permute-start | bytes 786440 | tf_op jit(solution)/shard_map/ppermute | solution.py:492
  43.6 29.3 %collective-permute-start.3 = (f32[128,512]{1,0:T(8,128)S(1)}, f32[128,512]{1,0:T(8,128)S(1)}, u32[]{:S(2)}, u32[]{:S(2)}) collective-permute-start(f32[128,512]{1,0:T(8,128)S(1)} %forward.3.after), channel_id=1, source_target_pairs={{0,8},{4,12},{8,0},{12,4},{1,9},{5,13},{9,1},{13,5},{2,10},{6,14},... | collective-permute-start | bytes 786440 | tf_op jit(solution)/shard_map/ppermute | solution.py:492
  56.9 15.9 %collective-permute-start.5 = (f32[128,256]{1,0:T(8,128)S(1)}, f32[128,256]{1,0:T(8,128)S(1)}, u32[]{:S(2)}, u32[]{:S(2)}) collective-permute-start(f32[128,256]{1,0:T(8,128)S(1)} %forward.5), channel_id=1, source_target_pairs={{0,8},{4,12},{8,0},{12,4},{1,9},{5,13},{9,1},{13,5},{2,10},{6,14},... | collective-permute-start | bytes 393224 | tf_op jit(solution)/shard_map/ppermute | solution.py:492
  62.1 12.8 %copy-start.1 = (s32[1024]{0:T(1024)S(1)}, s32[1024]{0:T(1024)}, u32[]{:S(2)}) copy-start(s32[1024]{0:T(1024)} %param.11) | copy-start | bytes 12292
  62.1 12.8 %copy-start.2 = (f32[8]{0:T(128)S(1)}, f32[8]{0:T(128)}, u32[]{:S(2)}) copy-start(f32[8]{0:T(128)} %table.1) | copy-start | bytes 100
  62.1 12.7 %collective-permute-start.6 = (f32[128,256]{1,0:T(8,128)S(1)}, f32[128,256]{1,0:T(8,128)S(1)}, u32[]{:S(2)}, u32[]{:S(2)}) collective-permute-start(f32[128,256]{1,0:T(8,128)S(1)} %forward.4.after), channel_id=1, source_target_pairs={{0,8},{4,12},{8,0},{12,4},{1,9},{5,13},{9,1},{13,5},{2,10},{6,14},... | collective-permute-start | bytes 393224 | tf_op jit(solution)/shard_map/ppermute | solution.py:492
  75.7 3.7 %collective-permute-start.7 = (f32[16,128]{1,0:T(8,128)S(1)}, f32[16,128]{1,0:T(8,128)S(1)}, u32[]{:S(2)}, u32[]{:S(2)}) collective-permute-start(f32[16,128]{1,0:T(8,128)S(1)} %get-tuple-element.42.own.mine), channel_id=1, source_target_pairs={{0,2},{2,0},{1,3},{3,1},{4,6},{6,4},{5,7},{7,5},{8,10},{10,8},{9,1... | collective-permute-start | bytes 24584 | tf_op jit(solution)/shard_map/ppermute | solution.py:492
  80.1 12.9 %collective-permute-start.8 = (bf16[128,1024]{1,0:T(8,128)(2,1)S(1)}, bf16[128,1024]{1,0:T(8,128)(2,1)S(1)}, u32[]{:S(2)}, u32[]{:S(2)}) collective-permute-start(bf16[128,1024]{1,0:T(8,128)(2,1)S(1)} %weights.1.refs_0_), channel_id=1, source_target_pairs={{0,8},{4,12},{8,0},{12,4},{1,9},{5,13},{9,1},{13,5},{2,10},{6,14},... | collective-permute-start | bytes 786440 | tf_op jit(solution)/shard_map/ppermute | solution.py:492
  80.2 14.9 %collective-permute-start.13 = (bf16[128,1024]{1,0:T(8,128)(2,1)S(1)}, bf16[128,1024]{1,0:T(8,128)(2,1)S(1)}, u32[]{:S(2)}, u32[]{:S(2)}) collective-permute-start(bf16[128,1024]{1,0:T(8,128)(2,1)S(1)} %weights.1.refs_0_), channel_id=1, source_target_pairs={{0,4},{4,0},{8,12},{12,8},{1,5},{5,1},{9,13},{13,9},{2,6},{6,2},{1... | collective-permute-start | bytes 786440 | tf_op jit(solution)/shard_map/ppermute | solution.py:492
  93.0 8.2 %collective-permute-start.10 = (bf16[128,1024]{1,0:T(8,128)(2,1)S(1)}, bf16[128,1024]{1,0:T(8,128)(2,1)S(1)}, u32[]{:S(2)}, u32[]{:S(2)}) collective-permute-start(bf16[128,1024]{1,0:T(8,128)(2,1)S(1)} %collective-permute-done.8.refs_0_), channel_id=1, source_target_pairs={{0,4},{4,0},{8,12},{12,8},{1,5},{5,1},{9,13},{13,9},{2,6},{6,2},{1... | collective-permute-start | bytes 786440 | tf_op jit(solution)/shard_map/ppermute | solution.py:492
  93.0 8.2 %collective-permute-start.15 = (bf16[128,1024]{1,0:T(8,128)(2,1)S(1)}, bf16[128,1024]{1,0:T(8,128)(2,1)S(1)}, u32[]{:S(2)}, u32[]{:S(2)}) collective-permute-start(bf16[128,1024]{1,0:T(8,128)(2,1)S(1)} %weights.1.refs_0_), channel_id=1, source_target_pairs={{0,1},{1,0},{2,3},{3,2},{4,5},{5,4},{6,7},{7,6},{8,9},{9,8},{10,11... | collective-permute-start | bytes 786440 | tf_op jit(solution)/shard_map/ppermute | solution.py:492
  93.0 1.9 %collective-permute-start.12 = (f32[512,1]{1,0:T(8,128)S(1)}, f32[512,1]{1,0:T(8,128)S(1)}, u32[]{:S(2)}, u32[]{:S(2)}) collective-permute-start(f32[512,1]{1,0:T(8,128)S(1)} %copy.27.phi.after.refs_2_.refs_4_), channel_id=1, source_target_pairs={{0,1},{1,0},{2,3},{3,2},{4,5},{5,4},{6,7},{7,6},{8,9},{9,8},{10,11... | collective-permute-start | bytes 6152 | tf_op jit(solution)/shard_map/ppermute | solution.py:492
  94.9 25.7 %collective-permute-start.9 = (bf16[128,1024]{1,0:T(8,128)(2,1)S(1)}, bf16[128,1024]{1,0:T(8,128)(2,1)S(1)}, u32[]{:S(2)}, u32[]{:S(2)}) collective-permute-start(bf16[128,1024]{1,0:T(8,128)(2,1)S(1)} %collective-permute-done.8.refs_0_), channel_id=1, source_target_pairs={{0,1},{1,0},{2,3},{3,2},{4,5},{5,4},{6,7},{7,6},{8,9},{9,8},{10,11... | collective-permute-start | bytes 786440 | tf_op jit(solution)/shard_map/ppermute | solution.py:492
  95.1 15.9 %collective-permute-start.14 = (bf16[128,1024]{1,0:T(8,128)(2,1)S(1)}, bf16[128,1024]{1,0:T(8,128)(2,1)S(1)}, u32[]{:S(2)}, u32[]{:S(2)}) collective-permute-start(bf16[128,1024]{1,0:T(8,128)(2,1)S(1)} %collective-permute-done.13.refs_0_), channel_id=1, source_target_pairs={{0,1},{1,0},{2,3},{3,2},{4,5},{5,4},{6,7},{7,6},{8,9},{9,8},{10,11... | collective-permute-start | bytes 786440 | tf_op jit(solution)/shard_map/ppermute | solution.py:492
  101.2 19.4 %collective-permute-start.11 = (bf16[128,1024]{1,0:T(8,128)(2,1)S(1)}, bf16[128,1024]{1,0:T(8,128)(2,1)S(1)}, u32[]{:S(2)}, u32[]{:S(2)}) collective-permute-start(bf16[128,1024]{1,0:T(8,128)(2,1)S(1)} %collective-permute-done.10.refs_2_), channel_id=1, source_target_pairs={{0,1},{1,0},{2,3},{3,2},{4,5},{5,4},{6,7},{7,6},{8,9},{9,8},{10,11... | collective-permute-start | bytes 786440 | tf_op jit(solution)/shard_map/ppermute | solution.py:492

commit v7 on v6

--- a/solution.py
+++ b/solution.py
@@ -37,6 +37,8 @@
 
 def cross_kernel(where, phi, patterns, model, after, send, keep, *refs, column, tk, steps, beta, first, turns):
     turned, refs = refs[: len(turns)], refs[len(turns) :]
+    if turns:
+        *refs, tbuf, tsem = refs
     if first:
         held, mbuf, acc, squares, msem, psem = refs
     else:
@@ -51,6 +53,13 @@
             both.append(pltpu.make_async_copy(patterns.at[:, pl.ds(at, tk)], held.at[:, pl.ds(at, tk)], psem.at[slot]))
         return both
 
+    def stores(i):
+        slot = lax.rem(i, 2)
+        for t, out in enumerate(turned):
+            width = out.shape[0] // steps
+            rows = pl.ds(pl.multiple_of(i * width, width), width)
+            yield pltpu.make_async_copy(tbuf.at[t, slot], out.at[rows], tsem.at[t, slot])
+
     for i in range(min(SLOTS - 1, steps)):
         for copy in copies(i):
             copy.start()
@@ -66,17 +75,26 @@
             for copy in copies(i + SLOTS - 1):
                 copy.start()
 
+        if turns:
+
+            @pl.when(i >= 2)
+            def _():
+                for copy in stores(i - 2):
+                    copy.wait()
+
         tile = mbuf[lax.rem(i, SLOTS)]
         part = held[:, pl.ds(pl.multiple_of(i * tk, tk), tk)]
         acc[...] += jnp.dot(part, tile, preferred_element_type=jnp.float32)
         wide = tile.astype(jnp.float32)
         squares[...] += jnp.sum((wide * wide).reshape(tk // 8, 8, tn), axis=0)
-        for own, out in zip(turns, turned):
+        for t, (own, out) in enumerate(zip(turns, turned)):
             pixels = out.shape[0]
             width = pixels // steps
             side = where[1] if own else 1 - where[1]
             piece = held[:, pl.ds(pl.multiple_of(side * pixels + i * width, width), width)]
-            out[pl.ds(pl.multiple_of(i * width, width), width), :] = piece.T
+            tbuf[t, lax.rem(i, 2)] = piece.T
+        for copy in stores(i):
+            copy.start()
         return carry
 
     lax.fori_loop(0, steps, body, 0)
@@ -86,6 +104,9 @@
     half = send.shape[0]
     send[...] = acc[pl.ds(pl.multiple_of((1 - where[0]) * half, half), half), :]
     keep[...] = acc[pl.ds(pl.multiple_of(where[0] * half, half), half), :]
+    for i in range(max(0, steps - 2), steps):
+        for copy in stores(i):
+            copy.wait()
 
 
 def cross_chunk(where, phi, patterns, model, after, column, tn, beta, first, turns):
@@ -93,7 +114,8 @@
     tk = min(2048, depth)
     half = rows // 2
     shapes = [jax.ShapeDtypeStruct((half, tn), jnp.float32)] * 2
-    shapes += [pltpu.VMEM((depth // 2, rows), patterns.dtype)] * len(turns)
+    shapes += [pltpu.HBM((depth // 2, rows), patterns.dtype)] * len(turns)
+    places = [VMEM, VMEM] + [HBM] * len(turns)
     scratch = [
         pltpu.VMEM((SLOTS, tk, tn), jnp.bfloat16),
         pltpu.VMEM((rows, tn), jnp.float32),
@@ -103,6 +125,10 @@
     if first:
         shapes.append(pltpu.VMEM(patterns.shape, patterns.dtype))
         scratch.append(pltpu.SemaphoreType.DMA((SLOTS,)))
+        places.append(VMEM)
+    if turns:
+        scratch.append(pltpu.VMEM((len(turns), 2, tk // 2, rows), patterns.dtype))
+        scratch.append(pltpu.SemaphoreType.DMA((len(turns), 2)))
     patterns = pltpu.with_memory_space_constraint(patterns, pltpu.HBM if first else pltpu.VMEM)
     model = pltpu.with_memory_space_constraint(model, pltpu.HBM)
     return pl.pallas_call(
@@ -111,7 +137,7 @@
         ),
         out_shape=shapes,
         in_specs=[SMEM, VMEM, HBM if first else VMEM, HBM, ANY],
-        out_specs=[VMEM] * len(shapes),
+        out_specs=places,
         scratch_shapes=scratch,
         compiler_params=params(20 * MIB),
         cost_estimate=cost(2 * rows * depth * tn, 2 * depth * (rows + tn)),
@@ -258,15 +284,15 @@
     )(pltpu.with_memory_space_constraint(source, pltpu.HBM), after)
 
 
-def begin_kernel(where, model, after, *refs, side, tm):
+def begin_kernel(where, model, after, *refs, side, tm, start):
     *sums, token, buf, sem = refs
     token[...] = jnp.zeros_like(token)
     size = sums[0].shape[0]
-    steps = size * PARTS // tm
+    steps = size * len(sums) // tm
 
     def fetch(i):
         slot = lax.rem(i, 4)
-        at = pl.multiple_of(where[side] * size * PARTS + i * tm, tm)
+        at = pl.multiple_of((where[side] * PARTS + start) * size + i * tm, tm)
         return pltpu.make_async_copy(model.at[pl.ds(at, tm)], buf.at[slot], sem.at[slot])
 
     for i in range(min(3, steps)):
@@ -283,19 +309,20 @@
         sums[part][rows, :] = prior_weight * buf[lax.rem(i, 4)].astype(jnp.float32)
         return carry
 
-    for part in range(PARTS):
-        lax.fori_loop(part * steps // PARTS, (part + 1) * steps // PARTS, functools.partial(body, part), 0)
-
-
-def begin(where, model, after):
+    n = len(sums)
+    for part in range(n):
+        lax.fori_loop(part * steps // n, (part + 1) * steps // n, functools.partial(body, part), 0)
+
+
+def begin(where, model, after, start, stop):
     pixels, columns = model.shape[0] // 2, model.shape[1]
     tm = min(512, pixels // PARTS)
     *total, token = pl.pallas_call(
-        functools.partial(begin_kernel, side=1, tm=tm),
-        out_shape=[pltpu.VMEM((pixels // PARTS, columns), jnp.float32)] * PARTS
+        functools.partial(begin_kernel, side=1, tm=tm, start=start),
+        out_shape=[pltpu.VMEM((pixels // PARTS, columns), jnp.float32)] * (stop - start)
         + [jax.ShapeDtypeStruct((8, 128), jnp.float32)],
         in_specs=[SMEM, HBM, ANY],
-        out_specs=[VMEM] * (PARTS + 1),
+        out_specs=[VMEM] * (stop - start + 1),
         scratch_shapes=[pltpu.VMEM((4, tm, columns), jnp.bfloat16), pltpu.SemaphoreType.DMA((4,))],
         compiler_params=params(10 * MIB),
         name="begin",
@@ -552,10 +579,14 @@
             psib = exchange(turned[False], "pat", 2, 1)
         if c >= 1 and c < chunks:
             after = relay(c - 1, keep)
-    after = relay(chunks - 1, keep)
     split = pix == 4 and count % 128 == 0
+    ready = keep
     if split:
-        total, token = begin(where, model, after)
+        total, ready = begin(where, model, after, 0, PARTS // 2)
+    after = relay(chunks - 1, ready)
+    if split:
+        more, token = begin(where, model, after, PARTS // 2, PARTS)
+        total = total + more
     else:
         token = psib = load(psib, after)
     held = [term for c in range(chunks) for term in terms[c]]

time: 138 us -> 135 us (0.978)
  local copies, waits for them, and re-layouts: 3.5 us -> 0.25 us
    unnamed x6 -> x4, local copies, waits for them, and re-layouts: 3.26 us -> 0.01 us
    pallas_call x1 -> x2, Pallas kernels: 8.81 us -> 9.94 us  [begin(): pl.pallas_call(functools.partial(begin_kernel, side=1, tm=tm, start=start...]
  transfers between devices with their start and end apart: 16 -> 16, of which waited for: 8 -> 8; matrix products, arithmetic and copies ran while one was open for 0% -> 0% of each run, Pallas kernels for 28% -> 31%
where the time goes in v7:
time: 135 us; the launch traced here: 134 us
  Pallas kernels  80.5 us (60%)
  waiting for transfers between devices  36.9 us (27%)
  starting transfers between devices  15.7 us (12%)
    ppermute x16, waiting for transfers between devices, exchange(): return lax.ppermute(value, axis, [(i, i ^ distance) for i in range(size)])  36.9 us
    pallas_call x3, Pallas kernels, numer_pass(): pl.pallas_call(functools.partial(pass_kernel, blocks=blocks, pix=pix, fir...  35.8 us
    pallas_call x3, Pallas kernels, cross_chunk(): pl.pallas_call(functools.partial(cross_kernel, column=column, tk=tk, step...  31.5 us
    ppermute x16, starting transfers between devices, exchange(): return lax.ppermute(value, axis, [(i, i ^ distance) for i in range(size)])  15.7 us
    pallas_call x2, Pallas kernels, begin(): pl.pallas_call(functools.partial(begin_kernel, side=1, tm=tm, start=start...  9.94 us
  transfers between devices with their start and end apart: 16, of which 8 were waited for; matrix products, arithmetic and copies ran while one was open for 0% of the time, Pallas kernels for 31%

profile of v7, /device:TPU:0, one launch (start us, length us, event | category | flops | bytes accessed | tf_op | source)
XLA Modules:
  0.0 134.3 jit_solution(7600527081986487103)
XLA Ops:
  0.0 0.8 select_reduce_fusion
  0.8 0.1 copy.27.phi.after.refs_2_.refs_4_
  0.9 0.1 stack.38.where
  1.0 13.4 %cross.3 = (f32[256,512]{1,0:T(8,128)S(1)}, f32[256,512]{1,0:T(8,128)S(1)}, bf16[512,16384]{1,0:T(8,128)(2,1)S(1)}) custom-call(s32[12]{0:T(128)S(1)} %stack.38.where, f32[512,1]{1,0:T(8,128)S(1)} %copy.27.phi.after.refs_2_.refs_4_, bf16[512,16384]{1,0:T(8,128)(2,1)} %patterns.1, bf16[16384,1024]{1,0:T(8,128)(2,1)} %model.9, ...), custom_call_target="tpu_custom_call" | custom-call | flops 8589934592 | bytes 33554432 | tf_op jit(solution)/shard_map/cross/pallas_call | solution.py:134
  14.5 3.1 %collective-permute-start = (f32[256,512]{1,0:T(8,128)S(1)}, f32[256,512]{1,0:T(8,128)S(1)}, u32[]{:S(2)}, u32[]{:S(2)}) collective-permute-start(f32[256,512]{1,0:T(8,128)S(1)} %get-tuple-element.36), channel_id=1, source_target_pairs={{0,4},{4,0},{8,12},{12,8},{1,5},{5,1},{9,13},{13,9},{2,6},{6,2},{1... | collective-permute-start | bytes 1572872 | tf_op jit(solution)/shard_map/ppermute | solution.py:519
  17.6 9.1 %cross.4 = (f32[256,256]{1,0:T(8,128)S(1)}, f32[256,256]{1,0:T(8,128)S(1)}, bf16[8192,512]{1,0:T(8,128)(2,1)}) custom-call(s32[12]{0:T(128)S(1)} %stack.38.where, f32[512,1]{1,0:T(8,128)S(1)} %copy.27.phi.after.refs_2_.refs_4_, bf16[512,16384]{1,0:T(8,128)(2,1)S(1)} %get-tuple-element.32.patterns, bf16[16384,1024]{1,0:T(8,128)(2,1)} %model.9, ...), custom_call_target="tpu_custom_call" | custom-call | flops 4294967296 | bytes 25165824 | tf_op jit(solution)/shard_map/cross/pallas_call | solution.py:134
  26.7 2.8 %collective-permute-done.refs_1_ = f32[256,512]{1,0:T(8,128)S(1)} collective-permute-done((f32[256,512]{1,0:T(8,128)S(1)}, f32[256,512]{1,0:T(8,128)S(1)}, u32[]{:S(2)}, u32[]{:S(2)}) %collective-permute-start) | collective-permute-done | bytes 524320 | tf_op jit(solution)/shard_map/ppermute | solution.py:519
  29.5 0.6 forward.3.after
  30.1 8.9 %cross.5 = (f32[256,256]{1,0:T(8,128)S(1)}, f32[256,256]{1,0:T(8,128)S(1)}, bf16[8192,512]{1,0:T(8,128)(2,1)}) custom-call(s32[12]{0:T(128)S(1)} %stack.38.where, f32[512,1]{1,0:T(8,128)S(1)} %copy.27.phi.after.refs_2_.refs_4_, bf16[512,16384]{1,0:T(8,128)(2,1)S(1)} %get-tuple-element.32.patterns, bf16[16384,1024]{1,0:T(8,128)(2,1)} %model.9, ...), custom_call_target="tpu_custom_call" | custom-call | flops 4294967296 | bytes 25165824 | tf_op jit(solution)/shard_map/cross/pallas_call | solution.py:134
  39.1 0.1 collective-permute-start.1
  39.1 1.8 %collective-permute-start.2 = (f32[256,256]{1,0:T(8,128)S(1)}, f32[256,256]{1,0:T(8,128)S(1)}, u32[]{:S(2)}, u32[]{:S(2)}) collective-permute-start(f32[256,256]{1,0:T(8,128)S(1)} %get-tuple-element.39), channel_id=1, source_target_pairs={{0,4},{4,0},{8,12},{12,8},{1,5},{5,1},{9,13},{13,9},{2,6},{6,2},{1... | collective-permute-start | bytes 786440 | tf_op jit(solution)/shard_map/ppermute | solution.py:519
  41.0 0.3 collective-permute-start.3
  41.2 2.8 %collective-permute-start.4 = (f32[128,512]{1,0:T(8,128)S(1)}, f32[128,512]{1,0:T(8,128)S(1)}, u32[]{:S(2)}, u32[]{:S(2)}) collective-permute-start(f32[128,512]{1,0:T(8,128)S(1)} %forward.3.after), channel_id=1, source_target_pairs={{0,8},{4,12},{8,0},{12,4},{1,9},{5,13},{9,1},{13,5},{2,10},{6,14},... | collective-permute-start | bytes 786440 | tf_op jit(solution)/shard_map/ppermute | solution.py:519
  44.0 10.0 %collective-permute-done.2.refs_1_.refs_4_ = f32[256,256]{1,0:T(8,128)S(1)} collective-permute-done((f32[256,256]{1,0:T(8,128)S(1)}, f32[256,256]{1,0:T(8,128)S(1)}, u32[]{:S(2)}, u32[]{:S(2)}) %collective-permute-start.2) | collective-permute-done | bytes 262176 | tf_op jit(solution)/shard_map/ppermute | solution.py:519
  54.0 0.6 forward.4.after
  54.6 1.9 %collective-permute-start.5 = (f32[128,256]{1,0:T(8,128)S(1)}, f32[128,256]{1,0:T(8,128)S(1)}, u32[]{:S(2)}, u32[]{:S(2)}) collective-permute-start(f32[128,256]{1,0:T(8,128)S(1)} %forward.4.after), channel_id=1, source_target_pairs={{0,8},{4,12},{8,0},{12,4},{1,9},{5,13},{9,1},{13,5},{2,10},{6,14},... | collective-permute-start | bytes 393224 | tf_op jit(solution)/shard_map/ppermute | solution.py:519
  56.5 5.0 %begin.2 = (f32[2048,1024]{1,0:T(8,128)S(1)}, f32[2048,1024]{1,0:T(8,128)S(1)}, f32[8,128]{1,0:T(8,128)S(1)}) custom-call(s32[12]{0:T(128)S(1)} %stack.38.where, bf16[16384,1024]{1,0:T(8,128)(2,1)} %model.9, f32[128,256]{1,0:T(8,128)S(1)} %forward.4.after), custom_call_target="tpu_custom_call" | custom-call | tf_op jit(solution)/shard_map/begin/pallas_call | solution.py:320
  61.5 0.0 collective-permute-done.3.refs_1_.refs_7_
  61.5 0.6 forward.5.after
  62.0 0.0 copy-start
  62.1 0.0 copy-start.1
  62.1 1.1 collective-permute-start.6
  63.2 5.0 %begin.3 = (f32[2048,1024]{1,0:T(8,128)S(1)}, f32[2048,1024]{1,0:T(8,128)S(1)}, f32[8,128]{1,0:T(8,128)S(1)}) custom-call(s32[12]{0:T(128)S(1)} %stack.38.where, bf16[16384,1024]{1,0:T(8,128)(2,1)} %model.9, f32[128,256]{1,0:T(8,128)S(1)} %forward.5.after), custom_call_target="tpu_custom_call" | custom-call | tf_op jit(solution)/shard_map/begin/pallas_call | solution.py:320
  68.2 0.2 collective-permute-done.5.refs_5_
  68.4 0.0 collective-permute-done.4.refs_2_
  68.4 4.1 %collective-permute-done.6.refs_8_ = f32[128,256]{1,0:T(8,128)S(1)} collective-permute-done((f32[128,256]{1,0:T(8,128)S(1)}, f32[128,256]{1,0:T(8,128)S(1)}, u32[]{:S(2)}, u32[]{:S(2)}) %collective-permute-start.6) | collective-permute-done | bytes 131104 | tf_op jit(solution)/shard_map/ppermute | solution.py:519
  72.5 0.0 copy-done
  72.5 0.0 copy-done.1
  72.5 0.8 softmax.1
  73.3 1.6 %collective-permute-start.7 = (f32[16,128]{1,0:T(8,128)S(1)}, f32[16,128]{1,0:T(8,128)S(1)}, u32[]{:S(2)}, u32[]{:S(2)}) collective-permute-start(f32[16,128]{1,0:T(8,128)S(1)} %get-tuple-element.44.own.mine), channel_id=1, source_target_pairs={{0,2},{2,0},{1,3},{3,1},{4,6},{6,4},{5,7},{7,5},{8,10},{10,8},{9,1... | collective-permute-start | bytes 24584 | tf_op jit(solution)/shard_map/ppermute | solution.py:519
  74.9 2.1 %collective-permute-done.7.other = f32[16,128]{1,0:T(8,128)S(1)} collective-permute-done((f32[16,128]{1,0:T(8,128)S(1)}, f32[16,128]{1,0:T(8,128)S(1)}, u32[]{:S(2)}, u32[]{:S(2)}) %collective-permute-start.7) | collective-permute-done | bytes 8224 | tf_op jit(solution)/shard_map/ppermute | solution.py:519
  77.0 0.7 weights.1.refs_0_
  77.8 0.1 collective-permute-start.8
  77.9 1.9 %collective-permute-start.13 = (bf16[128,1024]{1,0:T(8,128)(2,1)S(1)}, bf16[128,1024]{1,0:T(8,128)(2,1)S(1)}, u32[]{:S(2)}, u32[]{:S(2)}) collective-permute-start(bf16[128,1024]{1,0:T(8,128)(2,1)S(1)} %weights.1.refs_0_), channel_id=1, source_target_pairs={{0,4},{4,0},{8,12},{12,8},{1,5},{5,1},{9,13},{13,9},{2,6},{6,2},{1... | collective-permute-start | bytes 786440 | tf_op jit(solution)/shard_map/ppermute | solution.py:519
  79.8 10.5 %collective-permute-done.8.refs_0_ = bf16[128,1024]{1,0:T(8,128)(2,1)S(1)} collective-permute-done((bf16[128,1024]{1,0:T(8,128)(2,1)S(1)}, bf16[128,1024]{1,0:T(8,128)(2,1)S(1)}, u32[]{:S(2)}, u32[]{:S(2)}) %collective-permute-start.8) | collective-permute-done | bytes 262176 | tf_op jit(solution)/shard_map/ppermute | solution.py:519
  90.3 0.0 collective-permute-start.10
  90.3 0.0 collective-permute-start.15
  90.3 0.5 collective-permute-start.12
  90.8 1.4 %collective-permute-done.12.refs_3_.refs_5_ = f32[512,1]{1,0:T(8,128)S(1)} collective-permute-done((f32[512,1]{1,0:T(8,128)S(1)}, f32[512,1]{1,0:T(8,128)S(1)}, u32[]{:S(2)}, u32[]{:S(2)}) %collective-permute-start.12) | collective-permute-done | bytes 2080 | tf_op jit(solution)/shard_map/ppermute | solution.py:519
  92.2 0.1 collective-permute-start.9
  92.3 0.0 collective-permute-done.13.refs_0_
  92.3 0.4 collective-permute-start.14
  92.7 5.7 %collective-permute-done.10.refs_2_ = bf16[128,1024]{1,0:T(8,128)(2,1)S(1)} collective-permute-done((bf16[128,1024]{1,0:T(8,128)(2,1)S(1)}, bf16[128,1024]{1,0:T(8,128)(2,1)S(1)}, u32[]{:S(2)}, u32[]{:S(2)}) %collective-permute-start.10) | collective-permute-done | bytes 262176 | tf_op jit(solution)/shard_map/ppermute | solution.py:519
  98.4 0.0 collective-permute-start.11
  98.5 0.0 collective-permute-done.15.refs_1_
  98.5 0.0 collective-permute-done.1.psib
  98.5 9.7 %numer.3 = (f32[2048,1024]{1,0:T(8,128)S(1)}, f32[2048,1024]{1,0:T(8,128)S(1)}, f32[2048,1024]{1,0:T(8,128)S(1)}, f32[2048,1024]{1,0:T(8,128)S(1)}, f32[1,1024]{1,0:T(1,128)S(1)}) custom-call(s32[12]{0:T(128)S(1)} %stack.38.where, ...), custom_call_target="tpu_custom_call", output_to_operand_aliasing={{0}: (7, {}), {1}: (8, {}), {2}: (9, {}), {3}: (10, {})} | custom-call | flops 4294967296 | bytes 33554432 | tf_op jit(solution)/shard_map/numer/pallas_call | solution.py:424
  108.2 0.0 collective-permute-done.14.refs_1_
  108.2 9.7 %numer.4 = (f32[2048,1024]{1,0:T(8,128)S(1)}, f32[2048,1024]{1,0:T(8,128)S(1)}, f32[2048,1024]{1,0:T(8,128)S(1)}, f32[2048,1024]{1,0:T(8,128)S(1)}, f32[1,1024]{1,0:T(1,128)S(1)}) custom-call(s32[12]{0:T(128)S(1)} %stack.38.where, ...), custom_call_target="tpu_custom_call", output_to_operand_aliasing={{0}: (8, {}), {1}: (9, {}), {2}: (10, {}), {3}: (11, {})} | custom-call | flops 4294967296 | bytes 33554432 | tf_op jit(solution)/shard_map/numer/pallas_call | solution.py:424
  117.9 0.0 collective-permute-done.9.refs_1_
  117.9 0.0 collective-permute-done.11.refs_3_
  117.9 16.4 %numer.5 = bf16[8192,1024]{1,0:T(8,128)(2,1)} custom-call(s32[12]{0:T(128)S(1)} %stack.38.where, bf16[8192,512]{1,0:T(8,128)(2,1)} %get-tuple-element.33.pown, bf16[8192,512]{1,0:T(8,128)(2,1)} %collective-permute-done.1.psib, bf16[128,1024]{1,0:T(8,128)(2,1)S(1)} %collective-permute-done.8.refs_0_, bf16[128,1024]{1,0:T(8,128)(2,1)S(1)} %collective-permute-done.9.refs_1_, ...), custom_call_target="tpu_custom_call" | custom-call | flops 8589934592 | bytes 33554432 | tf_op jit(solution)/shard_map/numer/pallas_call | solution.py:424
Async XLA Ops:
  14.5 15.0 %collective-permute-start = (f32[256,512]{1,0:T(8,128)S(1)}, f32[256,512]{1,0:T(8,128)S(1)}, u32[]{:S(2)}, u32[]{:S(2)}) collective-permute-start(f32[256,512]{1,0:T(8,128)S(1)} %get-tuple-element.36), channel_id=1, source_target_pairs={{0,4},{4,0},{8,12},{12,8},{1,5},{5,1},{9,13},{13,9},{2,6},{6,2},{1... | collective-permute-start | bytes 1572872 | tf_op jit(solution)/shard_map/ppermute | solution.py:519
  39.1 59.4 %collective-permute-start.1 = (bf16[8192,512]{1,0:T(8,128)(2,1)}, bf16[8192,512]{1,0:T(8,128)(2,1)}, u32[]{:S(2)}, u32[]{:S(2)}) collective-permute-start(bf16[8192,512]{1,0:T(8,128)(2,1)} %get-tuple-element.37), channel_id=1, source_target_pairs={{0,1},{1,0},{2,3},{3,2},{4,5},{5,4},{6,7},{7,6},{8,9},{9,8},{10,11... | collective-permute-start | bytes 25165832 | tf_op jit(solution)/shard_map/ppermute | solution.py:519
  39.1 14.9 %collective-permute-start.2 = (f32[256,256]{1,0:T(8,128)S(1)}, f32[256,256]{1,0:T(8,128)S(1)}, u32[]{:S(2)}, u32[]{:S(2)}) collective-permute-start(f32[256,256]{1,0:T(8,128)S(1)} %get-tuple-element.39), channel_id=1, source_target_pairs={{0,4},{4,0},{8,12},{12,8},{1,5},{5,1},{9,13},{13,9},{2,6},{6,2},{1... | collective-permute-start | bytes 786440 | tf_op jit(solution)/shard_map/ppermute | solution.py:519
  41.0 20.5 %collective-permute-start.3 = (f32[256,256]{1,0:T(8,128)S(1)}, f32[256,256]{1,0:T(8,128)S(1)}, u32[]{:S(2)}, u32[]{:S(2)}) collective-permute-start(f32[256,256]{1,0:T(8,128)S(1)} %get-tuple-element.41), channel_id=1, source_target_pairs={{0,4},{4,0},{8,12},{12,8},{1,5},{5,1},{9,13},{13,9},{2,6},{6,2},{1... | collective-permute-start | bytes 786440 | tf_op jit(solution)/shard_map/ppermute | solution.py:519
  41.2 27.2 %collective-permute-start.4 = (f32[128,512]{1,0:T(8,128)S(1)}, f32[128,512]{1,0:T(8,128)S(1)}, u32[]{:S(2)}, u32[]{:S(2)}) collective-permute-start(f32[128,512]{1,0:T(8,128)S(1)} %forward.3.after), channel_id=1, source_target_pairs={{0,8},{4,12},{8,0},{12,4},{1,9},{5,13},{9,1},{13,5},{2,10},{6,14},... | collective-permute-start | bytes 786440 | tf_op jit(solution)/shard_map/ppermute | solution.py:519
  54.6 13.8 %collective-permute-start.5 = (f32[128,256]{1,0:T(8,128)S(1)}, f32[128,256]{1,0:T(8,128)S(1)}, u32[]{:S(2)}, u32[]{:S(2)}) collective-permute-start(f32[128,256]{1,0:T(8,128)S(1)} %forward.4.after), channel_id=1, source_target_pairs={{0,8},{4,12},{8,0},{12,4},{1,9},{5,13},{9,1},{13,5},{2,10},{6,14},... | collective-permute-start | bytes 393224 | tf_op jit(solution)/shard_map/ppermute | solution.py:519
  62.0 10.5 %copy-start = (s32[1024]{0:T(1024)S(1)}, s32[1024]{0:T(1024)}, u32[]{:S(2)}) copy-start(s32[1024]{0:T(1024)} %param.11) | copy-start | bytes 12292
  62.1 10.5 %copy-start.1 = (f32[8]{0:T(128)S(1)}, f32[8]{0:T(128)}, u32[]{:S(2)}) copy-start(f32[8]{0:T(128)} %table.1) | copy-start | bytes 100
  62.1 10.4 %collective-permute-start.6 = (f32[128,256]{1,0:T(8,128)S(1)}, f32[128,256]{1,0:T(8,128)S(1)}, u32[]{:S(2)}, u32[]{:S(2)}) collective-permute-start(f32[128,256]{1,0:T(8,128)S(1)} %forward.5.after), channel_id=1, source_target_pairs={{0,8},{4,12},{8,0},{12,4},{1,9},{5,13},{9,1},{13,5},{2,10},{6,14},... | collective-permute-start | bytes 393224 | tf_op jit(solution)/shard_map/ppermute | solution.py:519
  73.3 3.7 %collective-permute-start.7 = (f32[16,128]{1,0:T(8,128)S(1)}, f32[16,128]{1,0:T(8,128)S(1)}, u32[]{:S(2)}, u32[]{:S(2)}) collective-permute-start(f32[16,128]{1,0:T(8,128)S(1)} %get-tuple-element.44.own.mine), channel_id=1, source_target_pairs={{0,2},{2,0},{1,3},{3,1},{4,6},{6,4},{5,7},{7,5},{8,10},{10,8},{9,1... | collective-permute-start | bytes 24584 | tf_op jit(solution)/shard_map/ppermute | solution.py:519
  77.8 12.5 %collective-permute-start.8 = (bf16[128,1024]{1,0:T(8,128)(2,1)S(1)}, bf16[128,1024]{1,0:T(8,128)(2,1)S(1)}, u32[]{:S(2)}, u32[]{:S(2)}) collective-permute-start(bf16[128,1024]{1,0:T(8,128)(2,1)S(1)} %weights.1.refs_0_), channel_id=1, source_target_pairs={{0,8},{4,12},{8,0},{12,4},{1,9},{5,13},{9,1},{13,5},{2,10},{6,14},... | collective-permute-start | bytes 786440 | tf_op jit(solution)/shard_map/ppermute | solution.py:519
  77.9 14.5 %collective-permute-start.13 = (bf16[128,1024]{1,0:T(8,128)(2,1)S(1)}, bf16[128,1024]{1,0:T(8,128)(2,1)S(1)}, u32[]{:S(2)}, u32[]{:S(2)}) collective-permute-start(bf16[128,1024]{1,0:T(8,128)(2,1)S(1)} %weights.1.refs_0_), channel_id=1, source_target_pairs={{0,4},{4,0},{8,12},{12,8},{1,5},{5,1},{9,13},{13,9},{2,6},{6,2},{1... | collective-permute-start | bytes 786440 | tf_op jit(solution)/shard_map/ppermute | solution.py:519
  90.3 8.2 %collective-permute-start.10 = (bf16[128,1024]{1,0:T(8,128)(2,1)S(1)}, bf16[128,1024]{1,0:T(8,128)(2,1)S(1)}, u32[]{:S(2)}, u32[]{:S(2)}) collective-permute-start(bf16[128,1024]{1,0:T(8,128)(2,1)S(1)} %collective-permute-done.8.refs_0_), channel_id=1, source_target_pairs={{0,4},{4,0},{8,12},{12,8},{1,5},{5,1},{9,13},{13,9},{2,6},{6,2},{1... | collective-permute-start | bytes 786440 | tf_op jit(solution)/shard_map/ppermute | solution.py:519
  90.3 8.2 %collective-permute-start.15 = (bf16[128,1024]{1,0:T(8,128)(2,1)S(1)}, bf16[128,1024]{1,0:T(8,128)(2,1)S(1)}, u32[]{:S(2)}, u32[]{:S(2)}) collective-permute-start(bf16[128,1024]{1,0:T(8,128)(2,1)S(1)} %weights.1.refs_0_), channel_id=1, source_target_pairs={{0,1},{1,0},{2,3},{3,2},{4,5},{5,4},{6,7},{7,6},{8,9},{9,8},{10,11... | collective-permute-start | bytes 786440 | tf_op jit(solution)/shard_map/ppermute | solution.py:519
  90.3 1.9 %collective-permute-start.12 = (f32[512,1]{1,0:T(8,128)S(1)}, f32[512,1]{1,0:T(8,128)S(1)}, u32[]{:S(2)}, u32[]{:S(2)}) collective-permute-start(f32[512,1]{1,0:T(8,128)S(1)} %copy.27.phi.after.refs_2_.refs_4_), channel_id=1, source_target_pairs={{0,1},{1,0},{2,3},{3,2},{4,5},{5,4},{6,7},{7,6},{8,9},{9,8},{10,11... | collective-permute-start | bytes 6152 | tf_op jit(solution)/shard_map/ppermute | solution.py:519
  92.2 25.7 %collective-permute-start.9 = (bf16[128,1024]{1,0:T(8,128)(2,1)S(1)}, bf16[128,1024]{1,0:T(8,128)(2,1)S(1)}, u32[]{:S(2)}, u32[]{:S(2)}) collective-permute-start(bf16[128,1024]{1,0:T(8,128)(2,1)S(1)} %collective-permute-done.8.refs_0_), channel_id=1, source_target_pairs={{0,1},{1,0},{2,3},{3,2},{4,5},{5,4},{6,7},{7,6},{8,9},{9,8},{10,11... | collective-permute-start | bytes 786440 | tf_op jit(solution)/shard_map/ppermute | solution.py:519
  92.3 15.8 %collective-permute-start.14 = (bf16[128,1024]{1,0:T(8,128)(2,1)S(1)}, bf16[128,1024]{1,0:T(8,128)(2,1)S(1)}, u32[]{:S(2)}, u32[]{:S(2)}) collective-permute-start(bf16[128,1024]{1,0:T(8,128)(2,1)S(1)} %collective-permute-done.13.refs_0_), channel_id=1, source_target_pairs={{0,1},{1,0},{2,3},{3,2},{4,5},{5,4},{6,7},{7,6},{8,9},{9,8},{10,11... | collective-permute-start | bytes 786440 | tf_op jit(solution)/shard_map/ppermute | solution.py:519
  98.4 19.4 %collective-permute-start.11 = (bf16[128,1024]{1,0:T(8,128)(2,1)S(1)}, bf16[128,1024]{1,0:T(8,128)(2,1)S(1)}, u32[]{:S(2)}, u32[]{:S(2)}) collective-permute-start(bf16[128,1024]{1,0:T(8,128)(2,1)S(1)} %collective-permute-done.10.refs_2_), channel_id=1, source_target_pairs={{0,1},{1,0},{2,3},{3,2},{4,5},{5,4},{6,7},{7,6},{8,9},{9,8},{10,11... | collective-permute-start | bytes 786440 | tf_op jit(solution)/shard_map/ppermute | solution.py:519

commit v8 on v7

--- a/solution.py
+++ b/solution.py
@@ -12,6 +12,9 @@
 SLOTS = 4
 PARTS = 4
 SUB = 256
+AHEAD = 6
+OUT = 4
+TURN = 3
 VMEM = pl.BlockSpec(memory_space=pltpu.VMEM)
 SMEM = pl.BlockSpec(memory_space=pltpu.SMEM)
 HBM = pl.BlockSpec(memory_space=pltpu.HBM)
@@ -54,7 +57,7 @@
         return both
 
     def stores(i):
-        slot = lax.rem(i, 2)
+        slot = lax.rem(i, TURN)
         for t, out in enumerate(turned):
             width = out.shape[0] // steps
             rows = pl.ds(pl.multiple_of(i * width, width), width)
@@ -77,9 +80,9 @@
 
         if turns:
 
-            @pl.when(i >= 2)
+            @pl.when(i >= TURN)
             def _():
-                for copy in stores(i - 2):
+                for copy in stores(i - TURN):
                     copy.wait()
 
         tile = mbuf[lax.rem(i, SLOTS)]
@@ -92,7 +95,7 @@
             width = pixels // steps
             side = where[1] if own else 1 - where[1]
             piece = held[:, pl.ds(pl.multiple_of(side * pixels + i * width, width), width)]
-            tbuf[t, lax.rem(i, 2)] = piece.T
+            tbuf[t, lax.rem(i, TURN)] = piece.T
         for copy in stores(i):
             copy.start()
         return carry
@@ -104,7 +107,7 @@
     half = send.shape[0]
     send[...] = acc[pl.ds(pl.multiple_of((1 - where[0]) * half, half), half), :]
     keep[...] = acc[pl.ds(pl.multiple_of(where[0] * half, half), half), :]
-    for i in range(max(0, steps - 2), steps):
+    for i in range(max(0, steps - TURN), steps):
         for copy in stores(i):
             copy.wait()
 
@@ -127,8 +130,8 @@
         scratch.append(pltpu.SemaphoreType.DMA((SLOTS,)))
         places.append(VMEM)
     if turns:
-        scratch.append(pltpu.VMEM((len(turns), 2, tk // 2, rows), patterns.dtype))
-        scratch.append(pltpu.SemaphoreType.DMA((len(turns), 2)))
+        scratch.append(pltpu.VMEM((len(turns), TURN, tk // 2, rows), patterns.dtype))
+        scratch.append(pltpu.SemaphoreType.DMA((len(turns), TURN)))
     patterns = pltpu.with_memory_space_constraint(patterns, pltpu.HBM if first else pltpu.VMEM)
     model = pltpu.with_memory_space_constraint(model, pltpu.HBM)
     return pl.pallas_call(
@@ -236,7 +239,7 @@
         out_shape=[jax.ShapeDtypeStruct((count, tn), jnp.bfloat16) for tn in widths],
         in_specs=[SMEM] + [VMEM] * 5,
         out_specs=[VMEM] * len(widths),
-        compiler_params=params(4 * MIB),
+        compiler_params=params(22 * MIB),
         name="weights",
     )(where, phi, exps, own, mine, other)
 
@@ -343,14 +346,14 @@
         wide[k * count : (k + 1) * count, :] = pairs[k][...]
 
     def pieces(i):
-        slot = lax.rem(i, 3)
+        slot = lax.rem(i, AHEAD)
         rows = pl.ds(pl.multiple_of(i * tm, tm), tm)
         for k in range(mine):
             columns = pl.ds(pl.multiple_of(where[base + blocks[k // 2]], count), count)
             part = (pown, psib)[k % 2].at[rows, columns]
             yield pltpu.make_async_copy(part, tiles.at[slot, :, pl.ds(k * count, count)], tsem.at[slot, k])
 
-    for i in range(min(2, steps)):
+    for i in range(min(AHEAD - 1, steps)):
         for copy in pieces(i):
             copy.start()
     for k, part in enumerate(pairs):
@@ -364,29 +367,29 @@
         den[...] = seen
 
     def store(i):
-        slot = lax.rem(i, 2)
+        slot = lax.rem(i, OUT)
         return pltpu.make_async_copy(buf.at[slot], out.at[pl.ds(pl.multiple_of(i * tm, tm), tm)], sem.at[slot])
 
     def body(part, i, carry):
         for copy in pieces(i):
             copy.wait()
 
-        @pl.when(i + 2 < steps)
+        @pl.when(i + AHEAD - 1 < steps)
         def _():
-            for copy in pieces(i + 2):
+            for copy in pieces(i + AHEAD - 1):
                 copy.start()
 
         if last:
 
-            @pl.when(i >= 2)
+            @pl.when(i >= OUT)
             def _():
-                store(i - 2).wait()
+                store(i - OUT).wait()
 
         for r in range(0, tm, sub):
             rows = pl.ds(pl.multiple_of(i * tm + r - part * (pixels // PARTS), sub), sub)
-            dot = jnp.dot(tiles[lax.rem(i, 3), r : r + sub, :], wide[...], preferred_element_type=jnp.float32)
+            dot = jnp.dot(tiles[lax.rem(i, AHEAD), r : r + sub, :], wide[...], preferred_element_type=jnp.float32)
             if last:
-                buf[lax.rem(i, 2), r : r + sub, :] = ((dot + totals[part][rows, :]) * scale).astype(jnp.bfloat16)
+                buf[lax.rem(i, OUT), r : r + sub, :] = ((dot + totals[part][rows, :]) * scale).astype(jnp.bfloat16)
             else:
                 sums[part][rows, :] += dot
         if last:
@@ -396,7 +399,7 @@
     for part in range(PARTS):
         lax.fori_loop(part * steps // PARTS, (part + 1) * steps // PARTS, functools.partial(body, part), 0)
     if last:
-        for i in range(max(0, steps - 2), steps):
+        for i in range(max(0, steps - OUT), steps):
             store(i).wait()
 
 
@@ -411,12 +414,12 @@
     in_specs = [SMEM, HBM, HBM] + [VMEM] * (len(args) - 3)
     scratch = [
         pltpu.VMEM((len(pairs) * count, columns), jnp.bfloat16),
-        pltpu.VMEM((3, tm, len(pairs) * count), jnp.bfloat16),
-        pltpu.SemaphoreType.DMA((3, len(pairs))),
+        pltpu.VMEM((AHEAD, tm, len(pairs) * count), jnp.bfloat16),
+        pltpu.SemaphoreType.DMA((AHEAD, len(pairs))),
     ]
     if last:
         shape, out_specs, aliases = jax.ShapeDtypeStruct((pixels, columns), jnp.bfloat16), HBM, {}
-        scratch = [pltpu.VMEM((2, tm, columns), jnp.bfloat16), pltpu.SemaphoreType.DMA((2,))] + scratch
+        scratch = [pltpu.VMEM((OUT, tm, columns), jnp.bfloat16), pltpu.SemaphoreType.DMA((OUT,))] + scratch
     else:
         shape = [pltpu.VMEM(total[0].shape, jnp.float32)] * PARTS + [jax.ShapeDtypeStruct((1, columns), jnp.float32)]
         out_specs = [VMEM] * (PARTS + 1)
@@ -430,7 +433,7 @@
         out_specs=out_specs,
         scratch_shapes=scratch,
         input_output_aliases=aliases,
-        compiler_params=params(12 * MIB),
+        compiler_params=params(14 * MIB),
         cost_estimate=cost(2 * pixels * columns * count * len(pairs), 4 * pixels * columns),
         name="numer",
     )(*args)
@@ -526,7 +529,7 @@
     count = rows // pix
     tn = min(256, columns)
     chunks = columns // tn
-    widths = [2 * tn] + [tn] * (chunks - 2) if chunks >= 4 else [tn] * chunks
+    widths = [columns // 2, columns * 3 // 8, columns // 8] if chunks >= 4 else [tn] * chunks
     starts = [sum(widths[:c]) for c in range(len(widths))]
     chunks = len(widths)
     beta = (patterns.shape[1] * pix) ** -0.5

time: 135 us -> 131 us (0.970)
  waiting for transfers between devices: 36.9 us -> 30.9 us
  Pallas kernels: 80.5 us -> 82 us
    ppermute x16, waiting for transfers between devices: 36.9 us -> 30.9 us  [exchange(): return lax.ppermute(value, axis, [(i, i ^ distance) for i in range(size)])]
    pallas_call x3, Pallas kernels: 31.5 us -> 35.4 us  [cross_chunk(): pl.pallas_call(functools.partial(cross_kernel, column=column, tk=tk, step...]
    pallas_call x3, Pallas kernels: 35.8 us -> 33.4 us  [numer_pass(): pl.pallas_call(functools.partial(pass_kernel, blocks=blocks, pix=pix, fir...]
  transfers between devices with their start and end apart: 16 -> 16, of which waited for: 8 -> 6; matrix products, arithmetic and copies ran while one was open for 0% -> 0% of each run, Pallas kernels for 31% -> 34%
where the time goes in v8:
time: 131 us
  Pallas kernels  82 us (63%)
  waiting for transfers between devices  30.9 us (24%)
  starting transfers between devices  16.4 us (13%)
    pallas_call x3, Pallas kernels, cross_chunk(): pl.pallas_call(functools.partial(cross_kernel, column=column, tk=tk, step...  35.4 us
    pallas_call x3, Pallas kernels, numer_pass(): pl.pallas_call(functools.partial(pass_kernel, blocks=blocks, pix=pix, fir...  33.4 us
    ppermute x16, waiting for transfers between devices, exchange(): return lax.ppermute(value, axis, [(i, i ^ distance) for i in range(size)])  30.9 us
    ppermute x16, starting transfers between devices, exchange(): return lax.ppermute(value, axis, [(i, i ^ distance) for i in range(size)])  16.4 us
    pallas_call x2, Pallas kernels, begin(): pl.pallas_call(functools.partial(begin_kernel, side=1, tm=tm, start=start...  9.94 us
  transfers between devices with their start and end apart: 16, of which 6 were waited for; matrix products, arithmetic and copies ran while one was open for 0% of the time, Pallas kernels for 34%

profile of v8, /device:TPU:0, one launch (start us, length us, event | category | flops | bytes accessed | tf_op | source)
XLA Modules:
  0.0 130.5 jit_solution(7489088157969135719)
XLA Ops:
  0.0 0.8 select_reduce_fusion
  0.8 0.1 copy.27.phi.after.refs_2_.refs_4_
  0.9 0.1 stack.38.where
  1.0 13.4 %cross.3 = (f32[256,512]{1,0:T(8,128)S(1)}, f32[256,512]{1,0:T(8,128)S(1)}, bf16[512,16384]{1,0:T(8,128)(2,1)S(1)}) custom-call(s32[12]{0:T(128)S(1)} %stack.38.where, f32[512,1]{1,0:T(8,128)S(1)} %copy.27.phi.after.refs_2_.refs_4_, bf16[512,16384]{1,0:T(8,128)(2,1)} %patterns.1, bf16[16384,1024]{1,0:T(8,128)(2,1)} %model.9, ...), custom_call_target="tpu_custom_call" | custom-call | flops 8589934592 | bytes 33554432 | tf_op jit(solution)/shard_map/cross/pallas_call | solution.py:137
  14.5 3.1 %collective-permute-start = (f32[256,512]{1,0:T(8,128)S(1)}, f32[256,512]{1,0:T(8,128)S(1)}, u32[]{:S(2)}, u32[]{:S(2)}) collective-permute-start(f32[256,512]{1,0:T(8,128)S(1)} %get-tuple-element.36), channel_id=1, source_target_pairs={{0,4},{4,0},{8,12},{12,8},{1,5},{5,1},{9,13},{13,9},{2,6},{6,2},{1... | collective-permute-start | bytes 1572872 | tf_op jit(solution)/shard_map/ppermute | solution.py:522
  17.6 13.3 %cross.4 = (f32[256,384]{1,0:T(8,128)S(1)}, f32[256,384]{1,0:T(8,128)S(1)}, bf16[8192,512]{1,0:T(8,128)(2,1)}) custom-call(s32[12]{0:T(128)S(1)} %stack.38.where, f32[512,1]{1,0:T(8,128)S(1)} %copy.27.phi.after.refs_2_.refs_4_, bf16[512,16384]{1,0:T(8,128)(2,1)S(1)} %get-tuple-element.32.patterns, bf16[16384,1024]{1,0:T(8,128)(2,1)} %model.9, ...), custom_call_target="tpu_custom_call" | custom-call | flops 6442450944 | bytes 29360128 | tf_op jit(solution)/shard_map/cross/pallas_call | solution.py:137
  30.9 0.0 collective-permute-done.refs_1_
  31.0 0.6 forward.3.after
  31.5 8.6 %cross.5 = (f32[256,128]{1,0:T(8,128)S(1)}, f32[256,128]{1,0:T(8,128)S(1)}, bf16[8192,512]{1,0:T(8,128)(2,1)}) custom-call(s32[12]{0:T(128)S(1)} %stack.38.where, f32[512,1]{1,0:T(8,128)S(1)} %copy.27.phi.after.refs_2_.refs_4_, bf16[512,16384]{1,0:T(8,128)(2,1)S(1)} %get-tuple-element.32.patterns, bf16[16384,1024]{1,0:T(8,128)(2,1)} %model.9, ...), custom_call_target="tpu_custom_call" | custom-call | flops 2147483648 | bytes 20971520 | tf_op jit(solution)/shard_map/cross/pallas_call | solution.py:137
  40.2 0.1 collective-permute-start.1
  40.3 0.4 collective-permute-start.2
  40.7 2.7 %collective-permute-start.4 = (f32[128,512]{1,0:T(8,128)S(1)}, f32[128,512]{1,0:T(8,128)S(1)}, u32[]{:S(2)}, u32[]{:S(2)}) collective-permute-start(f32[128,512]{1,0:T(8,128)S(1)} %forward.3.after), channel_id=1, source_target_pairs={{0,8},{4,12},{8,0},{12,4},{1,9},{5,13},{9,1},{13,5},{2,10},{6,14},... | collective-permute-start | bytes 786440 | tf_op jit(solution)/shard_map/ppermute | solution.py:522
  43.4 1.6 %collective-permute-start.3 = (f32[256,128]{1,0:T(8,128)S(1)}, f32[256,128]{1,0:T(8,128)S(1)}, u32[]{:S(2)}, u32[]{:S(2)}) collective-permute-start(f32[256,128]{1,0:T(8,128)S(1)} %get-tuple-element.41), channel_id=1, source_target_pairs={{0,4},{4,0},{8,12},{12,8},{1,5},{5,1},{9,13},{13,9},{2,6},{6,2},{1... | collective-permute-start | bytes 393224 | tf_op jit(solution)/shard_map/ppermute | solution.py:522
  45.0 13.0 %collective-permute-done.2.refs_1_.refs_4_ = f32[256,384]{1,0:T(8,128)S(1)} collective-permute-done((f32[256,384]{1,0:T(8,128)S(1)}, f32[256,384]{1,0:T(8,128)S(1)}, u32[]{:S(2)}, u32[]{:S(2)}) %collective-permute-start.2) | collective-permute-done | bytes 393248 | tf_op jit(solution)/shard_map/ppermute | solution.py:522
  57.9 0.6 forward.4.after
  58.5 0.6 collective-permute-start.5
  59.1 5.0 %begin.2 = (f32[2048,1024]{1,0:T(8,128)S(1)}, f32[2048,1024]{1,0:T(8,128)S(1)}, f32[8,128]{1,0:T(8,128)S(1)}) custom-call(s32[12]{0:T(128)S(1)} %stack.38.where, bf16[16384,1024]{1,0:T(8,128)(2,1)} %model.9, f32[128,384]{1,0:T(8,128)S(1)} %forward.4.after), custom_call_target="tpu_custom_call" | custom-call | tf_op jit(solution)/shard_map/begin/pallas_call | solution.py:323
  64.1 0.0 collective-permute-done.3.refs_1_.refs_7_
  64.1 0.6 forward.5.after
  64.7 0.0 copy-start
  64.7 0.0 copy-start.1
  64.7 2.4 %collective-permute-start.6 = (f32[128,128]{1,0:T(8,128)S(1)}, f32[128,128]{1,0:T(8,128)S(1)}, u32[]{:S(2)}, u32[]{:S(2)}) collective-permute-start(f32[128,128]{1,0:T(8,128)S(1)} %forward.5.after), channel_id=1, source_target_pairs={{0,8},{4,12},{8,0},{12,4},{1,9},{5,13},{9,1},{13,5},{2,10},{6,14},... | collective-permute-start | bytes 196616 | tf_op jit(solution)/shard_map/ppermute | solution.py:522
  67.1 5.0 %begin.3 = (f32[2048,1024]{1,0:T(8,128)S(1)}, f32[2048,1024]{1,0:T(8,128)S(1)}, f32[8,128]{1,0:T(8,128)S(1)}) custom-call(s32[12]{0:T(128)S(1)} %stack.38.where, bf16[16384,1024]{1,0:T(8,128)(2,1)} %model.9, f32[128,128]{1,0:T(8,128)S(1)} %forward.5.after), custom_call_target="tpu_custom_call" | custom-call | tf_op jit(solution)/shard_map/begin/pallas_call | solution.py:323
  72.1 0.0 collective-permute-done.5.refs_5_
  72.1 0.2 collective-permute-done.6.refs_8_
  72.3 0.0 collective-permute-done.4.refs_2_
  72.3 0.0 copy-done
  72.4 0.0 copy-done.1
  72.4 0.8 softmax.1
  73.2 1.5 %collective-permute-start.7 = (f32[16,128]{1,0:T(8,128)S(1)}, f32[16,128]{1,0:T(8,128)S(1)}, u32[]{:S(2)}, u32[]{:S(2)}) collective-permute-start(f32[16,128]{1,0:T(8,128)S(1)} %get-tuple-element.44.own.mine), channel_id=1, source_target_pairs={{0,2},{2,0},{1,3},{3,1},{4,6},{6,4},{5,7},{7,5},{8,10},{10,8},{9,1... | collective-permute-start | bytes 24584 | tf_op jit(solution)/shard_map/ppermute | solution.py:522
  74.7 2.2 %collective-permute-done.7.other = f32[16,128]{1,0:T(8,128)S(1)} collective-permute-done((f32[16,128]{1,0:T(8,128)S(1)}, f32[16,128]{1,0:T(8,128)S(1)}, u32[]{:S(2)}, u32[]{:S(2)}) %collective-permute-start.7) | collective-permute-done | bytes 8224 | tf_op jit(solution)/shard_map/ppermute | solution.py:522
  76.9 0.7 weights.1.refs_0_
  77.6 0.5 collective-permute-start.8
  78.1 2.5 %collective-permute-start.13 = (bf16[128,1024]{1,0:T(8,128)(2,1)S(1)}, bf16[128,1024]{1,0:T(8,128)(2,1)S(1)}, u32[]{:S(2)}, u32[]{:S(2)}) collective-permute-start(bf16[128,1024]{1,0:T(8,128)(2,1)S(1)} %weights.1.refs_0_), channel_id=1, source_target_pairs={{0,4},{4,0},{8,12},{12,8},{1,5},{5,1},{9,13},{13,9},{2,6},{6,2},{1... | collective-permute-start | bytes 786440 | tf_op jit(solution)/shard_map/ppermute | solution.py:522
  80.5 9.1 %collective-permute-done.8.refs_0_ = bf16[128,1024]{1,0:T(8,128)(2,1)S(1)} collective-permute-done((bf16[128,1024]{1,0:T(8,128)(2,1)S(1)}, bf16[128,1024]{1,0:T(8,128)(2,1)S(1)}, u32[]{:S(2)}, u32[]{:S(2)}) %collective-permute-start.8) | collective-permute-done | bytes 262176 | tf_op jit(solution)/shard_map/ppermute | solution.py:522
  89.7 0.0 collective-permute-start.10
  89.7 0.0 collective-permute-start.15
  89.7 0.5 collective-permute-start.12
  90.2 1.4 %collective-permute-done.12.refs_3_.refs_5_ = f32[512,1]{1,0:T(8,128)S(1)} collective-permute-done((f32[512,1]{1,0:T(8,128)S(1)}, f32[512,1]{1,0:T(8,128)S(1)}, u32[]{:S(2)}, u32[]{:S(2)}) %collective-permute-start.12) | collective-permute-done | bytes 2080 | tf_op jit(solution)/shard_map/ppermute | solution.py:522
  91.6 0.1 collective-permute-start.9
  91.7 0.0 collective-permute-done.13.refs_0_
  91.7 0.4 collective-permute-start.14
  92.1 5.0 %collective-permute-done.10.refs_2_ = bf16[128,1024]{1,0:T(8,128)(2,1)S(1)} collective-permute-done((bf16[128,1024]{1,0:T(8,128)(2,1)S(1)}, bf16[128,1024]{1,0:T(8,128)(2,1)S(1)}, u32[]{:S(2)}, u32[]{:S(2)}) %collective-permute-start.10) | collective-permute-done | bytes 262176 | tf_op jit(solution)/shard_map/ppermute | solution.py:522
  97.1 0.0 collective-permute-start.11
  97.1 0.0 collective-permute-done.15.refs_1_
  97.1 0.0 collective-permute-done.1.psib
  97.1 9.0 %numer.3 = (f32[2048,1024]{1,0:T(8,128)S(1)}, f32[2048,1024]{1,0:T(8,128)S(1)}, f32[2048,1024]{1,0:T(8,128)S(1)}, f32[2048,1024]{1,0:T(8,128)S(1)}, f32[1,1024]{1,0:T(1,128)S(1)}) custom-call(s32[12]{0:T(128)S(1)} %stack.38.where, ...), custom_call_target="tpu_custom_call", output_to_operand_aliasing={{0}: (7, {}), {1}: (8, {}), {2}: (9, {}), {3}: (10, {})} | custom-call | flops 4294967296 | bytes 33554432 | tf_op jit(solution)/shard_map/numer/pallas_call | solution.py:427
  106.2 0.0 collective-permute-done.14.refs_1_
  106.2 9.0 %numer.4 = (f32[2048,1024]{1,0:T(8,128)S(1)}, f32[2048,1024]{1,0:T(8,128)S(1)}, f32[2048,1024]{1,0:T(8,128)S(1)}, f32[2048,1024]{1,0:T(8,128)S(1)}, f32[1,1024]{1,0:T(1,128)S(1)}) custom-call(s32[12]{0:T(128)S(1)} %stack.38.where, ...), custom_call_target="tpu_custom_call", output_to_operand_aliasing={{0}: (8, {}), {1}: (9, {}), {2}: (10, {}), {3}: (11, {})} | custom-call | flops 4294967296 | bytes 33554432 | tf_op jit(solution)/shard_map/numer/pallas_call | solution.py:427
  115.2 0.0 collective-permute-done.9.refs_1_
  115.2 0.0 collective-permute-done.11.refs_3_
  115.2 15.3 %numer.5 = bf16[8192,1024]{1,0:T(8,128)(2,1)} custom-call(s32[12]{0:T(128)S(1)} %stack.38.where, bf16[8192,512]{1,0:T(8,128)(2,1)} %get-tuple-element.33.pown, bf16[8192,512]{1,0:T(8,128)(2,1)} %collective-permute-done.1.psib, bf16[128,1024]{1,0:T(8,128)(2,1)S(1)} %collective-permute-done.8.refs_0_, bf16[128,1024]{1,0:T(8,128)(2,1)S(1)} %collective-permute-done.9.refs_1_, ...), custom_call_target="tpu_custom_call" | custom-call | flops 8589934592 | bytes 33554432 | tf_op jit(solution)/shard_map/numer/pallas_call | solution.py:427
Async XLA Ops:
  14.5 16.5 %collective-permute-start = (f32[256,512]{1,0:T(8,128)S(1)}, f32[256,512]{1,0:T(8,128)S(1)}, u32[]{:S(2)}, u32[]{:S(2)}) collective-permute-start(f32[256,512]{1,0:T(8,128)S(1)} %get-tuple-element.36), channel_id=1, source_target_pairs={{0,4},{4,0},{8,12},{12,8},{1,5},{5,1},{9,13},{13,9},{2,6},{6,2},{1... | collective-permute-start | bytes 1572872 | tf_op jit(solution)/shard_map/ppermute | solution.py:522
  40.2 56.9 %collective-permute-start.1 = (bf16[8192,512]{1,0:T(8,128)(2,1)}, bf16[8192,512]{1,0:T(8,128)(2,1)}, u32[]{:S(2)}, u32[]{:S(2)}) collective-permute-start(bf16[8192,512]{1,0:T(8,128)(2,1)} %get-tuple-element.37), channel_id=1, source_target_pairs={{0,1},{1,0},{2,3},{3,2},{4,5},{5,4},{6,7},{7,6},{8,9},{9,8},{10,11... | collective-permute-start | bytes 25165832 | tf_op jit(solution)/shard_map/ppermute | solution.py:522
  40.3 17.7 %collective-permute-start.2 = (f32[256,384]{1,0:T(8,128)S(1)}, f32[256,384]{1,0:T(8,128)S(1)}, u32[]{:S(2)}, u32[]{:S(2)}) collective-permute-start(f32[256,384]{1,0:T(8,128)S(1)} %get-tuple-element.39), channel_id=1, source_target_pairs={{0,4},{4,0},{8,12},{12,8},{1,5},{5,1},{9,13},{13,9},{2,6},{6,2},{1... | collective-permute-start | bytes 1179656 | tf_op jit(solution)/shard_map/ppermute | solution.py:522
  40.7 31.7 %collective-permute-start.4 = (f32[128,512]{1,0:T(8,128)S(1)}, f32[128,512]{1,0:T(8,128)S(1)}, u32[]{:S(2)}, u32[]{:S(2)}) collective-permute-start(f32[128,512]{1,0:T(8,128)S(1)} %forward.3.after), channel_id=1, source_target_pairs={{0,8},{4,12},{8,0},{12,4},{1,9},{5,13},{9,1},{13,5},{2,10},{6,14},... | collective-permute-start | bytes 786440 | tf_op jit(solution)/shard_map/ppermute | solution.py:522
  43.4 20.7 %collective-permute-start.3 = (f32[256,128]{1,0:T(8,128)S(1)}, f32[256,128]{1,0:T(8,128)S(1)}, u32[]{:S(2)}, u32[]{:S(2)}) collective-permute-start(f32[256,128]{1,0:T(8,128)S(1)} %get-tuple-element.41), channel_id=1, source_target_pairs={{0,4},{4,0},{8,12},{12,8},{1,5},{5,1},{9,13},{13,9},{2,6},{6,2},{1... | collective-permute-start | bytes 393224 | tf_op jit(solution)/shard_map/ppermute | solution.py:522
  58.5 13.6 %collective-permute-start.5 = (f32[128,384]{1,0:T(8,128)S(1)}, f32[128,384]{1,0:T(8,128)S(1)}, u32[]{:S(2)}, u32[]{:S(2)}) collective-permute-start(f32[128,384]{1,0:T(8,128)S(1)} %forward.4.after), channel_id=1, source_target_pairs={{0,8},{4,12},{8,0},{12,4},{1,9},{5,13},{9,1},{13,5},{2,10},{6,14},... | collective-permute-start | bytes 589832 | tf_op jit(solution)/shard_map/ppermute | solution.py:522
  64.7 7.7 %copy-start = (s32[1024]{0:T(1024)S(1)}, s32[1024]{0:T(1024)}, u32[]{:S(2)}) copy-start(s32[1024]{0:T(1024)} %param.11) | copy-start | bytes 12292
  64.7 7.6 %copy-start.1 = (f32[8]{0:T(128)S(1)}, f32[8]{0:T(128)}, u32[]{:S(2)}) copy-start(f32[8]{0:T(128)} %table.1) | copy-start | bytes 100
  64.7 7.6 %collective-permute-start.6 = (f32[128,128]{1,0:T(8,128)S(1)}, f32[128,128]{1,0:T(8,128)S(1)}, u32[]{:S(2)}, u32[]{:S(2)}) collective-permute-start(f32[128,128]{1,0:T(8,128)S(1)} %forward.5.after), channel_id=1, source_target_pairs={{0,8},{4,12},{8,0},{12,4},{1,9},{5,13},{9,1},{13,5},{2,10},{6,14},... | collective-permute-start | bytes 196616 | tf_op jit(solution)/shard_map/ppermute | solution.py:522
  73.2 3.7 %collective-permute-start.7 = (f32[16,128]{1,0:T(8,128)S(1)}, f32[16,128]{1,0:T(8,128)S(1)}, u32[]{:S(2)}, u32[]{:S(2)}) collective-permute-start(f32[16,128]{1,0:T(8,128)S(1)} %get-tuple-element.44.own.mine), channel_id=1, source_target_pairs={{0,2},{2,0},{1,3},{3,1},{4,6},{6,4},{5,7},{7,5},{8,10},{10,8},{9,1... | collective-permute-start | bytes 24584 | tf_op jit(solution)/shard_map/ppermute | solution.py:522
  77.6 12.0 %collective-permute-start.8 = (bf16[128,1024]{1,0:T(8,128)(2,1)S(1)}, bf16[128,1024]{1,0:T(8,128)(2,1)S(1)}, u32[]{:S(2)}, u32[]{:S(2)}) collective-permute-start(bf16[128,1024]{1,0:T(8,128)(2,1)S(1)} %weights.1.refs_0_), channel_id=1, source_target_pairs={{0,8},{4,12},{8,0},{12,4},{1,9},{5,13},{9,1},{13,5},{2,10},{6,14},... | collective-permute-start | bytes 786440 | tf_op jit(solution)/shard_map/ppermute | solution.py:522
  78.1 13.6 %collective-permute-start.13 = (bf16[128,1024]{1,0:T(8,128)(2,1)S(1)}, bf16[128,1024]{1,0:T(8,128)(2,1)S(1)}, u32[]{:S(2)}, u32[]{:S(2)}) collective-permute-start(bf16[128,1024]{1,0:T(8,128)(2,1)S(1)} %weights.1.refs_0_), channel_id=1, source_target_pairs={{0,4},{4,0},{8,12},{12,8},{1,5},{5,1},{9,13},{13,9},{2,6},{6,2},{1... | collective-permute-start | bytes 786440 | tf_op jit(solution)/shard_map/ppermute | solution.py:522
  89.7 7.4 %collective-permute-start.10 = (bf16[128,1024]{1,0:T(8,128)(2,1)S(1)}, bf16[128,1024]{1,0:T(8,128)(2,1)S(1)}, u32[]{:S(2)}, u32[]{:S(2)}) collective-permute-start(bf16[128,1024]{1,0:T(8,128)(2,1)S(1)} %collective-permute-done.8.refs_0_), channel_id=1, source_target_pairs={{0,4},{4,0},{8,12},{12,8},{1,5},{5,1},{9,13},{13,9},{2,6},{6,2},{1... | collective-permute-start | bytes 786440 | tf_op jit(solution)/shard_map/ppermute | solution.py:522
  89.7 7.4 %collective-permute-start.15 = (bf16[128,1024]{1,0:T(8,128)(2,1)S(1)}, bf16[128,1024]{1,0:T(8,128)(2,1)S(1)}, u32[]{:S(2)}, u32[]{:S(2)}) collective-permute-start(bf16[128,1024]{1,0:T(8,128)(2,1)S(1)} %weights.1.refs_0_), channel_id=1, source_target_pairs={{0,1},{1,0},{2,3},{3,2},{4,5},{5,4},{6,7},{7,6},{8,9},{9,8},{10,11... | collective-permute-start | bytes 786440 | tf_op jit(solution)/shard_map/ppermute | solution.py:522
  89.7 1.9 %collective-permute-start.12 = (f32[512,1]{1,0:T(8,128)S(1)}, f32[512,1]{1,0:T(8,128)S(1)}, u32[]{:S(2)}, u32[]{:S(2)}) collective-permute-start(f32[512,1]{1,0:T(8,128)S(1)} %copy.27.phi.after.refs_2_.refs_4_), channel_id=1, source_target_pairs={{0,1},{1,0},{2,3},{3,2},{4,5},{5,4},{6,7},{7,6},{8,9},{9,8},{10,11... | collective-permute-start | bytes 6152 | tf_op jit(solution)/shard_map/ppermute | solution.py:522
  91.6 23.7 %collective-permute-start.9 = (bf16[128,1024]{1,0:T(8,128)(2,1)S(1)}, bf16[128,1024]{1,0:T(8,128)(2,1)S(1)}, u32[]{:S(2)}, u32[]{:S(2)}) collective-permute-start(bf16[128,1024]{1,0:T(8,128)(2,1)S(1)} %collective-permute-done.8.refs_0_), channel_id=1, source_target_pairs={{0,1},{1,0},{2,3},{3,2},{4,5},{5,4},{6,7},{7,6},{8,9},{9,8},{10,11... | collective-permute-start | bytes 786440 | tf_op jit(solution)/shard_map/ppermute | solution.py:522
  91.7 14.5 %collective-permute-start.14 = (bf16[128,1024]{1,0:T(8,128)(2,1)S(1)}, bf16[128,1024]{1,0:T(8,128)(2,1)S(1)}, u32[]{:S(2)}, u32[]{:S(2)}) collective-permute-start(bf16[128,1024]{1,0:T(8,128)(2,1)S(1)} %collective-permute-done.13.refs_0_), channel_id=1, source_target_pairs={{0,1},{1,0},{2,3},{3,2},{4,5},{5,4},{6,7},{7,6},{8,9},{9,8},{10,11... | collective-permute-start | bytes 786440 | tf_op jit(solution)/shard_map/ppermute | solution.py:522
  97.1 18.1 %collective-permute-start.11 = (bf16[128,1024]{1,0:T(8,128)(2,1)S(1)}, bf16[128,1024]{1,0:T(8,128)(2,1)S(1)}, u32[]{:S(2)}, u32[]{:S(2)}) collective-permute-start(bf16[128,1024]{1,0:T(8,128)(2,1)S(1)} %collective-permute-done.10.refs_2_), channel_id=1, source_target_pairs={{0,1},{1,0},{2,3},{3,2},{4,5},{5,4},{6,7},{7,6},{8,9},{9,8},{10,11... | collective-permute-start | bytes 786440 | tf_op jit(solution)/shard_map/ppermute | solution.py:522

commit v9 on v8

--- a/solution.py
+++ b/solution.py
@@ -36,6 +36,51 @@
 
 def bit_reverse(value, bits):
     return sum(((value >> i) & 1) << (bits - 1 - i) for i in range(bits))
+
+
+EXPONENTS = range(-12, 21)
+
+
+def encoded(rows, tn):
+    return jax.ShapeDtypeStruct((rows * 3 // 4 + 8, tn), jnp.int32)
+
+
+def power_of_two(exponent, sign):
+    total = jnp.zeros(exponent.shape, jnp.float32)
+    for e in EXPONENTS:
+        total = total + jnp.where(exponent == e, 2.0 ** (sign * (e - 22)), 0.0)
+    return total
+
+
+def encode(values, out):
+    rows, tn = values.shape
+    n = rows // 4
+    top = jnp.max(jnp.max(jnp.abs(values), axis=0, keepdims=True), axis=1, keepdims=True)
+    top = jnp.broadcast_to(top, (8, 128))
+    exponent = jnp.full(top.shape, EXPONENTS[0], jnp.int32)
+    for e in EXPONENTS[:-1]:
+        exponent = exponent + jnp.where(top > 2.0**e, 1, 0)
+    factor = power_of_two(exponent, -1)[:1, :1]
+    code = (values * factor + 12582912.0).astype(jnp.int32) - 8388608
+    last = code[3 * n :, :]
+    for k in range(3):
+        part = jnp.bitwise_and(lax.shift_right_logical(last, 8 * k), 255)
+        out[k * n : (k + 1) * n, :] = jnp.bitwise_or(code[k * n : (k + 1) * n, :], lax.shift_left(part, 24))
+    out[3 * n :, :] = jnp.broadcast_to(exponent[:, :1], (8, tn))
+
+
+def decode(words, out):
+    rows = out.shape[0]
+    n = rows // 4
+    factor = power_of_two(words[3 * n :, :128], 1)[:1, :1]
+    last = None
+    for k in range(3):
+        word = words[k * n : (k + 1) * n, :]
+        code = jnp.bitwise_and(word, 16777215)
+        out[k * n : (k + 1) * n, :] = (code.astype(jnp.float32) - 4194304.0) * factor
+        high = lax.shift_left(lax.shift_right_logical(word, 24), 8 * k)
+        last = high if last is None else jnp.bitwise_or(last, high)
+    out[3 * n :, :] = (last.astype(jnp.float32) - 4194304.0) * factor
 
 
 def cross_kernel(where, phi, patterns, model, after, send, keep, *refs, column, tk, steps, beta, first, turns):
@@ -104,8 +149,8 @@
     sq = jnp.sum(squares[...], axis=0, keepdims=True)
     scale = phi[...]
     acc[...] = beta * (scale * acc[...] - 0.5 * (scale * scale) * sq)
-    half = send.shape[0]
-    send[...] = acc[pl.ds(pl.multiple_of((1 - where[0]) * half, half), half), :]
+    half = keep.shape[0]
+    encode(acc[pl.ds(pl.multiple_of((1 - where[0]) * half, half), half), :], send)
     keep[...] = acc[pl.ds(pl.multiple_of(where[0] * half, half), half), :]
     for i in range(max(0, steps - TURN), steps):
         for copy in stores(i):
@@ -116,7 +161,7 @@
     rows, depth = patterns.shape
     tk = min(2048, depth)
     half = rows // 2
-    shapes = [jax.ShapeDtypeStruct((half, tn), jnp.float32)] * 2
+    shapes = [encoded(half, tn), jax.ShapeDtypeStruct((half, tn), jnp.float32)]
     shapes += [pltpu.HBM((depth // 2, rows), patterns.dtype)] * len(turns)
     places = [VMEM, VMEM] + [HBM] * len(turns)
     scratch = [
@@ -148,29 +193,38 @@
     )(where, phi, patterns, model, after)
 
 
-def forward_kernel(where, after, *refs, base):
-    parts, out = refs[:-1], refs[-1]
-    size = out.shape[0]
+def forward_kernel(where, after, *refs, base, terms):
+    parts, out, decoded = refs[:terms], refs[terms], refs[terms + 1 :]
+    size = (out.shape[0] - 8) * 4 // 3
     total = None
     for t, part in enumerate(parts):
+        if t > 0:
+            decode(part, decoded[t - 1])
+            part = decoded[t - 1]
         piece = part[pl.ds(pl.multiple_of(where[base + t], size), size), :]
         total = piece if total is None else total + piece
-    out[...] = total
+    encode(total, out)
+
+
+def sizes_of(parts):
+    return [((p.shape[0] - 8) * 4 // 3, p.shape[1]) for p in parts]
 
 
 def forward(where, base, parts, size, after):
     return pl.pallas_call(
-        functools.partial(forward_kernel, base=base),
-        out_shape=jax.ShapeDtypeStruct((size, parts[0].shape[1]), jnp.float32),
+        functools.partial(forward_kernel, base=base, terms=len(parts)),
+        out_shape=encoded(size, parts[0].shape[1]),
         in_specs=[SMEM, ANY] + [VMEM] * len(parts),
         out_specs=VMEM,
-        compiler_params=params(4 * MIB),
+        scratch_shapes=[pltpu.VMEM(shape, jnp.float32) for shape in sizes_of(parts[1:])],
+        compiler_params=params(6 * MIB),
         name="forward",
     )(where, after, *parts)
 
 
 def softmax_kernel(where, table, classes, after, *refs, chunks, terms, base):
-    parts, (exps, stats) = refs[:-2], refs[-2:]
+    parts, refs = refs[: chunks * terms], refs[chunks * terms :]
+    exps, stats, decoded = refs[0], refs[1], refs[2:]
     count = exps.shape[0]
     logw = jnp.zeros(classes.shape, jnp.float32)
     for q in range(table.shape[0]):
@@ -181,7 +235,12 @@
         total = None
         for t in range(terms):
             rows = pl.ds(pl.multiple_of(where[base + t], count), count)
-            part = parts[c * terms + t][rows, :]
+            part = parts[c * terms + t]
+            if t > 0:
+                room = decoded[c * (terms - 1) + t - 1]
+                decode(part, room)
+                part = room
+            part = part[rows, :]
             total = part if total is None else total + part
         exps[:, at : at + tn] = total + logw[:, at : at + tn]
         at += tn
@@ -204,6 +263,11 @@
         ),
         in_specs=[SMEM, SMEM, VMEM, ANY] + [VMEM] * len(parts),
         out_specs=(VMEM, VMEM),
+        scratch_shapes=[
+            pltpu.VMEM(shape, jnp.float32)
+            for c in range(chunks)
+            for shape in sizes_of(parts[c * terms + 1 : (c + 1) * terms])
+        ],
         compiler_params=params(6 * MIB),
         name="softmax",
     )(where, table, classes, after, *parts)
@@ -529,7 +593,7 @@
     count = rows // pix
     tn = min(256, columns)
     chunks = columns // tn
-    widths = [columns // 2, columns * 3 // 8, columns // 8] if chunks >= 4 else [tn] * chunks
+    widths = [columns // 2, columns // 4, columns // 4] if chunks >= 4 else [tn] * chunks
     starts = [sum(widths[:c]) for c in range(len(widths))]
     chunks = len(widths)
     beta = (patterns.shape[1] * pix) ** -0.5

time: 131 us -> 123 us (0.939)
  waiting for transfers between devices: 30.9 us -> 24.6 us
  Pallas kernels: 82 us -> 79 us
    ppermute x16, waiting for transfers between devices: 30.9 us -> 24.6 us  [exchange(): return lax.ppermute(value, axis, [(i, i ^ distance) for i in range(size)])]
    pallas_call x3, Pallas kernels: 35.4 us -> 31.5 us  [cross_chunk(): pl.pallas_call(functools.partial(cross_kernel, column=column, tk=tk, step...]
  transfers between devices with their start and end apart: 16 -> 16, of which waited for: 6 -> 7; matrix products, arithmetic and copies ran while one was open for 0% -> 0% of each run, Pallas kernels for 34% -> 33%
where the time goes in v9:
time: 123 us
  Pallas kernels  79 us (64%)
  waiting for transfers between devices  24.6 us (20%)
  starting transfers between devices  17.7 us (14%)
    pallas_call x3, Pallas kernels, numer_pass(): pl.pallas_call(functools.partial(pass_kernel, blocks=blocks, pix=pix, fir...  33 us
    pallas_call x3, Pallas kernels, cross_chunk(): pl.pallas_call(functools.partial(cross_kernel, column=column, tk=tk, step...  31.5 us
    ppermute x16, waiting for transfers between devices, exchange(): return lax.ppermute(value, axis, [(i, i ^ distance) for i in range(size)])  24.6 us
    ppermute x16, starting transfers between devices, exchange(): return lax.ppermute(value, axis, [(i, i ^ distance) for i in range(size)])  17.7 us
    pallas_call x2, Pallas kernels, begin(): pl.pallas_call(functools.partial(begin_kernel, side=1, tm=tm, start=start...  9.94 us
    pallas_call x3, Pallas kernels, forward(): pl.pallas_call(functools.partial(forward_kernel, base=base, terms=len(par...  2.58 us
  transfers between devices with their start and end apart: 16, of which 7 were waited for; matrix products, arithmetic and copies ran while one was open for 0% of the time, Pallas kernels for 33%

profile of v9, /device:TPU:0, one launch (start us, length us, event | category | flops | bytes accessed | tf_op | source)
XLA Modules:
  0.0 122.5 jit_solution(15069329340481163978)
XLA Ops:
  0.0 0.8 select_reduce_fusion
  0.8 0.1 copy.27.phi.after.refs_2_.refs_4_
  0.9 0.1 stack.38.where
  1.0 13.7 %cross.3 = (s32[200,512]{1,0:T(8,128)S(1)}, f32[256,512]{1,0:T(8,128)S(1)}, bf16[512,16384]{1,0:T(8,128)(2,1)S(1)}) custom-call(s32[12]{0:T(128)S(1)} %stack.38.where, f32[512,1]{1,0:T(8,128)S(1)} %copy.27.phi.after.refs_2_.refs_4_, bf16[512,16384]{1,0:T(8,128)(2,1)} %patterns.1, bf16[16384,1024]{1,0:T(8,128)(2,1)} %model.9, ...), custom_call_target="tpu_custom_call" | custom-call | flops 8589934592 | bytes 33554432 | tf_op jit(solution)/shard_map/cross/pallas_call | solution.py:182
  14.7 3.1 %collective-permute-start = (s32[200,512]{1,0:T(8,128)S(1)}, s32[200,512]{1,0:T(8,128)S(1)}, u32[]{:S(2)}, u32[]{:S(2)}) collective-permute-start(s32[200,512]{1,0:T(8,128)S(1)} %get-tuple-element.36), channel_id=1, source_target_pairs={{0,4},{4,0},{8,12},{12,8},{1,5},{5,1},{9,13},{13,9},{2,6},{6,2},{1... | collective-permute-start | bytes 1228808 | tf_op jit(solution)/shard_map/ppermute | solution.py:586
  17.8 9.0 %cross.4 = (s32[200,256]{1,0:T(8,128)S(1)}, f32[256,256]{1,0:T(8,128)S(1)}, bf16[8192,512]{1,0:T(8,128)(2,1)}) custom-call(s32[12]{0:T(128)S(1)} %stack.38.where, f32[512,1]{1,0:T(8,128)S(1)} %copy.27.phi.after.refs_2_.refs_4_, bf16[512,16384]{1,0:T(8,128)(2,1)S(1)} %get-tuple-element.32.patterns, bf16[16384,1024]{1,0:T(8,128)(2,1)} %model.9, ...), custom_call_target="tpu_custom_call" | custom-call | flops 4294967296 | bytes 25165824 | tf_op jit(solution)/shard_map/cross/pallas_call | solution.py:182
  26.8 0.5 collective-permute-done.refs_1_
  27.3 0.9 forward.3.after
  28.2 8.9 %cross.5 = (s32[200,256]{1,0:T(8,128)S(1)}, f32[256,256]{1,0:T(8,128)S(1)}, bf16[8192,512]{1,0:T(8,128)(2,1)}) custom-call(s32[12]{0:T(128)S(1)} %stack.38.where, f32[512,1]{1,0:T(8,128)S(1)} %copy.27.phi.after.refs_2_.refs_4_, bf16[512,16384]{1,0:T(8,128)(2,1)S(1)} %get-tuple-element.32.patterns, bf16[16384,1024]{1,0:T(8,128)(2,1)} %model.9, ...), custom_call_target="tpu_custom_call" | custom-call | flops 4294967296 | bytes 25165824 | tf_op jit(solution)/shard_map/cross/pallas_call | solution.py:182
  37.1 0.1 collective-permute-start.1
  37.2 1.8 %collective-permute-start.2 = (s32[200,256]{1,0:T(8,128)S(1)}, s32[200,256]{1,0:T(8,128)S(1)}, u32[]{:S(2)}, u32[]{:S(2)}) collective-permute-start(s32[200,256]{1,0:T(8,128)S(1)} %get-tuple-element.39), channel_id=1, source_target_pairs={{0,4},{4,0},{8,12},{12,8},{1,5},{5,1},{9,13},{13,9},{2,6},{6,2},{1... | collective-permute-start | bytes 614408 | tf_op jit(solution)/shard_map/ppermute | solution.py:586
  39.0 0.3 collective-permute-start.3
  39.3 2.7 %collective-permute-start.4 = (s32[104,512]{1,0:T(8,128)S(1)}, s32[104,512]{1,0:T(8,128)S(1)}, u32[]{:S(2)}, u32[]{:S(2)}) collective-permute-start(s32[104,512]{1,0:T(8,128)S(1)} %forward.3.after), channel_id=1, source_target_pairs={{0,8},{4,12},{8,0},{12,4},{1,9},{5,13},{9,1},{13,5},{2,10},{6,14},... | collective-permute-start | bytes 638984 | tf_op jit(solution)/shard_map/ppermute | solution.py:586
  42.0 7.7 %collective-permute-done.2.refs_1_.refs_4_ = s32[200,256]{1,0:T(8,128)S(1)} collective-permute-done((s32[200,256]{1,0:T(8,128)S(1)}, s32[200,256]{1,0:T(8,128)S(1)}, u32[]{:S(2)}, u32[]{:S(2)}) %collective-permute-start.2) | collective-permute-done | bytes 204832 | tf_op jit(solution)/shard_map/ppermute | solution.py:586
  49.8 0.8 forward.4.after
  50.6 1.9 %collective-permute-start.5 = (s32[104,256]{1,0:T(8,128)S(1)}, s32[104,256]{1,0:T(8,128)S(1)}, u32[]{:S(2)}, u32[]{:S(2)}) collective-permute-start(s32[104,256]{1,0:T(8,128)S(1)} %forward.4.after), channel_id=1, source_target_pairs={{0,8},{4,12},{8,0},{12,4},{1,9},{5,13},{9,1},{13,5},{2,10},{6,14},... | collective-permute-start | bytes 319496 | tf_op jit(solution)/shard_map/ppermute | solution.py:586
  52.5 5.0 %begin.2 = (f32[2048,1024]{1,0:T(8,128)S(1)}, f32[2048,1024]{1,0:T(8,128)S(1)}, f32[8,128]{1,0:T(8,128)S(1)}) custom-call(s32[12]{0:T(128)S(1)} %stack.38.where, bf16[16384,1024]{1,0:T(8,128)(2,1)} %model.9, s32[104,256]{1,0:T(8,128)S(1)} %forward.4.after), custom_call_target="tpu_custom_call" | custom-call | tf_op jit(solution)/shard_map/begin/pallas_call | solution.py:387
  57.5 0.0 collective-permute-done.3.refs_1_.refs_7_
  57.5 0.8 forward.5.after
  58.4 0.0 copy-start
  58.4 0.0 copy-start.1
  58.4 1.1 collective-permute-start.6
  59.5 5.0 %begin.3 = (f32[2048,1024]{1,0:T(8,128)S(1)}, f32[2048,1024]{1,0:T(8,128)S(1)}, f32[8,128]{1,0:T(8,128)S(1)}) custom-call(s32[12]{0:T(128)S(1)} %stack.38.where, bf16[16384,1024]{1,0:T(8,128)(2,1)} %model.9, s32[104,256]{1,0:T(8,128)S(1)} %forward.5.after), custom_call_target="tpu_custom_call" | custom-call | tf_op jit(solution)/shard_map/begin/pallas_call | solution.py:387
  64.5 0.0 collective-permute-done.5.refs_5_
  64.5 0.0 collective-permute-done.4.refs_2_
  64.5 0.4 collective-permute-done.6.refs_8_
  64.9 0.0 copy-done
  64.9 0.0 copy-done.1
  64.9 1.2 softmax.1
  66.1 1.5 %collective-permute-start.7 = (f32[16,128]{1,0:T(8,128)S(1)}, f32[16,128]{1,0:T(8,128)S(1)}, u32[]{:S(2)}, u32[]{:S(2)}) collective-permute-start(f32[16,128]{1,0:T(8,128)S(1)} %get-tuple-element.44.own.mine), channel_id=1, source_target_pairs={{0,2},{2,0},{1,3},{3,1},{4,6},{6,4},{5,7},{7,5},{8,10},{10,8},{9,1... | collective-permute-start | bytes 24584 | tf_op jit(solution)/shard_map/ppermute | solution.py:586
  67.7 2.2 %collective-permute-done.7.other = f32[16,128]{1,0:T(8,128)S(1)} collective-permute-done((f32[16,128]{1,0:T(8,128)S(1)}, f32[16,128]{1,0:T(8,128)S(1)}, u32[]{:S(2)}, u32[]{:S(2)}) %collective-permute-start.7) | collective-permute-done | bytes 8224 | tf_op jit(solution)/shard_map/ppermute | solution.py:586
  69.8 0.7 weights.1.refs_0_
  70.6 1.6 %collective-permute-start.8 = (bf16[128,1024]{1,0:T(8,128)(2,1)S(1)}, bf16[128,1024]{1,0:T(8,128)(2,1)S(1)}, u32[]{:S(2)}, u32[]{:S(2)}) collective-permute-start(bf16[128,1024]{1,0:T(8,128)(2,1)S(1)} %weights.1.refs_0_), channel_id=1, source_target_pairs={{0,8},{4,12},{8,0},{12,4},{1,9},{5,13},{9,1},{13,5},{2,10},{6,14},... | collective-permute-start | bytes 786440 | tf_op jit(solution)/shard_map/ppermute | solution.py:586
  72.1 2.5 %collective-permute-start.13 = (bf16[128,1024]{1,0:T(8,128)(2,1)S(1)}, bf16[128,1024]{1,0:T(8,128)(2,1)S(1)}, u32[]{:S(2)}, u32[]{:S(2)}) collective-permute-start(bf16[128,1024]{1,0:T(8,128)(2,1)S(1)} %weights.1.refs_0_), channel_id=1, source_target_pairs={{0,4},{4,0},{8,12},{12,8},{1,5},{5,1},{9,13},{13,9},{2,6},{6,2},{1... | collective-permute-start | bytes 786440 | tf_op jit(solution)/shard_map/ppermute | solution.py:586
  74.6 7.9 %collective-permute-done.8.refs_0_ = bf16[128,1024]{1,0:T(8,128)(2,1)S(1)} collective-permute-done((bf16[128,1024]{1,0:T(8,128)(2,1)S(1)}, bf16[128,1024]{1,0:T(8,128)(2,1)S(1)}, u32[]{:S(2)}, u32[]{:S(2)}) %collective-permute-start.8) | collective-permute-done | bytes 262176 | tf_op jit(solution)/shard_map/ppermute | solution.py:586
  82.5 0.0 collective-permute-start.10
  82.5 0.0 collective-permute-start.15
  82.5 0.5 collective-permute-start.12
  83.0 1.4 %collective-permute-done.12.refs_3_.refs_5_ = f32[512,1]{1,0:T(8,128)S(1)} collective-permute-done((f32[512,1]{1,0:T(8,128)S(1)}, f32[512,1]{1,0:T(8,128)S(1)}, u32[]{:S(2)}, u32[]{:S(2)}) %collective-permute-start.12) | collective-permute-done | bytes 2080 | tf_op jit(solution)/shard_map/ppermute | solution.py:586
  84.4 0.1 collective-permute-start.9
  84.5 0.0 collective-permute-done.13.refs_0_
  84.5 0.4 collective-permute-start.14
  84.9 4.5 %collective-permute-done.10.refs_2_ = bf16[128,1024]{1,0:T(8,128)(2,1)S(1)} collective-permute-done((bf16[128,1024]{1,0:T(8,128)(2,1)S(1)}, bf16[128,1024]{1,0:T(8,128)(2,1)S(1)}, u32[]{:S(2)}, u32[]{:S(2)}) %collective-permute-start.10) | collective-permute-done | bytes 262176 | tf_op jit(solution)/shard_map/ppermute | solution.py:586
  89.4 0.0 collective-permute-start.11
  89.4 0.0 collective-permute-done.15.refs_1_
  89.4 0.0 collective-permute-done.1.psib
  89.5 8.9 %numer.3 = (f32[2048,1024]{1,0:T(8,128)S(1)}, f32[2048,1024]{1,0:T(8,128)S(1)}, f32[2048,1024]{1,0:T(8,128)S(1)}, f32[2048,1024]{1,0:T(8,128)S(1)}, f32[1,1024]{1,0:T(1,128)S(1)}) custom-call(s32[12]{0:T(128)S(1)} %stack.38.where, ...), custom_call_target="tpu_custom_call", output_to_operand_aliasing={{0}: (7, {}), {1}: (8, {}), {2}: (9, {}), {3}: (10, {})} | custom-call | flops 4294967296 | bytes 33554432 | tf_op jit(solution)/shard_map/numer/pallas_call | solution.py:491
  98.4 0.0 collective-permute-done.14.refs_1_
  98.4 8.9 %numer.4 = (f32[2048,1024]{1,0:T(8,128)S(1)}, f32[2048,1024]{1,0:T(8,128)S(1)}, f32[2048,1024]{1,0:T(8,128)S(1)}, f32[2048,1024]{1,0:T(8,128)S(1)}, f32[1,1024]{1,0:T(1,128)S(1)}) custom-call(s32[12]{0:T(128)S(1)} %stack.38.where, ...), custom_call_target="tpu_custom_call", output_to_operand_aliasing={{0}: (8, {}), {1}: (9, {}), {2}: (10, {}), {3}: (11, {})} | custom-call | flops 4294967296 | bytes 33554432 | tf_op jit(solution)/shard_map/numer/pallas_call | solution.py:491
  107.3 0.0 collective-permute-done.9.refs_1_
  107.3 0.0 collective-permute-done.11.refs_3_
  107.3 15.2 %numer.5 = bf16[8192,1024]{1,0:T(8,128)(2,1)} custom-call(s32[12]{0:T(128)S(1)} %stack.38.where, bf16[8192,512]{1,0:T(8,128)(2,1)} %get-tuple-element.33.pown, bf16[8192,512]{1,0:T(8,128)(2,1)} %collective-permute-done.1.psib, bf16[128,1024]{1,0:T(8,128)(2,1)S(1)} %collective-permute-done.8.refs_0_, bf16[128,1024]{1,0:T(8,128)(2,1)S(1)} %collective-permute-done.9.refs_1_, ...), custom_call_target="tpu_custom_call" | custom-call | flops 8589934592 | bytes 33554432 | tf_op jit(solution)/shard_map/numer/pallas_call | solution.py:491
Async XLA Ops:
  14.7 12.6 %collective-permute-start = (s32[200,512]{1,0:T(8,128)S(1)}, s32[200,512]{1,0:T(8,128)S(1)}, u32[]{:S(2)}, u32[]{:S(2)}) collective-permute-start(s32[200,512]{1,0:T(8,128)S(1)} %get-tuple-element.36), channel_id=1, source_target_pairs={{0,4},{4,0},{8,12},{12,8},{1,5},{5,1},{9,13},{13,9},{2,6},{6,2},{1... | collective-permute-start | bytes 1228808 | tf_op jit(solution)/shard_map/ppermute | solution.py:586
  37.1 52.3 %collective-permute-start.1 = (bf16[8192,512]{1,0:T(8,128)(2,1)}, bf16[8192,512]{1,0:T(8,128)(2,1)}, u32[]{:S(2)}, u32[]{:S(2)}) collective-permute-start(bf16[8192,512]{1,0:T(8,128)(2,1)} %get-tuple-element.37), channel_id=1, source_target_pairs={{0,1},{1,0},{2,3},{3,2},{4,5},{5,4},{6,7},{7,6},{8,9},{9,8},{10,11... | collective-permute-start | bytes 25165832 | tf_op jit(solution)/shard_map/ppermute | solution.py:586
  37.2 12.6 %collective-permute-start.2 = (s32[200,256]{1,0:T(8,128)S(1)}, s32[200,256]{1,0:T(8,128)S(1)}, u32[]{:S(2)}, u32[]{:S(2)}) collective-permute-start(s32[200,256]{1,0:T(8,128)S(1)} %get-tuple-element.39), channel_id=1, source_target_pairs={{0,4},{4,0},{8,12},{12,8},{1,5},{5,1},{9,13},{13,9},{2,6},{6,2},{1... | collective-permute-start | bytes 614408 | tf_op jit(solution)/shard_map/ppermute | solution.py:586
  39.0 18.5 %collective-permute-start.3 = (s32[200,256]{1,0:T(8,128)S(1)}, s32[200,256]{1,0:T(8,128)S(1)}, u32[]{:S(2)}, u32[]{:S(2)}) collective-permute-start(s32[200,256]{1,0:T(8,128)S(1)} %get-tuple-element.41), channel_id=1, source_target_pairs={{0,4},{4,0},{8,12},{12,8},{1,5},{5,1},{9,13},{13,9},{2,6},{6,2},{1... | collective-permute-start | bytes 614408 | tf_op jit(solution)/shard_map/ppermute | solution.py:586
  39.3 25.2 %collective-permute-start.4 = (s32[104,512]{1,0:T(8,128)S(1)}, s32[104,512]{1,0:T(8,128)S(1)}, u32[]{:S(2)}, u32[]{:S(2)}) collective-permute-start(s32[104,512]{1,0:T(8,128)S(1)} %forward.3.after), channel_id=1, source_target_pairs={{0,8},{4,12},{8,0},{12,4},{1,9},{5,13},{9,1},{13,5},{2,10},{6,14},... | collective-permute-start | bytes 638984 | tf_op jit(solution)/shard_map/ppermute | solution.py:586
  50.6 13.9 %collective-permute-start.5 = (s32[104,256]{1,0:T(8,128)S(1)}, s32[104,256]{1,0:T(8,128)S(1)}, u32[]{:S(2)}, u32[]{:S(2)}) collective-permute-start(s32[104,256]{1,0:T(8,128)S(1)} %forward.4.after), channel_id=1, source_target_pairs={{0,8},{4,12},{8,0},{12,4},{1,9},{5,13},{9,1},{13,5},{2,10},{6,14},... | collective-permute-start | bytes 319496 | tf_op jit(solution)/shard_map/ppermute | solution.py:586
  58.4 6.6 %copy-start = (s32[1024]{0:T(1024)S(1)}, s32[1024]{0:T(1024)}, u32[]{:S(2)}) copy-start(s32[1024]{0:T(1024)} %param.11) | copy-start | bytes 12292
  58.4 6.5 %copy-start.1 = (f32[8]{0:T(128)S(1)}, f32[8]{0:T(128)}, u32[]{:S(2)}) copy-start(f32[8]{0:T(128)} %table.1) | copy-start | bytes 100
  58.4 6.5 %collective-permute-start.6 = (s32[104,256]{1,0:T(8,128)S(1)}, s32[104,256]{1,0:T(8,128)S(1)}, u32[]{:S(2)}, u32[]{:S(2)}) collective-permute-start(s32[104,256]{1,0:T(8,128)S(1)} %forward.5.after), channel_id=1, source_target_pairs={{0,8},{4,12},{8,0},{12,4},{1,9},{5,13},{9,1},{13,5},{2,10},{6,14},... | collective-permute-start | bytes 319496 | tf_op jit(solution)/shard_map/ppermute | solution.py:586
  66.1 3.7 %collective-permute-start.7 = (f32[16,128]{1,0:T(8,128)S(1)}, f32[16,128]{1,0:T(8,128)S(1)}, u32[]{:S(2)}, u32[]{:S(2)}) collective-permute-start(f32[16,128]{1,0:T(8,128)S(1)} %get-tuple-element.44.own.mine), channel_id=1, source_target_pairs={{0,2},{2,0},{1,3},{3,1},{4,6},{6,4},{5,7},{7,5},{8,10},{10,8},{9,1... | collective-permute-start | bytes 24584 | tf_op jit(solution)/shard_map/ppermute | solution.py:586
  70.6 11.9 %collective-permute-start.8 = (bf16[128,1024]{1,0:T(8,128)(2,1)S(1)}, bf16[128,1024]{1,0:T(8,128)(2,1)S(1)}, u32[]{:S(2)}, u32[]{:S(2)}) collective-permute-start(bf16[128,1024]{1,0:T(8,128)(2,1)S(1)} %weights.1.refs_0_), channel_id=1, source_target_pairs={{0,8},{4,12},{8,0},{12,4},{1,9},{5,13},{9,1},{13,5},{2,10},{6,14},... | collective-permute-start | bytes 786440 | tf_op jit(solution)/shard_map/ppermute | solution.py:586
  72.1 12.4 %collective-permute-start.13 = (bf16[128,1024]{1,0:T(8,128)(2,1)S(1)}, bf16[128,1024]{1,0:T(8,128)(2,1)S(1)}, u32[]{:S(2)}, u32[]{:S(2)}) collective-permute-start(bf16[128,1024]{1,0:T(8,128)(2,1)S(1)} %weights.1.refs_0_), channel_id=1, source_target_pairs={{0,4},{4,0},{8,12},{12,8},{1,5},{5,1},{9,13},{13,9},{2,6},{6,2},{1... | collective-permute-start | bytes 786440 | tf_op jit(solution)/shard_map/ppermute | solution.py:586
  82.5 7.0 %collective-permute-start.10 = (bf16[128,1024]{1,0:T(8,128)(2,1)S(1)}, bf16[128,1024]{1,0:T(8,128)(2,1)S(1)}, u32[]{:S(2)}, u32[]{:S(2)}) collective-permute-start(bf16[128,1024]{1,0:T(8,128)(2,1)S(1)} %collective-permute-done.8.refs_0_), channel_id=1, source_target_pairs={{0,4},{4,0},{8,12},{12,8},{1,5},{5,1},{9,13},{13,9},{2,6},{6,2},{1... | collective-permute-start | bytes 786440 | tf_op jit(solution)/shard_map/ppermute | solution.py:586
  82.5 7.0 %collective-permute-start.15 = (bf16[128,1024]{1,0:T(8,128)(2,1)S(1)}, bf16[128,1024]{1,0:T(8,128)(2,1)S(1)}, u32[]{:S(2)}, u32[]{:S(2)}) collective-permute-start(bf16[128,1024]{1,0:T(8,128)(2,1)S(1)} %weights.1.refs_0_), channel_id=1, source_target_pairs={{0,1},{1,0},{2,3},{3,2},{4,5},{5,4},{6,7},{7,6},{8,9},{9,8},{10,11... | collective-permute-start | bytes 786440 | tf_op jit(solution)/shard_map/ppermute | solution.py:586
  82.5 1.9 %collective-permute-start.12 = (f32[512,1]{1,0:T(8,128)S(1)}, f32[512,1]{1,0:T(8,128)S(1)}, u32[]{:S(2)}, u32[]{:S(2)}) collective-permute-start(f32[512,1]{1,0:T(8,128)S(1)} %copy.27.phi.after.refs_2_.refs_4_), channel_id=1, source_target_pairs={{0,1},{1,0},{2,3},{3,2},{4,5},{5,4},{6,7},{7,6},{8,9},{9,8},{10,11... | collective-permute-start | bytes 6152 | tf_op jit(solution)/shard_map/ppermute | solution.py:586
  84.4 22.9 %collective-permute-start.9 = (bf16[128,1024]{1,0:T(8,128)(2,1)S(1)}, bf16[128,1024]{1,0:T(8,128)(2,1)S(1)}, u32[]{:S(2)}, u32[]{:S(2)}) collective-permute-start(bf16[128,1024]{1,0:T(8,128)(2,1)S(1)} %collective-permute-done.8.refs_0_), channel_id=1, source_target_pairs={{0,1},{1,0},{2,3},{3,2},{4,5},{5,4},{6,7},{7,6},{8,9},{9,8},{10,11... | collective-permute-start | bytes 786440 | tf_op jit(solution)/shard_map/ppermute | solution.py:586
  84.5 13.9 %collective-permute-start.14 = (bf16[128,1024]{1,0:T(8,128)(2,1)S(1)}, bf16[128,1024]{1,0:T(8,128)(2,1)S(1)}, u32[]{:S(2)}, u32[]{:S(2)}) collective-permute-start(bf16[128,1024]{1,0:T(8,128)(2,1)S(1)} %collective-permute-done.13.refs_0_), channel_id=1, source_target_pairs={{0,1},{1,0},{2,3},{3,2},{4,5},{5,4},{6,7},{7,6},{8,9},{9,8},{10,11... | collective-permute-start | bytes 786440 | tf_op jit(solution)/shard_map/ppermute | solution.py:586
  89.4 17.9 %collective-permute-start.11 = (bf16[128,1024]{1,0:T(8,128)(2,1)S(1)}, bf16[128,1024]{1,0:T(8,128)(2,1)S(1)}, u32[]{:S(2)}, u32[]{:S(2)}) collective-permute-start(bf16[128,1024]{1,0:T(8,128)(2,1)S(1)} %collective-permute-done.10.refs_2_), channel_id=1, source_target_pairs={{0,1},{1,0},{2,3},{3,2},{4,5},{5,4},{6,7},{7,6},{8,9},{9,8},{10,11... | collective-permute-start | bytes 786440 | tf_op jit(solution)/shard_map/ppermute | solution.py:586

commit v10 on v9

--- a/solution.py
+++ b/solution.py
@@ -12,7 +12,6 @@
 SLOTS = 4
 PARTS = 4
 SUB = 256
-AHEAD = 6
 OUT = 4
 TURN = 3
 VMEM = pl.BlockSpec(memory_space=pltpu.VMEM)
@@ -397,7 +396,7 @@
     return total, token
 
 
-def pass_kernel(where, pown, psib, *refs, blocks, pix, first, last, base, tm, sub):
+def pass_kernel(where, pown, psib, *refs, blocks, pix, first, last, base, tm, sub, ahead):
     mine = 2 * len(blocks)
     count = pown.shape[1] // pix
     pixels = pown.shape[0]
@@ -410,14 +409,14 @@
         wide[k * count : (k + 1) * count, :] = pairs[k][...]
 
     def pieces(i):
-        slot = lax.rem(i, AHEAD)
+        slot = lax.rem(i, ahead)
         rows = pl.ds(pl.multiple_of(i * tm, tm), tm)
         for k in range(mine):
             columns = pl.ds(pl.multiple_of(where[base + blocks[k // 2]], count), count)
             part = (pown, psib)[k % 2].at[rows, columns]
             yield pltpu.make_async_copy(part, tiles.at[slot, :, pl.ds(k * count, count)], tsem.at[slot, k])
 
-    for i in range(min(AHEAD - 1, steps)):
+    for i in range(min(ahead - 1, steps)):
         for copy in pieces(i):
             copy.start()
     for k, part in enumerate(pairs):
@@ -438,9 +437,9 @@
         for copy in pieces(i):
             copy.wait()
 
-        @pl.when(i + AHEAD - 1 < steps)
+        @pl.when(i + ahead - 1 < steps)
         def _():
-            for copy in pieces(i + AHEAD - 1):
+            for copy in pieces(i + ahead - 1):
                 copy.start()
 
         if last:
@@ -451,7 +450,7 @@
 
         for r in range(0, tm, sub):
             rows = pl.ds(pl.multiple_of(i * tm + r - part * (pixels // PARTS), sub), sub)
-            dot = jnp.dot(tiles[lax.rem(i, AHEAD), r : r + sub, :], wide[...], preferred_element_type=jnp.float32)
+            dot = jnp.dot(tiles[lax.rem(i, ahead), r : r + sub, :], wide[...], preferred_element_type=jnp.float32)
             if last:
                 buf[lax.rem(i, OUT), r : r + sub, :] = ((dot + totals[part][rows, :]) * scale).astype(jnp.bfloat16)
             else:
@@ -470,7 +469,8 @@
 def numer_pass(where, base, pown, psib, blocks, pairs, phis, pix, total, den=None, last=False):
     first = den is None
     pixels, count, columns = pown.shape[0], pairs[0].shape[0], pairs[0].shape[1]
-    tm = min(512, pixels // PARTS)
+    tm = min(512 if last else 1024, pixels // PARTS)
+    ahead = 6 if last else 4
     constrain = pltpu.with_memory_space_constraint
     args = [where, constrain(pown, pltpu.HBM), constrain(psib, pltpu.HBM), *pairs, *phis]
     args += [] if first else [den]
@@ -478,8 +478,8 @@
     in_specs = [SMEM, HBM, HBM] + [VMEM] * (len(args) - 3)
     scratch = [
         pltpu.VMEM((len(pairs) * count, columns), jnp.bfloat16),
-        pltpu.VMEM((AHEAD, tm, len(pairs) * count), jnp.bfloat16),
-        pltpu.SemaphoreType.DMA((AHEAD, len(pairs))),
+        pltpu.VMEM((ahead, tm, len(pairs) * count), jnp.bfloat16),
+        pltpu.SemaphoreType.DMA((ahead, len(pairs))),
     ]
     if last:
         shape, out_specs, aliases = jax.ShapeDtypeStruct((pixels, columns), jnp.bfloat16), HBM, {}
@@ -490,7 +490,8 @@
         aliases = {len(args) - PARTS + part: part for part in range(PARTS)}
     result = pl.pallas_call(
         functools.partial(
-            pass_kernel, blocks=blocks, pix=pix, first=first, last=last, base=base, tm=tm, sub=min(SUB if last else 512, tm)
+            pass_kernel, blocks=blocks, pix=pix, first=first, last=last, base=base, tm=tm,
+            sub=min(SUB if last else 512, tm), ahead=ahead,
         ),
         out_shape=shape,
         in_specs=in_specs,

time: 123 us -> 121 us (0.984)
  Pallas kernels: 79 us -> 76.6 us
    pallas_call x3, Pallas kernels: 33 us -> 30.6 us  [numer_pass(): pl.pallas_call(functools.partial(pass_kernel, blocks=blocks, pix=pix, fir...]
  transfers between devices with their start and end apart: 16 -> 16, of which waited for: 7 -> 7; matrix products, arithmetic and copies ran while one was open for 0% -> 0% of each run, Pallas kernels for 33% -> 32%
where the time goes in v10:
time: 121 us; the launch traced here: 120 us
  Pallas kernels  76.6 us (63%)
  waiting for transfers between devices  24.6 us (20%)
  starting transfers between devices  17.7 us (15%)
    pallas_call x3, Pallas kernels, cross_chunk(): pl.pallas_call(functools.partial(cross_kernel, column=column, tk=tk, step...  31.5 us
    pallas_call x3, Pallas kernels, numer_pass(): pl.pallas_call(functools.partial(pass_kernel, blocks=blocks, pix=pix, fir...  30.6 us
    ppermute x16, waiting for transfers between devices, exchange(): return lax.ppermute(value, axis, [(i, i ^ distance) for i in range(size)])  24.6 us
    ppermute x16, starting transfers between devices, exchange(): return lax.ppermute(value, axis, [(i, i ^ distance) for i in range(size)])  17.7 us
    pallas_call x2, Pallas kernels, begin(): pl.pallas_call(functools.partial(begin_kernel, side=1, tm=tm, start=start...  9.94 us
    pallas_call x3, Pallas kernels, forward(): pl.pallas_call(functools.partial(forward_kernel, base=base, terms=len(par...  2.58 us
  transfers between devices with their start and end apart: 16, of which 7 were waited for; matrix products, arithmetic and copies ran while one was open for 0% of the time, Pallas kernels for 32%

profile of v10, /device:TPU:0, one launch (start us, length us, event | category | flops | bytes accessed | tf_op | source)
XLA Modules:
  0.0 120.3 jit_solution(10673712103284458514)
XLA Ops:
  0.0 0.8 select_reduce_fusion
  0.8 0.1 copy.27.phi.after.refs_2_.refs_4_
  0.9 0.1 stack.38.where
  1.0 13.7 %cross.3 = (s32[200,512]{1,0:T(8,128)S(1)}, f32[256,512]{1,0:T(8,128)S(1)}, bf16[512,16384]{1,0:T(8,128)(2,1)S(1)}) custom-call(s32[12]{0:T(128)S(1)} %stack.38.where, f32[512,1]{1,0:T(8,128)S(1)} %copy.27.phi.after.refs_2_.refs_4_, bf16[512,16384]{1,0:T(8,128)(2,1)} %patterns.1, bf16[16384,1024]{1,0:T(8,128)(2,1)} %model.9, ...), custom_call_target="tpu_custom_call" | custom-call | flops 8589934592 | bytes 33554432 | tf_op jit(solution)/shard_map/cross/pallas_call | solution.py:181
  14.7 3.1 %collective-permute-start = (s32[200,512]{1,0:T(8,128)S(1)}, s32[200,512]{1,0:T(8,128)S(1)}, u32[]{:S(2)}, u32[]{:S(2)}) collective-permute-start(s32[200,512]{1,0:T(8,128)S(1)} %get-tuple-element.36), channel_id=1, source_target_pairs={{0,4},{4,0},{8,12},{12,8},{1,5},{5,1},{9,13},{13,9},{2,6},{6,2},{1... | collective-permute-start | bytes 1228808 | tf_op jit(solution)/shard_map/ppermute | solution.py:587
  17.8 9.0 %cross.4 = (s32[200,256]{1,0:T(8,128)S(1)}, f32[256,256]{1,0:T(8,128)S(1)}, bf16[8192,512]{1,0:T(8,128)(2,1)}) custom-call(s32[12]{0:T(128)S(1)} %stack.38.where, f32[512,1]{1,0:T(8,128)S(1)} %copy.27.phi.after.refs_2_.refs_4_, bf16[512,16384]{1,0:T(8,128)(2,1)S(1)} %get-tuple-element.32.patterns, bf16[16384,1024]{1,0:T(8,128)(2,1)} %model.9, ...), custom_call_target="tpu_custom_call" | custom-call | flops 4294967296 | bytes 25165824 | tf_op jit(solution)/shard_map/cross/pallas_call | solution.py:181
  26.8 0.5 collective-permute-done.refs_1_
  27.3 0.9 forward.3.after
  28.2 8.9 %cross.5 = (s32[200,256]{1,0:T(8,128)S(1)}, f32[256,256]{1,0:T(8,128)S(1)}, bf16[8192,512]{1,0:T(8,128)(2,1)}) custom-call(s32[12]{0:T(128)S(1)} %stack.38.where, f32[512,1]{1,0:T(8,128)S(1)} %copy.27.phi.after.refs_2_.refs_4_, bf16[512,16384]{1,0:T(8,128)(2,1)S(1)} %get-tuple-element.32.patterns, bf16[16384,1024]{1,0:T(8,128)(2,1)} %model.9, ...), custom_call_target="tpu_custom_call" | custom-call | flops 4294967296 | bytes 25165824 | tf_op jit(solution)/shard_map/cross/pallas_call | solution.py:181
  37.1 0.1 collective-permute-start.1
  37.2 1.8 %collective-permute-start.2 = (s32[200,256]{1,0:T(8,128)S(1)}, s32[200,256]{1,0:T(8,128)S(1)}, u32[]{:S(2)}, u32[]{:S(2)}) collective-permute-start(s32[200,256]{1,0:T(8,128)S(1)} %get-tuple-element.39), channel_id=1, source_target_pairs={{0,4},{4,0},{8,12},{12,8},{1,5},{5,1},{9,13},{13,9},{2,6},{6,2},{1... | collective-permute-start | bytes 614408 | tf_op jit(solution)/shard_map/ppermute | solution.py:587
  39.0 0.3 collective-permute-start.3
  39.3 2.8 %collective-permute-start.4 = (s32[104,512]{1,0:T(8,128)S(1)}, s32[104,512]{1,0:T(8,128)S(1)}, u32[]{:S(2)}, u32[]{:S(2)}) collective-permute-start(s32[104,512]{1,0:T(8,128)S(1)} %forward.3.after), channel_id=1, source_target_pairs={{0,8},{4,12},{8,0},{12,4},{1,9},{5,13},{9,1},{13,5},{2,10},{6,14},... | collective-permute-start | bytes 638984 | tf_op jit(solution)/shard_map/ppermute | solution.py:587
  42.1 7.7 %collective-permute-done.2.refs_1_.refs_4_ = s32[200,256]{1,0:T(8,128)S(1)} collective-permute-done((s32[200,256]{1,0:T(8,128)S(1)}, s32[200,256]{1,0:T(8,128)S(1)}, u32[]{:S(2)}, u32[]{:S(2)}) %collective-permute-start.2) | collective-permute-done | bytes 204832 | tf_op jit(solution)/shard_map/ppermute | solution.py:587
  49.8 0.8 forward.4.after
  50.6 1.9 %collective-permute-start.5 = (s32[104,256]{1,0:T(8,128)S(1)}, s32[104,256]{1,0:T(8,128)S(1)}, u32[]{:S(2)}, u32[]{:S(2)}) collective-permute-start(s32[104,256]{1,0:T(8,128)S(1)} %forward.4.after), channel_id=1, source_target_pairs={{0,8},{4,12},{8,0},{12,4},{1,9},{5,13},{9,1},{13,5},{2,10},{6,14},... | collective-permute-start | bytes 319496 | tf_op jit(solution)/shard_map/ppermute | solution.py:587
  52.5 5.0 %begin.2 = (f32[2048,1024]{1,0:T(8,128)S(1)}, f32[2048,1024]{1,0:T(8,128)S(1)}, f32[8,128]{1,0:T(8,128)S(1)}) custom-call(s32[12]{0:T(128)S(1)} %stack.38.where, bf16[16384,1024]{1,0:T(8,128)(2,1)} %model.9, s32[104,256]{1,0:T(8,128)S(1)} %forward.4.after), custom_call_target="tpu_custom_call" | custom-call | tf_op jit(solution)/shard_map/begin/pallas_call | solution.py:386
  57.5 0.0 collective-permute-done.3.refs_1_.refs_7_
  57.5 0.8 forward.5.after
  58.3 0.0 copy-start
  58.4 0.0 copy-start.1
  58.4 1.1 collective-permute-start.6
  59.5 5.0 %begin.3 = (f32[2048,1024]{1,0:T(8,128)S(1)}, f32[2048,1024]{1,0:T(8,128)S(1)}, f32[8,128]{1,0:T(8,128)S(1)}) custom-call(s32[12]{0:T(128)S(1)} %stack.38.where, bf16[16384,1024]{1,0:T(8,128)(2,1)} %model.9, s32[104,256]{1,0:T(8,128)S(1)} %forward.5.after), custom_call_target="tpu_custom_call" | custom-call | tf_op jit(solution)/shard_map/begin/pallas_call | solution.py:386
  64.5 0.0 collective-permute-done.5.refs_5_
  64.5 0.0 collective-permute-done.4.refs_2_
  64.5 0.4 collective-permute-done.6.refs_8_
  64.9 0.0 copy-done
  64.9 0.0 copy-done.1
  64.9 1.2 %softmax.1 = (f32[128,1024]{1,0:T(8,128)S(1)}, f32[16,128]{1,0:T(8,128)S(1)}) custom-call(s32[12]{0:T(128)S(1)} %stack.38.where, f32[8]{0:T(128)S(1)} %copy-done.1, s32[1,1024]{1,0:T(1,128)S(1)} %bitcast.10, f32[8,128]{1,0:T(8,128)S(1)} %get-tuple-element.42.after, f32[256,512]{1,0:T(8,128)S(1)} %get-tuple-element.35.refs_0_, ...), custom_call_target="tpu_custom_call" | custom-call | tf_op jit(solution)/shard_map/softmax/pallas_call | solution.py:257
  66.1 1.5 %collective-permute-start.7 = (f32[16,128]{1,0:T(8,128)S(1)}, f32[16,128]{1,0:T(8,128)S(1)}, u32[]{:S(2)}, u32[]{:S(2)}) collective-permute-start(f32[16,128]{1,0:T(8,128)S(1)} %get-tuple-element.44.own.mine), channel_id=1, source_target_pairs={{0,2},{2,0},{1,3},{3,1},{4,6},{6,4},{5,7},{7,5},{8,10},{10,8},{9,1... | collective-permute-start | bytes 24584 | tf_op jit(solution)/shard_map/ppermute | solution.py:587
  67.7 2.2 %collective-permute-done.7.other = f32[16,128]{1,0:T(8,128)S(1)} collective-permute-done((f32[16,128]{1,0:T(8,128)S(1)}, f32[16,128]{1,0:T(8,128)S(1)}, u32[]{:S(2)}, u32[]{:S(2)}) %collective-permute-start.7) | collective-permute-done | bytes 8224 | tf_op jit(solution)/shard_map/ppermute | solution.py:587
  69.8 0.7 weights.1.refs_0_
  70.6 1.6 %collective-permute-start.8 = (bf16[128,1024]{1,0:T(8,128)(2,1)S(1)}, bf16[128,1024]{1,0:T(8,128)(2,1)S(1)}, u32[]{:S(2)}, u32[]{:S(2)}) collective-permute-start(bf16[128,1024]{1,0:T(8,128)(2,1)S(1)} %weights.1.refs_0_), channel_id=1, source_target_pairs={{0,8},{4,12},{8,0},{12,4},{1,9},{5,13},{9,1},{13,5},{2,10},{6,14},... | collective-permute-start | bytes 786440 | tf_op jit(solution)/shard_map/ppermute | solution.py:587
  72.1 2.5 %collective-permute-start.13 = (bf16[128,1024]{1,0:T(8,128)(2,1)S(1)}, bf16[128,1024]{1,0:T(8,128)(2,1)S(1)}, u32[]{:S(2)}, u32[]{:S(2)}) collective-permute-start(bf16[128,1024]{1,0:T(8,128)(2,1)S(1)} %weights.1.refs_0_), channel_id=1, source_target_pairs={{0,4},{4,0},{8,12},{12,8},{1,5},{5,1},{9,13},{13,9},{2,6},{6,2},{1... | collective-permute-start | bytes 786440 | tf_op jit(solution)/shard_map/ppermute | solution.py:587
  74.6 7.9 %collective-permute-done.8.refs_0_ = bf16[128,1024]{1,0:T(8,128)(2,1)S(1)} collective-permute-done((bf16[128,1024]{1,0:T(8,128)(2,1)S(1)}, bf16[128,1024]{1,0:T(8,128)(2,1)S(1)}, u32[]{:S(2)}, u32[]{:S(2)}) %collective-permute-start.8) | collective-permute-done | bytes 262176 | tf_op jit(solution)/shard_map/ppermute | solution.py:587
  82.5 0.0 collective-permute-start.10
  82.5 0.0 collective-permute-start.15
  82.5 0.5 collective-permute-start.12
  83.0 1.4 %collective-permute-done.12.refs_3_.refs_5_ = f32[512,1]{1,0:T(8,128)S(1)} collective-permute-done((f32[512,1]{1,0:T(8,128)S(1)}, f32[512,1]{1,0:T(8,128)S(1)}, u32[]{:S(2)}, u32[]{:S(2)}) %collective-permute-start.12) | collective-permute-done | bytes 2080 | tf_op jit(solution)/shard_map/ppermute | solution.py:587
  84.4 0.1 collective-permute-start.9
  84.5 0.0 collective-permute-done.13.refs_0_
  84.5 0.4 collective-permute-start.14
  84.9 4.6 %collective-permute-done.10.refs_2_ = bf16[128,1024]{1,0:T(8,128)(2,1)S(1)} collective-permute-done((bf16[128,1024]{1,0:T(8,128)(2,1)S(1)}, bf16[128,1024]{1,0:T(8,128)(2,1)S(1)}, u32[]{:S(2)}, u32[]{:S(2)}) %collective-permute-start.10) | collective-permute-done | bytes 262176 | tf_op jit(solution)/shard_map/ppermute | solution.py:587
  89.5 0.0 collective-permute-start.11
  89.5 0.0 collective-permute-done.15.refs_1_
  89.5 0.0 collective-permute-done.1.psib
  89.5 7.6 %numer.3 = (f32[2048,1024]{1,0:T(8,128)S(1)}, f32[2048,1024]{1,0:T(8,128)S(1)}, f32[2048,1024]{1,0:T(8,128)S(1)}, f32[2048,1024]{1,0:T(8,128)S(1)}, f32[1,1024]{1,0:T(1,128)S(1)}) custom-call(s32[12]{0:T(128)S(1)} %stack.38.where, ...), custom_call_target="tpu_custom_call", output_to_operand_aliasing={{0}: (7, {}), {1}: (8, {}), {2}: (9, {}), {3}: (10, {})} | custom-call | flops 4294967296 | bytes 33554432 | tf_op jit(solution)/shard_map/numer/pallas_call | solution.py:491
  97.1 0.0 collective-permute-done.14.refs_1_
  97.1 7.8 %numer.4 = (f32[2048,1024]{1,0:T(8,128)S(1)}, f32[2048,1024]{1,0:T(8,128)S(1)}, f32[2048,1024]{1,0:T(8,128)S(1)}, f32[2048,1024]{1,0:T(8,128)S(1)}, f32[1,1024]{1,0:T(1,128)S(1)}) custom-call(s32[12]{0:T(128)S(1)} %stack.38.where, ...), custom_call_target="tpu_custom_call", output_to_operand_aliasing={{0}: (8, {}), {1}: (9, {}), {2}: (10, {}), {3}: (11, {})} | custom-call | flops 4294967296 | bytes 33554432 | tf_op jit(solution)/shard_map/numer/pallas_call | solution.py:491
  104.9 0.0 collective-permute-done.9.refs_1_
  104.9 0.0 collective-permute-done.11.refs_3_
  105.0 15.2 %numer.5 = bf16[8192,1024]{1,0:T(8,128)(2,1)} custom-call(s32[12]{0:T(128)S(1)} %stack.38.where, bf16[8192,512]{1,0:T(8,128)(2,1)} %get-tuple-element.33.pown, bf16[8192,512]{1,0:T(8,128)(2,1)} %collective-permute-done.1.psib, bf16[128,1024]{1,0:T(8,128)(2,1)S(1)} %collective-permute-done.8.refs_0_, bf16[128,1024]{1,0:T(8,128)(2,1)S(1)} %collective-permute-done.9.refs_1_, ...), custom_call_target="tpu_custom_call" | custom-call | flops 8589934592 | bytes 33554432 | tf_op jit(solution)/shard_map/numer/pallas_call | solution.py:491
Async XLA Ops:
  14.7 12.6 %collective-permute-start = (s32[200,512]{1,0:T(8,128)S(1)}, s32[200,512]{1,0:T(8,128)S(1)}, u32[]{:S(2)}, u32[]{:S(2)}) collective-permute-start(s32[200,512]{1,0:T(8,128)S(1)} %get-tuple-element.36), channel_id=1, source_target_pairs={{0,4},{4,0},{8,12},{12,8},{1,5},{5,1},{9,13},{13,9},{2,6},{6,2},{1... | collective-permute-start | bytes 1228808 | tf_op jit(solution)/shard_map/ppermute | solution.py:587
  37.1 52.4 %collective-permute-start.1 = (bf16[8192,512]{1,0:T(8,128)(2,1)}, bf16[8192,512]{1,0:T(8,128)(2,1)}, u32[]{:S(2)}, u32[]{:S(2)}) collective-permute-start(bf16[8192,512]{1,0:T(8,128)(2,1)} %get-tuple-element.37), channel_id=1, source_target_pairs={{0,1},{1,0},{2,3},{3,2},{4,5},{5,4},{6,7},{7,6},{8,9},{9,8},{10,11... | collective-permute-start | bytes 25165832 | tf_op jit(solution)/shard_map/ppermute | solution.py:587
  37.2 12.6 %collective-permute-start.2 = (s32[200,256]{1,0:T(8,128)S(1)}, s32[200,256]{1,0:T(8,128)S(1)}, u32[]{:S(2)}, u32[]{:S(2)}) collective-permute-start(s32[200,256]{1,0:T(8,128)S(1)} %get-tuple-element.39), channel_id=1, source_target_pairs={{0,4},{4,0},{8,12},{12,8},{1,5},{5,1},{9,13},{13,9},{2,6},{6,2},{1... | collective-permute-start | bytes 614408 | tf_op jit(solution)/shard_map/ppermute | solution.py:587
  39.0 18.5 %collective-permute-start.3 = (s32[200,256]{1,0:T(8,128)S(1)}, s32[200,256]{1,0:T(8,128)S(1)}, u32[]{:S(2)}, u32[]{:S(2)}) collective-permute-start(s32[200,256]{1,0:T(8,128)S(1)} %get-tuple-element.41), channel_id=1, source_target_pairs={{0,4},{4,0},{8,12},{12,8},{1,5},{5,1},{9,13},{13,9},{2,6},{6,2},{1... | collective-permute-start | bytes 614408 | tf_op jit(solution)/shard_map/ppermute | solution.py:587
  39.3 25.2 %collective-permute-start.4 = (s32[104,512]{1,0:T(8,128)S(1)}, s32[104,512]{1,0:T(8,128)S(1)}, u32[]{:S(2)}, u32[]{:S(2)}) collective-permute-start(s32[104,512]{1,0:T(8,128)S(1)} %forward.3.after), channel_id=1, source_target_pairs={{0,8},{4,12},{8,0},{12,4},{1,9},{5,13},{9,1},{13,5},{2,10},{6,14},... | collective-permute-start | bytes 638984 | tf_op jit(solution)/shard_map/ppermute | solution.py:587
  50.6 13.9 %collective-permute-start.5 = (s32[104,256]{1,0:T(8,128)S(1)}, s32[104,256]{1,0:T(8,128)S(1)}, u32[]{:S(2)}, u32[]{:S(2)}) collective-permute-start(s32[104,256]{1,0:T(8,128)S(1)} %forward.4.after), channel_id=1, source_target_pairs={{0,8},{4,12},{8,0},{12,4},{1,9},{5,13},{9,1},{13,5},{2,10},{6,14},... | collective-permute-start | bytes 319496 | tf_op jit(solution)/shard_map/ppermute | solution.py:587
  58.3 6.6 %copy-start = (s32[1024]{0:T(1024)S(1)}, s32[1024]{0:T(1024)}, u32[]{:S(2)}) copy-start(s32[1024]{0:T(1024)} %param.11) | copy-start | bytes 12292
  58.4 6.5 %copy-start.1 = (f32[8]{0:T(128)S(1)}, f32[8]{0:T(128)}, u32[]{:S(2)}) copy-start(f32[8]{0:T(128)} %table.1) | copy-start | bytes 100
  58.4 6.5 %collective-permute-start.6 = (s32[104,256]{1,0:T(8,128)S(1)}, s32[104,256]{1,0:T(8,128)S(1)}, u32[]{:S(2)}, u32[]{:S(2)}) collective-permute-start(s32[104,256]{1,0:T(8,128)S(1)} %forward.5.after), channel_id=1, source_target_pairs={{0,8},{4,12},{8,0},{12,4},{1,9},{5,13},{9,1},{13,5},{2,10},{6,14},... | collective-permute-start | bytes 319496 | tf_op jit(solution)/shard_map/ppermute | solution.py:587
  66.1 3.7 %collective-permute-start.7 = (f32[16,128]{1,0:T(8,128)S(1)}, f32[16,128]{1,0:T(8,128)S(1)}, u32[]{:S(2)}, u32[]{:S(2)}) collective-permute-start(f32[16,128]{1,0:T(8,128)S(1)} %get-tuple-element.44.own.mine), channel_id=1, source_target_pairs={{0,2},{2,0},{1,3},{3,1},{4,6},{6,4},{5,7},{7,5},{8,10},{10,8},{9,1... | collective-permute-start | bytes 24584 | tf_op jit(solution)/shard_map/ppermute | solution.py:587
  70.6 11.9 %collective-permute-start.8 = (bf16[128,1024]{1,0:T(8,128)(2,1)S(1)}, bf16[128,1024]{1,0:T(8,128)(2,1)S(1)}, u32[]{:S(2)}, u32[]{:S(2)}) collective-permute-start(bf16[128,1024]{1,0:T(8,128)(2,1)S(1)} %weights.1.refs_0_), channel_id=1, source_target_pairs={{0,8},{4,12},{8,0},{12,4},{1,9},{5,13},{9,1},{13,5},{2,10},{6,14},... | collective-permute-start | bytes 786440 | tf_op jit(solution)/shard_map/ppermute | solution.py:587
  72.1 12.4 %collective-permute-start.13 = (bf16[128,1024]{1,0:T(8,128)(2,1)S(1)}, bf16[128,1024]{1,0:T(8,128)(2,1)S(1)}, u32[]{:S(2)}, u32[]{:S(2)}) collective-permute-start(bf16[128,1024]{1,0:T(8,128)(2,1)S(1)} %weights.1.refs_0_), channel_id=1, source_target_pairs={{0,4},{4,0},{8,12},{12,8},{1,5},{5,1},{9,13},{13,9},{2,6},{6,2},{1... | collective-permute-start | bytes 786440 | tf_op jit(solution)/shard_map/ppermute | solution.py:587
  82.5 7.0 %collective-permute-start.10 = (bf16[128,1024]{1,0:T(8,128)(2,1)S(1)}, bf16[128,1024]{1,0:T(8,128)(2,1)S(1)}, u32[]{:S(2)}, u32[]{:S(2)}) collective-permute-start(bf16[128,1024]{1,0:T(8,128)(2,1)S(1)} %collective-permute-done.8.refs_0_), channel_id=1, source_target_pairs={{0,4},{4,0},{8,12},{12,8},{1,5},{5,1},{9,13},{13,9},{2,6},{6,2},{1... | collective-permute-start | bytes 786440 | tf_op jit(solution)/shard_map/ppermute | solution.py:587
  82.5 7.0 %collective-permute-start.15 = (bf16[128,1024]{1,0:T(8,128)(2,1)S(1)}, bf16[128,1024]{1,0:T(8,128)(2,1)S(1)}, u32[]{:S(2)}, u32[]{:S(2)}) collective-permute-start(bf16[128,1024]{1,0:T(8,128)(2,1)S(1)} %weights.1.refs_0_), channel_id=1, source_target_pairs={{0,1},{1,0},{2,3},{3,2},{4,5},{5,4},{6,7},{7,6},{8,9},{9,8},{10,11... | collective-permute-start | bytes 786440 | tf_op jit(solution)/shard_map/ppermute | solution.py:587
  82.5 1.9 %collective-permute-start.12 = (f32[512,1]{1,0:T(8,128)S(1)}, f32[512,1]{1,0:T(8,128)S(1)}, u32[]{:S(2)}, u32[]{:S(2)}) collective-permute-start(f32[512,1]{1,0:T(8,128)S(1)} %copy.27.phi.after.refs_2_.refs_4_), channel_id=1, source_target_pairs={{0,1},{1,0},{2,3},{3,2},{4,5},{5,4},{6,7},{7,6},{8,9},{9,8},{10,11... | collective-permute-start | bytes 6152 | tf_op jit(solution)/shard_map/ppermute | solution.py:587
  84.4 20.5 %collective-permute-start.9 = (bf16[128,1024]{1,0:T(8,128)(2,1)S(1)}, bf16[128,1024]{1,0:T(8,128)(2,1)S(1)}, u32[]{:S(2)}, u32[]{:S(2)}) collective-permute-start(bf16[128,1024]{1,0:T(8,128)(2,1)S(1)} %collective-permute-done.8.refs_0_), channel_id=1, source_target_pairs={{0,1},{1,0},{2,3},{3,2},{4,5},{5,4},{6,7},{7,6},{8,9},{9,8},{10,11... | collective-permute-start | bytes 786440 | tf_op jit(solution)/shard_map/ppermute | solution.py:587
  84.5 12.6 %collective-permute-start.14 = (bf16[128,1024]{1,0:T(8,128)(2,1)S(1)}, bf16[128,1024]{1,0:T(8,128)(2,1)S(1)}, u32[]{:S(2)}, u32[]{:S(2)}) collective-permute-start(bf16[128,1024]{1,0:T(8,128)(2,1)S(1)} %collective-permute-done.13.refs_0_), channel_id=1, source_target_pairs={{0,1},{1,0},{2,3},{3,2},{4,5},{5,4},{6,7},{7,6},{8,9},{9,8},{10,11... | collective-permute-start | bytes 786440 | tf_op jit(solution)/shard_map/ppermute | solution.py:587
  89.5 15.5 %collective-permute-start.11 = (bf16[128,1024]{1,0:T(8,128)(2,1)S(1)}, bf16[128,1024]{1,0:T(8,128)(2,1)S(1)}, u32[]{:S(2)}, u32[]{:S(2)}) collective-permute-start(bf16[128,1024]{1,0:T(8,128)(2,1)S(1)} %collective-permute-done.10.refs_2_), channel_id=1, source_target_pairs={{0,1},{1,0},{2,3},{3,2},{4,5},{5,4},{6,7},{7,6},{8,9},{9,8},{10,11... | collective-permute-start | bytes 786440 | tf_op jit(solution)/shard_map/ppermute | solution.py:587
